TPU v7x, 256 devices: a whole 4x4x8 slice. The times are simulated.
256 devices in a mesh: strip: 32 (over y, z_hi, core), seg: 8 (over x, z_lo).
Axes of the slice: x: 4, y: 4, z: 8 (z_hi: 4, z_lo: 2; z = z_hi * 2 + z_lo), core: 2. Of those that a mesh axis runs over, the one named last changes fastest.
Arguments:
- gradient: float32 [9, 32, 4096], P(None, 'strip', 'seg'), may hold values from -72 to 72
- live_blocks: int32 [32, 8], P('strip', 'seg'), may hold values from 8 to 16, as said below
- loc_cam_jac: bfloat16 [18, 6, 32, 16384], P(None, None, 'strip', 'seg'), may hold values from -0.59765625 to 0.59765625
- loc_point_jac: bfloat16 [6, 6, 32, 16384], P(None, None, 'strip', 'seg'), may hold values from -6 to 6
- loc_cams: int32 [6, 32, 16384], P(None, 'strip', 'seg'), may hold values from 0 to 511
- fwd_cam_jac: bfloat16 [2, 18, 2, 32, 32768], P(None, None, None, 'strip', 'seg'), may hold values from -0.59765625 to 0.59765625
- fwd_point_jac: bfloat16 [2, 6, 2, 32, 32768], P(None, None, None, 'strip', 'seg'), may hold values from -6 to 6
- fwd_cams: int32 [2, 2, 32, 32768], P(None, None, 'strip', 'seg'), may hold values from 0 to 511
- side_cam_jac: bfloat16 [2, 18, 2, 32, 24576], P(None, None, None, 'strip', 'seg'), may hold values from -0.59765625 to 0.59765625
- side_point_jac: bfloat16 [2, 6, 2, 32, 24576], P(None, None, None, 'strip', 'seg'), may hold values from -6 to 6
- side_cams: int32 [2, 2, 32, 24576], P(None, None, 'strip', 'seg'), may hold values from 0 to 511
Outputs:
- solution_step: float32 [9, 32, 4096], P(None, 'strip', 'seg')
- residual: float32 [9, 32, 4096], P(None, 'strip', 'seg')
Inputs may be any that keep to these rules, and one draw needn't show every extreme that they name: `live_blocks`: the largest count, 16, is reached by some segment in every draw.
All inputs are finite; a program needn't handle non-finite values.
Results may differ from a plain program's by a relative error of at most 0.0054.
Values may be sent and summed in bfloat16 or wider, within the bound.
No kernel may reach another device: no remote copies, remote signals or barrier semaphores. Data moves between devices by JAX's collectives and lax.ppermute only.
A program may use at most 128 MiB of HBM per device.

v0:
```python
import jax
import jax.numpy as jnp
from jax import lax
from jax.sharding import PartitionSpec as P

BLOCK = 128
ITERS = 2


camera_damping = 1.0
point_damping = 1.0


def from_behind(shard, axis, by):
    size = lax.axis_size(axis)
    pairs = [(i, i + by) for i in range(size) if 0 <= i + by < size]
    return lax.ppermute(shard, axis, pairs)


def partner_2(shard, axis, apart):
    return lax.ppermute(shard, axis, [(i, i ^ 1 << apart) for i in range(lax.axis_size(axis))])


def observe(cam_jac, point_jac, cam_index, vector):
    across = cam_jac.astype(jnp.float32).reshape((2, 9) + cam_index.shape)
    along = point_jac.astype(jnp.float32).reshape((2, 3) + cam_index.shape)
    cameras = vector[:, cam_index]
    predicted = jnp.sum(across * cameras[None], axis=1)
    gathered = jnp.sum(along * predicted[:, None], axis=(0, 2))
    return (predicted, gathered)


def hessian(point_jac):
    along = point_jac.astype(jnp.float32).reshape((2, 3) + point_jac.shape[1:])
    entry_pairs = [(0, 0), (0, 1), (0, 2), (1, 1), (1, 2), (2, 2)]
    return jnp.stack([jnp.sum(along[:, i] * along[:, j], axis=(0, 1)) for i, j in entry_pairs])


def invert_blocks(blocks):
    a = blocks[0] + point_damping
    b = blocks[1]
    c = blocks[2]
    d = blocks[3] + point_damping
    e = blocks[4]
    f = blocks[5] + point_damping
    first = d * f - e * e
    second = c * e - b * f
    third = b * e - c * d
    determinant = a * first + b * second + c * third
    return (
        jnp.stack([first, second, third, a * f - c * c, b * c - a * e, a * d - b * b]) / determinant
    )


def solve_blocks(inverse, summed):
    return jnp.stack(
        [
            inverse[0] * summed[0] + inverse[1] * summed[1] + inverse[2] * summed[2],
            inverse[1] * summed[0] + inverse[3] * summed[1] + inverse[4] * summed[2],
            inverse[2] * summed[0] + inverse[4] * summed[1] + inverse[5] * summed[2],
        ]
    )


def return_terms(cam_jac, point_jac, cam_index, predicted, solved, weight, columns):
    across = cam_jac.astype(jnp.float32).reshape((2, 9) + cam_index.shape)
    along = point_jac.astype(jnp.float32).reshape((2, 3) + cam_index.shape)
    fitted = jnp.sum(along * solved[None, :, None], axis=1)
    residue = (predicted - fitted) * weight
    terms = jnp.sum(across * residue[:, None], axis=0)
    return jnp.zeros((9, columns), jnp.float32).at[:, cam_index].add(terms)


def per_device(
    gradient,
    live_blocks,
    loc_cam_jac,
    loc_point_jac,
    loc_cams,
    fwd_cam_jac,
    fwd_point_jac,
    fwd_cams,
    side_cam_jac,
    side_point_jac,
    side_cams,
):
    columns = gradient.shape[2]
    seg_pos = lax.axis_index("seg")
    strip_pos = lax.axis_index("strip")
    seg_count = lax.axis_size("seg")
    flip_levels = seg_count.bit_length() - 1
    seg_ok = (seg_pos > 0).astype(jnp.float32)
    strip_ok = (strip_pos > 0).astype(jnp.float32)
    loc_cj = loc_cam_jac[:, :, 0]
    loc_pj = loc_point_jac[:, :, 0]
    loc_ix = loc_cams[:, 0]
    fwd_own = (fwd_cam_jac[0, :, :, 0], fwd_point_jac[0, :, :, 0], fwd_cams[0, :, 0])
    fwd_guest = (fwd_cam_jac[1, :, :, 0], fwd_point_jac[1, :, :, 0], fwd_cams[1, :, 0])
    side_own = (side_cam_jac[0, :, :, 0], side_point_jac[0, :, :, 0], side_cams[0, :, 0])
    side_guest = (side_cam_jac[1, :, :, 0], side_point_jac[1, :, :, 0], side_cams[1, :, 0])
    positions = jnp.arange(loc_ix.shape[1], dtype=jnp.int32) // BLOCK
    live_weight = (positions < live_blocks[0, 0]).astype(jnp.float32)

    def fwd_to_owner(values):
        return from_behind(values, "seg", -1)

    def side_to_owner(values):
        moved = from_behind(values, "strip", -1)
        for level in range(flip_levels):
            moved = partner_2(moved, "seg", level)
        return moved

    inverse_loc = invert_blocks(hessian(loc_pj))
    inverse_fwd = invert_blocks(hessian(fwd_own[1]) + fwd_to_owner(hessian(fwd_guest[1])))
    inverse_side = invert_blocks(hessian(side_own[1]) + side_to_owner(hessian(side_guest[1])))

    def squares(values):
        return lax.psum(jnp.sum(values * values), ("strip", "seg"))

    residual = -gradient[:, 0]
    solution_step = jnp.zeros_like(residual)
    direction = residual
    norm_now = squares(residual)
    for iteration in range(ITERS):
        result = camera_damping * direction
        own_pred, own_sum = observe(fwd_own[0], fwd_own[1], fwd_own[2], direction)
        guest_pred, guest_sum = observe(fwd_guest[0], fwd_guest[1], fwd_guest[2], direction)
        fwd_incoming = fwd_to_owner(guest_sum)
        side_pred, side_sum = observe(side_own[0], side_own[1], side_own[2], direction)
        partner_pred, partner_sum = observe(side_guest[0], side_guest[1], side_guest[2], direction)
        side_incoming = side_to_owner(partner_sum)
        predicted, gathered = observe(loc_cj, loc_pj, loc_ix, direction)
        solved = solve_blocks(inverse_loc, gathered)
        result = result + return_terms(
            loc_cj, loc_pj, loc_ix, predicted, solved, live_weight, columns
        )
        fwd_solved = solve_blocks(inverse_fwd, own_sum + fwd_incoming)
        result = result + return_terms(
            fwd_own[0], fwd_own[1], fwd_own[2], own_pred, fwd_solved, 1.0, columns
        )
        result = result + return_terms(
            fwd_guest[0],
            fwd_guest[1],
            fwd_guest[2],
            guest_pred,
            from_behind(fwd_solved, "seg", 1),
            seg_ok,
            columns,
        )
        side_solved = solve_blocks(inverse_side, side_sum + side_incoming)
        result = result + return_terms(
            side_own[0], side_own[1], side_own[2], side_pred, side_solved, 1.0, columns
        )
        side_moved = from_behind(side_solved.astype(jnp.bfloat16), "strip", 1).astype(
            side_solved.dtype
        )
        for side_level in range(flip_levels):
            side_moved = partner_2(side_moved.astype(jnp.bfloat16), "seg", side_level).astype(
                side_moved.dtype
            )
        result = result + return_terms(
            side_guest[0], side_guest[1], side_guest[2], partner_pred, side_moved, strip_ok, columns
        )
        alpha = norm_now / lax.psum(jnp.sum(direction * result), ("strip", "seg"))
        solution_step = solution_step + alpha * direction
        residual = residual - alpha * result
        norm_next = squares(residual)
        direction = residual + norm_next / norm_now * direction
        norm_now = norm_next
    return (solution_step[:, None], residual[:, None])


def solution(mesh):
    placed = (
        P(None, "strip", "seg"),
        P("strip", "seg"),
        P(None, None, "strip", "seg"),
        P(None, None, "strip", "seg"),
        P(None, "strip", "seg"),
        P(None, None, None, "strip", "seg"),
        P(None, None, None, "strip", "seg"),
        P(None, None, "strip", "seg"),
        P(None, None, None, "strip", "seg"),
        P(None, None, None, "strip", "seg"),
        P(None, None, "strip", "seg"),
    )
    return jax.shard_map(
        per_device,
        mesh=mesh,
        in_specs=placed,
        out_specs=(P(None, "strip", "seg"), P(None, "strip", "seg")),
        check_vma=False,
    )
```

profile of v0, /device:TPU:1, one launch (start us, length us, event | category | flops | bytes accessed | tf_op | source)
XLA Modules:
  0.0 1151.9 jit_solution(10868611863683471624)
XLA Ops:
  9.6 20.9 %gather_fusion.3 = f32[6144,9]{1,0:T(8,128)} fusion(f32[9,512]{0,1:T(8,128)S(1)} %negate_bitcast_fusion, s32[6144]{0:T(1024)S(1)} %broadcast_clamp_fusion.4), kind=kCustom, calls=%fused_computation.3 | custom fusion | bytes 466944 | tf_op jit(solution)/shard_map/gather | solution.py:27
  33.3 20.9 %gather_fusion.4 = f32[6144,9]{1,0:T(8,128)} fusion(f32[9,512]{0,1:T(8,128)S(1)} %negate_bitcast_fusion, s32[6144]{0:T(1024)S(1)} %broadcast_clamp_fusion.3), kind=kCustom, calls=%fused_computation.4 | custom fusion | bytes 466944 | tf_op jit(solution)/shard_map/gather | solution.py:27
  63.7 27.7 %gather_fusion.1 = f32[8192,9]{1,0:T(8,128)} fusion(f32[9,512]{0,1:T(8,128)S(1)} %negate_bitcast_fusion, s32[8192]{0:T(1024)S(1)} %broadcast_clamp_fusion.2), kind=kCustom, calls=%fused_computation.1 | custom fusion | bytes 622592 | tf_op jit(solution)/shard_map/gather | solution.py:27
  95.5 27.7 %gather_fusion.2 = f32[8192,9]{1,0:T(8,128)} fusion(f32[9,512]{0,1:T(8,128)S(1)} %negate_bitcast_fusion, s32[8192]{0:T(1024)S(1)} %broadcast_clamp_fusion.1), kind=kCustom, calls=%fused_computation.2 | custom fusion | bytes 622592 | tf_op jit(solution)/shard_map/gather | solution.py:27
  131.4 41.0 %gather_fusion = f32[12288,9]{1,0:T(8,128)} fusion(f32[9,512]{0,1:T(8,128)S(1)} %negate_bitcast_fusion, s32[12288]{0:T(1024)S(1)} %broadcast_clamp_fusion), kind=kCustom, calls=%fused_computation | custom fusion | bytes 933888 | tf_op jit(solution)/shard_map/gather | solution.py:27
  192.9 66.3 %scatter_fusion = f32[9,512]{0,1:T(8,128)S(1)} fusion(f32[9,512]{0,1:T(8,128)S(1)} %negate_bitcast_fusion, s32[12288]{0:T(1024)S(1)} %bitcast.213, f32[12288,9]{1,0:T(8,128)} %bitcast.156), kind=kCustom, calls=%fused_computation.10 | custom fusion | flops 110592 | bytes 1376256 | tf_op jit(solution)/shard_map/scatter-add | solution.py:71
  272.6 44.4 %scatter_custom_fusion.1 = f32[9,512]{0,1:T(8,128)S(1)} fusion(s32[8192]{0:T(1024)} %bitcast.234, f32[8192,9]{1,0:T(8,128)} %bitcast.185, f32[]{:T(128)} %constant.13.clone.1), kind=kCustom, calls=%fused_computation.102 | custom fusion | flops 73728 | bytes 18944 | tf_op jit(solution)/shard_map/scatter-add | solution.py:71
  330.1 10.0 collective-permute-start.11
  343.2 44.4 %scatter_fusion.1 = f32[9,512]{0,1:T(8,128)S(1)} fusion(f32[9,512]{0,1:T(8,128)S(1)} %add.455, s32[8192]{0:T(1024)} %bitcast.228, f32[8192,9]{1,0:T(8,128)} %bitcast.179), kind=kCustom, calls=%fused_computation.12 | custom fusion | flops 73728 | bytes 917504 | tf_op jit(solution)/shard_map/scatter-add | solution.py:71
  395.9 33.5 %scatter_custom_fusion.3 = f32[9,512]{0,1:T(8,128)S(1)} fusion(s32[6144]{0:T(1024)} %bitcast.237, f32[6144,9]{1,0:T(8,128)} %bitcast.193, f32[]{:T(128)} %constant.13.clone.1), kind=kCustom, calls=%fused_computation.100 | custom fusion | flops 55296 | bytes 18944 | tf_op jit(solution)/shard_map/scatter-add | solution.py:71
  433.7 33.6 %scatter_fusion.2 = f32[9,512]{0,1:T(8,128)S(1)} fusion(f32[9,512]{0,1:T(8,128)S(1)} %add.471, s32[6144]{0:T(1024)} %bitcast.231, f32[6144,9]{1,0:T(8,128)} %bitcast.191), kind=kCustom, calls=%fused_computation.14 | custom fusion | flops 55296 | bytes 688128 | tf_op jit(solution)/shard_map/scatter-add | solution.py:71
  467.9 79.7 %all-reduce = (f32[]{:T(128)}, f32[]{:T(128)}) all-reduce(f32[]{:T(128)} %multiply_reduce_fusion.51, f32[]{:T(128)} %multiply_reduce_fusion.4), channel_id=1, replica_groups=mesh['strip'=32,'seg'=8] {'strip','seg'}, use_global_device_ids=true, to_apply=%region_1.2 | all-reduce | flops 2 | bytes 16 | tf_op jit(solution)/shard_map/psum | solution.py:118
  549.7 72.8 %psum.30 = f32[]{:T(128)} all-reduce(f32[]{:T(128)} %multiply_reduce_fusion.3), channel_id=1, replica_groups=mesh['strip'=32,'seg'=8] {'strip','seg'}, use_global_device_ids=true, to_apply=%region_65.66 | all-reduce | flops 1 | bytes 8 | tf_op jit(solution)/shard_map/psum | solution.py:118
  623.8 20.9 %gather_fusion.8 = f32[6144,9]{1,0:T(8,128)} fusion(f32[9,512]{0,1:T(8,128)S(1)} %multiply_add_fusion, s32[6144]{0:T(1024)S(1)} %copy-done.43), kind=kCustom, calls=%fused_computation.8 | custom fusion | bytes 466944 | tf_op jit(solution)/shard_map/gather | solution.py:27
  644.8 20.9 %gather_fusion.9 = f32[6144,9]{1,0:T(8,128)} fusion(f32[9,512]{0,1:T(8,128)S(1)} %multiply_add_fusion, s32[6144]{0:T(1024)S(1)} %copy-done.45), kind=kCustom, calls=%fused_computation.9 | custom fusion | bytes 466944 | tf_op jit(solution)/shard_map/gather | solution.py:27
  665.7 27.7 %gather_fusion.6 = f32[8192,9]{1,0:T(8,128)} fusion(f32[9,512]{0,1:T(8,128)S(1)} %multiply_add_fusion, s32[8192]{0:T(1024)S(1)} %copy-done.39), kind=kCustom, calls=%fused_computation.6 | custom fusion | bytes 622592 | tf_op jit(solution)/shard_map/gather | solution.py:27
  693.4 27.7 %gather_fusion.7 = f32[8192,9]{1,0:T(8,128)} fusion(f32[9,512]{0,1:T(8,128)S(1)} %multiply_add_fusion, s32[8192]{0:T(1024)S(1)} %copy-done.41), kind=kCustom, calls=%fused_computation.7 | custom fusion | bytes 622592 | tf_op jit(solution)/shard_map/gather | solution.py:27
  721.0 41.0 %gather_fusion.5 = f32[12288,9]{1,0:T(8,128)} fusion(f32[9,512]{0,1:T(8,128)S(1)} %multiply_add_fusion, s32[12288]{0:T(1024)S(1)} %copy-done.14), kind=kCustom, calls=%fused_computation.5 | custom fusion | bytes 933888 | tf_op jit(solution)/shard_map/gather | solution.py:27
  810.6 66.1 %scatter_fusion.3 = f32[9,512]{0,1:T(8,128)S(1)} fusion(f32[9,512]{0,1:T(8,128)S(1)} %copy-done.2, s32[12288]{0:T(1024)S(1)} %bitcast.214, f32[12288,9]{1,0:T(8,128)} %bitcast.155), kind=kCustom, calls=%fused_computation.15 | custom fusion | flops 110592 | bytes 1376256 | tf_op jit(solution)/shard_map/scatter-add | solution.py:71
  885.4 44.4 %scatter_custom_fusion.6 = f32[9,512]{0,1:T(8,128)S(1)} fusion(s32[8192]{0:T(1024)} %bitcast.235, f32[8192,9]{1,0:T(8,128)} %bitcast.184, f32[]{:T(128)} %constant.13.clone.1), kind=kCustom, calls=%fused_computation.98 | custom fusion | flops 73728 | bytes 18944 | tf_op jit(solution)/shard_map/scatter-add | solution.py:71
  948.8 44.4 %scatter_fusion.4 = f32[9,512]{0,1:T(8,128)S(1)} fusion(f32[9,512]{0,1:T(8,128)S(1)} %add.486, s32[8192]{0:T(1024)S(1)} %bitcast.229, f32[8192,9]{1,0:T(8,128)} %bitcast.178), kind=kCustom, calls=%fused_computation.17 | custom fusion | flops 73728 | bytes 917504 | tf_op jit(solution)/shard_map/scatter-add | solution.py:71
  1003.7 33.5 %scatter_custom_fusion.8 = f32[9,512]{0,1:T(8,128)S(1)} fusion(s32[6144]{0:T(1024)} %bitcast.238, f32[6144,9]{1,0:T(8,128)} %bitcast.192, f32[]{:T(128)} %constant.13.clone.1), kind=kCustom, calls=%fused_computation.96 | custom fusion | flops 55296 | bytes 18944 | tf_op jit(solution)/shard_map/scatter-add | solution.py:71
  1040.0 33.6 %scatter_fusion.5 = f32[9,512]{0,1:T(8,128)S(1)} fusion(f32[9,512]{0,1:T(8,128)S(1)} %add.494, s32[6144]{0:T(1024)S(1)} %bitcast.232, f32[6144,9]{1,0:T(8,128)} %bitcast.190), kind=kCustom, calls=%fused_computation.19 | custom fusion | flops 55296 | bytes 688128 | tf_op jit(solution)/shard_map/scatter-add | solution.py:71
  1074.3 74.6 %psum.31 = f32[]{:T(128)} all-reduce(f32[]{:T(128)} %multiply_reduce_fusion.2), channel_id=1, replica_groups=mesh['strip'=32,'seg'=8] {'strip','seg'}, use_global_device_ids=true, to_apply=%region_97.98 | all-reduce | flops 1 | bytes 8 | tf_op jit(solution)/shard_map/psum | solution.py:164
  (321 shorter events, 187.3 us)
Async XLA Ops:
  2.7 258.3 %collective-permute-start.3 = (f32[6,3072]{1,0:T(8,128)}, f32[6,3072]{1,0:T(8,128)}, u32[]{:S(2)}, u32[]{:S(2)}) collective-permute-start(f32[6,3072]{1,0:T(8,128)} %stack.178), channel_id=1, source_target_pairs={{8,0},{16,8},{24,16},{32,24},{40,32},{48,40},{56,48},{64,56},{72,6... | collective-permute-start | bytes 221192 | tf_op jit(solution)/shard_map/ppermute | solution.py:17
  58.9 123.0 %collective-permute-start.7 = (f32[3,3072]{1,0:T(4,128)}, f32[3,3072]{1,0:T(4,128)}, u32[]{:S(2)}, u32[]{:S(2)}) collective-permute-start(f32[3,3072]{1,0:T(4,128)} %reduce_sum.792), channel_id=1, source_target_pairs={{8,0},{16,8},{24,16},{32,24},{40,32},{48,40},{56,48},{64,56},{72,6... | collective-permute-start | bytes 110600 | tf_op jit(solution)/shard_map/ppermute | solution.py:17
  62.3 201.4 %collective-permute-start = (f32[6,4096]{1,0:T(8,128)}, f32[6,4096]{1,0:T(8,128)}, u32[]{:S(2)}, u32[]{:S(2)}) collective-permute-start(f32[6,4096]{1,0:T(8,128)} %stack.162), channel_id=1, source_target_pairs={{1,0},{2,1},{3,2},{4,3},{5,4},{6,5},{7,6},{9,8},{10,9},{11,10},{12... | collective-permute-start | bytes 294920 | tf_op jit(solution)/shard_map/ppermute | solution.py:17
  128.9 131.2 %collective-permute-start.1 = (f32[3,4096]{1,0:T(4,128)}, f32[3,4096]{1,0:T(4,128)}, u32[]{:S(2)}, u32[]{:S(2)}) collective-permute-start(f32[3,4096]{1,0:T(4,128)} %reduce_sum.768), channel_id=1, source_target_pairs={{1,0},{2,1},{3,2},{4,3},{5,4},{6,5},{7,6},{9,8},{10,9},{11,10},{12... | collective-permute-start | bytes 147464 | tf_op jit(solution)/shard_map/ppermute | solution.py:17
  181.9 79.2 %collective-permute-start.8 = (f32[3,3072]{1,0:T(4,128)}, f32[3,3072]{1,0:T(4,128)}, u32[]{:S(2)}, u32[]{:S(2)}) collective-permute-start(f32[3,3072]{1,0:T(4,128)} %collective-permute-done.7), channel_id=1, source_target_pairs={{0,1},{1,0},{2,3},{3,2},{4,5},{5,4},{6,7},{7,6},{8,9},{9,8},{10,11... | collective-permute-start | bytes 110600 | tf_op jit(solution)/shard_map/ppermute | solution.py:21
  261.0 58.6 %collective-permute-start.4 = (f32[6,3072]{1,0:T(8,128)}, f32[6,3072]{1,0:T(8,128)}, u32[]{:S(2)}, u32[]{:S(2)}) collective-permute-start(f32[6,3072]{1,0:T(8,128)} %collective-permute-done.3), channel_id=1, source_target_pairs={{0,1},{1,0},{2,3},{3,2},{4,5},{5,4},{6,7},{7,6},{8,9},{9,8},{10,11... | collective-permute-start | bytes 221192 | tf_op jit(solution)/shard_map/ppermute | solution.py:21
  261.1 55.9 %collective-permute-start.9 = (f32[3,3072]{1,0:T(4,128)}, f32[3,3072]{1,0:T(4,128)}, u32[]{:S(2)}, u32[]{:S(2)}) collective-permute-start(f32[3,3072]{1,0:T(4,128)} %collective-permute-done.8), channel_id=1, source_target_pairs={{0,2},{1,3},{2,0},{3,1},{4,6},{5,7},{6,4},{7,5},{8,10},{9,11},{10,... | collective-permute-start | bytes 110600 | tf_op jit(solution)/shard_map/ppermute | solution.py:21
  265.8 53.8 %collective-permute-start.2 = (f32[3,4096]{1,0:T(4,128)}, f32[3,4096]{1,0:T(4,128)}, u32[]{:S(2)}, u32[]{:S(2)}) collective-permute-start(f32[3,4096]{1,0:T(4,128)} %pad_maximum_fusion), channel_id=1, source_target_pairs={{0,1},{1,2},{2,3},{3,4},{4,5},{5,6},{6,7},{8,9},{9,10},{10,11},{11... | collective-permute-start | bytes 147464 | tf_op jit(solution)/shard_map/ppermute | solution.py:17
  317.0 8.0 collective-permute-start.10
  319.6 3.7 collective-permute-start.5
  323.3 5.0 collective-permute-start.6
  330.1 57.5 %collective-permute-start.11 = (bf16[3,3072]{1,0:T(4,128)(2,1)S(1)}, bf16[3,3072]{1,0:T(4,128)(2,1)S(1)}, u32[]{:S(2)}, u32[]{:S(2)}) collective-permute-start(bf16[3,3072]{1,0:T(4,128)(2,1)S(1)} %fusion.36), channel_id=1, source_target_pairs={{0,8},{8,16},{16,24},{24,32},{32,40},{40,48},{48,56},{56,64},{64,7... | collective-permute-start | bytes 55304 | tf_op jit(solution)/shard_map/ppermute | solution.py:17
  387.6 3.0 collective-permute-start.12
  390.6 2.8 collective-permute-start.13
  393.4 36.1 %collective-permute-start.14 = (bf16[3,3072]{1,0:T(4,128)(2,1)}, bf16[3,3072]{1,0:T(4,128)(2,1)}, u32[]{:S(2)}, u32[]{:S(2)}) collective-permute-start(bf16[3,3072]{1,0:T(4,128)(2,1)} %collective-permute-done.13), channel_id=1, source_target_pairs={{0,4},{1,5},{2,6},{3,7},{4,0},{5,1},{6,2},{7,3},{8,12},{9,13},{10,... | collective-permute-start | bytes 55304 | tf_op jit(solution)/shard_map/ppermute | solution.py:21
  773.3 103.4 %collective-permute-start.17 = (f32[3,3072]{1,0:T(4,128)}, f32[3,3072]{1,0:T(4,128)}, u32[]{:S(2)}, u32[]{:S(2)}) collective-permute-start(f32[3,3072]{1,0:T(4,128)} %reduce_sum.824), channel_id=1, source_target_pairs={{8,0},{16,8},{24,16},{32,24},{40,32},{48,40},{56,48},{64,56},{72,6... | collective-permute-start | bytes 110600 | tf_op jit(solution)/shard_map/ppermute | solution.py:17
  790.5 88.7 %collective-permute-start.15 = (f32[3,4096]{1,0:T(4,128)}, f32[3,4096]{1,0:T(4,128)}, u32[]{:S(2)}, u32[]{:S(2)}) collective-permute-start(f32[3,4096]{1,0:T(4,128)} %reduce_sum.812), channel_id=1, source_target_pairs={{1,0},{2,1},{3,2},{4,3},{5,4},{6,5},{7,6},{9,8},{10,9},{11,10},{12... | collective-permute-start | bytes 147464 | tf_op jit(solution)/shard_map/ppermute | solution.py:17
  876.8 53.0 %collective-permute-start.18 = (f32[3,3072]{1,0:T(4,128)}, f32[3,3072]{1,0:T(4,128)S(1)}, u32[]{:S(2)}, u32[]{:S(2)}) collective-permute-start(f32[3,3072]{1,0:T(4,128)} %collective-permute-done.17), channel_id=1, source_target_pairs={{0,1},{1,0},{2,3},{3,2},{4,5},{5,4},{6,7},{7,6},{8,9},{9,8},{10,11... | collective-permute-start | bytes 110600 | tf_op jit(solution)/shard_map/ppermute | solution.py:21
  880.2 52.3 %collective-permute-start.16 = (f32[3,4096]{1,0:T(4,128)S(1)}, f32[3,4096]{1,0:T(4,128)S(1)}, u32[]{:S(2)}, u32[]{:S(2)}) collective-permute-start(f32[3,4096]{1,0:T(4,128)S(1)} %pad_maximum_fusion.1), channel_id=1, source_target_pairs={{0,1},{1,2},{2,3},{3,4},{4,5},{5,6},{6,7},{8,9},{9,10},{10,11},{11... | collective-permute-start | bytes 147464 | tf_op jit(solution)/shard_map/ppermute | solution.py:17
  929.8 4.7 collective-permute-start.19
  934.5 4.4 collective-permute-start.20
  939.1 54.2 %collective-permute-start.21 = (bf16[3,3072]{1,0:T(4,128)(2,1)S(1)}, bf16[3,3072]{1,0:T(4,128)(2,1)S(1)}, u32[]{:S(2)}, u32[]{:S(2)}) collective-permute-start(bf16[3,3072]{1,0:T(4,128)(2,1)S(1)} %fusion.35), channel_id=1, source_target_pairs={{0,8},{8,16},{16,24},{24,32},{32,40},{40,48},{48,56},{56,64},{64,7... | collective-permute-start | bytes 55304 | tf_op jit(solution)/shard_map/ppermute | solution.py:17
  996.0 3.0 collective-permute-start.23
  999.0 38.3 %collective-permute-start.24 = (bf16[3,3072]{1,0:T(4,128)(2,1)S(1)}, bf16[3,3072]{1,0:T(4,128)(2,1)S(1)}, u32[]{:S(2)}, u32[]{:S(2)}) collective-permute-start(bf16[3,3072]{1,0:T(4,128)(2,1)S(1)} %collective-permute-done.23), channel_id=1, source_target_pairs={{0,4},{1,5},{2,6},{3,7},{4,0},{5,1},{6,2},{7,3},{8,12},{9,13},{10,... | collective-permute-start | bytes 55304 | tf_op jit(solution)/shard_map/ppermute | solution.py:21
  (56 other events, 2689.2 us)
where the time goes:
time: 1160 us; the launch traced here: 1150 us
  other arithmetic  488 us (42%)
  local copies, waits for them, and re-layouts  356 us (31%)
  blocking collectives  227 us (20%)
  starting transfers between devices  56.6 us (5%)
  waiting for transfers between devices  17.4 us (1%)
    scatter-add x10, other arithmetic, return_terms(): return jnp.zeros((9, columns), jnp.float32).at[:, cam_index].add(terms)  444 us
    gather x20, local copies, waits for them, and re-layouts, observe(): cameras = vector[:, cam_index]  311 us
    psum x2, blocking collectives, squares(): return lax.psum(jnp.sum(values * values), ('strip', 'seg'))  152 us
    psum x1, blocking collectives, per_device(): alpha = norm_now / lax.psum(jnp.sum(direction * result), ('strip', 'seg'))  74.6 us
    ppermute x10, starting transfers between devices, from_behind(): return lax.ppermute(shard, axis, pairs)  35.1 us
    reduce_sum x10, local copies, waits for them, and re-layouts, return_terms(): terms = jnp.sum(across * residue[:, None], axis=0)  29.3 us
  transfers between devices with their start and end apart: 25, of which 8 were waited for; matrix products, arithmetic and copies ran while one was open for 53% of the time, Pallas kernels for 0%

commit v1 on v0

v1 whole, which is shorter than its diff:
```python
import jax
import jax.numpy as jnp
from jax import lax
from jax.experimental import pallas as pl
from jax.experimental.pallas import tpu as pltpu
from jax.sharding import PartitionSpec as P

AXES = ("strip", "seg")
LANES = 128
JAC = 9
PAGES = 4
ROWS = JAC * PAGES
LIFT = 40
STACK = 2 * LIFT
STEP = 16
SYM = ((0, 0), (0, 1), (0, 2), (1, 1), (1, 2), (2, 2))
DAMP = 1.0
VMEM = pl.BlockSpec(memory_space=pltpu.VMEM)
SMEM = pl.BlockSpec(memory_space=pltpu.SMEM)
F32 = jnp.float32


def fetch(table, index):
    lane = index & (LANES - 1)
    odd = (index & LANES) != 0
    upper = index >= 2 * LANES
    found = []
    for j in range(JAC):
        page = [
            jnp.take_along_axis(
                jnp.broadcast_to(table[pl.ds(PAGES * j + k, 1), :], index.shape), lane, axis=1
            )
            for k in range(PAGES)
        ]
        low = jnp.where(odd, page[1], page[0])
        high = jnp.where(odd, page[3], page[2])
        found.append(jnp.where(upper, high, low))
    return found


def predict(across, values):
    return [sum(across[JAC * r + j] * values[j] for j in range(JAC)) for r in range(2)]


def project(along, seen):
    return [along[k] * seen[0] + along[3 + k] * seen[1] for k in range(3)]


def normal(along):
    return [along[i] * along[j] + along[3 + i] * along[3 + j] for i, j in SYM]


def invert(h):
    a, b, c, d, e, f = h[0] + DAMP, h[1], h[2], h[3] + DAMP, h[4], h[5] + DAMP
    first = d * f - e * e
    second = c * e - b * f
    third = b * e - c * d
    scale = 1.0 / (a * first + b * second + c * third)
    return [
        m * scale for m in (first, second, third, a * f - c * c, b * c - a * e, a * d - b * b)
    ]


def solve(m, b):
    return [
        m[0] * b[0] + m[1] * b[1] + m[2] * b[2],
        m[1] * b[0] + m[3] * b[1] + m[4] * b[2],
        m[2] * b[0] + m[4] * b[1] + m[5] * b[2],
    ]


def residue(along, seen, z):
    return [seen[r] - sum(along[3 * r + k] * z[k] for k in range(3)) for r in range(2)]


def spread(terms, index, stage, total):
    count = index.shape[0]
    page = index >> 7
    hit = [page == h for h in range(PAGES)]
    for j in range(JAC):
        coarse = terms[j].astype(jnp.bfloat16).astype(F32)
        fine = terms[j] - coarse
        for h in range(PAGES):
            row = PAGES * j + h
            stage[pl.ds(row, count, stride=STACK), :] = jnp.where(hit[h], coarse, 0.0)
            stage[pl.ds(LIFT + row, count, stride=STACK), :] = jnp.where(hit[h], fine, 0.0)
    lane = (index & (LANES - 1)).astype(F32)
    place = lax.broadcasted_iota(jnp.int32, (LANES, LANES), 0).astype(F32).astype(jnp.bfloat16)
    one, none = jnp.ones((), jnp.bfloat16), jnp.zeros((), jnp.bfloat16)
    group = 4 if count % 4 == 0 else 3
    for start in range(0, count, group):
        left, right = [], []
        for row in range(start, start + group):
            left.append(stage[pl.ds(row * STACK, STACK), :].astype(jnp.bfloat16))
            wide = jnp.broadcast_to(lane[row : row + 1], (16, LANES)).astype(jnp.bfloat16)
            wide = jnp.concatenate([wide] * (LANES // 16), axis=0)
            right.append(jnp.where(wide == place, one, none))
        total[...] += lax.dot_general(
            jnp.concatenate(left, axis=1),
            jnp.concatenate(right, axis=1),
            (((1,), (1,)), ((), ())),
            preferred_element_type=F32,
        )


def folded(total):
    return total[0:ROWS, :] + total[LIFT : LIFT + ROWS, :]


def weave(cams, index):
    half = cams.shape[2]
    for s in range(2):
        for o in range(2):
            index[s, pl.ds(o, half, stride=2), :] = cams[s, o]


def pair_look(cam, point, index, table, seen_out, loose, sums, with_h, squares, weights):
    rows = cam.shape[2]
    half = rows // 2
    for s in range(2):

        def body(i, carry, s=s):
            at = pl.ds(pl.multiple_of(i * STEP, STEP), STEP)
            across = [cam[s, j, at, :].astype(F32) for j in range(2 * JAC)]
            along = [point[s, j, at, :].astype(F32) for j in range(6)]
            seen = predict(across, fetch(table, index[s, at, :]))
            for r in range(2):
                seen_out[s, r, at, :] = seen[r]
            parts = project(along, seen)
            if with_h:
                parts = parts + normal(along)
            for n, part in enumerate(parts):
                loose[n, at, :] = part
            if squares is not None:
                squares[...] += weights[s] * (seen[0] * seen[0] + seen[1] * seen[1])
            return carry

        lax.fori_loop(0, rows // STEP, body, 0)
        for n in range(9 if with_h else 3):
            sums[s, n] = (
                loose[n, pl.ds(0, half, stride=2), :] + loose[n, pl.ds(1, half, stride=2), :]
            )


def pair_return(cam, point, index, seen_in, z, weights, stage, total):
    rows = cam.shape[2]
    for s in range(2):

        def body(i, carry, s=s):
            at = pl.ds(pl.multiple_of(i * STEP, STEP), STEP)
            across = [cam[s, j, at, :].astype(F32) for j in range(2 * JAC)]
            along = [point[s, j, at, :].astype(F32) for j in range(6)]
            left = residue(
                along, [seen_in[s, r, at, :] for r in range(2)], [z[s, k, at, :] for k in range(3)]
            )
            left = [weights[s] * e for e in left]
            terms = [across[j] * left[0] + across[JAC + j] * left[1] for j in range(JAC)]
            spread(terms, index[s, at, :], stage, total)
            return carry

        lax.fori_loop(0, rows // STEP, body, 0)


def pair_solve(mine, other, inverse_out, inverse_in, z, products, weights):
    half = mine.shape[2]
    for s in range(2):
        for i in range(half // 8):
            at = pl.ds(8 * i, 8)
            b = [mine[s, k, at, :] + other[s][k, at, :] for k in range(3)]
            if inverse_in is None:
                inverse = invert(
                    [mine[s, 3 + k, at, :] + other[s][3 + k, at, :] for k in range(6)]
                )
                for k in range(6):
                    inverse_out[s, k, at, :] = inverse[k]
            else:
                inverse = [inverse_in[s, k, at, :] for k in range(6)]
            solved = solve(inverse, b)
            if products is not None:
                products[...] += weights[s] * sum(
                    mine[s, k, at, :] * solved[k] for k in range(3)
                )
            for k in range(3):
                for o in range(2):
                    z[s, k, pl.ds(16 * i + o, 8, stride=2), :] = solved[k]


def look_kernel(
    table, fcam, fpoint, fcams, scam, spoint, scams,
    fseen, fsums, sseen, ssums,
    findex, sindex, floose, sloose,
):
    weave(fcams, findex)
    weave(scams, sindex)
    pair_look(fcam, fpoint, findex, table, fseen, floose, fsums, True, None, None)
    pair_look(scam, spoint, sindex, table, sseen, sloose, ssums, True, None, None)


def local_kernel(live, table, cam, point, cams, out, product, stage, total):
    total[...] = jnp.zeros_like(total)
    stage[...] = jnp.zeros_like(stage)
    product[...] = jnp.zeros_like(product)
    watched = cams.shape[0] // 16

    def body(i, carry):
        at = pl.ds(pl.multiple_of(i * LANES, LANES), LANES)
        index = cams[pl.ds(i, watched, stride=16), :]
        across = [cam[j, :, at].astype(F32) for j in range(2 * JAC)]
        along = [point[j, :, at].astype(F32) for j in range(6)]
        seen = predict(across, fetch(table, index))
        summed = [jnp.sum(x, axis=0, keepdims=True) for x in project(along, seen) + normal(along)]
        z = solve(invert(summed[3:]), summed[:3])
        left = residue(along, seen, z)
        terms = [across[j] * left[0] + across[JAC + j] * left[1] for j in range(JAC)]
        product[0:1, :] += jnp.sum(seen[0] * left[0] + seen[1] * left[1], axis=0, keepdims=True)
        spread(terms, index, stage, total)
        return carry

    lax.fori_loop(0, live[0], body, 0)
    out[...] = folded(total)


def middle_kernel(
    weights, table, extra, fcam, fpoint, fcams, scam, spoint, scams,
    fseen, fsums, fown, fguest, sseen, ssums, sown, sguest,
    result, finverse, sinverse, fseen2, fsums2, sseen2, ssums2, dots,
    findex, sindex, floose, sloose, fz, sz, stage, total, squares,
):
    weave(fcams, findex)
    weave(scams, sindex)
    total[...] = jnp.zeros_like(total)
    stage[...] = jnp.zeros_like(stage)
    fweights = (1.0, weights[0])
    sweights = (1.0, weights[1])
    pair_solve(fsums, (fown, fguest), finverse, None, fz, None, None)
    pair_return(fcam, fpoint, findex, fseen, fz, fweights, stage, total)
    pair_solve(ssums, (sown, sguest), sinverse, None, sz, None, None)
    pair_return(scam, spoint, sindex, sseen, sz, sweights, stage, total)
    step = folded(total) + extra[...]
    result[...] = step
    squares[...] = jnp.zeros_like(squares)
    pair_look(fcam, fpoint, findex, result, fseen2, floose, fsums2, False, squares, fweights)
    pair_look(scam, spoint, sindex, result, sseen2, sloose, ssums2, False, squares, sweights)
    base = table[...]
    dots[...] = jnp.zeros_like(dots)
    for row, value in enumerate((base * base, base * step, step * step, squares[...])):
        dots[row : row + 1, :] = jnp.sum(value, axis=0, keepdims=True)


def dots_kernel(
    weights, dots, product, fsums, fown, fguest, finverse, ssums, sown, sguest, sinverse,
    fz, sz, out, products,
):
    products[...] = jnp.zeros_like(products)
    pair_solve(fsums, (fown, fguest), None, finverse, fz, products, (1.0, weights[0]))
    pair_solve(ssums, (sown, sguest), None, sinverse, sz, products, (1.0, weights[1]))
    curve = dots[3:4, :] + product[0:1, :] - jnp.sum(products[...], axis=0, keepdims=True)
    rows = jnp.concatenate([dots[0:3, :], curve], axis=0)
    sums = jnp.sum(rows, axis=1, keepdims=True)
    place = lax.broadcasted_iota(jnp.int32, (1, LANES), 1)
    line = jnp.zeros((1, LANES), F32)
    for n in range(4):
        line = line + jnp.where(place == n, sums[n : n + 1, :], 0.0)
    out[...] = jnp.broadcast_to(line, out.shape)


def last_kernel(
    weights, extra, fcam, fpoint, fcams, scam, spoint, scams, fseen, fz, sseen, sz,
    result, findex, sindex, stage, total,
):
    weave(fcams, findex)
    weave(scams, sindex)
    total[...] = jnp.zeros_like(total)
    stage[...] = jnp.zeros_like(stage)
    pair_return(fcam, fpoint, findex, fseen, fz, (1.0, weights[0]), stage, total)
    pair_return(scam, spoint, sindex, sseen, sz, (1.0, weights[1]), stage, total)
    result[...] = folded(total) + extra[...]


def close_kernel(sums, base, first, second, step_out, residual_out):
    line = jnp.sum(sums[...], axis=0, keepdims=True)
    place = lax.broadcasted_iota(jnp.int32, line.shape, 1)
    rr, bp, pp, curve = [
        jnp.sum(jnp.where(place == n, line, 0.0), axis=1, keepdims=True) for n in range(4)
    ]
    whole = rr + bp
    alpha = rr / whole
    rest = bp / whole
    new = alpha * (alpha * pp - rest * bp)
    gamma = rest + new / rr
    bend = gamma * gamma * rr - 2.0 * gamma * alpha * bp + alpha * alpha * pp
    bend = bend + gamma * gamma * bp - 2.0 * gamma * alpha * pp + alpha * alpha * curve
    again = new / bend
    d0, p, t = base[...], first[...], second[...]
    direction = gamma * d0 - alpha * p
    image = gamma * d0 + (gamma - alpha) * p - alpha * t
    step_out[...] = -(alpha * d0 + again * direction)
    residual_out[...] = -(rest * d0 - alpha * p - again * image)


def call(kernel, ins, outs, scratch, flops, name):
    outs = [jax.ShapeDtypeStruct(shape, F32) for shape in outs]
    specs = [SMEM if i == 0 and x.ndim == 1 else VMEM for i, x in enumerate(ins)]
    return pl.pallas_call(
        kernel,
        out_shape=outs,
        in_specs=specs,
        out_specs=[VMEM] * len(outs),
        scratch_shapes=scratch,
        compiler_params=pltpu.CompilerParams(vmem_limit_bytes=40 << 20),
        cost_estimate=pl.CostEstimate(flops=flops, bytes_accessed=2 << 20, transcendentals=0),
        name=name,
    )(*ins)


def rows_of(array):
    kinds, parts, two, _, points = array.shape
    array = array.reshape(kinds, parts, two, points // LANES, LANES)
    return array.transpose(0, 1, 3, 2, 4).reshape(kinds, parts, two * points // LANES, LANES)


def per_device(
    gradient, live_blocks, loc_cam_jac, loc_point_jac, loc_cams,
    fwd_cam_jac, fwd_point_jac, fwd_cams, side_cam_jac, side_point_jac, side_cams,
):
    strips, segs = lax.axis_size("strip"), lax.axis_size("seg")
    cells = [(s, g) for s in range(strips) for g in range(segs)]

    def pairs(move):
        found = []
        for s, g in cells:
            t, h = move(s, g)
            if 0 <= t < strips and 0 <= h < segs:
                found.append((s * segs + g, t * segs + h))
        return found

    fwd_down = pairs(lambda s, g: (s, g - 1))
    fwd_up = pairs(lambda s, g: (s, g + 1))
    side_down = pairs(lambda s, g: (s - 1, segs - 1 - g))
    side_up = pairs(lambda s, g: (s + 1, segs - 1 - g))

    weights = jnp.stack(
        [(lax.axis_index("seg") > 0).astype(F32), (lax.axis_index("strip") > 0).astype(F32)]
    )
    base = gradient.reshape(ROWS, LANES)
    live = live_blocks.reshape(1)
    lcam, lpoint = loc_cam_jac[:, :, 0], loc_point_jac[:, :, 0]
    lcams = loc_cams.reshape(-1, LANES)
    fcam, fpoint = rows_of(fwd_cam_jac), rows_of(fwd_point_jac)
    scam, spoint = rows_of(side_cam_jac), rows_of(side_point_jac)
    fcams = fwd_cams.reshape(2, 2, -1, LANES)
    scams = side_cams.reshape(2, 2, -1, LANES)
    fr, sr = fcam.shape[2], scam.shape[2]
    watched = lcam.shape[1]

    def both(values, up, down):
        return lax.ppermute(values[1], AXES, down), lax.ppermute(values[0], AXES, up)

    index_scratch = [pltpu.VMEM((2, fr, LANES), jnp.int32), pltpu.VMEM((2, sr, LANES), jnp.int32)]
    z_scratch = [pltpu.VMEM((2, 3, fr, LANES), F32), pltpu.VMEM((2, 3, sr, LANES), F32)]
    total_scratch = [pltpu.VMEM((STEP * STACK, LANES), F32), pltpu.VMEM((STACK, LANES), F32)]

    fseen, fsums, sseen, ssums = call(
        look_kernel,
        [base, fcam, fpoint, fcams, scam, spoint, scams],
        [(2, 2, fr, LANES), (2, 9, fr // 2, LANES), (2, 2, sr, LANES), (2, 9, sr // 2, LANES)],
        index_scratch + [pltpu.VMEM((9, fr, LANES), F32), pltpu.VMEM((9, sr, LANES), F32)],
        10**9,
        "look",
    )
    fown, fguest = both(fsums, fwd_up, fwd_down)
    sown, sguest = both(ssums, side_up, side_down)

    def local(table):
        return call(
            local_kernel,
            [live, table, lcam, lpoint, lcams],
            [(ROWS, LANES), (8, LANES)],
            [pltpu.VMEM((watched * STACK, LANES), F32), pltpu.VMEM((STACK, LANES), F32)],
            5 * 10**9,
            "local",
        )

    extra, _ = local(base)
    p, finverse, sinverse, fseen, fsums, sseen, ssums, dots = call(
        middle_kernel,
        [weights, base, extra, fcam, fpoint, fcams, scam, spoint, scams,
         fseen, fsums, fown, fguest, sseen, ssums, sown, sguest],
        [(ROWS, LANES), (2, 6, fr // 2, LANES), (2, 6, sr // 2, LANES),
         (2, 2, fr, LANES), (2, 3, fr // 2, LANES), (2, 2, sr, LANES), (2, 3, sr // 2, LANES),
         (8, LANES)],
        index_scratch + [pltpu.VMEM((3, fr, LANES), F32), pltpu.VMEM((3, sr, LANES), F32)]
        + z_scratch + total_scratch + [pltpu.VMEM((STEP, LANES), F32)],
        10**10,
        "middle",
    )
    fown, fguest = both(fsums, fwd_up, fwd_down)
    sown, sguest = both(ssums, side_up, side_down)
    extra, product = local(p)
    fz, sz, line = call(
        dots_kernel,
        [weights, dots, product, fsums, fown, fguest, finverse, ssums, sown, sguest, sinverse],
        [(2, 3, fr, LANES), (2, 3, sr, LANES), (segs, LANES)],
        [pltpu.VMEM((8, LANES), F32)],
        10**8,
        "dots",
    )
    line = lax.all_to_all(line, "seg", 0, 0, tiled=True)
    line = jnp.broadcast_to(jnp.sum(line, axis=0, keepdims=True), (strips, LANES))
    line = lax.all_to_all(line, "strip", 0, 0, tiled=True)
    (t,) = call(
        last_kernel,
        [weights, extra, fcam, fpoint, fcams, scam, spoint, scams, fseen, fz, sseen, sz],
        [(ROWS, LANES)],
        index_scratch + total_scratch,
        5 * 10**9,
        "last",
    )
    step, residual = call(
        close_kernel, [line, base, p, t], [(ROWS, LANES)] * 2, [], 10**6, "close"
    )
    return step.reshape(gradient.shape), residual.reshape(gradient.shape)


def solution(mesh):
    placed = (
        P(None, "strip", "seg"),
        P("strip", "seg"),
        P(None, None, "strip", "seg"),
        P(None, None, "strip", "seg"),
        P(None, "strip", "seg"),
        P(None, None, None, "strip", "seg"),
        P(None, None, None, "strip", "seg"),
        P(None, None, "strip", "seg"),
        P(None, None, None, "strip", "seg"),
        P(None, None, None, "strip", "seg"),
        P(None, None, "strip", "seg"),
    )
    return jax.shard_map(
        per_device,
        mesh=mesh,
        in_specs=placed,
        out_specs=(P(None, "strip", "seg"), P(None, "strip", "seg")),
        check_vma=False,
    )
```

time: 1160 us -> 101 us (0.09)
  other arithmetic: 488 us -> 0.91 us
  local copies, waits for them, and re-layouts: 356 us -> 9.43 us
  blocking collectives: 227 us -> 10.8 us
  Pallas kernels: 0 us -> 32 us
  waiting for transfers between devices: 17.4 us -> 2.39 us
  starting transfers between devices: 56.6 us -> 43.2 us
    scatter-add x10 -> x0, other arithmetic: 444 us -> none  [return_terms(): return jnp.zeros((9, columns), jnp.float32).at[:, cam_index].add(terms)]
    gather x20 -> x0, local copies, waits for them, and re-layouts: 311 us -> none  [observe(): cameras = vector[:, cam_index]]
    psum x3 -> x0, blocking collectives: 227 us -> none  [the longest x2 152 us: squares(): return lax.psum(jnp.sum(values * values), ('strip', 'seg'))]
    reduce_sum x20 -> x0, local copies, waits for them, and re-layouts: 35.9 us -> none  [the longest x10 29.3 us: return_terms(): terms = jnp.sum(across * residue[:, None], axis=0)]
    pallas_call x0 -> x7, Pallas kernels: none -> 32 us  [call(): pl.pallas_call(kernel, out_shape=outs, in_specs=specs, out_specs=[VMEM] *...]
    reduce_sum x55 -> x1, other arithmetic: 30.8 us -> 0.03 us  [per_device(): jnp.sum(line, axis=0, keepdims=True)]
    ppermute x25 -> x8, starting transfers between devices: 56.6 us -> 27.2 us  [the longest x4 20.8 us: both(): lax.ppermute(values[0], AXES, up)]
    ppermute x25 -> x8, waiting for transfers between devices: 17.4 us -> 0.02 us  [the longest x4 0.01 us: both(): lax.ppermute(values[0], AXES, up)]
  transfers between devices with their start and end apart: 25 -> 9, of which waited for: 8 -> 1; matrix products, arithmetic and copies ran while one was open for 53% -> 1% of each run, Pallas kernels for 0% -> 19%
where the time goes in v1:
time: 101 us; the launch traced here: 100 us
  starting transfers between devices  43.2 us (43%)
  Pallas kernels  32 us (32%)
  blocking collectives  10.8 us (11%)
  local copies, waits for them, and re-layouts  9.43 us (9%)
  waiting for transfers between devices  2.39 us (2%)
  between operations  1.66 us (2%)
    pallas_call x7, Pallas kernels, call(): pl.pallas_call(kernel, out_shape=outs, in_specs=specs, out_specs=[VMEM] *...  32 us
    ppermute x4, starting transfers between devices, both(): lax.ppermute(values[0], AXES, up)  20.8 us
    all_to_all x1, starting transfers between devices, per_device(): line = lax.all_to_all(line, 'strip', 0, 0, tiled=True)  16 us
    all_to_all x1, blocking collectives, per_device(): line = lax.all_to_all(line, 'seg', 0, 0, tiled=True)  10.8 us
    ppermute x4, starting transfers between devices, both(): lax.ppermute(values[1], AXES, down)  6.42 us
    unnamed x38, local copies, waits for them, and re-layouts  6.12 us
    all_to_all x1, waiting for transfers between devices, per_device(): line = lax.all_to_all(line, 'strip', 0, 0, tiled=True)  2.37 us
  transfers between devices with their start and end apart: 9, of which 1 were waited for; matrix products, arithmetic and copies ran while one was open for 1% of the time, Pallas kernels for 19%

profile of v1, /device:TPU:1, one launch (start us, length us, event | category | flops | bytes accessed | tf_op | source)
XLA Modules:
  0.0 100.4 jit_solution(5714218741470273754)
XLA Ops:
  0.6 0.8 reduce.1
  1.5 1.1 %copy-done.1 = bf16[2,18,2,1,4096]{4,2,3,1,0:T(2,128)(2,1)S(1)} copy-done((bf16[2,18,2,1,4096]{4,2,3,1,0:T(2,128)(2,1)S(1)}, bf16[2,18,2,1,4096]{4,2,3,1,0:T(2,128)(2,1)}, u32[]{:S(2)}) %copy-start.1) | copy-done | bytes 589848
  2.6 1.0 %copy-done.3 = bf16[2,18,2,1,3072]{4,2,3,1,0:T(2,128)(2,1)S(1)} copy-done((bf16[2,18,2,1,3072]{4,2,3,1,0:T(2,128)(2,1)S(1)}, bf16[2,18,2,1,3072]{4,2,3,1,0:T(2,128)(2,1)}, u32[]{:S(2)}) %copy-start.3) | copy-done | bytes 442392
  3.6 0.9 copy-done.6
  4.5 0.9 copy-done.8
  5.4 2.3 %look.1 = (f32[2,2,64,128]{3,2,1,0:T(8,128)S(1)}, f32[2,9,32,128]{3,2,1,0:T(8,128)S(1)}, f32[2,2,48,128]{3,2,1,0:T(8,128)S(1)}, f32[2,9,24,128]{3,2,1,0:T(8,128)S(1)}) custom-call(f32[36,128]{1,0:T(8,128)S(1)} %reshape.57.table.base, bf16[2,18,64,128]{3,2,1,0:T(8,128)(2,1)S(1)} %bitcast.54, bf16[2,6,64,128]{3,2,1,0:T(8,128)(2,1)S(1)} %bitcast.62, ...), custom_call_target="tpu_custom_call" | custom-call | flops 1000000000 | bytes 2097152 | tf_op jit(solution)/shard_map/look/pallas_call | solution.py:304
  8.4 0.7 slice_bitcast_fusion.2
  9.1 9.8 %collective-permute-start.3 = (f32[9,24,128]{2,1,0:T(8,128)}, f32[9,24,128]{2,1,0:T(8,128)S(1)}, u32[]{:S(2)}, u32[]{:S(2)}) collective-permute-start(f32[9,24,128]{2,1,0:T(8,128)} %get-tuple-element.50), channel_id=1, source_target_pairs={{0,15},{1,14},{2,13},{3,12},{4,11},{5,10},{6,9},{7,8},{8,23},{9,22... | collective-permute-start | bytes 331784 | tf_op jit(solution)/shard_map/ppermute | solution.py:357
  18.9 1.9 %collective-permute-start.2 = (f32[9,24,128]{2,1,0:T(8,128)}, f32[9,24,128]{2,1,0:T(8,128)S(1)}, u32[]{:S(2)}, u32[]{:S(2)}) collective-permute-start(f32[9,24,128]{2,1,0:T(8,128)} %get-tuple-element.51), channel_id=1, source_target_pairs={{8,7},{9,6},{10,5},{11,4},{12,3},{13,2},{14,1},{15,0},{16,15},{17,... | collective-permute-start | bytes 331784 | tf_op jit(solution)/shard_map/ppermute | solution.py:357
  20.8 0.7 slice_bitcast_fusion
  21.6 1.3 %collective-permute-start.1 = (f32[9,32,128]{2,1,0:T(8,128)}, f32[9,32,128]{2,1,0:T(8,128)S(1)}, u32[]{:S(2)}, u32[]{:S(2)}) collective-permute-start(f32[9,32,128]{2,1,0:T(8,128)} %get-tuple-element.48), channel_id=1, source_target_pairs={{0,1},{1,2},{2,3},{3,4},{4,5},{5,6},{6,7},{8,9},{9,10},{10,11},{11... | collective-permute-start | bytes 442376 | tf_op jit(solution)/shard_map/ppermute | solution.py:357
  22.9 1.3 %collective-permute-start = (f32[9,32,128]{2,1,0:T(8,128)}, f32[9,32,128]{2,1,0:T(8,128)S(1)}, u32[]{:S(2)}, u32[]{:S(2)}) collective-permute-start(f32[9,32,128]{2,1,0:T(8,128)} %get-tuple-element.49), channel_id=1, source_target_pairs={{1,0},{2,1},{3,2},{4,3},{5,4},{6,5},{7,6},{9,8},{10,9},{11,10},{12... | collective-permute-start | bytes 442376 | tf_op jit(solution)/shard_map/ppermute | solution.py:357
  24.9 6.6 %local.2 = (f32[36,128]{1,0:T(8,128)S(1)}, f32[8,128]{1,0:T(8,128)}) custom-call(s32[1]{0:T(128)} %bitcast.48.live, f32[36,128]{1,0:T(8,128)S(1)} %reshape.57.table.base, bf16[18,6,2048]{2,1,0:T(8,128)(2,1)S(1)} %bitcast.52, bf16[6,6,2048]{2,1,0:T(8,128)(2,1)S(1)} %bitcast.60, s32[96,128]{1,0:T(8,128)S(1)} %bitcast.71), custom_call_target="tpu_custom_call" | custom-call | flops 5000000000 | bytes 2097152 | tf_op jit(solution)/shard_map/local/pallas_call | solution.py:304
  31.7 0.9 copy-done.14
  32.6 9.3 %middle.1 = (f32[36,128]{1,0:T(8,128)S(1)}, f32[2,6,32,128]{3,2,1,0:T(8,128)S(1)}, f32[2,6,24,128]{3,2,1,0:T(8,128)S(1)}, f32[2,2,64,128]{3,2,1,0:T(8,128)S(1)},...) custom-call(f32[2]{0:T(128)S(1)} %add_convert_fusion.weights, ...), custom_call_target="tpu_custom_call" | custom-call | flops 10000000000 | bytes 2097152 | tf_op jit(solution)/shard_map/middle/pallas_call | solution.py:304
  42.5 8.2 %collective-permute-start.7 = (f32[3,24,128]{2,1,0:T(8,128)S(1)}, f32[3,24,128]{2,1,0:T(8,128)S(1)}, u32[]{:S(2)}, u32[]{:S(2)}) collective-permute-start(f32[3,24,128]{2,1,0:T(8,128)S(1)} %get-tuple-element.54), channel_id=1, source_target_pairs={{0,15},{1,14},{2,13},{3,12},{4,11},{5,10},{6,9},{7,8},{8,23},{9,22... | collective-permute-start | bytes 110600 | tf_op jit(solution)/shard_map/ppermute | solution.py:357
  50.7 1.9 %collective-permute-start.6 = (f32[3,24,128]{2,1,0:T(8,128)S(1)}, f32[3,24,128]{2,1,0:T(8,128)S(1)}, u32[]{:S(2)}, u32[]{:S(2)}) collective-permute-start(f32[3,24,128]{2,1,0:T(8,128)S(1)} %get-tuple-element.55), channel_id=1, source_target_pairs={{8,7},{9,6},{10,5},{11,4},{12,3},{13,2},{14,1},{15,0},{16,15},{17,... | collective-permute-start | bytes 110600 | tf_op jit(solution)/shard_map/ppermute | solution.py:357
  52.6 1.5 %collective-permute-start.5 = (f32[3,32,128]{2,1,0:T(8,128)S(1)}, f32[3,32,128]{2,1,0:T(8,128)S(1)}, u32[]{:S(2)}, u32[]{:S(2)}) collective-permute-start(f32[3,32,128]{2,1,0:T(8,128)S(1)} %get-tuple-element.52), channel_id=1, source_target_pairs={{0,1},{1,2},{2,3},{3,4},{4,5},{5,6},{6,7},{8,9},{9,10},{10,11},{11... | collective-permute-start | bytes 147464 | tf_op jit(solution)/shard_map/ppermute | solution.py:357
  54.1 1.3 %collective-permute-start.4 = (f32[3,32,128]{2,1,0:T(8,128)S(1)}, f32[3,32,128]{2,1,0:T(8,128)S(1)}, u32[]{:S(2)}, u32[]{:S(2)}) collective-permute-start(f32[3,32,128]{2,1,0:T(8,128)S(1)} %get-tuple-element.53), channel_id=1, source_target_pairs={{1,0},{2,1},{3,2},{4,3},{5,4},{6,5},{7,6},{9,8},{10,9},{11,10},{12... | collective-permute-start | bytes 147464 | tf_op jit(solution)/shard_map/ppermute | solution.py:357
  55.4 6.0 %local.3 = (f32[36,128]{1,0:T(8,128)S(1)}, f32[8,128]{1,0:T(8,128)S(1)}) custom-call(s32[1]{0:T(128)} %bitcast.49.live, f32[36,128]{1,0:T(8,128)S(1)} %get-tuple-element.28.table.first, bf16[18,6,2048]{2,1,0:T(8,128)(2,1)S(1)} %bitcast.53, bf16[6,6,2048]{2,1,0:T(8,128)(2,1)S(1)} %bitcast.61, s32[96,128]{1,0:T(8,128)S(1)} %bitcast.72), custom_call_target="tpu_custom_call" | custom-call | flops 5000000000 | bytes 2097152 | tf_op jit(solution)/shard_map/local/pallas_call | solution.py:304
  62.2 10.8 %all_to_all.17 = f32[8,1,128]{2,1,0:T(1,128)S(1)} all-to-all(f32[8,1,128]{2,1,0:T(1,128)S(1)} %bitcast.51), channel_id=1, replica_groups=mesh['strip'=32,'seg'=8] {'seg'}, dimensions={0} | all-to-all | bytes 8192 | tf_op jit(solution)/shard_map/all_to_all | solution.py:408
  73.7 16.0 %all-to-all-start.1 = ((f32[32,1,128]{2,1,0:T(1,128)}), f32[32,1,128]{2,1,0:T(1,128)S(1)}, u32[]{:S(2)}, u32[]{:S(2)}) async-start(f32[32,1,128]{2,1,0:T(1,128)} %broadcast_in_dim.2), calls=%async_computation.1 | async-start | bytes 32768 | tf_op jit(solution)/shard_map/all_to_all | solution.py:410
  89.7 6.9 %last.1.second = f32[36,128]{1,0:T(8,128)S(1)} custom-call(f32[2]{0:T(128)S(1)} %add_convert_fusion.weights, f32[36,128]{1,0:T(8,128)S(1)} %get-tuple-element.35.extra, bf16[2,18,64,128]{3,2,1,0:T(8,128)(2,1)S(1)} %bitcast.56, bf16[2,6,64,128]{3,2,1,0:T(8,128)(2,1)S(1)} %bitcast.64, s32[2,2,32,128]{3,2,1,0:T(8,128)S(1)} %bitcast.70, ...), custom_call_target="tpu_custom_call" | custom-call | flops 5000000000 | bytes 2097152 | tf_op jit(solution)/shard_map/last/pallas_call | solution.py:304
  96.6 2.4 %all-to-all-done.1 = f32[32,1,128]{2,1,0:T(1,128)S(1)} async-done(((f32[32,1,128]{2,1,0:T(1,128)}), f32[32,1,128]{2,1,0:T(1,128)S(1)}, u32[]{:S(2)}, u32[]{:S(2)}) %all-to-all-start.1) | async-done | bytes 16416 | tf_op jit(solution)/shard_map/all_to_all | solution.py:410
  (51 shorter events, 4.2 us)
Async XLA Ops:
  1.5 1.1 %copy-start.1 = (bf16[2,18,2,1,4096]{4,2,3,1,0:T(2,128)(2,1)S(1)}, bf16[2,18,2,1,4096]{4,2,3,1,0:T(2,128)(2,1)}, u32[]{:S(2)}) copy-start(bf16[2,18,2,1,4096]{4,2,3,1,0:T(2,128)(2,1)} %param.16) | copy-start | bytes 1769476
  2.6 1.0 %copy-start.3 = (bf16[2,18,2,1,3072]{4,2,3,1,0:T(2,128)(2,1)S(1)}, bf16[2,18,2,1,3072]{4,2,3,1,0:T(2,128)(2,1)}, u32[]{:S(2)}) copy-start(bf16[2,18,2,1,3072]{4,2,3,1,0:T(2,128)(2,1)} %param.19) | copy-start | bytes 1327108
  3.6 0.9 copy-start.6
  4.5 0.9 copy-start.8
  8.4 16.5 %copy-start = (bf16[18,6,1,2048]{3,1,2,0:T(8,128)(2,1)S(1)}, bf16[18,6,1,2048]{3,1,2,0:T(8,128)(2,1)}, u32[]{:S(2)}) copy-start(bf16[18,6,1,2048]{3,1,2,0:T(8,128)(2,1)} %param.13) | copy-start | bytes 1327108
  9.1 22.6 %collective-permute-start.3 = (f32[9,24,128]{2,1,0:T(8,128)}, f32[9,24,128]{2,1,0:T(8,128)S(1)}, u32[]{:S(2)}, u32[]{:S(2)}) collective-permute-start(f32[9,24,128]{2,1,0:T(8,128)} %get-tuple-element.50), channel_id=1, source_target_pairs={{0,15},{1,14},{2,13},{3,12},{4,11},{5,10},{6,9},{7,8},{8,23},{9,22... | collective-permute-start | bytes 331784 | tf_op jit(solution)/shard_map/ppermute | solution.py:357
  18.9 12.7 %collective-permute-start.2 = (f32[9,24,128]{2,1,0:T(8,128)}, f32[9,24,128]{2,1,0:T(8,128)S(1)}, u32[]{:S(2)}, u32[]{:S(2)}) collective-permute-start(f32[9,24,128]{2,1,0:T(8,128)} %get-tuple-element.51), channel_id=1, source_target_pairs={{8,7},{9,6},{10,5},{11,4},{12,3},{13,2},{14,1},{15,0},{16,15},{17,... | collective-permute-start | bytes 331784 | tf_op jit(solution)/shard_map/ppermute | solution.py:357
  20.8 4.0 %copy-start.5 = (bf16[6,6,1,2048]{3,1,2,0:T(8,128)(2,1)S(1)}, bf16[6,6,1,2048]{3,1,2,0:T(8,128)(2,1)}, u32[]{:S(2)}) copy-start(bf16[6,6,1,2048]{3,1,2,0:T(8,128)(2,1)} %param.14) | copy-start | bytes 442372
  20.8 4.0 %copy-start.11 = (s32[6,1,2048]{2,1,0:T(1,128)S(1)}, s32[6,1,2048]{2,1,0:T(1,128)}, u32[]{:S(2)}) copy-start(s32[6,1,2048]{2,1,0:T(1,128)} %param.15) | copy-start | bytes 147460
  21.6 10.0 %collective-permute-start.1 = (f32[9,32,128]{2,1,0:T(8,128)}, f32[9,32,128]{2,1,0:T(8,128)S(1)}, u32[]{:S(2)}, u32[]{:S(2)}) collective-permute-start(f32[9,32,128]{2,1,0:T(8,128)} %get-tuple-element.48), channel_id=1, source_target_pairs={{0,1},{1,2},{2,3},{3,4},{4,5},{5,6},{6,7},{8,9},{9,10},{10,11},{11... | collective-permute-start | bytes 442376 | tf_op jit(solution)/shard_map/ppermute | solution.py:357
  22.9 8.8 %collective-permute-start = (f32[9,32,128]{2,1,0:T(8,128)}, f32[9,32,128]{2,1,0:T(8,128)S(1)}, u32[]{:S(2)}, u32[]{:S(2)}) collective-permute-start(f32[9,32,128]{2,1,0:T(8,128)} %get-tuple-element.49), channel_id=1, source_target_pairs={{1,0},{2,1},{3,2},{4,3},{5,4},{6,5},{7,6},{9,8},{10,9},{11,10},{12... | collective-permute-start | bytes 442376 | tf_op jit(solution)/shard_map/ppermute | solution.py:357
  24.8 6.8 %copy-start.2 = (bf16[2,18,2,1,4096]{4,2,3,1,0:T(2,128)(2,1)S(1)}, bf16[2,18,2,1,4096]{4,2,3,1,0:T(2,128)(2,1)}, u32[]{:S(2)}) copy-start(bf16[2,18,2,1,4096]{4,2,3,1,0:T(2,128)(2,1)} %param.16) | copy-start | bytes 1769476
  24.9 6.8 %copy-start.4 = (bf16[2,18,2,1,3072]{4,2,3,1,0:T(2,128)(2,1)S(1)}, bf16[2,18,2,1,3072]{4,2,3,1,0:T(2,128)(2,1)}, u32[]{:S(2)}) copy-start(bf16[2,18,2,1,3072]{4,2,3,1,0:T(2,128)(2,1)} %param.19) | copy-start | bytes 1327108
  24.9 6.8 %copy-start.7 = (bf16[2,6,2,1,4096]{4,2,3,1,0:T(2,128)(2,1)S(1)}, bf16[2,6,2,1,4096]{4,2,3,1,0:T(2,128)(2,1)}, u32[]{:S(2)}) copy-start(bf16[2,6,2,1,4096]{4,2,3,1,0:T(2,128)(2,1)} %param.17) | copy-start | bytes 589828
  24.9 6.8 %copy-start.9 = (bf16[2,6,2,1,3072]{4,2,3,1,0:T(2,128)(2,1)S(1)}, bf16[2,6,2,1,3072]{4,2,3,1,0:T(2,128)(2,1)}, u32[]{:S(2)}) copy-start(bf16[2,6,2,1,3072]{4,2,3,1,0:T(2,128)(2,1)} %param.20) | copy-start | bytes 442372
  31.7 0.9 copy-start.14
  41.9 10.8 %copy-start.17 = (f32[2,2,48,128]{3,2,1,0:T(8,128)}, f32[2,2,48,128]{3,2,1,0:T(8,128)S(1)}, u32[]{:S(2)}) copy-start(f32[2,2,48,128]{3,2,1,0:T(8,128)S(1)} %get-tuple-element.38.sseen) | copy-start | bytes 294916
  42.5 19.0 %collective-permute-start.7 = (f32[3,24,128]{2,1,0:T(8,128)S(1)}, f32[3,24,128]{2,1,0:T(8,128)S(1)}, u32[]{:S(2)}, u32[]{:S(2)}) collective-permute-start(f32[3,24,128]{2,1,0:T(8,128)S(1)} %get-tuple-element.54), channel_id=1, source_target_pairs={{0,15},{1,14},{2,13},{3,12},{4,11},{5,10},{6,9},{7,8},{8,23},{9,22... | collective-permute-start | bytes 110600 | tf_op jit(solution)/shard_map/ppermute | solution.py:357
  50.7 10.8 %collective-permute-start.6 = (f32[3,24,128]{2,1,0:T(8,128)S(1)}, f32[3,24,128]{2,1,0:T(8,128)S(1)}, u32[]{:S(2)}, u32[]{:S(2)}) collective-permute-start(f32[3,24,128]{2,1,0:T(8,128)S(1)} %get-tuple-element.55), channel_id=1, source_target_pairs={{8,7},{9,6},{10,5},{11,4},{12,3},{13,2},{14,1},{15,0},{16,15},{17,... | collective-permute-start | bytes 110600 | tf_op jit(solution)/shard_map/ppermute | solution.py:357
  52.6 8.9 %collective-permute-start.5 = (f32[3,32,128]{2,1,0:T(8,128)S(1)}, f32[3,32,128]{2,1,0:T(8,128)S(1)}, u32[]{:S(2)}, u32[]{:S(2)}) collective-permute-start(f32[3,32,128]{2,1,0:T(8,128)S(1)} %get-tuple-element.52), channel_id=1, source_target_pairs={{0,1},{1,2},{2,3},{3,4},{4,5},{5,6},{6,7},{8,9},{9,10},{10,11},{11... | collective-permute-start | bytes 147464 | tf_op jit(solution)/shard_map/ppermute | solution.py:357
  54.1 7.4 %collective-permute-start.4 = (f32[3,32,128]{2,1,0:T(8,128)S(1)}, f32[3,32,128]{2,1,0:T(8,128)S(1)}, u32[]{:S(2)}, u32[]{:S(2)}) collective-permute-start(f32[3,32,128]{2,1,0:T(8,128)S(1)} %get-tuple-element.53), channel_id=1, source_target_pairs={{1,0},{2,1},{3,2},{4,3},{5,4},{6,5},{7,6},{9,8},{10,9},{11,10},{12... | collective-permute-start | bytes 147464 | tf_op jit(solution)/shard_map/ppermute | solution.py:357
  61.5 28.2 %copy-start.16 = (f32[2,2,64,128]{3,2,1,0:T(8,128)S(1)}, f32[2,2,64,128]{3,2,1,0:T(8,128)}, u32[]{:S(2)}) copy-start(f32[2,2,64,128]{3,2,1,0:T(8,128)} %copy-done.15) | copy-start | bytes 393220
  61.5 28.2 %copy-start.18 = (f32[2,2,48,128]{3,2,1,0:T(8,128)S(1)}, f32[2,2,48,128]{3,2,1,0:T(8,128)}, u32[]{:S(2)}) copy-start(f32[2,2,48,128]{3,2,1,0:T(8,128)} %copy-done.17) | copy-start | bytes 294916
  73.7 25.3 %all-to-all-start.1 = ((f32[32,1,128]{2,1,0:T(1,128)}), f32[32,1,128]{2,1,0:T(1,128)S(1)}, u32[]{:S(2)}, u32[]{:S(2)}) async-start(f32[32,1,128]{2,1,0:T(1,128)} %broadcast_in_dim.2), calls=%async_computation.1 | async-start | bytes 32768 | tf_op jit(solution)/shard_map/all_to_all | solution.py:410
  (4 other events, 3.0 us)

commit v2 on v1

--- a/solution.py
+++ b/solution.py
@@ -17,6 +17,7 @@
 DAMP = 1.0
 VMEM = pl.BlockSpec(memory_space=pltpu.VMEM)
 SMEM = pl.BlockSpec(memory_space=pltpu.SMEM)
+FAR = pl.BlockSpec(memory_space=pltpu.HBM)
 F32 = jnp.float32
 
 
@@ -114,7 +115,7 @@
             index[s, pl.ds(o, half, stride=2), :] = cams[s, o]
 
 
-def pair_look(cam, point, index, table, seen_out, loose, sums, with_h, squares, weights):
+def pair_look(cam, point, index, table, seen_out, loose, sums, sends, odd, with_h, squares, weights):
     rows = cam.shape[2]
     half = rows // 2
     for s in range(2):
@@ -141,6 +142,13 @@
                 loose[n, pl.ds(0, half, stride=2), :] + loose[n, pl.ds(1, half, stride=2), :]
             )
 
+    for flag in range(2):
+
+        @pl.when((odd > 0.5) == (flag == 1))
+        def _(flag=flag):
+            for s in range(2):
+                sends[s ^ flag][...] = sums[s]
+
 
 def pair_return(cam, point, index, seen_in, z, weights, stage, total):
     rows = cam.shape[2]
@@ -161,16 +169,19 @@
         lax.fori_loop(0, rows // STEP, body, 0)
 
 
-def pair_solve(mine, other, inverse_out, inverse_in, z, products, weights):
+def pair_solve(mine, met, odd, inverse_out, inverse_in, z, products, weights):
     half = mine.shape[2]
     for s in range(2):
+        first = (odd > 0.5) == (s == 1)
         for i in range(half // 8):
             at = pl.ds(8 * i, 8)
-            b = [mine[s, k, at, :] + other[s][k, at, :] for k in range(3)]
+
+            def joined(k, at=at, first=first):
+                return mine[s, k, at, :] + jnp.where(first, met[0][k, at, :], met[1][k, at, :])
+
+            b = [joined(k) for k in range(3)]
             if inverse_in is None:
-                inverse = invert(
-                    [mine[s, 3 + k, at, :] + other[s][3 + k, at, :] for k in range(6)]
-                )
+                inverse = invert([joined(3 + k) for k in range(6)])
                 for k in range(6):
                     inverse_out[s, k, at, :] = inverse[k]
             else:
@@ -186,14 +197,36 @@
 
 
 def look_kernel(
-    table, fcam, fpoint, fcams, scam, spoint, scams,
-    fseen, fsums, sseen, ssums,
-    findex, sindex, floose, sloose,
+    weights, gradient, fcam_at, fpoint_at, fcams_at, scam_at, spoint_at, scams_at,
+    table, fseen, fsums, fsend0, fsend1, sseen, ssums, ssend0, ssend1,
+    lines, fcam, fpoint, fcams, scam, spoint, scams, findex, sindex, floose, sloose, arrived,
 ):
+    moves = [
+        pltpu.make_async_copy(source, target, arrived.at[n])
+        for n, (source, target) in enumerate(
+            (
+                (gradient, lines), (fcams_at, fcams), (scams_at, scams), (fcam_at, fcam),
+                (fpoint_at, fpoint), (scam_at, scam), (spoint_at, spoint),
+            )
+        )
+    ]
+    for move in moves:
+        move.start()
+    for move in moves[:3]:
+        move.wait()
+    for j in range(JAC):
+        for k in range(PAGES):
+            table[pl.ds(PAGES * j + k, 1), :] = lines[j, :, pl.ds(LANES * k, LANES)]
     weave(fcams, findex)
     weave(scams, sindex)
-    pair_look(fcam, fpoint, findex, table, fseen, floose, fsums, True, None, None)
-    pair_look(scam, spoint, sindex, table, sseen, sloose, ssums, True, None, None)
+    for move in moves[3:5]:
+        move.wait()
+    sends = (fsend0, fsend1)
+    pair_look(fcam, fpoint, findex, table, fseen, floose, fsums, sends, weights[2], True, None, None)
+    for move in moves[5:]:
+        move.wait()
+    sends = (ssend0, ssend1)
+    pair_look(scam, spoint, sindex, table, sseen, sloose, ssums, sends, weights[3], True, None, None)
 
 
 def local_kernel(live, table, cam, point, cams, out, product, stage, total):
@@ -222,8 +255,9 @@
 
 def middle_kernel(
     weights, table, extra, fcam, fpoint, fcams, scam, spoint, scams,
-    fseen, fsums, fown, fguest, sseen, ssums, sown, sguest,
-    result, finverse, sinverse, fseen2, fsums2, sseen2, ssums2, dots,
+    fseen, fsums, fmet0, fmet1, sseen, ssums, smet0, smet1,
+    result, finverse, sinverse, fseen2, fsums2, fsend0, fsend1,
+    sseen2, ssums2, ssend0, ssend1, dots,
     findex, sindex, floose, sloose, fz, sz, stage, total, squares,
 ):
     weave(fcams, findex)
@@ -232,15 +266,23 @@
     stage[...] = jnp.zeros_like(stage)
     fweights = (1.0, weights[0])
     sweights = (1.0, weights[1])
-    pair_solve(fsums, (fown, fguest), finverse, None, fz, None, None)
+    pair_solve(fsums, (fmet0, fmet1), weights[2], finverse, None, fz, None, None)
     pair_return(fcam, fpoint, findex, fseen, fz, fweights, stage, total)
-    pair_solve(ssums, (sown, sguest), sinverse, None, sz, None, None)
+    pair_solve(ssums, (smet0, smet1), weights[3], sinverse, None, sz, None, None)
     pair_return(scam, spoint, sindex, sseen, sz, sweights, stage, total)
     step = folded(total) + extra[...]
     result[...] = step
     squares[...] = jnp.zeros_like(squares)
-    pair_look(fcam, fpoint, findex, result, fseen2, floose, fsums2, False, squares, fweights)
-    pair_look(scam, spoint, sindex, result, sseen2, sloose, ssums2, False, squares, sweights)
+    sends = (fsend0, fsend1)
+    pair_look(
+        fcam, fpoint, findex, result, fseen2, floose, fsums2, sends, weights[2], False,
+        squares, fweights,
+    )
+    sends = (ssend0, ssend1)
+    pair_look(
+        scam, spoint, sindex, result, sseen2, sloose, ssums2, sends, weights[3], False,
+        squares, sweights,
+    )
     base = table[...]
     dots[...] = jnp.zeros_like(dots)
     for row, value in enumerate((base * base, base * step, step * step, squares[...])):
@@ -248,12 +290,16 @@
 
 
 def dots_kernel(
-    weights, dots, product, fsums, fown, fguest, finverse, ssums, sown, sguest, sinverse,
+    weights, dots, product, fsums, fmet0, fmet1, finverse, ssums, smet0, smet1, sinverse,
     fz, sz, out, products,
 ):
     products[...] = jnp.zeros_like(products)
-    pair_solve(fsums, (fown, fguest), None, finverse, fz, products, (1.0, weights[0]))
-    pair_solve(ssums, (sown, sguest), None, sinverse, sz, products, (1.0, weights[1]))
+    pair_solve(
+        fsums, (fmet0, fmet1), weights[2], None, finverse, fz, products, (1.0, weights[0])
+    )
+    pair_solve(
+        ssums, (smet0, smet1), weights[3], None, sinverse, sz, products, (1.0, weights[1])
+    )
     curve = dots[3:4, :] + product[0:1, :] - jnp.sum(products[...], axis=0, keepdims=True)
     rows = jnp.concatenate([dots[0:3, :], curve], axis=0)
     sums = jnp.sum(rows, axis=1, keepdims=True)
@@ -294,20 +340,25 @@
     d0, p, t = base[...], first[...], second[...]
     direction = gamma * d0 - alpha * p
     image = gamma * d0 + (gamma - alpha) * p - alpha * t
-    step_out[...] = -(alpha * d0 + again * direction)
-    residual_out[...] = -(rest * d0 - alpha * p - again * image)
-
-
-def call(kernel, ins, outs, scratch, flops, name):
+    step = -(alpha * d0 + again * direction)
+    residual = -(rest * d0 - alpha * p - again * image)
+    for j in range(JAC):
+        for k in range(PAGES):
+            row = PAGES * j + k
+            step_out[j, :, pl.ds(LANES * k, LANES)] = step[row : row + 1, :]
+            residual_out[j, :, pl.ds(LANES * k, LANES)] = residual[row : row + 1, :]
+
+
+def call(kernel, ins, outs, scratch, flops, name, place=VMEM, room=12):
     outs = [jax.ShapeDtypeStruct(shape, F32) for shape in outs]
-    specs = [SMEM if i == 0 and x.ndim == 1 else VMEM for i, x in enumerate(ins)]
+    specs = [SMEM if i == 0 and x.ndim == 1 else place for i, x in enumerate(ins)]
     return pl.pallas_call(
         kernel,
         out_shape=outs,
         in_specs=specs,
         out_specs=[VMEM] * len(outs),
         scratch_shapes=scratch,
-        compiler_params=pltpu.CompilerParams(vmem_limit_bytes=40 << 20),
+        compiler_params=pltpu.CompilerParams(vmem_limit_bytes=room << 20),
         cost_estimate=pl.CostEstimate(flops=flops, bytes_accessed=2 << 20, transcendentals=0),
         name=name,
     )(*ins)
@@ -334,15 +385,13 @@
                 found.append((s * segs + g, t * segs + h))
         return found
 
-    fwd_down = pairs(lambda s, g: (s, g - 1))
-    fwd_up = pairs(lambda s, g: (s, g + 1))
-    side_down = pairs(lambda s, g: (s - 1, segs - 1 - g))
-    side_up = pairs(lambda s, g: (s + 1, segs - 1 - g))
-
-    weights = jnp.stack(
-        [(lax.axis_index("seg") > 0).astype(F32), (lax.axis_index("strip") > 0).astype(F32)]
-    )
-    base = gradient.reshape(ROWS, LANES)
+    fwd_rounds = pairs(lambda s, g: (s, g ^ 1)), pairs(lambda s, g: (s, (g + 1 ^ 1) - 1))
+    side_rounds = (
+        pairs(lambda s, g: (s ^ 1, segs - 1 - g)),
+        pairs(lambda s, g: ((s + 1 ^ 1) - 1, segs - 1 - g)),
+    )
+    seg, strip = lax.axis_index("seg"), lax.axis_index("strip")
+    weights = jnp.stack([seg > 0, strip > 0, (seg & 1) > 0, (strip & 1) > 0]).astype(F32)
     live = live_blocks.reshape(1)
     lcam, lpoint = loc_cam_jac[:, :, 0], loc_point_jac[:, :, 0]
     lcams = loc_cams.reshape(-1, LANES)
@@ -353,23 +402,34 @@
     fr, sr = fcam.shape[2], scam.shape[2]
     watched = lcam.shape[1]
 
-    def both(values, up, down):
-        return lax.ppermute(values[1], AXES, down), lax.ppermute(values[0], AXES, up)
+    def meet(sends, rounds):
+        return [lax.ppermute(send, AXES, pairs) for send, pairs in zip(sends, rounds)]
 
     index_scratch = [pltpu.VMEM((2, fr, LANES), jnp.int32), pltpu.VMEM((2, sr, LANES), jnp.int32)]
     z_scratch = [pltpu.VMEM((2, 3, fr, LANES), F32), pltpu.VMEM((2, 3, sr, LANES), F32)]
     total_scratch = [pltpu.VMEM((STEP * STACK, LANES), F32), pltpu.VMEM((STACK, LANES), F32)]
 
-    fseen, fsums, sseen, ssums = call(
+    def sends_of(parts):
+        return [(parts, fr // 2, LANES)] * 2, [(parts, sr // 2, LANES)] * 2
+
+    far = [gradient, fcam, fpoint, fcams, scam, spoint, scams]
+    fshapes, sshapes = sends_of(9)
+    base, fseen, fsums, *sends, sseen, ssums, ssend0, ssend1 = call(
         look_kernel,
-        [base, fcam, fpoint, fcams, scam, spoint, scams],
-        [(2, 2, fr, LANES), (2, 9, fr // 2, LANES), (2, 2, sr, LANES), (2, 9, sr // 2, LANES)],
-        index_scratch + [pltpu.VMEM((9, fr, LANES), F32), pltpu.VMEM((9, sr, LANES), F32)],
+        [weights] + far,
+        [(ROWS, LANES), (2, 2, fr, LANES), (2, 9, fr // 2, LANES)] + fshapes
+        + [(2, 2, sr, LANES), (2, 9, sr // 2, LANES)] + sshapes,
+        [pltpu.VMEM(far[n].shape, far[n].dtype) for n in (0, 1, 2, 3, 4, 5, 6)]
+        + index_scratch
+        + [pltpu.VMEM((9, fr, LANES), F32), pltpu.VMEM((9, sr, LANES), F32)]
+        + [pltpu.SemaphoreType.DMA((len(far),))],
         10**9,
         "look",
-    )
-    fown, fguest = both(fsums, fwd_up, fwd_down)
-    sown, sguest = both(ssums, side_up, side_down)
+        FAR,
+        63,
+    )
+    smet = meet((ssend0, ssend1), side_rounds)
+    fmet = meet(sends, fwd_rounds)
 
     def local(table):
         return call(
@@ -382,32 +442,31 @@
         )
 
     extra, _ = local(base)
-    p, finverse, sinverse, fseen, fsums, sseen, ssums, dots = call(
+    fshapes, sshapes = sends_of(3)
+    p, finverse, sinverse, fseen, fsums2, fsend0, fsend1, sseen, ssums2, ssend0, ssend1, dots = call(
         middle_kernel,
         [weights, base, extra, fcam, fpoint, fcams, scam, spoint, scams,
-         fseen, fsums, fown, fguest, sseen, ssums, sown, sguest],
+         fseen, fsums, *fmet, sseen, ssums, *smet],
         [(ROWS, LANES), (2, 6, fr // 2, LANES), (2, 6, sr // 2, LANES),
-         (2, 2, fr, LANES), (2, 3, fr // 2, LANES), (2, 2, sr, LANES), (2, 3, sr // 2, LANES),
-         (8, LANES)],
+         (2, 2, fr, LANES), (2, 3, fr // 2, LANES)] + fshapes
+        + [(2, 2, sr, LANES), (2, 3, sr // 2, LANES)] + sshapes + [(8, LANES)],
         index_scratch + [pltpu.VMEM((3, fr, LANES), F32), pltpu.VMEM((3, sr, LANES), F32)]
         + z_scratch + total_scratch + [pltpu.VMEM((STEP, LANES), F32)],
         10**10,
         "middle",
     )
-    fown, fguest = both(fsums, fwd_up, fwd_down)
-    sown, sguest = both(ssums, side_up, side_down)
+    smet = meet((ssend0, ssend1), side_rounds)
+    fmet = meet((fsend0, fsend1), fwd_rounds)
     extra, product = local(p)
     fz, sz, line = call(
         dots_kernel,
-        [weights, dots, product, fsums, fown, fguest, finverse, ssums, sown, sguest, sinverse],
-        [(2, 3, fr, LANES), (2, 3, sr, LANES), (segs, LANES)],
+        [weights, dots, product, fsums2, *fmet, finverse, ssums2, *smet, sinverse],
+        [(2, 3, fr, LANES), (2, 3, sr, LANES), (strips * segs, LANES)],
         [pltpu.VMEM((8, LANES), F32)],
         10**8,
         "dots",
     )
-    line = lax.all_to_all(line, "seg", 0, 0, tiled=True)
-    line = jnp.broadcast_to(jnp.sum(line, axis=0, keepdims=True), (strips, LANES))
-    line = lax.all_to_all(line, "strip", 0, 0, tiled=True)
+    line = lax.all_to_all(line, AXES, 0, 0, tiled=True)
     (t,) = call(
         last_kernel,
         [weights, extra, fcam, fpoint, fcams, scam, spoint, scams, fseen, fz, sseen, sz],
@@ -417,9 +476,9 @@
         "last",
     )
     step, residual = call(
-        close_kernel, [line, base, p, t], [(ROWS, LANES)] * 2, [], 10**6, "close"
-    )
-    return step.reshape(gradient.shape), residual.reshape(gradient.shape)
+        close_kernel, [line, base, p, t], [gradient.shape] * 2, [], 10**6, "close"
+    )
+    return step, residual
 
 
 def solution(mesh):

time: 101 us -> 81.9 us (0.81)
  blocking collectives: 10.8 us -> 0 us
  local copies, waits for them, and re-layouts: 9.43 us -> 1.27 us
  starting transfers between devices: 43.2 us -> 38.5 us
  waiting for transfers between devices: 2.39 us -> 6.11 us
    all_to_all x1 -> x0, blocking collectives: 10.8 us -> none  [per_device(): line = lax.all_to_all(line, 'seg', 0, 0, tiled=True)]
    ppermute x8, starting transfers between devices: 27.2 us -> 21.7 us  [meet(): lax.ppermute(send, AXES, pairs)]
    unnamed x38 -> x32, local copies, waits for them, and re-layouts: 6.12 us -> 1.27 us
    all_to_all x1, waiting for transfers between devices: 2.37 us -> 6.09 us  [per_device(): line = lax.all_to_all(line, AXES, 0, 0, tiled=True)]
    squeeze x4 -> x0, local copies, waits for them, and re-layouts: 1.44 us -> none  [both(): values[0]]
    reshape x3 -> x0, local copies, waits for them, and re-layouts: 1.26 us -> none  [the longest x2 1.25 us: per_device(): return (step.reshape(gradient.shape), residual.reshape(gradient.shape))]
  transfers between devices with their start and end apart: 9 -> 9, of which waited for: 1 -> 1; matrix products, arithmetic and copies ran while one was open for 1% -> 0% of each run, Pallas kernels for 19% -> 20%
where the time goes in v2:
time: 81.9 us; the launch traced here: 80.8 us
  starting transfers between devices  38.5 us (47%)
  Pallas kernels  32.8 us (40%)
  waiting for transfers between devices  6.11 us (7%)
  between operations  1.6 us (2%)
  local copies, waits for them, and re-layouts  1.27 us (2%)
    pallas_call x7, Pallas kernels, call(): pl.pallas_call(kernel, out_shape=outs, in_specs=specs, out_specs=[VMEM] *...  32.8 us
    ppermute x8, starting transfers between devices, meet(): lax.ppermute(send, AXES, pairs)  21.7 us
    all_to_all x1, starting transfers between devices, per_device(): line = lax.all_to_all(line, AXES, 0, 0, tiled=True)  16.8 us
    all_to_all x1, waiting for transfers between devices, per_device(): line = lax.all_to_all(line, AXES, 0, 0, tiled=True)  6.09 us
  transfers between devices with their start and end apart: 9, of which 1 were waited for; matrix products, arithmetic and copies ran while one was open for 0% of the time, Pallas kernels for 20%

profile of v2, /device:TPU:1, one launch (start us, length us, event | category | flops | bytes accessed | tf_op | source)
XLA Modules:
  0.0 80.8 jit_solution(12478720859959025687)
XLA Ops:
  0.6 0.6 add_convert_fusion.weights
  1.2 5.5 %look.1 = (f32[36,128]{1,0:T(8,128)}, f32[2,2,64,128]{3,2,1,0:T(8,128)}, f32[2,9,32,128]{3,2,1,0:T(8,128)}, f32[9,32,128]{2,1,0:T(8,128)}, f32[9,32,128]{2,1,0:T...) custom-call(f32[4]{0:T(128)} %add_convert_fusion.weights, ...), custom_call_target="tpu_custom_call" | custom-call | flops 1000000000 | bytes 2097152 | tf_op jit(solution)/shard_map/look/pallas_call | solution.py:355
  6.7 5.3 %collective-permute-start.2 = (f32[9,24,128]{2,1,0:T(8,128)}, f32[9,24,128]{2,1,0:T(8,128)S(1)}, u32[]{:S(2)}, u32[]{:S(2)}) collective-permute-start(f32[9,24,128]{2,1,0:T(8,128)} %get-tuple-element.37), channel_id=1, source_target_pairs={{0,15},{1,14},{2,13},{3,12},{4,11},{5,10},{6,9},{7,8},{8,7},{9,6},... | collective-permute-start | bytes 331784 | tf_op jit(solution)/shard_map/ppermute | solution.py:406
  12.0 4.6 %collective-permute-start.3 = (f32[9,24,128]{2,1,0:T(8,128)}, f32[9,24,128]{2,1,0:T(8,128)S(1)}, u32[]{:S(2)}, u32[]{:S(2)}) collective-permute-start(f32[9,24,128]{2,1,0:T(8,128)} %get-tuple-element.38), channel_id=1, source_target_pairs={{8,23},{9,22},{10,21},{11,20},{12,19},{13,18},{14,17},{15,16},{16,... | collective-permute-start | bytes 331784 | tf_op jit(solution)/shard_map/ppermute | solution.py:406
  16.7 0.3 collective-permute-start
  16.9 0.7 collective-permute-start.1
  18.3 0.7 copy-done
  19.0 0.0 copy-start.8
  19.0 0.0 copy-start.9
  19.0 0.0 copy-start.11
  19.1 4.8 %local.2 = (f32[36,128]{1,0:T(8,128)S(1)}, f32[8,128]{1,0:T(8,128)}) custom-call(s32[1]{0:T(128)} %bitcast.34.live, f32[36,128]{1,0:T(8,128)S(1)} %copy-done, bf16[18,6,2048]{2,1,0:T(8,128)(2,1)S(1)} %bitcast.37, bf16[6,6,2048]{2,1,0:T(8,128)(2,1)S(1)} %bitcast.45, s32[96,128]{1,0:T(8,128)S(1)} %bitcast.56), custom_call_target="tpu_custom_call" | custom-call | flops 5000000000 | bytes 2097152 | tf_op jit(solution)/shard_map/local/pallas_call | solution.py:355
  23.9 0.0 collective-permute-done.1.fmet1
  24.0 0.5 copy-done.2
  24.5 9.4 %middle.1 = (f32[36,128]{1,0:T(8,128)S(1)}, f32[2,6,32,128]{3,2,1,0:T(8,128)S(1)}, f32[2,6,24,128]{3,2,1,0:T(8,128)S(1)}, f32[2,2,64,128]{3,2,1,0:T(8,128)S(1)},...) custom-call(f32[4]{0:T(128)S(1)} %copy-done.2, ...), custom_call_target="tpu_custom_call" | custom-call | flops 10000000000 | bytes 2097152 | tf_op jit(solution)/shard_map/middle/pallas_call | solution.py:355
  33.8 0.1 collective-permute-start.6
  33.9 8.8 %collective-permute-start.7 = (f32[3,24,128]{2,1,0:T(8,128)S(1)}, f32[3,24,128]{2,1,0:T(8,128)S(1)}, u32[]{:S(2)}, u32[]{:S(2)}) collective-permute-start(f32[3,24,128]{2,1,0:T(8,128)S(1)} %get-tuple-element.48), channel_id=1, source_target_pairs={{8,23},{9,22},{10,21},{11,20},{12,19},{13,18},{14,17},{15,16},{16,... | collective-permute-start | bytes 110600 | tf_op jit(solution)/shard_map/ppermute | solution.py:406
  42.7 1.4 %collective-permute-start.4 = (f32[3,32,128]{2,1,0:T(8,128)S(1)}, f32[3,32,128]{2,1,0:T(8,128)S(1)}, u32[]{:S(2)}, u32[]{:S(2)}) collective-permute-start(f32[3,32,128]{2,1,0:T(8,128)S(1)} %get-tuple-element.43), channel_id=1, source_target_pairs={{0,1},{1,0},{2,3},{3,2},{4,5},{5,4},{6,7},{7,6},{8,9},{9,8},{10,11... | collective-permute-start | bytes 147464 | tf_op jit(solution)/shard_map/ppermute | solution.py:406
  44.1 0.7 collective-permute-start.5
  44.7 4.2 %local.3 = (f32[36,128]{1,0:T(8,128)S(1)}, f32[8,128]{1,0:T(8,128)S(1)}) custom-call(s32[1]{0:T(128)} %bitcast.35.live, f32[36,128]{1,0:T(8,128)S(1)} %get-tuple-element.40.table.first, bf16[18,6,2048]{2,1,0:T(8,128)(2,1)S(1)} %bitcast.38, bf16[6,6,2048]{2,1,0:T(8,128)(2,1)S(1)} %bitcast.46, s32[96,128]{1,0:T(8,128)S(1)} %bitcast.57), custom_call_target="tpu_custom_call" | custom-call | flops 5000000000 | bytes 2097152 | tf_op jit(solution)/shard_map/local/pallas_call | solution.py:355
  49.0 1.4 %dots.1 = (f32[2,3,64,128]{3,2,1,0:T(8,128)S(1)}, f32[2,3,48,128]{3,2,1,0:T(8,128)S(1)}, f32[256,128]{1,0:T(8,128)}) custom-call(f32[4]{0:T(128)S(1)} %copy-done.2, f32[8,128]{1,0:T(8,128)S(1)} %get-tuple-element.39.dots, f32[8,128]{1,0:T(8,128)S(1)} %get-tuple-element.41.product, f32[2,3,32,128]{3,2,1,0:T(8,128)S(1)} %get-tuple-element.42.fsums, ...), custom_call_target="tpu_custom_call" | custom-call | flops 100000000 | bytes 2097152 | tf_op jit(solution)/shard_map/dots/pallas_call | solution.py:355
  50.3 16.8 %all-to-all-start = ((f32[256,1,128]{2,1,0:T(1,128)}), f32[256,1,128]{2,1,0:T(1,128)S(1)}, u32[]{:S(2)}, u32[]{:S(2)}) async-start(f32[256,1,128]{2,1,0:T(1,128)} %bitcast.23), calls=%async_computation | async-start | bytes 262144 | tf_op jit(solution)/shard_map/all_to_all | solution.py:469
  67.1 6.9 %last.1.second = f32[36,128]{1,0:T(8,128)S(1)} custom-call(f32[4]{0:T(128)S(1)} %copy-done.2, f32[36,128]{1,0:T(8,128)S(1)} %get-tuple-element.51.extra, bf16[2,18,64,128]{3,2,1,0:T(8,128)(2,1)S(1)} %bitcast.41, bf16[2,6,64,128]{3,2,1,0:T(8,128)(2,1)S(1)} %bitcast.49, s32[2,2,32,128]{3,2,1,0:T(8,128)S(1)} %bitcast.55, bf16[2,18,48,128]{3,2,1,0:T(8,128)(2,1)S(1)} %bitcast.44, ...), custom_call_target="tpu_custom_call" | custom-call | flops 5000000000 | bytes 2097152 | tf_op jit(solution)/shard_map/last/pallas_call | solution.py:355
  74.0 6.1 %all-to-all-done = f32[256,1,128]{2,1,0:T(1,128)S(1)} async-done(((f32[256,1,128]{2,1,0:T(1,128)}), f32[256,1,128]{2,1,0:T(1,128)S(1)}, u32[]{:S(2)}, u32[]{:S(2)}) %all-to-all-start) | async-done | bytes 131104 | tf_op jit(solution)/shard_map/all_to_all | solution.py:469
  80.1 0.8 close.1
  (34 shorter events, 0.1 us)
Async XLA Ops:
  1.2 17.0 %copy-start.3 = (bf16[18,6,1,2048]{3,1,2,0:T(8,128)(2,1)S(1)}, bf16[18,6,1,2048]{3,1,2,0:T(8,128)(2,1)}, u32[]{:S(2)}) copy-start(bf16[18,6,1,2048]{3,1,2,0:T(8,128)(2,1)} %param.13) | copy-start | bytes 1327108
  1.2 17.0 %copy-start.6 = (bf16[6,6,1,2048]{3,1,2,0:T(8,128)(2,1)S(1)}, bf16[6,6,1,2048]{3,1,2,0:T(8,128)(2,1)}, u32[]{:S(2)}) copy-start(bf16[6,6,1,2048]{3,1,2,0:T(8,128)(2,1)} %param.14) | copy-start | bytes 442372
  1.2 17.0 %copy-start.10 = (s32[6,1,2048]{2,1,0:T(1,128)S(1)}, s32[6,1,2048]{2,1,0:T(1,128)}, u32[]{:S(2)}) copy-start(s32[6,1,2048]{2,1,0:T(1,128)} %param.15) | copy-start | bytes 147460
  6.7 17.1 %collective-permute-start.2 = (f32[9,24,128]{2,1,0:T(8,128)}, f32[9,24,128]{2,1,0:T(8,128)S(1)}, u32[]{:S(2)}, u32[]{:S(2)}) collective-permute-start(f32[9,24,128]{2,1,0:T(8,128)} %get-tuple-element.37), channel_id=1, source_target_pairs={{0,15},{1,14},{2,13},{3,12},{4,11},{5,10},{6,9},{7,8},{8,7},{9,6},... | collective-permute-start | bytes 331784 | tf_op jit(solution)/shard_map/ppermute | solution.py:406
  12.0 11.8 %collective-permute-start.3 = (f32[9,24,128]{2,1,0:T(8,128)}, f32[9,24,128]{2,1,0:T(8,128)S(1)}, u32[]{:S(2)}, u32[]{:S(2)}) collective-permute-start(f32[9,24,128]{2,1,0:T(8,128)} %get-tuple-element.38), channel_id=1, source_target_pairs={{8,23},{9,22},{10,21},{11,20},{12,19},{13,18},{14,17},{15,16},{16,... | collective-permute-start | bytes 331784 | tf_op jit(solution)/shard_map/ppermute | solution.py:406
  16.7 7.2 %collective-permute-start = (f32[9,32,128]{2,1,0:T(8,128)}, f32[9,32,128]{2,1,0:T(8,128)S(1)}, u32[]{:S(2)}, u32[]{:S(2)}) collective-permute-start(f32[9,32,128]{2,1,0:T(8,128)} %get-tuple-element.33), channel_id=1, source_target_pairs={{0,1},{1,0},{2,3},{3,2},{4,5},{5,4},{6,7},{7,6},{8,9},{9,8},{10,11... | collective-permute-start | bytes 442376 | tf_op jit(solution)/shard_map/ppermute | solution.py:406
  16.9 6.9 %collective-permute-start.1 = (f32[9,32,128]{2,1,0:T(8,128)}, f32[9,32,128]{2,1,0:T(8,128)S(1)}, u32[]{:S(2)}, u32[]{:S(2)}) collective-permute-start(f32[9,32,128]{2,1,0:T(8,128)} %get-tuple-element.34), channel_id=1, source_target_pairs={{1,2},{2,1},{3,4},{4,3},{5,6},{6,5},{9,10},{10,9},{11,12},{12,11},... | collective-permute-start | bytes 442376 | tf_op jit(solution)/shard_map/ppermute | solution.py:406
  18.3 0.7 copy-start
  19.0 4.9 %copy-start.1 = (f32[36,128]{1,0:T(8,128)S(1)}, f32[36,128]{1,0:T(8,128)}, u32[]{:S(2)}) copy-start(f32[36,128]{1,0:T(8,128)} %get-tuple-element.29.table.base) | copy-start | bytes 55300
  19.0 4.9 %copy-start.4 = (bf16[2,18,2,1,4096]{4,2,3,1,0:T(2,128)(2,1)S(1)}, bf16[2,18,2,1,4096]{4,2,3,1,0:T(2,128)(2,1)}, u32[]{:S(2)}) copy-start(bf16[2,18,2,1,4096]{4,2,3,1,0:T(2,128)(2,1)} %param.16) | copy-start | bytes 1769476
  19.0 4.9 %copy-start.5 = (bf16[2,18,2,1,3072]{4,2,3,1,0:T(2,128)(2,1)S(1)}, bf16[2,18,2,1,3072]{4,2,3,1,0:T(2,128)(2,1)}, u32[]{:S(2)}) copy-start(bf16[2,18,2,1,3072]{4,2,3,1,0:T(2,128)(2,1)} %param.19) | copy-start | bytes 1327108
  19.0 4.9 %copy-start.7 = (bf16[2,6,2,1,4096]{4,2,3,1,0:T(2,128)(2,1)S(1)}, bf16[2,6,2,1,4096]{4,2,3,1,0:T(2,128)(2,1)}, u32[]{:S(2)}) copy-start(bf16[2,6,2,1,4096]{4,2,3,1,0:T(2,128)(2,1)} %param.17) | copy-start | bytes 589828
  19.0 4.9 %copy-start.8 = (bf16[2,6,2,1,3072]{4,2,3,1,0:T(2,128)(2,1)S(1)}, bf16[2,6,2,1,3072]{4,2,3,1,0:T(2,128)(2,1)}, u32[]{:S(2)}) copy-start(bf16[2,6,2,1,3072]{4,2,3,1,0:T(2,128)(2,1)} %param.20) | copy-start | bytes 442372
  19.0 4.9 %copy-start.9 = (s32[2,2,1,4096]{3,2,1,0:T(1,128)S(1)}, s32[2,2,1,4096]{3,2,1,0:T(1,128)}, u32[]{:S(2)}) copy-start(s32[2,2,1,4096]{3,2,1,0:T(1,128)} %param.18) | copy-start | bytes 196612
  19.0 4.9 %copy-start.11 = (s32[2,2,1,3072]{3,2,1,0:T(1,128)S(1)}, s32[2,2,1,3072]{3,2,1,0:T(1,128)}, u32[]{:S(2)}) copy-start(s32[2,2,1,3072]{3,2,1,0:T(1,128)} %param.21) | copy-start | bytes 147460
  19.0 4.9 %copy-start.12 = (f32[2,9,32,128]{3,2,1,0:T(8,128)S(1)}, f32[2,9,32,128]{3,2,1,0:T(8,128)}, u32[]{:S(2)}) copy-start(f32[2,9,32,128]{3,2,1,0:T(8,128)} %get-tuple-element.32.fsums) | copy-start | bytes 884740
  19.1 4.9 %copy-start.13 = (f32[2,9,24,128]{3,2,1,0:T(8,128)S(1)}, f32[2,9,24,128]{3,2,1,0:T(8,128)}, u32[]{:S(2)}) copy-start(f32[2,9,24,128]{3,2,1,0:T(8,128)} %get-tuple-element.36.ssums) | copy-start | bytes 663556
  19.1 4.9 %copy-start.14 = (f32[2,2,64,128]{3,2,1,0:T(8,128)S(1)}, f32[2,2,64,128]{3,2,1,0:T(8,128)}, u32[]{:S(2)}) copy-start(f32[2,2,64,128]{3,2,1,0:T(8,128)} %get-tuple-element.31.fseen) | copy-start | bytes 393220
  19.1 4.9 %copy-start.15 = (f32[2,2,48,128]{3,2,1,0:T(8,128)S(1)}, f32[2,2,48,128]{3,2,1,0:T(8,128)}, u32[]{:S(2)}) copy-start(f32[2,2,48,128]{3,2,1,0:T(8,128)} %get-tuple-element.35.sseen) | copy-start | bytes 294916
  33.8 15.1 %collective-permute-start.6 = (f32[3,24,128]{2,1,0:T(8,128)S(1)}, f32[3,24,128]{2,1,0:T(8,128)S(1)}, u32[]{:S(2)}, u32[]{:S(2)}) collective-permute-start(f32[3,24,128]{2,1,0:T(8,128)S(1)} %get-tuple-element.47), channel_id=1, source_target_pairs={{0,15},{1,14},{2,13},{3,12},{4,11},{5,10},{6,9},{7,8},{8,7},{9,6},... | collective-permute-start | bytes 110600 | tf_op jit(solution)/shard_map/ppermute | solution.py:406
  33.9 15.0 %collective-permute-start.7 = (f32[3,24,128]{2,1,0:T(8,128)S(1)}, f32[3,24,128]{2,1,0:T(8,128)S(1)}, u32[]{:S(2)}, u32[]{:S(2)}) collective-permute-start(f32[3,24,128]{2,1,0:T(8,128)S(1)} %get-tuple-element.48), channel_id=1, source_target_pairs={{8,23},{9,22},{10,21},{11,20},{12,19},{13,18},{14,17},{15,16},{16,... | collective-permute-start | bytes 110600 | tf_op jit(solution)/shard_map/ppermute | solution.py:406
  42.7 6.2 %collective-permute-start.4 = (f32[3,32,128]{2,1,0:T(8,128)S(1)}, f32[3,32,128]{2,1,0:T(8,128)S(1)}, u32[]{:S(2)}, u32[]{:S(2)}) collective-permute-start(f32[3,32,128]{2,1,0:T(8,128)S(1)} %get-tuple-element.43), channel_id=1, source_target_pairs={{0,1},{1,0},{2,3},{3,2},{4,5},{5,4},{6,7},{7,6},{8,9},{9,8},{10,11... | collective-permute-start | bytes 147464 | tf_op jit(solution)/shard_map/ppermute | solution.py:406
  44.1 4.9 %collective-permute-start.5 = (f32[3,32,128]{2,1,0:T(8,128)S(1)}, f32[3,32,128]{2,1,0:T(8,128)S(1)}, u32[]{:S(2)}, u32[]{:S(2)}) collective-permute-start(f32[3,32,128]{2,1,0:T(8,128)S(1)} %get-tuple-element.44), channel_id=1, source_target_pairs={{1,2},{2,1},{3,4},{4,3},{5,6},{6,5},{9,10},{10,9},{11,12},{12,11},... | collective-permute-start | bytes 147464 | tf_op jit(solution)/shard_map/ppermute | solution.py:406
  50.3 29.8 %all-to-all-start = ((f32[256,1,128]{2,1,0:T(1,128)}), f32[256,1,128]{2,1,0:T(1,128)S(1)}, u32[]{:S(2)}, u32[]{:S(2)}) async-start(f32[256,1,128]{2,1,0:T(1,128)} %bitcast.23), calls=%async_computation | async-start | bytes 262144 | tf_op jit(solution)/shard_map/all_to_all | solution.py:469
  (1 other events, 0.6 us)

commit v3 on v2

--- a/solution.py
+++ b/solution.py
@@ -13,6 +13,8 @@
 LIFT = 40
 STACK = 2 * LIFT
 STEP = 16
+LOOK_UNROLL = 1
+RETURN_UNROLL = 1
 SYM = ((0, 0), (0, 1), (0, 2), (1, 1), (1, 2), (2, 2))
 DAMP = 1.0
 VMEM = pl.BlockSpec(memory_space=pltpu.VMEM)
@@ -115,124 +117,165 @@
             index[s, pl.ds(o, half, stride=2), :] = cams[s, o]
 
 
-def pair_look(cam, point, index, table, seen_out, loose, sums, sends, odd, with_h, squares, weights):
+def pair_look(cam, point, index, table, seen_out, loose, sends, odd, with_h, squares, held, done):
     rows = cam.shape[2]
     half = rows // 2
-    for s in range(2):
-
-        def body(i, carry, s=s):
+    for turn in range(2):
+        s = turn ^ odd
+        share = part_of(s, held)
+
+        def body(i, carry, s=s, turn=turn, share=share):
             at = pl.ds(pl.multiple_of(i * STEP, STEP), STEP)
             across = [cam[s, j, at, :].astype(F32) for j in range(2 * JAC)]
             along = [point[s, j, at, :].astype(F32) for j in range(6)]
             seen = predict(across, fetch(table, index[s, at, :]))
             for r in range(2):
-                seen_out[s, r, at, :] = seen[r]
+                seen_out[turn, r, at, :] = seen[r]
             parts = project(along, seen)
             if with_h:
                 parts = parts + normal(along)
             for n, part in enumerate(parts):
                 loose[n, at, :] = part
             if squares is not None:
-                squares[...] += weights[s] * (seen[0] * seen[0] + seen[1] * seen[1])
+                squares[...] += share * (seen[0] * seen[0] + seen[1] * seen[1])
             return carry
 
-        lax.fori_loop(0, rows // STEP, body, 0)
+        lax.fori_loop(0, rows // STEP, body, 0, unroll=LOOK_UNROLL)
         for n in range(9 if with_h else 3):
-            sums[s, n] = (
+            sends[turn][n] = (
                 loose[n, pl.ds(0, half, stride=2), :] + loose[n, pl.ds(1, half, stride=2), :]
             )
-
-    for flag in range(2):
-
-        @pl.when((odd > 0.5) == (flag == 1))
-        def _(flag=flag):
-            for s in range(2):
-                sends[s ^ flag][...] = sums[s]
-
-
-def pair_return(cam, point, index, seen_in, z, weights, stage, total):
+        if done is not None:
+            done(turn)
+
+
+def part_of(side, held):
+    return jnp.where(side == 0, 1, held).astype(F32)
+
+
+def pair_return(cam, point, index, seen_in, z, odd, held, stage, total):
     rows = cam.shape[2]
-    for s in range(2):
-
-        def body(i, carry, s=s):
+    for turn in range(2):
+        s = turn ^ odd
+        share = part_of(s, held)
+
+        def body(i, carry, s=s, turn=turn, share=share):
             at = pl.ds(pl.multiple_of(i * STEP, STEP), STEP)
             across = [cam[s, j, at, :].astype(F32) for j in range(2 * JAC)]
             along = [point[s, j, at, :].astype(F32) for j in range(6)]
             left = residue(
-                along, [seen_in[s, r, at, :] for r in range(2)], [z[s, k, at, :] for k in range(3)]
+                along,
+                [seen_in[turn, r, at, :] for r in range(2)],
+                [z[turn, k, at, :] for k in range(3)],
             )
-            left = [weights[s] * e for e in left]
+            left = [share * e for e in left]
             terms = [across[j] * left[0] + across[JAC + j] * left[1] for j in range(JAC)]
             spread(terms, index[s, at, :], stage, total)
             return carry
 
-        lax.fori_loop(0, rows // STEP, body, 0)
-
-
-def pair_solve(mine, met, odd, inverse_out, inverse_in, z, products, weights):
-    half = mine.shape[2]
-    for s in range(2):
-        first = (odd > 0.5) == (s == 1)
+        lax.fori_loop(0, rows // STEP, body, 0, unroll=RETURN_UNROLL)
+
+
+def pair_solve(sent, met, inverse_out, inverse_in, z, products, odd, held):
+    half = sent[0].shape[1]
+    for turn in range(2):
+        share = part_of(turn ^ odd, held)
         for i in range(half // 8):
             at = pl.ds(8 * i, 8)
-
-            def joined(k, at=at, first=first):
-                return mine[s, k, at, :] + jnp.where(first, met[0][k, at, :], met[1][k, at, :])
-
-            b = [joined(k) for k in range(3)]
+            mine = [sent[turn][k, at, :] for k in range(3)]
+            b = [mine[k] + met[turn][k, at, :] for k in range(3)]
             if inverse_in is None:
-                inverse = invert([joined(3 + k) for k in range(6)])
+                inverse = invert(
+                    [sent[turn][3 + k, at, :] + met[turn][3 + k, at, :] for k in range(6)]
+                )
                 for k in range(6):
-                    inverse_out[s, k, at, :] = inverse[k]
+                    inverse_out[turn, k, at, :] = inverse[k]
             else:
-                inverse = [inverse_in[s, k, at, :] for k in range(6)]
+                inverse = [inverse_in[turn, k, at, :] for k in range(6)]
             solved = solve(inverse, b)
             if products is not None:
-                products[...] += weights[s] * sum(
-                    mine[s, k, at, :] * solved[k] for k in range(3)
-                )
+                products[...] += share * sum(mine[k] * solved[k] for k in range(3))
             for k in range(3):
                 for o in range(2):
-                    z[s, k, pl.ds(16 * i + o, 8, stride=2), :] = solved[k]
+                    z[turn, k, pl.ds(16 * i + o, 8, stride=2), :] = solved[k]
+
+
+def place_of():
+    seg, strip = lax.axis_index("seg"), lax.axis_index("strip")
+    return (seg & 1, jnp.minimum(seg, 1)), (strip & 1, jnp.minimum(strip, 1))
+
+
+def in_rows(lines, table):
+    for j in range(JAC):
+        for k in range(PAGES):
+            table[pl.ds(PAGES * j + k, 1), :] = lines[j, :, pl.ds(LANES * k, LANES)]
 
 
 def look_kernel(
-    weights, gradient, fcam_at, fpoint_at, fcams_at, scam_at, spoint_at, scams_at,
-    table, fseen, fsums, fsend0, fsend1, sseen, ssums, ssend0, ssend1,
-    lines, fcam, fpoint, fcams, scam, spoint, scams, findex, sindex, floose, sloose, arrived,
+    gradient, fcam_at, fpoint_at, fcams_at, scam_at, spoint_at, scams_at,
+    fseen_at, fsend0_at, fsend1_at, sseen_at, ssend0_at, ssend1_at,
+    lines, fcam, fpoint, fcams, scam, spoint, scams,
+    fseen, fsend0, fsend1, sseen, ssend0, ssend1,
+    table, findex, sindex, floose, sloose, arrived, left,
 ):
+    (fodd, _), (sodd, _) = place_of()
     moves = [
         pltpu.make_async_copy(source, target, arrived.at[n])
         for n, (source, target) in enumerate(
             (
-                (gradient, lines), (fcams_at, fcams), (scams_at, scams), (fcam_at, fcam),
-                (fpoint_at, fpoint), (scam_at, scam), (spoint_at, spoint),
+                (gradient, lines), (scams_at, scams), (scam_at, scam), (spoint_at, spoint),
+                (fcams_at, fcams), (fcam_at, fcam), (fpoint_at, fpoint),
+            )
+        )
+    ]
+    back = [
+        pltpu.make_async_copy(source, target, left.at[n])
+        for n, (source, target) in enumerate(
+            (
+                (ssend0, ssend0_at), (ssend1, ssend1_at), (sseen, sseen_at),
+                (fsend0, fsend0_at), (fsend1, fsend1_at), (fseen, fseen_at),
             )
         )
     ]
     for move in moves:
         move.start()
-    for move in moves[:3]:
+    for move in moves[:2]:
         move.wait()
-    for j in range(JAC):
-        for k in range(PAGES):
-            table[pl.ds(PAGES * j + k, 1), :] = lines[j, :, pl.ds(LANES * k, LANES)]
+    in_rows(lines, table)
+    weave(scams, sindex)
+    for move in moves[2:4]:
+        move.wait()
+
+    def sent(first):
+        def done(turn):
+            back[first + turn].start()
+            if turn == 1:
+                back[first + 2].start()
+
+        return done
+
+    pair_look(
+        scam, spoint, sindex, table, sseen, sloose, (ssend0, ssend1), sodd, True, None, 0, sent(0)
+    )
+    moves[4].wait()
     weave(fcams, findex)
-    weave(scams, sindex)
-    for move in moves[3:5]:
-        move.wait()
-    sends = (fsend0, fsend1)
-    pair_look(fcam, fpoint, findex, table, fseen, floose, fsums, sends, weights[2], True, None, None)
     for move in moves[5:]:
         move.wait()
-    sends = (ssend0, ssend1)
-    pair_look(scam, spoint, sindex, table, sseen, sloose, ssums, sends, weights[3], True, None, None)
-
-
-def local_kernel(live, table, cam, point, cams, out, product, stage, total):
+    pair_look(
+        fcam, fpoint, findex, table, fseen, floose, (fsend0, fsend1), fodd, True, None, 0, sent(3)
+    )
+    for move in back:
+        move.wait()
+
+
+def local_kernel(live, values, cam, point, cams, out, product, stage, total, table):
     total[...] = jnp.zeros_like(total)
     stage[...] = jnp.zeros_like(stage)
     product[...] = jnp.zeros_like(product)
+    if values.shape[0] == JAC:
+        in_rows(values, table)
+    else:
+        table = values
     watched = cams.shape[0] // 16
 
     def body(i, carry):
@@ -254,34 +297,31 @@
 
 
 def middle_kernel(
-    weights, table, extra, fcam, fpoint, fcams, scam, spoint, scams,
-    fseen, fsums, fmet0, fmet1, sseen, ssums, smet0, smet1,
-    result, finverse, sinverse, fseen2, fsums2, fsend0, fsend1,
-    sseen2, ssums2, ssend0, ssend1, dots,
-    findex, sindex, floose, sloose, fz, sz, stage, total, squares,
+    lines, extra, fcam, fpoint, fcams, scam, spoint, scams,
+    fseen, fsent0, fsent1, fmet0, fmet1, sseen, ssent0, ssent1, smet0, smet1,
+    result, finverse, sinverse, fseen2, fsend0, fsend1, sseen2, ssend0, ssend1, dots,
+    table, findex, sindex, floose, sloose, fz, sz, stage, total, squares,
 ):
+    (fodd, fheld), (sodd, sheld) = place_of()
+    in_rows(lines, table)
     weave(fcams, findex)
     weave(scams, sindex)
     total[...] = jnp.zeros_like(total)
     stage[...] = jnp.zeros_like(stage)
-    fweights = (1.0, weights[0])
-    sweights = (1.0, weights[1])
-    pair_solve(fsums, (fmet0, fmet1), weights[2], finverse, None, fz, None, None)
-    pair_return(fcam, fpoint, findex, fseen, fz, fweights, stage, total)
-    pair_solve(ssums, (smet0, smet1), weights[3], sinverse, None, sz, None, None)
-    pair_return(scam, spoint, sindex, sseen, sz, sweights, stage, total)
+    pair_solve((fsent0, fsent1), (fmet0, fmet1), finverse, None, fz, None, fodd, fheld)
+    pair_return(fcam, fpoint, findex, fseen, fz, fodd, fheld, stage, total)
+    pair_solve((ssent0, ssent1), (smet0, smet1), sinverse, None, sz, None, sodd, sheld)
+    pair_return(scam, spoint, sindex, sseen, sz, sodd, sheld, stage, total)
     step = folded(total) + extra[...]
     result[...] = step
     squares[...] = jnp.zeros_like(squares)
     sends = (fsend0, fsend1)
     pair_look(
-        fcam, fpoint, findex, result, fseen2, floose, fsums2, sends, weights[2], False,
-        squares, fweights,
+        fcam, fpoint, findex, result, fseen2, floose, sends, fodd, False, squares, fheld, None
     )
     sends = (ssend0, ssend1)
     pair_look(
-        scam, spoint, sindex, result, sseen2, sloose, ssums2, sends, weights[3], False,
-        squares, sweights,
+        scam, spoint, sindex, result, sseen2, sloose, sends, sodd, False, squares, sheld, None
     )
     base = table[...]
     dots[...] = jnp.zeros_like(dots)
@@ -290,16 +330,13 @@
 
 
 def dots_kernel(
-    weights, dots, product, fsums, fmet0, fmet1, finverse, ssums, smet0, smet1, sinverse,
-    fz, sz, out, products,
+    dots, product, fsent0, fsent1, fmet0, fmet1, finverse,
+    ssent0, ssent1, smet0, smet1, sinverse, fz, sz, out, products,
 ):
+    (fodd, fheld), (sodd, sheld) = place_of()
     products[...] = jnp.zeros_like(products)
-    pair_solve(
-        fsums, (fmet0, fmet1), weights[2], None, finverse, fz, products, (1.0, weights[0])
-    )
-    pair_solve(
-        ssums, (smet0, smet1), weights[3], None, sinverse, sz, products, (1.0, weights[1])
-    )
+    pair_solve((fsent0, fsent1), (fmet0, fmet1), None, finverse, fz, products, fodd, fheld)
+    pair_solve((ssent0, ssent1), (smet0, smet1), None, sinverse, sz, products, sodd, sheld)
     curve = dots[3:4, :] + product[0:1, :] - jnp.sum(products[...], axis=0, keepdims=True)
     rows = jnp.concatenate([dots[0:3, :], curve], axis=0)
     sums = jnp.sum(rows, axis=1, keepdims=True)
@@ -311,19 +348,21 @@
 
 
 def last_kernel(
-    weights, extra, fcam, fpoint, fcams, scam, spoint, scams, fseen, fz, sseen, sz,
+    extra, fcam, fpoint, fcams, scam, spoint, scams, fseen, fz, sseen, sz,
     result, findex, sindex, stage, total,
 ):
+    (fodd, fheld), (sodd, sheld) = place_of()
     weave(fcams, findex)
     weave(scams, sindex)
     total[...] = jnp.zeros_like(total)
     stage[...] = jnp.zeros_like(stage)
-    pair_return(fcam, fpoint, findex, fseen, fz, (1.0, weights[0]), stage, total)
-    pair_return(scam, spoint, sindex, sseen, sz, (1.0, weights[1]), stage, total)
+    pair_return(fcam, fpoint, findex, fseen, fz, fodd, fheld, stage, total)
+    pair_return(scam, spoint, sindex, sseen, sz, sodd, sheld, stage, total)
     result[...] = folded(total) + extra[...]
 
 
-def close_kernel(sums, base, first, second, step_out, residual_out):
+def close_kernel(sums, lines, first, second, step_out, residual_out, base):
+    in_rows(lines, base)
     line = jnp.sum(sums[...], axis=0, keepdims=True)
     place = lax.broadcasted_iota(jnp.int32, line.shape, 1)
     rr, bp, pp, curve = [
@@ -349,14 +388,14 @@
             residual_out[j, :, pl.ds(LANES * k, LANES)] = residual[row : row + 1, :]
 
 
-def call(kernel, ins, outs, scratch, flops, name, place=VMEM, room=12):
+def call(kernel, ins, outs, scratch, flops, name, place=VMEM, to=VMEM, room=12):
     outs = [jax.ShapeDtypeStruct(shape, F32) for shape in outs]
     specs = [SMEM if i == 0 and x.ndim == 1 else place for i, x in enumerate(ins)]
     return pl.pallas_call(
         kernel,
         out_shape=outs,
         in_specs=specs,
-        out_specs=[VMEM] * len(outs),
+        out_specs=[to] * len(outs),
         scratch_shapes=scratch,
         compiler_params=pltpu.CompilerParams(vmem_limit_bytes=room << 20),
         cost_estimate=pl.CostEstimate(flops=flops, bytes_accessed=2 << 20, transcendentals=0),
@@ -390,8 +429,6 @@
         pairs(lambda s, g: (s ^ 1, segs - 1 - g)),
         pairs(lambda s, g: ((s + 1 ^ 1) - 1, segs - 1 - g)),
     )
-    seg, strip = lax.axis_index("seg"), lax.axis_index("strip")
-    weights = jnp.stack([seg > 0, strip > 0, (seg & 1) > 0, (strip & 1) > 0]).astype(F32)
     live = live_blocks.reshape(1)
     lcam, lpoint = loc_cam_jac[:, :, 0], loc_point_jac[:, :, 0]
     lcams = loc_cams.reshape(-1, LANES)
@@ -413,54 +450,60 @@
         return [(parts, fr // 2, LANES)] * 2, [(parts, sr // 2, LANES)] * 2
 
     far = [gradient, fcam, fpoint, fcams, scam, spoint, scams]
+    table = [pltpu.VMEM((ROWS, LANES), F32)]
     fshapes, sshapes = sends_of(9)
-    base, fseen, fsums, *sends, sseen, ssums, ssend0, ssend1 = call(
+    shapes = [(2, 2, fr, LANES)] + fshapes + [(2, 2, sr, LANES)] + sshapes
+    fseen, *fsent, sseen, ssent0, ssent1 = call(
         look_kernel,
-        [weights] + far,
-        [(ROWS, LANES), (2, 2, fr, LANES), (2, 9, fr // 2, LANES)] + fshapes
-        + [(2, 2, sr, LANES), (2, 9, sr // 2, LANES)] + sshapes,
-        [pltpu.VMEM(far[n].shape, far[n].dtype) for n in (0, 1, 2, 3, 4, 5, 6)]
+        far,
+        shapes,
+        [pltpu.VMEM(x.shape, x.dtype) for x in far]
+        + [pltpu.VMEM(shape, F32) for shape in shapes]
+        + table
         + index_scratch
         + [pltpu.VMEM((9, fr, LANES), F32), pltpu.VMEM((9, sr, LANES), F32)]
-        + [pltpu.SemaphoreType.DMA((len(far),))],
+        + [pltpu.SemaphoreType.DMA((len(far),)), pltpu.SemaphoreType.DMA((len(shapes),))],
         10**9,
         "look",
         FAR,
+        FAR,
         63,
     )
-    smet = meet((ssend0, ssend1), side_rounds)
-    fmet = meet(sends, fwd_rounds)
-
-    def local(table):
+    ssent = [ssent0, ssent1]
+    smet = meet(ssent, side_rounds)
+    fmet = meet(fsent, fwd_rounds)
+
+    def local(values):
         return call(
             local_kernel,
-            [live, table, lcam, lpoint, lcams],
+            [live, values, lcam, lpoint, lcams],
             [(ROWS, LANES), (8, LANES)],
-            [pltpu.VMEM((watched * STACK, LANES), F32), pltpu.VMEM((STACK, LANES), F32)],
+            [pltpu.VMEM((watched * STACK, LANES), F32), pltpu.VMEM((STACK, LANES), F32)] + table,
             5 * 10**9,
             "local",
         )
 
-    extra, _ = local(base)
+    extra, _ = local(gradient)
     fshapes, sshapes = sends_of(3)
-    p, finverse, sinverse, fseen, fsums2, fsend0, fsend1, sseen, ssums2, ssend0, ssend1, dots = call(
+    p, finverse, sinverse, fseen, fsend0, fsend1, sseen, ssend0, ssend1, dots = call(
         middle_kernel,
-        [weights, base, extra, fcam, fpoint, fcams, scam, spoint, scams,
-         fseen, fsums, *fmet, sseen, ssums, *smet],
-        [(ROWS, LANES), (2, 6, fr // 2, LANES), (2, 6, sr // 2, LANES),
-         (2, 2, fr, LANES), (2, 3, fr // 2, LANES)] + fshapes
-        + [(2, 2, sr, LANES), (2, 3, sr // 2, LANES)] + sshapes + [(8, LANES)],
-        index_scratch + [pltpu.VMEM((3, fr, LANES), F32), pltpu.VMEM((3, sr, LANES), F32)]
+        [gradient, extra, fcam, fpoint, fcams, scam, spoint, scams,
+         fseen, *fsent, *fmet, sseen, *ssent, *smet],
+        [(ROWS, LANES), (2, 6, fr // 2, LANES), (2, 6, sr // 2, LANES), (2, 2, fr, LANES)]
+        + fshapes + [(2, 2, sr, LANES)] + sshapes + [(8, LANES)],
+        table + index_scratch
+        + [pltpu.VMEM((3, fr, LANES), F32), pltpu.VMEM((3, sr, LANES), F32)]
         + z_scratch + total_scratch + [pltpu.VMEM((STEP, LANES), F32)],
         10**10,
         "middle",
     )
-    smet = meet((ssend0, ssend1), side_rounds)
-    fmet = meet((fsend0, fsend1), fwd_rounds)
+    fsent, ssent = [fsend0, fsend1], [ssend0, ssend1]
+    smet = meet(ssent, side_rounds)
+    fmet = meet(fsent, fwd_rounds)
     extra, product = local(p)
     fz, sz, line = call(
         dots_kernel,
-        [weights, dots, product, fsums2, *fmet, finverse, ssums2, *smet, sinverse],
+        [dots, product, *fsent, *fmet, finverse, *ssent, *smet, sinverse],
         [(2, 3, fr, LANES), (2, 3, sr, LANES), (strips * segs, LANES)],
         [pltpu.VMEM((8, LANES), F32)],
         10**8,
@@ -469,14 +512,14 @@
     line = lax.all_to_all(line, AXES, 0, 0, tiled=True)
     (t,) = call(
         last_kernel,
-        [weights, extra, fcam, fpoint, fcams, scam, spoint, scams, fseen, fz, sseen, sz],
+        [extra, fcam, fpoint, fcams, scam, spoint, scams, fseen, fz, sseen, sz],
         [(ROWS, LANES)],
         index_scratch + total_scratch,
         5 * 10**9,
         "last",
     )
     step, residual = call(
-        close_kernel, [line, base, p, t], [gradient.shape] * 2, [], 10**6, "close"
+        close_kernel, [line, gradient, p, t], [gradient.shape] * 2, table, 10**6, "close"
     )
     return step, residual
 

time: 81.9 us -> 76.2 us (0.930); the launches traced: 80.8 us -> 76.1 us
  Pallas kernels: 32.8 us -> 30 us
  local copies, waits for them, and re-layouts: 1.27 us -> 0.08 us
    all_to_all x1, starting transfers between devices: 16.8 us -> 13.8 us  [per_device(): line = lax.all_to_all(line, AXES, 0, 0, tiled=True)]
    pallas_call x7, Pallas kernels: 32.8 us -> 30 us  [call(): pl.pallas_call(kernel, out_shape=outs, in_specs=specs, out_specs=[to] * l...]
    ppermute x8, starting transfers between devices: 21.7 us -> 23.9 us  [meet(): lax.ppermute(send, AXES, pairs)]
    unnamed x32, local copies, waits for them, and re-layouts: 1.27 us -> 0.08 us
where the time goes in v3:
time: 76.2 us; the launch traced here: 76.1 us
  starting transfers between devices  37.7 us (49%)
  Pallas kernels  30 us (39%)
  waiting for transfers between devices  6.63 us (9%)
  between operations  1.65 us (2%)
    pallas_call x7, Pallas kernels, call(): pl.pallas_call(kernel, out_shape=outs, in_specs=specs, out_specs=[to] * l...  30 us
    ppermute x8, starting transfers between devices, meet(): lax.ppermute(send, AXES, pairs)  23.9 us
    all_to_all x1, starting transfers between devices, per_device(): line = lax.all_to_all(line, AXES, 0, 0, tiled=True)  13.8 us
    all_to_all x1, waiting for transfers between devices, per_device(): line = lax.all_to_all(line, AXES, 0, 0, tiled=True)  6.61 us
  transfers between devices with their start and end apart: 9, of which 1 were waited for; matrix products, arithmetic and copies ran while one was open for 0% of the time, Pallas kernels for 20%

profile of v3, /device:TPU:1, one launch (start us, length us, event | category | flops | bytes accessed | tf_op | source)
XLA Modules:
  0.0 76.1 jit_solution(8873148142953704355)
XLA Ops:
  0.7 4.3 %look.1 = (f32[2,2,64,128]{3,2,1,0:T(8,128)}, f32[9,32,128]{2,1,0:T(8,128)}, f32[9,32,128]{2,1,0:T(8,128)}, f32[2,2,48,128]{3,2,1,0:T(8,128)}, f32[9,24,128]{2,1,0:T(8,128)}, /*index=5*/f32[9,24,128]{2,1,0:T(8,128)}) custom-call(f32[9,1,512]{2,1,0:T(1,128)} %lines.3, bf16[2,18,64,128]{3,2,1,0:T(8,128)(2,1)} %bitcast.35, bf16[2,6,64,128]{3,2,1,0:T(8,128)(2,1)} %bitcast.43, ...), custom_call_target="tpu_custom_call" | custom-call | flops 1000000000 | bytes 2097152 | tf_op jit(solution)/shard_map/look/pallas_call | solution.py:394
  5.0 5.3 %collective-permute-start.2 = (f32[9,24,128]{2,1,0:T(8,128)}, f32[9,24,128]{2,1,0:T(8,128)S(1)}, u32[]{:S(2)}, u32[]{:S(2)}) collective-permute-start(f32[9,24,128]{2,1,0:T(8,128)} %get-tuple-element.29.ssent0), channel_id=1, source_target_pairs={{0,15},{1,14},{2,13},{3,12},{4,11},{5,10},{6,9},{7,8},{8,7},{9,6},... | collective-permute-start | bytes 331784 | tf_op jit(solution)/shard_map/ppermute | solution.py:443
  10.3 4.6 %collective-permute-start.3 = (f32[9,24,128]{2,1,0:T(8,128)}, f32[9,24,128]{2,1,0:T(8,128)S(1)}, u32[]{:S(2)}, u32[]{:S(2)}) collective-permute-start(f32[9,24,128]{2,1,0:T(8,128)} %get-tuple-element.30.ssent1), channel_id=1, source_target_pairs={{8,23},{9,22},{10,21},{11,20},{12,19},{13,18},{14,17},{15,16},{16,... | collective-permute-start | bytes 331784 | tf_op jit(solution)/shard_map/ppermute | solution.py:443
  14.9 0.3 collective-permute-start
  15.2 0.7 collective-permute-start.1
  16.6 0.0 copy-start.2
  16.6 0.0 copy-start.3
  16.6 0.0 copy-start.5
  16.6 0.0 copy-start.6
  16.6 0.0 copy-start.11
  16.7 0.0 copy-start.13
  16.7 4.8 %local.2 = (f32[36,128]{1,0:T(8,128)S(1)}, f32[8,128]{1,0:T(8,128)}) custom-call(s32[1]{0:T(128)} %bitcast.30.live, f32[9,1,512]{2,1,0:T(1,128)S(1)} %copy-done, bf16[18,6,2048]{2,1,0:T(8,128)(2,1)S(1)} %bitcast.33, bf16[6,6,2048]{2,1,0:T(8,128)(2,1)S(1)} %bitcast.41, s32[96,128]{1,0:T(8,128)S(1)} %bitcast.52), custom_call_target="tpu_custom_call" | custom-call | flops 5000000000 | bytes 2097152 | tf_op jit(solution)/shard_map/local/pallas_call | solution.py:394
  21.5 0.0 collective-permute-done.1.fmet1
  21.6 8.8 %middle.1 = (f32[36,128]{1,0:T(8,128)S(1)}, f32[2,6,32,128]{3,2,1,0:T(8,128)S(1)}, f32[2,6,24,128]{3,2,1,0:T(8,128)S(1)}, f32[2,2,64,128]{3,2,1,0:T(8,128)S(1)},...) custom-call(f32[9,1,512]{2,1,0:T(1,128)S(1)} %copy-done, ...), custom_call_target="tpu_custom_call" | custom-call | flops 10000000000 | bytes 2097152 | tf_op jit(solution)/shard_map/middle/pallas_call | solution.py:394
  30.4 0.1 collective-permute-start.6
  30.5 10.8 %collective-permute-start.7 = (f32[3,24,128]{2,1,0:T(8,128)S(1)}, f32[3,24,128]{2,1,0:T(8,128)S(1)}, u32[]{:S(2)}, u32[]{:S(2)}) collective-permute-start(f32[3,24,128]{2,1,0:T(8,128)S(1)} %get-tuple-element.38.ssent1), channel_id=1, source_target_pairs={{8,23},{9,22},{10,21},{11,20},{12,19},{13,18},{14,17},{15,16},{16,... | collective-permute-start | bytes 110600 | tf_op jit(solution)/shard_map/ppermute | solution.py:443
  41.3 1.5 %collective-permute-start.4 = (f32[3,32,128]{2,1,0:T(8,128)S(1)}, f32[3,32,128]{2,1,0:T(8,128)S(1)}, u32[]{:S(2)}, u32[]{:S(2)}) collective-permute-start(f32[3,32,128]{2,1,0:T(8,128)S(1)} %get-tuple-element.34.fsent0), channel_id=1, source_target_pairs={{0,1},{1,0},{2,3},{3,2},{4,5},{5,4},{6,7},{7,6},{8,9},{9,8},{10,11... | collective-permute-start | bytes 147464 | tf_op jit(solution)/shard_map/ppermute | solution.py:443
  42.8 0.7 collective-permute-start.5
  43.5 4.2 %local.3 = (f32[36,128]{1,0:T(8,128)S(1)}, f32[8,128]{1,0:T(8,128)S(1)}) custom-call(s32[1]{0:T(128)} %bitcast.31.live, f32[36,128]{1,0:T(8,128)S(1)} %get-tuple-element.32.values.first, bf16[18,6,2048]{2,1,0:T(8,128)(2,1)S(1)} %bitcast.34, bf16[6,6,2048]{2,1,0:T(8,128)(2,1)S(1)} %bitcast.42, s32[96,128]{1,0:T(8,128)S(1)} %bitcast.53), custom_call_target="tpu_custom_call" | custom-call | flops 5000000000 | bytes 2097152 | tf_op jit(solution)/shard_map/local/pallas_call | solution.py:394
  47.7 0.8 %dots.1 = (f32[2,3,64,128]{3,2,1,0:T(8,128)S(1)}, f32[2,3,48,128]{3,2,1,0:T(8,128)S(1)}, f32[256,128]{1,0:T(8,128)}) custom-call(f32[8,128]{1,0:T(8,128)S(1)} %get-tuple-element.31.dots, f32[8,128]{1,0:T(8,128)S(1)} %get-tuple-element.33.product, f32[3,32,128]{2,1,0:T(8,128)S(1)} %get-tuple-element.34.fsent0, f32[3,32,128]{2,1,0:T(8,128)S(1)} %get-tuple-element.35.fsent1, ...), custom_call_target="tpu_custom_call" | custom-call | flops 100000000 | bytes 2097152 | tf_op jit(solution)/shard_map/dots/pallas_call | solution.py:394
  48.5 13.8 %all-to-all-start = ((f32[256,1,128]{2,1,0:T(1,128)}), f32[256,1,128]{2,1,0:T(1,128)S(1)}, u32[]{:S(2)}, u32[]{:S(2)}) async-start(f32[256,1,128]{2,1,0:T(1,128)} %bitcast.27), calls=%async_computation | async-start | bytes 262144 | tf_op jit(solution)/shard_map/all_to_all | solution.py:512
  62.3 6.4 %last.1.second = f32[36,128]{1,0:T(8,128)S(1)} custom-call(f32[36,128]{1,0:T(8,128)S(1)} %get-tuple-element.41.extra, bf16[2,18,64,128]{3,2,1,0:T(8,128)(2,1)S(1)} %bitcast.37, bf16[2,6,64,128]{3,2,1,0:T(8,128)(2,1)S(1)} %bitcast.45, s32[2,2,32,128]{3,2,1,0:T(8,128)S(1)} %bitcast.51, bf16[2,18,48,128]{3,2,1,0:T(8,128)(2,1)S(1)} %bitcast.40, ...), custom_call_target="tpu_custom_call" | custom-call | flops 5000000000 | bytes 2097152 | tf_op jit(solution)/shard_map/last/pallas_call | solution.py:394
  68.7 6.6 %all-to-all-done = f32[256,1,128]{2,1,0:T(1,128)S(1)} async-done(((f32[256,1,128]{2,1,0:T(1,128)}), f32[256,1,128]{2,1,0:T(1,128)S(1)}, u32[]{:S(2)}, u32[]{:S(2)}) %all-to-all-start) | async-done | bytes 131104 | tf_op jit(solution)/shard_map/all_to_all | solution.py:512
  75.3 0.8 %close.1 = (f32[9,1,512]{2,1,0:T(1,128)}, f32[9,1,512]{2,1,0:T(1,128)}) custom-call(f32[256,128]{1,0:T(8,128)S(1)} %bitcast.32, f32[9,1,512]{2,1,0:T(1,128)S(1)} %copy-done, f32[36,128]{1,0:T(8,128)S(1)} %get-tuple-element.32.values.first, f32[36,128]{1,0:T(8,128)S(1)} %last.1.second), custom_call_target="tpu_custom_call" | custom-call | flops 1000000 | bytes 2097152 | tf_op jit(solution)/shard_map/close/pallas_call | solution.py:394
  (33 shorter events, 0.1 us)
Async XLA Ops:
  0.6 15.9 %copy-start = (f32[9,1,512]{2,1,0:T(1,128)S(1)}, f32[9,1,512]{2,1,0:T(1,128)}, u32[]{:S(2)}) copy-start(f32[9,1,512]{2,1,0:T(1,128)} %lines.3) | copy-start | bytes 55300
  0.6 15.9 %copy-start.1 = (bf16[18,6,1,2048]{3,1,2,0:T(8,128)(2,1)S(1)}, bf16[18,6,1,2048]{3,1,2,0:T(8,128)(2,1)}, u32[]{:S(2)}) copy-start(bf16[18,6,1,2048]{3,1,2,0:T(8,128)(2,1)} %param.13) | copy-start | bytes 1327108
  0.7 15.9 %copy-start.4 = (bf16[6,6,1,2048]{3,1,2,0:T(8,128)(2,1)S(1)}, bf16[6,6,1,2048]{3,1,2,0:T(8,128)(2,1)}, u32[]{:S(2)}) copy-start(bf16[6,6,1,2048]{3,1,2,0:T(8,128)(2,1)} %param.14) | copy-start | bytes 442372
  0.7 15.9 %copy-start.12 = (s32[6,1,2048]{2,1,0:T(1,128)S(1)}, s32[6,1,2048]{2,1,0:T(1,128)}, u32[]{:S(2)}) copy-start(s32[6,1,2048]{2,1,0:T(1,128)} %param.15) | copy-start | bytes 147460
  5.0 16.5 %collective-permute-start.2 = (f32[9,24,128]{2,1,0:T(8,128)}, f32[9,24,128]{2,1,0:T(8,128)S(1)}, u32[]{:S(2)}, u32[]{:S(2)}) collective-permute-start(f32[9,24,128]{2,1,0:T(8,128)} %get-tuple-element.29.ssent0), channel_id=1, source_target_pairs={{0,15},{1,14},{2,13},{3,12},{4,11},{5,10},{6,9},{7,8},{8,7},{9,6},... | collective-permute-start | bytes 331784 | tf_op jit(solution)/shard_map/ppermute | solution.py:443
  10.3 11.1 %collective-permute-start.3 = (f32[9,24,128]{2,1,0:T(8,128)}, f32[9,24,128]{2,1,0:T(8,128)S(1)}, u32[]{:S(2)}, u32[]{:S(2)}) collective-permute-start(f32[9,24,128]{2,1,0:T(8,128)} %get-tuple-element.30.ssent1), channel_id=1, source_target_pairs={{8,23},{9,22},{10,21},{11,20},{12,19},{13,18},{14,17},{15,16},{16,... | collective-permute-start | bytes 331784 | tf_op jit(solution)/shard_map/ppermute | solution.py:443
  14.9 6.5 %collective-permute-start = (f32[9,32,128]{2,1,0:T(8,128)}, f32[9,32,128]{2,1,0:T(8,128)S(1)}, u32[]{:S(2)}, u32[]{:S(2)}) collective-permute-start(f32[9,32,128]{2,1,0:T(8,128)} %get-tuple-element.26.fsent0), channel_id=1, source_target_pairs={{0,1},{1,0},{2,3},{3,2},{4,5},{5,4},{6,7},{7,6},{8,9},{9,8},{10,11... | collective-permute-start | bytes 442376 | tf_op jit(solution)/shard_map/ppermute | solution.py:443
  15.2 6.3 %collective-permute-start.1 = (f32[9,32,128]{2,1,0:T(8,128)}, f32[9,32,128]{2,1,0:T(8,128)S(1)}, u32[]{:S(2)}, u32[]{:S(2)}) collective-permute-start(f32[9,32,128]{2,1,0:T(8,128)} %get-tuple-element.27.fsent1), channel_id=1, source_target_pairs={{1,2},{2,1},{3,4},{4,3},{5,6},{6,5},{9,10},{10,9},{11,12},{12,11},... | collective-permute-start | bytes 442376 | tf_op jit(solution)/shard_map/ppermute | solution.py:443
  16.6 4.9 %copy-start.2 = (bf16[2,18,2,1,4096]{4,2,3,1,0:T(2,128)(2,1)S(1)}, bf16[2,18,2,1,4096]{4,2,3,1,0:T(2,128)(2,1)}, u32[]{:S(2)}) copy-start(bf16[2,18,2,1,4096]{4,2,3,1,0:T(2,128)(2,1)} %param.16) | copy-start | bytes 1769476
  16.6 4.9 %copy-start.3 = (bf16[2,18,2,1,3072]{4,2,3,1,0:T(2,128)(2,1)S(1)}, bf16[2,18,2,1,3072]{4,2,3,1,0:T(2,128)(2,1)}, u32[]{:S(2)}) copy-start(bf16[2,18,2,1,3072]{4,2,3,1,0:T(2,128)(2,1)} %param.19) | copy-start | bytes 1327108
  16.6 4.9 %copy-start.5 = (bf16[2,6,2,1,4096]{4,2,3,1,0:T(2,128)(2,1)S(1)}, bf16[2,6,2,1,4096]{4,2,3,1,0:T(2,128)(2,1)}, u32[]{:S(2)}) copy-start(bf16[2,6,2,1,4096]{4,2,3,1,0:T(2,128)(2,1)} %param.17) | copy-start | bytes 589828
  16.6 4.9 %copy-start.6 = (bf16[2,6,2,1,3072]{4,2,3,1,0:T(2,128)(2,1)S(1)}, bf16[2,6,2,1,3072]{4,2,3,1,0:T(2,128)(2,1)}, u32[]{:S(2)}) copy-start(bf16[2,6,2,1,3072]{4,2,3,1,0:T(2,128)(2,1)} %param.20) | copy-start | bytes 442372
  16.6 4.9 %copy-start.7 = (f32[9,32,128]{2,1,0:T(8,128)S(1)}, f32[9,32,128]{2,1,0:T(8,128)}, u32[]{:S(2)}) copy-start(f32[9,32,128]{2,1,0:T(8,128)} %get-tuple-element.26.fsent0) | copy-start | bytes 442372
  16.6 4.9 %copy-start.8 = (f32[9,32,128]{2,1,0:T(8,128)S(1)}, f32[9,32,128]{2,1,0:T(8,128)}, u32[]{:S(2)}) copy-start(f32[9,32,128]{2,1,0:T(8,128)} %get-tuple-element.27.fsent1) | copy-start | bytes 442372
  16.6 4.9 %copy-start.9 = (f32[9,24,128]{2,1,0:T(8,128)S(1)}, f32[9,24,128]{2,1,0:T(8,128)}, u32[]{:S(2)}) copy-start(f32[9,24,128]{2,1,0:T(8,128)} %get-tuple-element.29.ssent0) | copy-start | bytes 331780
  16.6 4.9 %copy-start.10 = (f32[9,24,128]{2,1,0:T(8,128)S(1)}, f32[9,24,128]{2,1,0:T(8,128)}, u32[]{:S(2)}) copy-start(f32[9,24,128]{2,1,0:T(8,128)} %get-tuple-element.30.ssent1) | copy-start | bytes 331780
  16.6 4.9 %copy-start.11 = (s32[2,2,1,4096]{3,2,1,0:T(1,128)S(1)}, s32[2,2,1,4096]{3,2,1,0:T(1,128)}, u32[]{:S(2)}) copy-start(s32[2,2,1,4096]{3,2,1,0:T(1,128)} %param.18) | copy-start | bytes 196612
  16.7 4.9 %copy-start.13 = (s32[2,2,1,3072]{3,2,1,0:T(1,128)S(1)}, s32[2,2,1,3072]{3,2,1,0:T(1,128)}, u32[]{:S(2)}) copy-start(s32[2,2,1,3072]{3,2,1,0:T(1,128)} %param.21) | copy-start | bytes 147460
  16.7 4.9 %copy-start.14 = (f32[2,2,64,128]{3,2,1,0:T(8,128)S(1)}, f32[2,2,64,128]{3,2,1,0:T(8,128)}, u32[]{:S(2)}) copy-start(f32[2,2,64,128]{3,2,1,0:T(8,128)} %get-tuple-element.25.fseen) | copy-start | bytes 393220
  30.4 17.3 %collective-permute-start.6 = (f32[3,24,128]{2,1,0:T(8,128)S(1)}, f32[3,24,128]{2,1,0:T(8,128)S(1)}, u32[]{:S(2)}, u32[]{:S(2)}) collective-permute-start(f32[3,24,128]{2,1,0:T(8,128)S(1)} %get-tuple-element.37.ssent0), channel_id=1, source_target_pairs={{0,15},{1,14},{2,13},{3,12},{4,11},{5,10},{6,9},{7,8},{8,7},{9,6},... | collective-permute-start | bytes 110600 | tf_op jit(solution)/shard_map/ppermute | solution.py:443
  30.5 17.2 %collective-permute-start.7 = (f32[3,24,128]{2,1,0:T(8,128)S(1)}, f32[3,24,128]{2,1,0:T(8,128)S(1)}, u32[]{:S(2)}, u32[]{:S(2)}) collective-permute-start(f32[3,24,128]{2,1,0:T(8,128)S(1)} %get-tuple-element.38.ssent1), channel_id=1, source_target_pairs={{8,23},{9,22},{10,21},{11,20},{12,19},{13,18},{14,17},{15,16},{16,... | collective-permute-start | bytes 110600 | tf_op jit(solution)/shard_map/ppermute | solution.py:443
  41.3 6.4 %collective-permute-start.4 = (f32[3,32,128]{2,1,0:T(8,128)S(1)}, f32[3,32,128]{2,1,0:T(8,128)S(1)}, u32[]{:S(2)}, u32[]{:S(2)}) collective-permute-start(f32[3,32,128]{2,1,0:T(8,128)S(1)} %get-tuple-element.34.fsent0), channel_id=1, source_target_pairs={{0,1},{1,0},{2,3},{3,2},{4,5},{5,4},{6,7},{7,6},{8,9},{9,8},{10,11... | collective-permute-start | bytes 147464 | tf_op jit(solution)/shard_map/ppermute | solution.py:443
  42.8 4.9 %collective-permute-start.5 = (f32[3,32,128]{2,1,0:T(8,128)S(1)}, f32[3,32,128]{2,1,0:T(8,128)S(1)}, u32[]{:S(2)}, u32[]{:S(2)}) collective-permute-start(f32[3,32,128]{2,1,0:T(8,128)S(1)} %get-tuple-element.35.fsent1), channel_id=1, source_target_pairs={{1,2},{2,1},{3,4},{4,3},{5,6},{6,5},{9,10},{10,9},{11,12},{12,11},... | collective-permute-start | bytes 147464 | tf_op jit(solution)/shard_map/ppermute | solution.py:443
  48.5 26.8 %all-to-all-start = ((f32[256,1,128]{2,1,0:T(1,128)}), f32[256,1,128]{2,1,0:T(1,128)S(1)}, u32[]{:S(2)}, u32[]{:S(2)}) async-start(f32[256,1,128]{2,1,0:T(1,128)} %bitcast.27), calls=%async_computation | async-start | bytes 262144 | tf_op jit(solution)/shard_map/all_to_all | solution.py:512
  (1 other events, 4.9 us)

commit v4 on v3

--- a/solution.py
+++ b/solution.py
@@ -10,11 +10,9 @@
 JAC = 9
 PAGES = 4
 ROWS = JAC * PAGES
-LIFT = 40
-STACK = 2 * LIFT
+STACK = 80
 STEP = 16
-LOOK_UNROLL = 1
-RETURN_UNROLL = 1
+LOCAL_GROUP = 8
 SYM = ((0, 0), (0, 1), (0, 2), (1, 1), (1, 2), (2, 2))
 DAMP = 1.0
 VMEM = pl.BlockSpec(memory_space=pltpu.VMEM)
@@ -77,37 +75,58 @@
 
 
 def spread(terms, index, stage, total):
+    add_in([stacked(terms, index, stage)], total)
+
+
+def add_in(parts, total):
+    total[...] += lax.dot_general(
+        jnp.concatenate([x for left, _ in parts for x in left], axis=1),
+        jnp.concatenate([x for _, right in parts for x in right], axis=1),
+        (((1,), (1,)), ((), ())),
+        preferred_element_type=F32,
+    )
+
+
+def stacked(terms, index, stage):
     count = index.shape[0]
     page = index >> 7
-    hit = [page == h for h in range(PAGES)]
-    for j in range(JAC):
-        coarse = terms[j].astype(jnp.bfloat16).astype(F32)
-        fine = terms[j] - coarse
-        for h in range(PAGES):
-            row = PAGES * j + h
-            stage[pl.ds(row, count, stride=STACK), :] = jnp.where(hit[h], coarse, 0.0)
-            stage[pl.ds(LIFT + row, count, stride=STACK), :] = jnp.where(hit[h], fine, 0.0)
+    coarse = terms[JAC - 1].astype(jnp.bfloat16).astype(F32)
+    fine = terms[JAC - 1] - coarse
+    for j in range(JAC - 1):
+        stage[pl.ds(j, count, stride=16), :] = terms[j]
+    for h in range(PAGES):
+        stage[pl.ds(8 + h, count, stride=16), :] = jnp.where(page == h, coarse, 0.0)
+        stage[pl.ds(12 + h, count, stride=16), :] = jnp.where(page == h, fine, 0.0)
+    page = page.astype(F32)
     lane = (index & (LANES - 1)).astype(F32)
     place = lax.broadcasted_iota(jnp.int32, (LANES, LANES), 0).astype(F32).astype(jnp.bfloat16)
     one, none = jnp.ones((), jnp.bfloat16), jnp.zeros((), jnp.bfloat16)
-    group = 4 if count % 4 == 0 else 3
-    for start in range(0, count, group):
-        left, right = [], []
-        for row in range(start, start + group):
-            left.append(stage[pl.ds(row * STACK, STACK), :].astype(jnp.bfloat16))
-            wide = jnp.broadcast_to(lane[row : row + 1], (16, LANES)).astype(jnp.bfloat16)
-            wide = jnp.concatenate([wide] * (LANES // 16), axis=0)
-            right.append(jnp.where(wide == place, one, none))
-        total[...] += lax.dot_general(
-            jnp.concatenate(left, axis=1),
-            jnp.concatenate(right, axis=1),
-            (((1,), (1,)), ((), ())),
-            preferred_element_type=F32,
+    left, right = [], []
+    for row in range(count):
+        raw = stage[pl.ds(16 * row, 8), :]
+        rest = stage[pl.ds(16 * row + 8, 8), :]
+        coarse = raw.astype(jnp.bfloat16).astype(F32)
+        both = jnp.concatenate([coarse, raw - coarse], axis=0).astype(jnp.bfloat16)
+        wide = jnp.broadcast_to(page[row : row + 1], (16, LANES)).astype(jnp.bfloat16)
+        tiles = [jnp.where(wide == h, both, none) for h in range(PAGES)]
+        tiles.append(jnp.concatenate([rest, jnp.zeros_like(rest)], axis=0).astype(jnp.bfloat16))
+        left.append(jnp.concatenate(tiles, axis=0))
+        wide = jnp.broadcast_to(lane[row : row + 1], (16, LANES)).astype(jnp.bfloat16)
+        wide = jnp.concatenate([wide] * (LANES // 16), axis=0)
+        right.append(jnp.where(wide == place, one, none))
+    return left, right
+
+
+def scatter_scratch(count):
+    return [pltpu.VMEM((16 * count, LANES), F32), pltpu.VMEM((STACK, LANES), F32)]
+
+
+def fold(total, out):
+    for h in range(PAGES):
+        out[pl.ds(h, JAC - 1, stride=PAGES), :] = (
+            total[pl.ds(16 * h, 8), :] + total[pl.ds(16 * h + 8, 8), :]
         )
-
-
-def folded(total):
-    return total[0:ROWS, :] + total[LIFT : LIFT + ROWS, :]
+    out[pl.ds(ROWS - PAGES, PAGES), :] = total[64:68, :] + total[68:72, :]
 
 
 def weave(cams, index):
@@ -140,7 +159,7 @@
                 squares[...] += share * (seen[0] * seen[0] + seen[1] * seen[1])
             return carry
 
-        lax.fori_loop(0, rows // STEP, body, 0, unroll=LOOK_UNROLL)
+        lax.fori_loop(0, rows // STEP, body, 0, unroll=True)
         for n in range(9 if with_h else 3):
             sends[turn][n] = (
                 loose[n, pl.ds(0, half, stride=2), :] + loose[n, pl.ds(1, half, stride=2), :]
@@ -173,7 +192,7 @@
             spread(terms, index[s, at, :], stage, total)
             return carry
 
-        lax.fori_loop(0, rows // STEP, body, 0, unroll=RETURN_UNROLL)
+        lax.fori_loop(0, rows // STEP, body, 0, unroll=True)
 
 
 def pair_solve(sent, met, inverse_out, inverse_in, z, products, odd, held):
@@ -270,7 +289,6 @@
 
 def local_kernel(live, values, cam, point, cams, out, product, stage, total, table):
     total[...] = jnp.zeros_like(total)
-    stage[...] = jnp.zeros_like(stage)
     product[...] = jnp.zeros_like(product)
     if values.shape[0] == JAC:
         in_rows(values, table)
@@ -278,7 +296,7 @@
         table = values
     watched = cams.shape[0] // 16
 
-    def body(i, carry):
+    def block(i, stage):
         at = pl.ds(pl.multiple_of(i * LANES, LANES), LANES)
         index = cams[pl.ds(i, watched, stride=16), :]
         across = [cam[j, :, at].astype(F32) for j in range(2 * JAC)]
@@ -286,14 +304,23 @@
         seen = predict(across, fetch(table, index))
         summed = [jnp.sum(x, axis=0, keepdims=True) for x in project(along, seen) + normal(along)]
         z = solve(invert(summed[3:]), summed[:3])
-        left = residue(along, seen, z)
+        share = (i < live[0]).astype(F32)
+        left = [share * e for e in residue(along, seen, z)]
         terms = [across[j] * left[0] + across[JAC + j] * left[1] for j in range(JAC)]
-        product[0:1, :] += jnp.sum(seen[0] * left[0] + seen[1] * left[1], axis=0, keepdims=True)
-        spread(terms, index, stage, total)
+        seen = jnp.sum(seen[0] * left[0] + seen[1] * left[1], axis=0, keepdims=True)
+        return seen, stacked(terms, index, stage)
+
+    def body(i, carry):
+        done = [
+            block(LOCAL_GROUP * i + n, stage.at[pl.ds(16 * watched * n, 16 * watched)])
+            for n in range(LOCAL_GROUP)
+        ]
+        product[0:1, :] += sum(seen for seen, _ in done)
+        add_in([parts for _, parts in done], total)
         return carry
 
-    lax.fori_loop(0, live[0], body, 0)
-    out[...] = folded(total)
+    lax.fori_loop(0, (live[0] + LOCAL_GROUP - 1) // LOCAL_GROUP, body, 0)
+    fold(total, out)
 
 
 def middle_kernel(
@@ -307,12 +334,12 @@
     weave(fcams, findex)
     weave(scams, sindex)
     total[...] = jnp.zeros_like(total)
-    stage[...] = jnp.zeros_like(stage)
     pair_solve((fsent0, fsent1), (fmet0, fmet1), finverse, None, fz, None, fodd, fheld)
     pair_return(fcam, fpoint, findex, fseen, fz, fodd, fheld, stage, total)
     pair_solve((ssent0, ssent1), (smet0, smet1), sinverse, None, sz, None, sodd, sheld)
     pair_return(scam, spoint, sindex, sseen, sz, sodd, sheld, stage, total)
-    step = folded(total) + extra[...]
+    fold(total, result)
+    step = result[...] + extra[...]
     result[...] = step
     squares[...] = jnp.zeros_like(squares)
     sends = (fsend0, fsend1)
@@ -355,10 +382,10 @@
     weave(fcams, findex)
     weave(scams, sindex)
     total[...] = jnp.zeros_like(total)
-    stage[...] = jnp.zeros_like(stage)
     pair_return(fcam, fpoint, findex, fseen, fz, fodd, fheld, stage, total)
     pair_return(scam, spoint, sindex, sseen, sz, sodd, sheld, stage, total)
-    result[...] = folded(total) + extra[...]
+    fold(total, result)
+    result[...] += extra[...]
 
 
 def close_kernel(sums, lines, first, second, step_out, residual_out, base):
@@ -444,7 +471,7 @@
 
     index_scratch = [pltpu.VMEM((2, fr, LANES), jnp.int32), pltpu.VMEM((2, sr, LANES), jnp.int32)]
     z_scratch = [pltpu.VMEM((2, 3, fr, LANES), F32), pltpu.VMEM((2, 3, sr, LANES), F32)]
-    total_scratch = [pltpu.VMEM((STEP * STACK, LANES), F32), pltpu.VMEM((STACK, LANES), F32)]
+    total_scratch = scatter_scratch(STEP)
 
     def sends_of(parts):
         return [(parts, fr // 2, LANES)] * 2, [(parts, sr // 2, LANES)] * 2
@@ -478,7 +505,7 @@
             local_kernel,
             [live, values, lcam, lpoint, lcams],
             [(ROWS, LANES), (8, LANES)],
-            [pltpu.VMEM((watched * STACK, LANES), F32), pltpu.VMEM((STACK, LANES), F32)] + table,
+            scatter_scratch(watched * LOCAL_GROUP) + table,
             5 * 10**9,
             "local",
         )

time: 76.2 us -> 71.1 us (0.933)
  Pallas kernels: 30 us -> 16.1 us
  waiting for transfers between devices: 6.63 us -> 12.7 us
  starting transfers between devices: 37.7 us -> 40.3 us
    pallas_call x7, Pallas kernels: 30 us -> 16.1 us  [call(): pl.pallas_call(kernel, out_shape=outs, in_specs=specs, out_specs=[to] * l...]
    all_to_all x1, waiting for transfers between devices: 6.61 us -> 10.4 us  [per_device(): line = lax.all_to_all(line, AXES, 0, 0, tiled=True)]
    all_to_all x1, starting transfers between devices: 13.8 us -> 17 us  [per_device(): line = lax.all_to_all(line, AXES, 0, 0, tiled=True)]
    ppermute x8, waiting for transfers between devices: 0.02 us -> 2.34 us  [meet(): lax.ppermute(send, AXES, pairs)]
  transfers between devices with their start and end apart: 9 -> 9, of which waited for: 1 -> 2; matrix products, arithmetic and copies ran while one was open for 0% -> 0% of each run, Pallas kernels for 20% -> 7%
where the time goes in v4:
time: 71.1 us; the launch traced here: 70.8 us
  starting transfers between devices  40.3 us (57%)
  Pallas kernels  16.1 us (23%)
  waiting for transfers between devices  12.7 us (18%)
  between operations  1.62 us (2%)
    ppermute x8, starting transfers between devices, meet(): lax.ppermute(send, AXES, pairs)  23.3 us
    all_to_all x1, starting transfers between devices, per_device(): line = lax.all_to_all(line, AXES, 0, 0, tiled=True)  17 us
    pallas_call x7, Pallas kernels, call(): pl.pallas_call(kernel, out_shape=outs, in_specs=specs, out_specs=[to] * l...  16.1 us
    all_to_all x1, waiting for transfers between devices, per_device(): line = lax.all_to_all(line, AXES, 0, 0, tiled=True)  10.4 us
    ppermute x8, waiting for transfers between devices, meet(): lax.ppermute(send, AXES, pairs)  2.34 us
  transfers between devices with their start and end apart: 9, of which 2 were waited for; matrix products, arithmetic and copies ran while one was open for 0% of the time, Pallas kernels for 7%

profile of v4, /device:TPU:1, one launch (start us, length us, event | category | flops | bytes accessed | tf_op | source)
XLA Modules:
  0.0 70.8 jit_solution(9110928855520001501)
XLA Ops:
  0.7 4.2 %look.1 = (f32[2,2,64,128]{3,2,1,0:T(8,128)}, f32[9,32,128]{2,1,0:T(8,128)}, f32[9,32,128]{2,1,0:T(8,128)}, f32[2,2,48,128]{3,2,1,0:T(8,128)}, f32[9,24,128]{2,1,0:T(8,128)}, /*index=5*/f32[9,24,128]{2,1,0:T(8,128)}) custom-call(f32[9,1,512]{2,1,0:T(1,128)} %lines.3, bf16[2,18,64,128]{3,2,1,0:T(8,128)(2,1)} %bitcast.35, bf16[2,6,64,128]{3,2,1,0:T(8,128)(2,1)} %bitcast.43, ...), custom_call_target="tpu_custom_call" | custom-call | flops 1000000000 | bytes 2097152 | tf_op jit(solution)/shard_map/look/pallas_call | solution.py:421
  4.9 5.3 %collective-permute-start.2 = (f32[9,24,128]{2,1,0:T(8,128)}, f32[9,24,128]{2,1,0:T(8,128)S(1)}, u32[]{:S(2)}, u32[]{:S(2)}) collective-permute-start(f32[9,24,128]{2,1,0:T(8,128)} %get-tuple-element.29.ssent0), channel_id=1, source_target_pairs={{0,15},{1,14},{2,13},{3,12},{4,11},{5,10},{6,9},{7,8},{8,7},{9,6},... | collective-permute-start | bytes 331784 | tf_op jit(solution)/shard_map/ppermute | solution.py:470
  10.2 4.6 %collective-permute-start.3 = (f32[9,24,128]{2,1,0:T(8,128)}, f32[9,24,128]{2,1,0:T(8,128)S(1)}, u32[]{:S(2)}, u32[]{:S(2)}) collective-permute-start(f32[9,24,128]{2,1,0:T(8,128)} %get-tuple-element.30.ssent1), channel_id=1, source_target_pairs={{8,23},{9,22},{10,21},{11,20},{12,19},{13,18},{14,17},{15,16},{16,... | collective-permute-start | bytes 331784 | tf_op jit(solution)/shard_map/ppermute | solution.py:470
  14.8 0.3 collective-permute-start
  15.1 0.7 collective-permute-start.1
  16.4 0.0 copy-start.2
  16.4 0.0 copy-start.3
  16.4 0.0 copy-start.5
  16.5 0.0 copy-start.6
  16.5 0.0 copy-start.11
  16.6 1.6 %local.2 = (f32[36,128]{1,0:T(8,128)S(1)}, f32[8,128]{1,0:T(8,128)}) custom-call(s32[1]{0:T(128)} %bitcast.30.live, f32[9,1,512]{2,1,0:T(1,128)S(1)} %copy-done, bf16[18,6,2048]{2,1,0:T(8,128)(2,1)S(1)} %bitcast.33, bf16[6,6,2048]{2,1,0:T(8,128)(2,1)S(1)} %bitcast.41, s32[96,128]{1,0:T(8,128)S(1)} %bitcast.52), custom_call_target="tpu_custom_call" | custom-call | flops 5000000000 | bytes 2097152 | tf_op jit(solution)/shard_map/local/pallas_call | solution.py:421
  18.1 2.3 %collective-permute-done.3.smet1 = f32[9,24,128]{2,1,0:T(8,128)S(1)} collective-permute-done((f32[9,24,128]{2,1,0:T(8,128)}, f32[9,24,128]{2,1,0:T(8,128)S(1)}, u32[]{:S(2)}, u32[]{:S(2)}) %collective-permute-start.3) | collective-permute-done | bytes 110624 | tf_op jit(solution)/shard_map/ppermute | solution.py:470
  20.6 5.2 %middle.1 = (f32[36,128]{1,0:T(8,128)S(1)}, f32[2,6,32,128]{3,2,1,0:T(8,128)S(1)}, f32[2,6,24,128]{3,2,1,0:T(8,128)S(1)}, f32[2,2,64,128]{3,2,1,0:T(8,128)S(1)},...) custom-call(f32[9,1,512]{2,1,0:T(1,128)S(1)} %copy-done, ...), custom_call_target="tpu_custom_call" | custom-call | flops 10000000000 | bytes 2097152 | tf_op jit(solution)/shard_map/middle/pallas_call | solution.py:421
  25.8 0.1 collective-permute-start.6
  25.9 10.3 %collective-permute-start.7 = (f32[3,24,128]{2,1,0:T(8,128)S(1)}, f32[3,24,128]{2,1,0:T(8,128)S(1)}, u32[]{:S(2)}, u32[]{:S(2)}) collective-permute-start(f32[3,24,128]{2,1,0:T(8,128)S(1)} %get-tuple-element.38.ssent1), channel_id=1, source_target_pairs={{8,23},{9,22},{10,21},{11,20},{12,19},{13,18},{14,17},{15,16},{16,... | collective-permute-start | bytes 110600 | tf_op jit(solution)/shard_map/ppermute | solution.py:470
  36.2 1.4 %collective-permute-start.4 = (f32[3,32,128]{2,1,0:T(8,128)S(1)}, f32[3,32,128]{2,1,0:T(8,128)S(1)}, u32[]{:S(2)}, u32[]{:S(2)}) collective-permute-start(f32[3,32,128]{2,1,0:T(8,128)S(1)} %get-tuple-element.34.fsent0), channel_id=1, source_target_pairs={{0,1},{1,0},{2,3},{3,2},{4,5},{5,4},{6,7},{7,6},{8,9},{9,8},{10,11... | collective-permute-start | bytes 147464 | tf_op jit(solution)/shard_map/ppermute | solution.py:470
  37.6 0.7 collective-permute-start.5
  38.2 1.0 %local.3 = (f32[36,128]{1,0:T(8,128)S(1)}, f32[8,128]{1,0:T(8,128)S(1)}) custom-call(s32[1]{0:T(128)} %bitcast.31.live, f32[36,128]{1,0:T(8,128)S(1)} %get-tuple-element.32.values.first, bf16[18,6,2048]{2,1,0:T(8,128)(2,1)S(1)} %bitcast.34, bf16[6,6,2048]{2,1,0:T(8,128)(2,1)S(1)} %bitcast.42, s32[96,128]{1,0:T(8,128)S(1)} %bitcast.53), custom_call_target="tpu_custom_call" | custom-call | flops 5000000000 | bytes 2097152 | tf_op jit(solution)/shard_map/local/pallas_call | solution.py:421
  39.2 0.0 collective-permute-done.4.fmet0
  39.2 0.8 %dots.1 = (f32[2,3,64,128]{3,2,1,0:T(8,128)S(1)}, f32[2,3,48,128]{3,2,1,0:T(8,128)S(1)}, f32[256,128]{1,0:T(8,128)}) custom-call(f32[8,128]{1,0:T(8,128)S(1)} %get-tuple-element.31.dots, f32[8,128]{1,0:T(8,128)S(1)} %get-tuple-element.33.product, f32[3,32,128]{2,1,0:T(8,128)S(1)} %get-tuple-element.34.fsent0, f32[3,32,128]{2,1,0:T(8,128)S(1)} %get-tuple-element.35.fsent1, ...), custom_call_target="tpu_custom_call" | custom-call | flops 100000000 | bytes 2097152 | tf_op jit(solution)/shard_map/dots/pallas_call | solution.py:421
  40.1 17.0 %all-to-all-start = ((f32[256,1,128]{2,1,0:T(1,128)}), f32[256,1,128]{2,1,0:T(1,128)S(1)}, u32[]{:S(2)}, u32[]{:S(2)}) async-start(f32[256,1,128]{2,1,0:T(1,128)} %bitcast.27), calls=%async_computation | async-start | bytes 262144 | tf_op jit(solution)/shard_map/all_to_all | solution.py:539
  57.1 2.6 %last.1.second = f32[36,128]{1,0:T(8,128)S(1)} custom-call(f32[36,128]{1,0:T(8,128)S(1)} %get-tuple-element.41.extra, bf16[2,18,64,128]{3,2,1,0:T(8,128)(2,1)S(1)} %bitcast.37, bf16[2,6,64,128]{3,2,1,0:T(8,128)(2,1)S(1)} %bitcast.45, s32[2,2,32,128]{3,2,1,0:T(8,128)S(1)} %bitcast.51, bf16[2,18,48,128]{3,2,1,0:T(8,128)(2,1)S(1)} %bitcast.40, ...), custom_call_target="tpu_custom_call" | custom-call | flops 5000000000 | bytes 2097152 | tf_op jit(solution)/shard_map/last/pallas_call | solution.py:421
  59.7 10.4 %all-to-all-done = f32[256,1,128]{2,1,0:T(1,128)S(1)} async-done(((f32[256,1,128]{2,1,0:T(1,128)}), f32[256,1,128]{2,1,0:T(1,128)S(1)}, u32[]{:S(2)}, u32[]{:S(2)}) %all-to-all-start) | async-done | bytes 131104 | tf_op jit(solution)/shard_map/all_to_all | solution.py:539
  70.1 0.8 %close.1 = (f32[9,1,512]{2,1,0:T(1,128)}, f32[9,1,512]{2,1,0:T(1,128)}) custom-call(f32[256,128]{1,0:T(8,128)S(1)} %bitcast.32, f32[9,1,512]{2,1,0:T(1,128)S(1)} %copy-done, f32[36,128]{1,0:T(8,128)S(1)} %get-tuple-element.32.values.first, f32[36,128]{1,0:T(8,128)S(1)} %last.1.second), custom_call_target="tpu_custom_call" | custom-call | flops 1000000 | bytes 2097152 | tf_op jit(solution)/shard_map/close/pallas_call | solution.py:421
  (33 shorter events, 0.1 us)
Async XLA Ops:
  0.6 15.8 %copy-start = (f32[9,1,512]{2,1,0:T(1,128)S(1)}, f32[9,1,512]{2,1,0:T(1,128)}, u32[]{:S(2)}) copy-start(f32[9,1,512]{2,1,0:T(1,128)} %lines.3) | copy-start | bytes 55300
  0.6 15.8 %copy-start.1 = (bf16[18,6,1,2048]{3,1,2,0:T(8,128)(2,1)S(1)}, bf16[18,6,1,2048]{3,1,2,0:T(8,128)(2,1)}, u32[]{:S(2)}) copy-start(bf16[18,6,1,2048]{3,1,2,0:T(8,128)(2,1)} %param.13) | copy-start | bytes 1327108
  0.7 15.8 %copy-start.4 = (bf16[6,6,1,2048]{3,1,2,0:T(8,128)(2,1)S(1)}, bf16[6,6,1,2048]{3,1,2,0:T(8,128)(2,1)}, u32[]{:S(2)}) copy-start(bf16[6,6,1,2048]{3,1,2,0:T(8,128)(2,1)} %param.14) | copy-start | bytes 442372
  0.7 15.8 %copy-start.12 = (s32[6,1,2048]{2,1,0:T(1,128)S(1)}, s32[6,1,2048]{2,1,0:T(1,128)}, u32[]{:S(2)}) copy-start(s32[6,1,2048]{2,1,0:T(1,128)} %param.15) | copy-start | bytes 147460
  4.9 13.3 %collective-permute-start.2 = (f32[9,24,128]{2,1,0:T(8,128)}, f32[9,24,128]{2,1,0:T(8,128)S(1)}, u32[]{:S(2)}, u32[]{:S(2)}) collective-permute-start(f32[9,24,128]{2,1,0:T(8,128)} %get-tuple-element.29.ssent0), channel_id=1, source_target_pairs={{0,15},{1,14},{2,13},{3,12},{4,11},{5,10},{6,9},{7,8},{8,7},{9,6},... | collective-permute-start | bytes 331784 | tf_op jit(solution)/shard_map/ppermute | solution.py:470
  10.2 10.3 %collective-permute-start.3 = (f32[9,24,128]{2,1,0:T(8,128)}, f32[9,24,128]{2,1,0:T(8,128)S(1)}, u32[]{:S(2)}, u32[]{:S(2)}) collective-permute-start(f32[9,24,128]{2,1,0:T(8,128)} %get-tuple-element.30.ssent1), channel_id=1, source_target_pairs={{8,23},{9,22},{10,21},{11,20},{12,19},{13,18},{14,17},{15,16},{16,... | collective-permute-start | bytes 331784 | tf_op jit(solution)/shard_map/ppermute | solution.py:470
  14.8 5.7 %collective-permute-start = (f32[9,32,128]{2,1,0:T(8,128)}, f32[9,32,128]{2,1,0:T(8,128)S(1)}, u32[]{:S(2)}, u32[]{:S(2)}) collective-permute-start(f32[9,32,128]{2,1,0:T(8,128)} %get-tuple-element.26.fsent0), channel_id=1, source_target_pairs={{0,1},{1,0},{2,3},{3,2},{4,5},{5,4},{6,7},{7,6},{8,9},{9,8},{10,11... | collective-permute-start | bytes 442376 | tf_op jit(solution)/shard_map/ppermute | solution.py:470
  15.1 5.4 %collective-permute-start.1 = (f32[9,32,128]{2,1,0:T(8,128)}, f32[9,32,128]{2,1,0:T(8,128)S(1)}, u32[]{:S(2)}, u32[]{:S(2)}) collective-permute-start(f32[9,32,128]{2,1,0:T(8,128)} %get-tuple-element.27.fsent1), channel_id=1, source_target_pairs={{1,2},{2,1},{3,4},{4,3},{5,6},{6,5},{9,10},{10,9},{11,12},{12,11},... | collective-permute-start | bytes 442376 | tf_op jit(solution)/shard_map/ppermute | solution.py:470
  16.4 4.0 %copy-start.2 = (bf16[2,18,2,1,4096]{4,2,3,1,0:T(2,128)(2,1)S(1)}, bf16[2,18,2,1,4096]{4,2,3,1,0:T(2,128)(2,1)}, u32[]{:S(2)}) copy-start(bf16[2,18,2,1,4096]{4,2,3,1,0:T(2,128)(2,1)} %param.16) | copy-start | bytes 1769476
  16.4 4.0 %copy-start.3 = (bf16[2,18,2,1,3072]{4,2,3,1,0:T(2,128)(2,1)S(1)}, bf16[2,18,2,1,3072]{4,2,3,1,0:T(2,128)(2,1)}, u32[]{:S(2)}) copy-start(bf16[2,18,2,1,3072]{4,2,3,1,0:T(2,128)(2,1)} %param.19) | copy-start | bytes 1327108
  16.4 4.0 %copy-start.5 = (bf16[2,6,2,1,4096]{4,2,3,1,0:T(2,128)(2,1)S(1)}, bf16[2,6,2,1,4096]{4,2,3,1,0:T(2,128)(2,1)}, u32[]{:S(2)}) copy-start(bf16[2,6,2,1,4096]{4,2,3,1,0:T(2,128)(2,1)} %param.17) | copy-start | bytes 589828
  16.5 4.0 %copy-start.6 = (bf16[2,6,2,1,3072]{4,2,3,1,0:T(2,128)(2,1)S(1)}, bf16[2,6,2,1,3072]{4,2,3,1,0:T(2,128)(2,1)}, u32[]{:S(2)}) copy-start(bf16[2,6,2,1,3072]{4,2,3,1,0:T(2,128)(2,1)} %param.20) | copy-start | bytes 442372
  16.5 4.0 %copy-start.7 = (f32[9,32,128]{2,1,0:T(8,128)S(1)}, f32[9,32,128]{2,1,0:T(8,128)}, u32[]{:S(2)}) copy-start(f32[9,32,128]{2,1,0:T(8,128)} %get-tuple-element.26.fsent0) | copy-start | bytes 442372
  16.5 4.0 %copy-start.8 = (f32[9,32,128]{2,1,0:T(8,128)S(1)}, f32[9,32,128]{2,1,0:T(8,128)}, u32[]{:S(2)}) copy-start(f32[9,32,128]{2,1,0:T(8,128)} %get-tuple-element.27.fsent1) | copy-start | bytes 442372
  16.5 4.0 %copy-start.9 = (f32[9,24,128]{2,1,0:T(8,128)S(1)}, f32[9,24,128]{2,1,0:T(8,128)}, u32[]{:S(2)}) copy-start(f32[9,24,128]{2,1,0:T(8,128)} %get-tuple-element.29.ssent0) | copy-start | bytes 331780
  16.5 4.0 %copy-start.10 = (f32[9,24,128]{2,1,0:T(8,128)S(1)}, f32[9,24,128]{2,1,0:T(8,128)}, u32[]{:S(2)}) copy-start(f32[9,24,128]{2,1,0:T(8,128)} %get-tuple-element.30.ssent1) | copy-start | bytes 331780
  16.5 4.0 %copy-start.11 = (s32[2,2,1,4096]{3,2,1,0:T(1,128)S(1)}, s32[2,2,1,4096]{3,2,1,0:T(1,128)}, u32[]{:S(2)}) copy-start(s32[2,2,1,4096]{3,2,1,0:T(1,128)} %param.18) | copy-start | bytes 196612
  16.5 4.0 %copy-start.13 = (s32[2,2,1,3072]{3,2,1,0:T(1,128)S(1)}, s32[2,2,1,3072]{3,2,1,0:T(1,128)}, u32[]{:S(2)}) copy-start(s32[2,2,1,3072]{3,2,1,0:T(1,128)} %param.21) | copy-start | bytes 147460
  16.5 4.0 %copy-start.14 = (f32[2,2,64,128]{3,2,1,0:T(8,128)S(1)}, f32[2,2,64,128]{3,2,1,0:T(8,128)}, u32[]{:S(2)}) copy-start(f32[2,2,64,128]{3,2,1,0:T(8,128)} %get-tuple-element.25.fseen) | copy-start | bytes 393220
  25.8 13.4 %collective-permute-start.6 = (f32[3,24,128]{2,1,0:T(8,128)S(1)}, f32[3,24,128]{2,1,0:T(8,128)S(1)}, u32[]{:S(2)}, u32[]{:S(2)}) collective-permute-start(f32[3,24,128]{2,1,0:T(8,128)S(1)} %get-tuple-element.37.ssent0), channel_id=1, source_target_pairs={{0,15},{1,14},{2,13},{3,12},{4,11},{5,10},{6,9},{7,8},{8,7},{9,6},... | collective-permute-start | bytes 110600 | tf_op jit(solution)/shard_map/ppermute | solution.py:470
  25.9 13.3 %collective-permute-start.7 = (f32[3,24,128]{2,1,0:T(8,128)S(1)}, f32[3,24,128]{2,1,0:T(8,128)S(1)}, u32[]{:S(2)}, u32[]{:S(2)}) collective-permute-start(f32[3,24,128]{2,1,0:T(8,128)S(1)} %get-tuple-element.38.ssent1), channel_id=1, source_target_pairs={{8,23},{9,22},{10,21},{11,20},{12,19},{13,18},{14,17},{15,16},{16,... | collective-permute-start | bytes 110600 | tf_op jit(solution)/shard_map/ppermute | solution.py:470
  36.2 3.0 %collective-permute-start.4 = (f32[3,32,128]{2,1,0:T(8,128)S(1)}, f32[3,32,128]{2,1,0:T(8,128)S(1)}, u32[]{:S(2)}, u32[]{:S(2)}) collective-permute-start(f32[3,32,128]{2,1,0:T(8,128)S(1)} %get-tuple-element.34.fsent0), channel_id=1, source_target_pairs={{0,1},{1,0},{2,3},{3,2},{4,5},{5,4},{6,7},{7,6},{8,9},{9,8},{10,11... | collective-permute-start | bytes 147464 | tf_op jit(solution)/shard_map/ppermute | solution.py:470
  37.6 1.7 %collective-permute-start.5 = (f32[3,32,128]{2,1,0:T(8,128)S(1)}, f32[3,32,128]{2,1,0:T(8,128)S(1)}, u32[]{:S(2)}, u32[]{:S(2)}) collective-permute-start(f32[3,32,128]{2,1,0:T(8,128)S(1)} %get-tuple-element.35.fsent1), channel_id=1, source_target_pairs={{1,2},{2,1},{3,4},{4,3},{5,6},{6,5},{9,10},{10,9},{11,12},{12,11},... | collective-permute-start | bytes 147464 | tf_op jit(solution)/shard_map/ppermute | solution.py:470
  40.1 30.0 %all-to-all-start = ((f32[256,1,128]{2,1,0:T(1,128)}), f32[256,1,128]{2,1,0:T(1,128)S(1)}, u32[]{:S(2)}, u32[]{:S(2)}) async-start(f32[256,1,128]{2,1,0:T(1,128)} %bitcast.27), calls=%async_computation | async-start | bytes 262144 | tf_op jit(solution)/shard_map/all_to_all | solution.py:539
  (1 other events, 4.0 us)

commit v5 on v4

--- a/solution.py
+++ b/solution.py
@@ -1,3 +1,5 @@
+import functools
+
 import jax
 import jax.numpy as jnp
 from jax import lax
@@ -169,12 +171,14 @@
 
 
 def part_of(side, held):
+    if isinstance(side, int):
+        return 1.0 if side == 0 else held.astype(F32)
     return jnp.where(side == 0, 1, held).astype(F32)
 
 
-def pair_return(cam, point, index, seen_in, z, odd, held, stage, total):
+def pair_return(cam, point, index, seen_in, z, odd, held, stage, total, turns=(0, 1)):
     rows = cam.shape[2]
-    for turn in range(2):
+    for turn in turns:
         s = turn ^ odd
         share = part_of(s, held)
 
@@ -195,28 +199,37 @@
         lax.fori_loop(0, rows // STEP, body, 0, unroll=True)
 
 
-def pair_solve(sent, met, inverse_out, inverse_in, z, products, odd, held):
+def pair_solve(sent, met, inverse_out, z):
     half = sent[0].shape[1]
     for turn in range(2):
-        share = part_of(turn ^ odd, held)
         for i in range(half // 8):
             at = pl.ds(8 * i, 8)
-            mine = [sent[turn][k, at, :] for k in range(3)]
-            b = [mine[k] + met[turn][k, at, :] for k in range(3)]
-            if inverse_in is None:
-                inverse = invert(
-                    [sent[turn][3 + k, at, :] + met[turn][3 + k, at, :] for k in range(6)]
-                )
-                for k in range(6):
-                    inverse_out[turn, k, at, :] = inverse[k]
-            else:
-                inverse = [inverse_in[turn, k, at, :] for k in range(6)]
-            solved = solve(inverse, b)
-            if products is not None:
-                products[...] += share * sum(mine[k] * solved[k] for k in range(3))
-            for k in range(3):
-                for o in range(2):
-                    z[turn, k, pl.ds(16 * i + o, 8, stride=2), :] = solved[k]
+            joined = [sent[turn][k, at, :] + met[turn][k, at, :] for k in range(9)]
+            inverse = invert(joined[3:])
+            for k in range(6):
+                inverse_out[turn, k, at, :] = inverse[k]
+            put_z(z, turn, i, solve(inverse, joined[:3]))
+
+
+def put_z(z, turn, i, solved):
+    for k in range(3):
+        for o in range(2):
+            z[turn, k, pl.ds(16 * i + o, 8, stride=2), :] = solved[k]
+
+
+def own_solve(own, met, inverse, z, products, odd):
+    for i in range(own.shape[1] // 8):
+        at = pl.ds(8 * i, 8)
+        b = [own[k, at, :] + met[k, at, :] for k in range(3)]
+        solved = solve([inverse[odd, k, at, :] for k in range(6)], b)
+        products[...] += sum(b[k] * solved[k] for k in range(3))
+        for k in range(3):
+            z[k, at, :] = solved[k]
+
+
+def widened(values, z, turn):
+    for i in range(values.shape[1] // 8):
+        put_z(z, turn, i, [values[k, pl.ds(8 * i, 8), :] for k in range(3)])
 
 
 def place_of():
@@ -326,7 +339,7 @@
 def middle_kernel(
     lines, extra, fcam, fpoint, fcams, scam, spoint, scams,
     fseen, fsent0, fsent1, fmet0, fmet1, sseen, ssent0, ssent1, smet0, smet1,
-    result, finverse, sinverse, fseen2, fsend0, fsend1, sseen2, ssend0, ssend1, dots,
+    result, finverse, sinverse, fseen2, fown, fguest, sseen2, sown, sguest, dots,
     table, findex, sindex, floose, sloose, fz, sz, stage, total, squares,
 ):
     (fodd, fheld), (sodd, sheld) = place_of()
@@ -334,22 +347,18 @@
     weave(fcams, findex)
     weave(scams, sindex)
     total[...] = jnp.zeros_like(total)
-    pair_solve((fsent0, fsent1), (fmet0, fmet1), finverse, None, fz, None, fodd, fheld)
+    pair_solve((fsent0, fsent1), (fmet0, fmet1), finverse, fz)
     pair_return(fcam, fpoint, findex, fseen, fz, fodd, fheld, stage, total)
-    pair_solve((ssent0, ssent1), (smet0, smet1), sinverse, None, sz, None, sodd, sheld)
+    pair_solve((ssent0, ssent1), (smet0, smet1), sinverse, sz)
     pair_return(scam, spoint, sindex, sseen, sz, sodd, sheld, stage, total)
     fold(total, result)
     step = result[...] + extra[...]
     result[...] = step
     squares[...] = jnp.zeros_like(squares)
-    sends = (fsend0, fsend1)
-    pair_look(
-        fcam, fpoint, findex, result, fseen2, floose, sends, fodd, False, squares, fheld, None
-    )
-    sends = (ssend0, ssend1)
-    pair_look(
-        scam, spoint, sindex, result, sseen2, sloose, sends, sodd, False, squares, sheld, None
-    )
+    sides = (fown, fguest)
+    pair_look(fcam, fpoint, findex, result, fseen2, floose, sides, 0, False, squares, fheld, None)
+    sides = (sown, sguest)
+    pair_look(scam, spoint, sindex, result, sseen2, sloose, sides, 0, False, squares, sheld, None)
     base = table[...]
     dots[...] = jnp.zeros_like(dots)
     for row, value in enumerate((base * base, base * step, step * step, squares[...])):
@@ -357,13 +366,12 @@
 
 
 def dots_kernel(
-    dots, product, fsent0, fsent1, fmet0, fmet1, finverse,
-    ssent0, ssent1, smet0, smet1, sinverse, fz, sz, out, products,
+    dots, product, fown, fmet, finverse, sown, smet, sinverse, fz, sz, out, products
 ):
-    (fodd, fheld), (sodd, sheld) = place_of()
+    (fodd, _), (sodd, _) = place_of()
     products[...] = jnp.zeros_like(products)
-    pair_solve((fsent0, fsent1), (fmet0, fmet1), None, finverse, fz, products, fodd, fheld)
-    pair_solve((ssent0, ssent1), (smet0, smet1), None, sinverse, sz, products, sodd, sheld)
+    own_solve(fown, fmet, finverse, fz, products, fodd)
+    own_solve(sown, smet, sinverse, sz, products, sodd)
     curve = dots[3:4, :] + product[0:1, :] - jnp.sum(products[...], axis=0, keepdims=True)
     rows = jnp.concatenate([dots[0:3, :], curve], axis=0)
     sums = jnp.sum(rows, axis=1, keepdims=True)
@@ -374,16 +382,24 @@
     out[...] = jnp.broadcast_to(line, out.shape)
 
 
+def relay_kernel(line, fz, sz, fout, sout):
+    fout[...] = fz[...]
+    sout[...] = sz[...]
+
+
 def last_kernel(
-    extra, fcam, fpoint, fcams, scam, spoint, scams, fseen, fz, sseen, sz,
-    result, findex, sindex, stage, total,
+    turn, extra, fcam, fpoint, fcams, scam, spoint, scams, fseen, fvalues, sseen, svalues,
+    result, findex, sindex, fz, sz, stage, total,
 ):
-    (fodd, fheld), (sodd, sheld) = place_of()
+    (_, fheld), (_, sheld) = place_of()
     weave(fcams, findex)
     weave(scams, sindex)
     total[...] = jnp.zeros_like(total)
-    pair_return(fcam, fpoint, findex, fseen, fz, fodd, fheld, stage, total)
-    pair_return(scam, spoint, sindex, sseen, sz, sodd, sheld, stage, total)
+    widened(fvalues, fz, turn)
+    widened(svalues, sz, turn)
+    turns = (turn,)
+    pair_return(fcam, fpoint, findex, fseen, fz, 0, fheld, stage, total, turns)
+    pair_return(scam, spoint, sindex, sseen, sz, 0, sheld, stage, total, turns)
     fold(total, result)
     result[...] += extra[...]
 
@@ -452,6 +468,9 @@
         return found
 
     fwd_rounds = pairs(lambda s, g: (s, g ^ 1)), pairs(lambda s, g: (s, (g + 1 ^ 1) - 1))
+    fwd_down, fwd_up = pairs(lambda s, g: (s, g - 1)), pairs(lambda s, g: (s, g + 1))
+    side_down = pairs(lambda s, g: (s - 1, segs - 1 - g))
+    side_up = pairs(lambda s, g: (s + 1, segs - 1 - g))
     side_rounds = (
         pairs(lambda s, g: (s ^ 1, segs - 1 - g)),
         pairs(lambda s, g: ((s + 1 ^ 1) - 1, segs - 1 - g)),
@@ -512,7 +531,7 @@
 
     extra, _ = local(gradient)
     fshapes, sshapes = sends_of(3)
-    p, finverse, sinverse, fseen, fsend0, fsend1, sseen, ssend0, ssend1, dots = call(
+    p, finverse, sinverse, fseen, fown, fguest, sseen, sown, sguest, dots = call(
         middle_kernel,
         [gradient, extra, fcam, fpoint, fcams, scam, spoint, scams,
          fseen, *fsent, *fmet, sseen, *ssent, *smet],
@@ -524,27 +543,34 @@
         10**10,
         "middle",
     )
-    fsent, ssent = [fsend0, fsend1], [ssend0, ssend1]
-    smet = meet(ssent, side_rounds)
-    fmet = meet(fsent, fwd_rounds)
+    smet = lax.ppermute(sguest, AXES, side_down)
+    fmet = lax.ppermute(fguest, AXES, fwd_down)
     extra, product = local(p)
+    zshapes = [(3, fr // 2, LANES), (3, sr // 2, LANES)]
     fz, sz, line = call(
         dots_kernel,
-        [dots, product, *fsent, *fmet, finverse, *ssent, *smet, sinverse],
-        [(2, 3, fr, LANES), (2, 3, sr, LANES), (strips * segs, LANES)],
+        [dots, product, fown, fmet, finverse, sown, smet, sinverse],
+        zshapes + [(strips * segs, LANES)],
         [pltpu.VMEM((8, LANES), F32)],
         10**8,
         "dots",
     )
+    fsent, ssent = call(relay_kernel, [line, fz, sz], zshapes, [], 10**6, "relay")
     line = lax.all_to_all(line, AXES, 0, 0, tiled=True)
-    (t,) = call(
-        last_kernel,
-        [extra, fcam, fpoint, fcams, scam, spoint, scams, fseen, fz, sseen, sz],
-        [(ROWS, LANES)],
-        index_scratch + total_scratch,
-        5 * 10**9,
-        "last",
-    )
+    ssent = lax.ppermute(ssent, AXES, side_up)
+    fsent = lax.ppermute(fsent, AXES, fwd_up)
+
+    def last(turn, extra, fvalues, svalues):
+        return call(
+            functools.partial(last_kernel, turn),
+            [extra, fcam, fpoint, fcams, scam, spoint, scams, fseen, fvalues, sseen, svalues],
+            [(ROWS, LANES)],
+            index_scratch + z_scratch + total_scratch,
+            5 * 10**9,
+            "last",
+        )[0]
+
+    t = last(1, last(0, extra, fz, sz), fsent, ssent)
     step, residual = call(
         close_kernel, [line, gradient, p, t], [gradient.shape] * 2, table, 10**6, "close"
     )

time: 71.1 us -> 68.3 us (0.961); the launches traced: 70.8 us -> 67.2 us
  waiting for transfers between devices: 12.7 us -> 5.33 us
  Pallas kernels: 16.1 us -> 19.6 us
    ppermute x0 -> x4, starting transfers between devices: none -> 12.7 us  [the longest x1 8.15 us: per_device(): ssent = lax.ppermute(ssent, AXES, side_up)]
    ppermute x8 -> x4, starting transfers between devices: 23.3 us -> 10.9 us  [meet(): lax.ppermute(send, AXES, pairs)]
    all_to_all x1, waiting for transfers between devices: 10.4 us -> 0.01 us  [per_device(): line = lax.all_to_all(line, AXES, 0, 0, tiled=True)]
    ppermute x0 -> x4, waiting for transfers between devices: none -> 3.99 us  [the longest x1 3.98 us: per_device(): smet = lax.ppermute(sguest, AXES, side_down)]
    pallas_call x7 -> x9, Pallas kernels: 16.1 us -> 19.6 us  [call(): pl.pallas_call(kernel, out_shape=outs, in_specs=specs, out_specs=[to] * l...]
    ppermute x8 -> x4, waiting for transfers between devices: 2.34 us -> 1.34 us  [meet(): lax.ppermute(send, AXES, pairs)]
  transfers between devices with their start and end apart: 9 -> 9, of which waited for: 2 -> 2; matrix products, arithmetic and copies ran while one was open for 0% -> 0% of each run, Pallas kernels for 7% -> 13%
where the time goes in v5:
time: 68.3 us; the launch traced here: 67.2 us
  starting transfers between devices  40.6 us (59%)
  Pallas kernels  19.6 us (29%)
  waiting for transfers between devices  5.33 us (8%)
  between operations  1.62 us (2%)
    pallas_call x9, Pallas kernels, call(): pl.pallas_call(kernel, out_shape=outs, in_specs=specs, out_specs=[to] * l...  19.6 us
    all_to_all x1, starting transfers between devices, per_device(): line = lax.all_to_all(line, AXES, 0, 0, tiled=True)  17.1 us
    ppermute x4, starting transfers between devices, meet(): lax.ppermute(send, AXES, pairs)  10.9 us
    ppermute x1, starting transfers between devices, per_device(): ssent = lax.ppermute(ssent, AXES, side_up)  8.15 us
    ppermute x1, waiting for transfers between devices, per_device(): smet = lax.ppermute(sguest, AXES, side_down)  3.98 us
    ppermute x1, starting transfers between devices, per_device(): smet = lax.ppermute(sguest, AXES, side_down)  1.92 us
  transfers between devices with their start and end apart: 9, of which 2 were waited for; matrix products, arithmetic and copies ran while one was open for 0% of the time, Pallas kernels for 13%

profile of v5, /device:TPU:1, one launch (start us, length us, event | category | flops | bytes accessed | tf_op | source)
XLA Modules:
  0.0 67.2 jit_solution(7910283418998390111)
XLA Ops:
  0.7 4.2 %look.1 = (f32[2,2,64,128]{3,2,1,0:T(8,128)}, f32[9,32,128]{2,1,0:T(8,128)}, f32[9,32,128]{2,1,0:T(8,128)}, f32[2,2,48,128]{3,2,1,0:T(8,128)}, f32[9,24,128]{2,1,0:T(8,128)}, /*index=5*/f32[9,24,128]{2,1,0:T(8,128)}) custom-call(f32[9,1,512]{2,1,0:T(1,128)} %lines.3, bf16[2,18,64,128]{3,2,1,0:T(8,128)(2,1)} %bitcast.35, bf16[2,6,64,128]{3,2,1,0:T(8,128)(2,1)} %bitcast.45, ...), custom_call_target="tpu_custom_call" | custom-call | flops 1000000000 | bytes 2097152 | tf_op jit(solution)/shard_map/look/pallas_call | solution.py:437
  4.9 5.3 %collective-permute-start.2 = (f32[9,24,128]{2,1,0:T(8,128)}, f32[9,24,128]{2,1,0:T(8,128)S(1)}, u32[]{:S(2)}, u32[]{:S(2)}) collective-permute-start(f32[9,24,128]{2,1,0:T(8,128)} %get-tuple-element.31.ssent0), channel_id=1, source_target_pairs={{0,15},{1,14},{2,13},{3,12},{4,11},{5,10},{6,9},{7,8},{8,7},{9,6},... | collective-permute-start | bytes 331784 | tf_op jit(solution)/shard_map/ppermute | solution.py:489
  10.2 4.6 %collective-permute-start.3 = (f32[9,24,128]{2,1,0:T(8,128)}, f32[9,24,128]{2,1,0:T(8,128)S(1)}, u32[]{:S(2)}, u32[]{:S(2)}) collective-permute-start(f32[9,24,128]{2,1,0:T(8,128)} %get-tuple-element.32.ssent1), channel_id=1, source_target_pairs={{8,23},{9,22},{10,21},{11,20},{12,19},{13,18},{14,17},{15,16},{16,... | collective-permute-start | bytes 331784 | tf_op jit(solution)/shard_map/ppermute | solution.py:489
  14.8 0.3 collective-permute-start
  15.1 0.7 collective-permute-start.1
  16.4 0.0 copy-start.2
  16.4 0.0 copy-start.5
  16.5 0.0 copy-start.6
  16.5 0.0 copy-start.13
  16.6 2.6 %local.2 = (f32[36,128]{1,0:T(8,128)S(1)}, f32[8,128]{1,0:T(8,128)}) custom-call(s32[1]{0:T(128)} %bitcast.30.live, f32[9,1,512]{2,1,0:T(1,128)S(1)} %copy-done, bf16[18,6,2048]{2,1,0:T(8,128)(2,1)S(1)} %bitcast.33, bf16[6,6,2048]{2,1,0:T(8,128)(2,1)S(1)} %bitcast.43, s32[96,128]{1,0:T(8,128)S(1)} %bitcast.57), custom_call_target="tpu_custom_call" | custom-call | flops 5000000000 | bytes 2097152 | tf_op jit(solution)/shard_map/local/pallas_call | solution.py:437
  19.1 1.3 %collective-permute-done.3.smet1 = f32[9,24,128]{2,1,0:T(8,128)S(1)} collective-permute-done((f32[9,24,128]{2,1,0:T(8,128)}, f32[9,24,128]{2,1,0:T(8,128)S(1)}, u32[]{:S(2)}, u32[]{:S(2)}) %collective-permute-start.3) | collective-permute-done | bytes 110624 | tf_op jit(solution)/shard_map/ppermute | solution.py:489
  20.6 5.2 %middle.1 = (f32[36,128]{1,0:T(8,128)S(1)}, f32[2,6,32,128]{3,2,1,0:T(8,128)S(1)}, f32[2,6,24,128]{3,2,1,0:T(8,128)S(1)}, f32[2,2,64,128]{3,2,1,0:T(8,128)S(1)},...) custom-call(f32[9,1,512]{2,1,0:T(1,128)S(1)} %copy-done, ...), custom_call_target="tpu_custom_call" | custom-call | flops 10000000000 | bytes 2097152 | tf_op jit(solution)/shard_map/middle/pallas_call | solution.py:437
  25.8 1.9 %collective-permute-start.5 = (f32[3,24,128]{2,1,0:T(8,128)S(1)}, f32[3,24,128]{2,1,0:T(8,128)S(1)}, u32[]{:S(2)}, u32[]{:S(2)}) collective-permute-start(f32[3,24,128]{2,1,0:T(8,128)S(1)} %get-tuple-element.40), channel_id=1, source_target_pairs={{8,7},{9,6},{10,5},{11,4},{12,3},{13,2},{14,1},{15,0},{16,15},{17,... | collective-permute-start | bytes 110600 | tf_op jit(solution)/shard_map/ppermute | solution.py:546
  27.7 1.3 %collective-permute-start.4 = (f32[3,32,128]{2,1,0:T(8,128)S(1)}, f32[3,32,128]{2,1,0:T(8,128)S(1)}, u32[]{:S(2)}, u32[]{:S(2)}) collective-permute-start(f32[3,32,128]{2,1,0:T(8,128)S(1)} %get-tuple-element.37), channel_id=1, source_target_pairs={{1,0},{2,1},{3,2},{4,3},{5,4},{6,5},{7,6},{9,8},{10,9},{11,10},{12... | collective-permute-start | bytes 147464 | tf_op jit(solution)/shard_map/ppermute | solution.py:547
  29.0 2.0 %local.3 = (f32[36,128]{1,0:T(8,128)S(1)}, f32[8,128]{1,0:T(8,128)S(1)}) custom-call(s32[1]{0:T(128)} %bitcast.31.live, f32[36,128]{1,0:T(8,128)S(1)} %get-tuple-element.34.values.first, bf16[18,6,2048]{2,1,0:T(8,128)(2,1)S(1)} %bitcast.34, bf16[6,6,2048]{2,1,0:T(8,128)(2,1)S(1)} %bitcast.44, s32[96,128]{1,0:T(8,128)S(1)} %bitcast.58), custom_call_target="tpu_custom_call" | custom-call | flops 5000000000 | bytes 2097152 | tf_op jit(solution)/shard_map/local/pallas_call | solution.py:437
  31.0 4.0 %collective-permute-done.5.smet = f32[3,24,128]{2,1,0:T(8,128)S(1)} collective-permute-done((f32[3,24,128]{2,1,0:T(8,128)S(1)}, f32[3,24,128]{2,1,0:T(8,128)S(1)}, u32[]{:S(2)}, u32[]{:S(2)}) %collective-permute-start.5) | collective-permute-done | bytes 36896 | tf_op jit(solution)/shard_map/ppermute | solution.py:546
  35.0 0.8 %dots.1 = (f32[3,32,128]{2,1,0:T(8,128)S(1)}, f32[3,24,128]{2,1,0:T(8,128)S(1)}, f32[256,128]{1,0:T(8,128)}) custom-call(f32[8,128]{1,0:T(8,128)S(1)} %get-tuple-element.33.dots, f32[8,128]{1,0:T(8,128)S(1)} %get-tuple-element.35.product, f32[3,32,128]{2,1,0:T(8,128)S(1)} %get-tuple-element.36.fown, f32[3,32,128]{2,1,0:T(8,128)S(1)} %collective-permute-done.4.fmet, ...), custom_call_target="tpu_custom_call" | custom-call | flops 100000000 | bytes 2097152 | tf_op jit(solution)/shard_map/dots/pallas_call | solution.py:437
  35.7 17.1 %all-to-all-start = ((f32[256,1,128]{2,1,0:T(1,128)}), f32[256,1,128]{2,1,0:T(1,128)S(1)}, u32[]{:S(2)}, u32[]{:S(2)}) async-start(f32[256,1,128]{2,1,0:T(1,128)} %bitcast.27), calls=%async_computation | async-start | bytes 262144 | tf_op jit(solution)/shard_map/all_to_all | solution.py:559
  52.8 0.9 %relay.1 = (f32[3,32,128]{2,1,0:T(8,128)S(1)}, f32[3,24,128]{2,1,0:T(8,128)S(1)}) custom-call(f32[256,128]{1,0:T(8,128)} %get-tuple-element.42.line, f32[3,32,128]{2,1,0:T(8,128)S(1)} %get-tuple-element.45.fvalues.fz, f32[3,24,128]{2,1,0:T(8,128)S(1)} %get-tuple-element.47.svalues.sz), custom_call_target="tpu_custom_call" | custom-call | flops 1000000 | bytes 2097152 | tf_op jit(solution)/shard_map/relay/pallas_call | solution.py:437
  53.8 8.1 %collective-permute-start.7 = (f32[3,24,128]{2,1,0:T(8,128)S(1)}, f32[3,24,128]{2,1,0:T(8,128)S(1)}, u32[]{:S(2)}, u32[]{:S(2)}) collective-permute-start(f32[3,24,128]{2,1,0:T(8,128)S(1)} %get-tuple-element.49), channel_id=1, source_target_pairs={{0,15},{1,14},{2,13},{3,12},{4,11},{5,10},{6,9},{7,8},{8,23},{9,22... | collective-permute-start | bytes 110600 | tf_op jit(solution)/shard_map/ppermute | solution.py:560
  61.9 1.3 %collective-permute-start.6 = (f32[3,32,128]{2,1,0:T(8,128)S(1)}, f32[3,32,128]{2,1,0:T(8,128)S(1)}, u32[]{:S(2)}, u32[]{:S(2)}) collective-permute-start(f32[3,32,128]{2,1,0:T(8,128)S(1)} %get-tuple-element.48), channel_id=1, source_target_pairs={{0,1},{1,2},{2,3},{3,4},{4,5},{5,6},{6,7},{8,9},{9,10},{10,11},{11... | collective-permute-start | bytes 147464 | tf_op jit(solution)/shard_map/ppermute | solution.py:561
  63.2 1.6 %last.2.extra = f32[36,128]{1,0:T(8,128)S(1)} custom-call(f32[36,128]{1,0:T(8,128)S(1)} %get-tuple-element.43.extra, bf16[2,18,64,128]{3,2,1,0:T(8,128)(2,1)S(1)} %bitcast.37, bf16[2,6,64,128]{3,2,1,0:T(8,128)(2,1)S(1)} %bitcast.47, s32[2,2,32,128]{3,2,1,0:T(8,128)S(1)} %bitcast.55, bf16[2,18,48,128]{3,2,1,0:T(8,128)(2,1)S(1)} %bitcast.41, ...), custom_call_target="tpu_custom_call" | custom-call | flops 5000000000 | bytes 2097152 | tf_op jit(solution)/shard_map/last/pallas_call | solution.py:437
  64.9 1.6 %last.3.second = f32[36,128]{1,0:T(8,128)S(1)} custom-call(f32[36,128]{1,0:T(8,128)S(1)} %last.2.extra, bf16[2,18,64,128]{3,2,1,0:T(8,128)(2,1)S(1)} %bitcast.38, bf16[2,6,64,128]{3,2,1,0:T(8,128)(2,1)S(1)} %bitcast.48, s32[2,2,32,128]{3,2,1,0:T(8,128)S(1)} %bitcast.56, bf16[2,18,48,128]{3,2,1,0:T(8,128)(2,1)S(1)} %bitcast.42, ...), custom_call_target="tpu_custom_call" | custom-call | flops 5000000000 | bytes 2097152 | tf_op jit(solution)/shard_map/last/pallas_call | solution.py:437
  66.4 0.8 %close.1 = (f32[9,1,512]{2,1,0:T(1,128)}, f32[9,1,512]{2,1,0:T(1,128)}) custom-call(f32[256,128]{1,0:T(8,128)S(1)} %bitcast.32, f32[9,1,512]{2,1,0:T(1,128)S(1)} %copy-done, f32[36,128]{1,0:T(8,128)S(1)} %get-tuple-element.34.values.first, f32[36,128]{1,0:T(8,128)S(1)} %last.3.second), custom_call_target="tpu_custom_call" | custom-call | flops 1000000 | bytes 2097152 | tf_op jit(solution)/shard_map/close/pallas_call | solution.py:437
  (35 shorter events, 0.1 us)
Async XLA Ops:
  0.6 15.8 %copy-start = (f32[9,1,512]{2,1,0:T(1,128)S(1)}, f32[9,1,512]{2,1,0:T(1,128)}, u32[]{:S(2)}) copy-start(f32[9,1,512]{2,1,0:T(1,128)} %lines.3) | copy-start | bytes 55300
  0.6 15.8 %copy-start.1 = (bf16[18,6,1,2048]{3,1,2,0:T(8,128)(2,1)S(1)}, bf16[18,6,1,2048]{3,1,2,0:T(8,128)(2,1)}, u32[]{:S(2)}) copy-start(bf16[18,6,1,2048]{3,1,2,0:T(8,128)(2,1)} %param.13) | copy-start | bytes 1327108
  0.7 15.8 %copy-start.4 = (bf16[6,6,1,2048]{3,1,2,0:T(8,128)(2,1)S(1)}, bf16[6,6,1,2048]{3,1,2,0:T(8,128)(2,1)}, u32[]{:S(2)}) copy-start(bf16[6,6,1,2048]{3,1,2,0:T(8,128)(2,1)} %param.14) | copy-start | bytes 442372
  0.7 15.8 %copy-start.12 = (s32[6,1,2048]{2,1,0:T(1,128)S(1)}, s32[6,1,2048]{2,1,0:T(1,128)}, u32[]{:S(2)}) copy-start(s32[6,1,2048]{2,1,0:T(1,128)} %param.15) | copy-start | bytes 147460
  4.9 14.3 %collective-permute-start.2 = (f32[9,24,128]{2,1,0:T(8,128)}, f32[9,24,128]{2,1,0:T(8,128)S(1)}, u32[]{:S(2)}, u32[]{:S(2)}) collective-permute-start(f32[9,24,128]{2,1,0:T(8,128)} %get-tuple-element.31.ssent0), channel_id=1, source_target_pairs={{0,15},{1,14},{2,13},{3,12},{4,11},{5,10},{6,9},{7,8},{8,7},{9,6},... | collective-permute-start | bytes 331784 | tf_op jit(solution)/shard_map/ppermute | solution.py:489
  10.2 10.3 %collective-permute-start.3 = (f32[9,24,128]{2,1,0:T(8,128)}, f32[9,24,128]{2,1,0:T(8,128)S(1)}, u32[]{:S(2)}, u32[]{:S(2)}) collective-permute-start(f32[9,24,128]{2,1,0:T(8,128)} %get-tuple-element.32.ssent1), channel_id=1, source_target_pairs={{8,23},{9,22},{10,21},{11,20},{12,19},{13,18},{14,17},{15,16},{16,... | collective-permute-start | bytes 331784 | tf_op jit(solution)/shard_map/ppermute | solution.py:489
  14.8 5.7 %collective-permute-start = (f32[9,32,128]{2,1,0:T(8,128)}, f32[9,32,128]{2,1,0:T(8,128)S(1)}, u32[]{:S(2)}, u32[]{:S(2)}) collective-permute-start(f32[9,32,128]{2,1,0:T(8,128)} %get-tuple-element.28.fsent0), channel_id=1, source_target_pairs={{0,1},{1,0},{2,3},{3,2},{4,5},{5,4},{6,7},{7,6},{8,9},{9,8},{10,11... | collective-permute-start | bytes 442376 | tf_op jit(solution)/shard_map/ppermute | solution.py:489
  15.1 5.4 %collective-permute-start.1 = (f32[9,32,128]{2,1,0:T(8,128)}, f32[9,32,128]{2,1,0:T(8,128)S(1)}, u32[]{:S(2)}, u32[]{:S(2)}) collective-permute-start(f32[9,32,128]{2,1,0:T(8,128)} %get-tuple-element.29.fsent1), channel_id=1, source_target_pairs={{1,2},{2,1},{3,4},{4,3},{5,6},{6,5},{9,10},{10,9},{11,12},{12,11},... | collective-permute-start | bytes 442376 | tf_op jit(solution)/shard_map/ppermute | solution.py:489
  16.4 4.0 %copy-start.2 = (bf16[2,18,2,1,4096]{4,2,3,1,0:T(2,128)(2,1)S(1)}, bf16[2,18,2,1,4096]{4,2,3,1,0:T(2,128)(2,1)}, u32[]{:S(2)}) copy-start(bf16[2,18,2,1,4096]{4,2,3,1,0:T(2,128)(2,1)} %param.16) | copy-start | bytes 1769476
  16.4 4.0 %copy-start.3 = (bf16[2,18,2,1,3072]{4,2,3,1,0:T(2,128)(2,1)S(1)}, bf16[2,18,2,1,3072]{4,2,3,1,0:T(2,128)(2,1)}, u32[]{:S(2)}) copy-start(bf16[2,18,2,1,3072]{4,2,3,1,0:T(2,128)(2,1)} %param.19) | copy-start | bytes 1327108
  16.4 4.0 %copy-start.5 = (bf16[2,6,2,1,4096]{4,2,3,1,0:T(2,128)(2,1)S(1)}, bf16[2,6,2,1,4096]{4,2,3,1,0:T(2,128)(2,1)}, u32[]{:S(2)}) copy-start(bf16[2,6,2,1,4096]{4,2,3,1,0:T(2,128)(2,1)} %param.17) | copy-start | bytes 589828
  16.5 4.0 %copy-start.6 = (bf16[2,6,2,1,3072]{4,2,3,1,0:T(2,128)(2,1)S(1)}, bf16[2,6,2,1,3072]{4,2,3,1,0:T(2,128)(2,1)}, u32[]{:S(2)}) copy-start(bf16[2,6,2,1,3072]{4,2,3,1,0:T(2,128)(2,1)} %param.20) | copy-start | bytes 442372
  16.5 4.0 %copy-start.7 = (f32[9,32,128]{2,1,0:T(8,128)S(1)}, f32[9,32,128]{2,1,0:T(8,128)}, u32[]{:S(2)}) copy-start(f32[9,32,128]{2,1,0:T(8,128)} %get-tuple-element.28.fsent0) | copy-start | bytes 442372
  16.5 4.0 %copy-start.8 = (f32[9,32,128]{2,1,0:T(8,128)S(1)}, f32[9,32,128]{2,1,0:T(8,128)}, u32[]{:S(2)}) copy-start(f32[9,32,128]{2,1,0:T(8,128)} %get-tuple-element.29.fsent1) | copy-start | bytes 442372
  16.5 4.0 %copy-start.9 = (f32[9,24,128]{2,1,0:T(8,128)S(1)}, f32[9,24,128]{2,1,0:T(8,128)}, u32[]{:S(2)}) copy-start(f32[9,24,128]{2,1,0:T(8,128)} %get-tuple-element.31.ssent0) | copy-start | bytes 331780
  16.5 4.0 %copy-start.10 = (f32[9,24,128]{2,1,0:T(8,128)S(1)}, f32[9,24,128]{2,1,0:T(8,128)}, u32[]{:S(2)}) copy-start(f32[9,24,128]{2,1,0:T(8,128)} %get-tuple-element.32.ssent1) | copy-start | bytes 331780
  16.5 4.0 %copy-start.11 = (s32[2,2,1,4096]{3,2,1,0:T(1,128)S(1)}, s32[2,2,1,4096]{3,2,1,0:T(1,128)}, u32[]{:S(2)}) copy-start(s32[2,2,1,4096]{3,2,1,0:T(1,128)} %param.18) | copy-start | bytes 196612
  16.5 4.0 %copy-start.13 = (s32[2,2,1,3072]{3,2,1,0:T(1,128)S(1)}, s32[2,2,1,3072]{3,2,1,0:T(1,128)}, u32[]{:S(2)}) copy-start(s32[2,2,1,3072]{3,2,1,0:T(1,128)} %param.21) | copy-start | bytes 147460
  16.5 4.0 %copy-start.14 = (f32[2,2,64,128]{3,2,1,0:T(8,128)S(1)}, f32[2,2,64,128]{3,2,1,0:T(8,128)}, u32[]{:S(2)}) copy-start(f32[2,2,64,128]{3,2,1,0:T(8,128)} %get-tuple-element.27.fseen) | copy-start | bytes 393220
  25.8 9.2 %collective-permute-start.5 = (f32[3,24,128]{2,1,0:T(8,128)S(1)}, f32[3,24,128]{2,1,0:T(8,128)S(1)}, u32[]{:S(2)}, u32[]{:S(2)}) collective-permute-start(f32[3,24,128]{2,1,0:T(8,128)S(1)} %get-tuple-element.40), channel_id=1, source_target_pairs={{8,7},{9,6},{10,5},{11,4},{12,3},{13,2},{14,1},{15,0},{16,15},{17,... | collective-permute-start | bytes 110600 | tf_op jit(solution)/shard_map/ppermute | solution.py:546
  27.7 7.3 %collective-permute-start.4 = (f32[3,32,128]{2,1,0:T(8,128)S(1)}, f32[3,32,128]{2,1,0:T(8,128)S(1)}, u32[]{:S(2)}, u32[]{:S(2)}) collective-permute-start(f32[3,32,128]{2,1,0:T(8,128)S(1)} %get-tuple-element.37), channel_id=1, source_target_pairs={{1,0},{2,1},{3,2},{4,3},{5,4},{6,5},{7,6},{9,8},{10,9},{11,10},{12... | collective-permute-start | bytes 147464 | tf_op jit(solution)/shard_map/ppermute | solution.py:547
  35.7 30.7 %all-to-all-start = ((f32[256,1,128]{2,1,0:T(1,128)}), f32[256,1,128]{2,1,0:T(1,128)S(1)}, u32[]{:S(2)}, u32[]{:S(2)}) async-start(f32[256,1,128]{2,1,0:T(1,128)} %bitcast.27), calls=%async_computation | async-start | bytes 262144 | tf_op jit(solution)/shard_map/all_to_all | solution.py:559
  53.8 11.1 %collective-permute-start.7 = (f32[3,24,128]{2,1,0:T(8,128)S(1)}, f32[3,24,128]{2,1,0:T(8,128)S(1)}, u32[]{:S(2)}, u32[]{:S(2)}) collective-permute-start(f32[3,24,128]{2,1,0:T(8,128)S(1)} %get-tuple-element.49), channel_id=1, source_target_pairs={{0,15},{1,14},{2,13},{3,12},{4,11},{5,10},{6,9},{7,8},{8,23},{9,22... | collective-permute-start | bytes 110600 | tf_op jit(solution)/shard_map/ppermute | solution.py:560
  61.9 2.9 %collective-permute-start.6 = (f32[3,32,128]{2,1,0:T(8,128)S(1)}, f32[3,32,128]{2,1,0:T(8,128)S(1)}, u32[]{:S(2)}, u32[]{:S(2)}) collective-permute-start(f32[3,32,128]{2,1,0:T(8,128)S(1)} %get-tuple-element.48), channel_id=1, source_target_pairs={{0,1},{1,2},{2,3},{3,4},{4,5},{5,6},{6,7},{8,9},{9,10},{10,11},{11... | collective-permute-start | bytes 147464 | tf_op jit(solution)/shard_map/ppermute | solution.py:561
  (1 other events, 4.0 us)

commit v6 on v5

--- a/solution.py
+++ b/solution.py
@@ -1,5 +1,3 @@
-import functools
-
 import jax
 import jax.numpy as jnp
 from jax import lax
@@ -225,6 +223,17 @@
         products[...] += sum(b[k] * solved[k] for k in range(3))
         for k in range(3):
             z[k, at, :] = solved[k]
+
+
+def both_solve(sent, met, inverse, z, products, odd):
+    for turn in range(2):
+        own = part_of(turn ^ odd, jnp.int32(0))
+        for i in range(sent[0].shape[1] // 8):
+            at = pl.ds(8 * i, 8)
+            b = [sent[turn][k, at, :] + met[turn][k, at, :] for k in range(3)]
+            solved = solve([inverse[turn, k, at, :] for k in range(6)], b)
+            products[...] += own * sum(b[k] * solved[k] for k in range(3))
+            put_z(z, turn, i, solved)
 
 
 def widened(values, z, turn):
@@ -339,7 +348,7 @@
 def middle_kernel(
     lines, extra, fcam, fpoint, fcams, scam, spoint, scams,
     fseen, fsent0, fsent1, fmet0, fmet1, sseen, ssent0, ssent1, smet0, smet1,
-    result, finverse, sinverse, fseen2, fown, fguest, sseen2, sown, sguest, dots,
+    result, finverse, sinverse, fseen2, fsend0, fsend1, sseen2, sown, sguest, dots,
     table, findex, sindex, floose, sloose, fz, sz, stage, total, squares,
 ):
     (fodd, fheld), (sodd, sheld) = place_of()
@@ -355,8 +364,10 @@
     step = result[...] + extra[...]
     result[...] = step
     squares[...] = jnp.zeros_like(squares)
-    sides = (fown, fguest)
-    pair_look(fcam, fpoint, findex, result, fseen2, floose, sides, 0, False, squares, fheld, None)
+    sends = (fsend0, fsend1)
+    pair_look(
+        fcam, fpoint, findex, result, fseen2, floose, sends, fodd, False, squares, fheld, None
+    )
     sides = (sown, sguest)
     pair_look(scam, spoint, sindex, result, sseen2, sloose, sides, 0, False, squares, sheld, None)
     base = table[...]
@@ -366,11 +377,12 @@
 
 
 def dots_kernel(
-    dots, product, fown, fmet, finverse, sown, smet, sinverse, fz, sz, out, products
+    dots, product, fsent0, fsent1, fmet0, fmet1, finverse, sown, smet, sinverse,
+    fz, sz, out, products,
 ):
     (fodd, _), (sodd, _) = place_of()
     products[...] = jnp.zeros_like(products)
-    own_solve(fown, fmet, finverse, fz, products, fodd)
+    both_solve((fsent0, fsent1), (fmet0, fmet1), finverse, fz, products, fodd)
     own_solve(sown, smet, sinverse, sz, products, sodd)
     curve = dots[3:4, :] + product[0:1, :] - jnp.sum(products[...], axis=0, keepdims=True)
     rows = jnp.concatenate([dots[0:3, :], curve], axis=0)
@@ -382,24 +394,27 @@
     out[...] = jnp.broadcast_to(line, out.shape)
 
 
-def relay_kernel(line, fz, sz, fout, sout):
-    fout[...] = fz[...]
-    sout[...] = sz[...]
-
-
 def last_kernel(
-    turn, extra, fcam, fpoint, fcams, scam, spoint, scams, fseen, fvalues, sseen, svalues,
-    result, findex, sindex, fz, sz, stage, total,
+    extra, fcam, fpoint, fcams, scam, spoint, scams, fseen, fz, sseen, svalues,
+    result, findex, sindex, sz, stage, total,
 ):
-    (_, fheld), (_, sheld) = place_of()
+    (fodd, fheld), (_, sheld) = place_of()
     weave(fcams, findex)
     weave(scams, sindex)
     total[...] = jnp.zeros_like(total)
-    widened(fvalues, fz, turn)
-    widened(svalues, sz, turn)
-    turns = (turn,)
-    pair_return(fcam, fpoint, findex, fseen, fz, 0, fheld, stage, total, turns)
-    pair_return(scam, spoint, sindex, sseen, sz, 0, sheld, stage, total, turns)
+    pair_return(fcam, fpoint, findex, fseen, fz, fodd, fheld, stage, total)
+    widened(svalues, sz, 0)
+    pair_return(scam, spoint, sindex, sseen, sz, 0, sheld, stage, total, (0,))
+    fold(total, result)
+    result[...] += extra[...]
+
+
+def guest_kernel(extra, scam, spoint, scams, sseen, svalues, result, sindex, sz, stage, total):
+    _, (_, sheld) = place_of()
+    weave(scams, sindex)
+    total[...] = jnp.zeros_like(total)
+    widened(svalues, sz, 1)
+    pair_return(scam, spoint, sindex, sseen, sz, 0, sheld, stage, total, (1,))
     fold(total, result)
     result[...] += extra[...]
 
@@ -468,7 +483,6 @@
         return found
 
     fwd_rounds = pairs(lambda s, g: (s, g ^ 1)), pairs(lambda s, g: (s, (g + 1 ^ 1) - 1))
-    fwd_down, fwd_up = pairs(lambda s, g: (s, g - 1)), pairs(lambda s, g: (s, g + 1))
     side_down = pairs(lambda s, g: (s - 1, segs - 1 - g))
     side_up = pairs(lambda s, g: (s + 1, segs - 1 - g))
     side_rounds = (
@@ -531,7 +545,7 @@
 
     extra, _ = local(gradient)
     fshapes, sshapes = sends_of(3)
-    p, finverse, sinverse, fseen, fown, fguest, sseen, sown, sguest, dots = call(
+    p, finverse, sinverse, fseen, fsend0, fsend1, sseen, sown, sguest, dots = call(
         middle_kernel,
         [gradient, extra, fcam, fpoint, fcams, scam, spoint, scams,
          fseen, *fsent, *fmet, sseen, *ssent, *smet],
@@ -544,33 +558,34 @@
         "middle",
     )
     smet = lax.ppermute(sguest, AXES, side_down)
-    fmet = lax.ppermute(fguest, AXES, fwd_down)
+    fmet = meet((fsend0, fsend1), fwd_rounds)
     extra, product = local(p)
-    zshapes = [(3, fr // 2, LANES), (3, sr // 2, LANES)]
     fz, sz, line = call(
         dots_kernel,
-        [dots, product, fown, fmet, finverse, sown, smet, sinverse],
-        zshapes + [(strips * segs, LANES)],
+        [dots, product, fsend0, fsend1, *fmet, finverse, sown, smet, sinverse],
+        [(2, 3, fr, LANES), (3, sr // 2, LANES), (strips * segs, LANES)],
         [pltpu.VMEM((8, LANES), F32)],
         10**8,
         "dots",
     )
-    fsent, ssent = call(relay_kernel, [line, fz, sz], zshapes, [], 10**6, "relay")
     line = lax.all_to_all(line, AXES, 0, 0, tiled=True)
-    ssent = lax.ppermute(ssent, AXES, side_up)
-    fsent = lax.ppermute(fsent, AXES, fwd_up)
-
-    def last(turn, extra, fvalues, svalues):
-        return call(
-            functools.partial(last_kernel, turn),
-            [extra, fcam, fpoint, fcams, scam, spoint, scams, fseen, fvalues, sseen, svalues],
-            [(ROWS, LANES)],
-            index_scratch + z_scratch + total_scratch,
-            5 * 10**9,
-            "last",
-        )[0]
-
-    t = last(1, last(0, extra, fz, sz), fsent, ssent)
+    ssent = lax.ppermute(sz, AXES, side_up)
+    (t,) = call(
+        last_kernel,
+        [extra, fcam, fpoint, fcams, scam, spoint, scams, fseen, fz, sseen, sz],
+        [(ROWS, LANES)],
+        index_scratch + z_scratch[1:] + total_scratch,
+        5 * 10**9,
+        "last",
+    )
+    (t,) = call(
+        guest_kernel,
+        [t, scam, spoint, scams, sseen, ssent],
+        [(ROWS, LANES)],
+        index_scratch[1:] + z_scratch[1:] + total_scratch,
+        2 * 10**9,
+        "guest",
+    )
     step, residual = call(
         close_kernel, [line, gradient, p, t], [gradient.shape] * 2, table, 10**6, "close"
     )

time: 68.3 us -> 68.4 us (level); the launches traced: 67.2 us -> 68.1 us
  starting transfers between devices: 40.6 us -> 44 us
  Pallas kernels: 19.6 us -> 18.2 us
  waiting for transfers between devices: 5.33 us -> 4.21 us
    ppermute x4 -> x6, starting transfers between devices: 10.9 us -> 15.3 us  [meet(): lax.ppermute(send, AXES, pairs)]
    ppermute x1, waiting for transfers between devices: 3.98 us -> 0.81 us  [per_device(): smet = lax.ppermute(sguest, AXES, side_down)]
    ppermute x3 -> x1, starting transfers between devices: 10.7 us -> 8.16 us  [per_device(): ssent = lax.ppermute(sz, AXES, side_up)]
    all_to_all x1, waiting for transfers between devices: 0.01 us -> 2.05 us  [per_device(): line = lax.all_to_all(line, AXES, 0, 0, tiled=True)]
    all_to_all x1, starting transfers between devices: 17.1 us -> 18.6 us  [per_device(): line = lax.all_to_all(line, AXES, 0, 0, tiled=True)]
    pallas_call x9 -> x8, Pallas kernels: 19.6 us -> 18.2 us  [call(): pl.pallas_call(kernel, out_shape=outs, in_specs=specs, out_specs=[to] * l...]
  transfers between devices with their start and end apart: 9 -> 9, of which waited for: 2 -> 3; matrix products, arithmetic and copies ran while one was open for 0% -> 0% of each run, Pallas kernels for 13% -> 11%
where the time goes in v6:
time: 68.4 us; the launch traced here: 68.1 us
  starting transfers between devices  44 us (64%)
  Pallas kernels  18.2 us (27%)
  waiting for transfers between devices  4.21 us (6%)
  between operations  1.61 us (2%)
    all_to_all x1, starting transfers between devices, per_device(): line = lax.all_to_all(line, AXES, 0, 0, tiled=True)  18.6 us
    pallas_call x8, Pallas kernels, call(): pl.pallas_call(kernel, out_shape=outs, in_specs=specs, out_specs=[to] * l...  18.2 us
    ppermute x6, starting transfers between devices, meet(): lax.ppermute(send, AXES, pairs)  15.3 us
    ppermute x1, starting transfers between devices, per_device(): ssent = lax.ppermute(sz, AXES, side_up)  8.16 us
    all_to_all x1, waiting for transfers between devices, per_device(): line = lax.all_to_all(line, AXES, 0, 0, tiled=True)  2.05 us
    ppermute x1, starting transfers between devices, per_device(): smet = lax.ppermute(sguest, AXES, side_down)  1.92 us
  transfers between devices with their start and end apart: 9, of which 3 were waited for; matrix products, arithmetic and copies ran while one was open for 0% of the time, Pallas kernels for 11%

profile of v6, /device:TPU:1, one launch (start us, length us, event | category | flops | bytes accessed | tf_op | source)
XLA Modules:
  0.0 68.1 jit_solution(16504929768721276525)
XLA Ops:
  0.7 4.2 %look.1 = (f32[2,2,64,128]{3,2,1,0:T(8,128)}, f32[9,32,128]{2,1,0:T(8,128)}, f32[9,32,128]{2,1,0:T(8,128)}, f32[2,2,48,128]{3,2,1,0:T(8,128)}, f32[9,24,128]{2,1,0:T(8,128)}, /*index=5*/f32[9,24,128]{2,1,0:T(8,128)}) custom-call(f32[9,1,512]{2,1,0:T(1,128)} %lines.3, bf16[2,18,64,128]{3,2,1,0:T(8,128)(2,1)} %bitcast.35, bf16[2,6,64,128]{3,2,1,0:T(8,128)(2,1)} %bitcast.44, ...), custom_call_target="tpu_custom_call" | custom-call | flops 1000000000 | bytes 2097152 | tf_op jit(solution)/shard_map/look/pallas_call | solution.py:452
  4.9 5.3 %collective-permute-start.2 = (f32[9,24,128]{2,1,0:T(8,128)}, f32[9,24,128]{2,1,0:T(8,128)S(1)}, u32[]{:S(2)}, u32[]{:S(2)}) collective-permute-start(f32[9,24,128]{2,1,0:T(8,128)} %get-tuple-element.29.ssent0), channel_id=1, source_target_pairs={{0,15},{1,14},{2,13},{3,12},{4,11},{5,10},{6,9},{7,8},{8,7},{9,6},... | collective-permute-start | bytes 331784 | tf_op jit(solution)/shard_map/ppermute | solution.py:503
  10.2 4.6 %collective-permute-start.3 = (f32[9,24,128]{2,1,0:T(8,128)}, f32[9,24,128]{2,1,0:T(8,128)S(1)}, u32[]{:S(2)}, u32[]{:S(2)}) collective-permute-start(f32[9,24,128]{2,1,0:T(8,128)} %get-tuple-element.30.ssent1), channel_id=1, source_target_pairs={{8,23},{9,22},{10,21},{11,20},{12,19},{13,18},{14,17},{15,16},{16,... | collective-permute-start | bytes 331784 | tf_op jit(solution)/shard_map/ppermute | solution.py:503
  14.8 0.3 collective-permute-start
  15.1 0.7 collective-permute-start.1
  16.4 0.0 copy-start.2
  16.4 0.0 copy-start.3
  16.5 0.0 copy-start.11
  16.5 0.0 copy-start.13
  16.6 2.6 %local.2 = (f32[36,128]{1,0:T(8,128)S(1)}, f32[8,128]{1,0:T(8,128)}) custom-call(s32[1]{0:T(128)} %bitcast.30.live, f32[9,1,512]{2,1,0:T(1,128)S(1)} %copy-done, bf16[18,6,2048]{2,1,0:T(8,128)(2,1)S(1)} %bitcast.33, bf16[6,6,2048]{2,1,0:T(8,128)(2,1)S(1)} %bitcast.42, s32[96,128]{1,0:T(8,128)S(1)} %bitcast.54), custom_call_target="tpu_custom_call" | custom-call | flops 5000000000 | bytes 2097152 | tf_op jit(solution)/shard_map/local/pallas_call | solution.py:452
  19.1 1.3 %collective-permute-done.3.smet1 = f32[9,24,128]{2,1,0:T(8,128)S(1)} collective-permute-done((f32[9,24,128]{2,1,0:T(8,128)}, f32[9,24,128]{2,1,0:T(8,128)S(1)}, u32[]{:S(2)}, u32[]{:S(2)}) %collective-permute-start.3) | collective-permute-done | bytes 110624 | tf_op jit(solution)/shard_map/ppermute | solution.py:503
  20.6 5.2 %middle.1 = (f32[36,128]{1,0:T(8,128)S(1)}, f32[2,6,32,128]{3,2,1,0:T(8,128)S(1)}, f32[2,6,24,128]{3,2,1,0:T(8,128)S(1)}, f32[2,2,64,128]{3,2,1,0:T(8,128)S(1)},...) custom-call(f32[9,1,512]{2,1,0:T(1,128)S(1)} %copy-done, ...), custom_call_target="tpu_custom_call" | custom-call | flops 10000000000 | bytes 2097152 | tf_op jit(solution)/shard_map/middle/pallas_call | solution.py:452
  25.7 1.9 %collective-permute-start.6 = (f32[3,24,128]{2,1,0:T(8,128)S(1)}, f32[3,24,128]{2,1,0:T(8,128)S(1)}, u32[]{:S(2)}, u32[]{:S(2)}) collective-permute-start(f32[3,24,128]{2,1,0:T(8,128)S(1)} %get-tuple-element.38), channel_id=1, source_target_pairs={{8,7},{9,6},{10,5},{11,4},{12,3},{13,2},{14,1},{15,0},{16,15},{17,... | collective-permute-start | bytes 110600 | tf_op jit(solution)/shard_map/ppermute | solution.py:560
  27.7 3.8 %collective-permute-start.4 = (f32[3,32,128]{2,1,0:T(8,128)S(1)}, f32[3,32,128]{2,1,0:T(8,128)S(1)}, u32[]{:S(2)}, u32[]{:S(2)}) collective-permute-start(f32[3,32,128]{2,1,0:T(8,128)S(1)} %get-tuple-element.34.fsent0), channel_id=1, source_target_pairs={{0,1},{1,0},{2,3},{3,2},{4,5},{5,4},{6,7},{7,6},{8,9},{9,8},{10,11... | collective-permute-start | bytes 147464 | tf_op jit(solution)/shard_map/ppermute | solution.py:503
  31.5 0.7 collective-permute-start.5
  32.2 1.9 %local.3 = (f32[36,128]{1,0:T(8,128)S(1)}, f32[8,128]{1,0:T(8,128)S(1)}) custom-call(s32[1]{0:T(128)} %bitcast.31.live, f32[36,128]{1,0:T(8,128)S(1)} %get-tuple-element.32.values.first, bf16[18,6,2048]{2,1,0:T(8,128)(2,1)S(1)} %bitcast.34, bf16[6,6,2048]{2,1,0:T(8,128)(2,1)S(1)} %bitcast.43, s32[96,128]{1,0:T(8,128)S(1)} %bitcast.55), custom_call_target="tpu_custom_call" | custom-call | flops 5000000000 | bytes 2097152 | tf_op jit(solution)/shard_map/local/pallas_call | solution.py:452
  34.1 0.8 %collective-permute-done.6.smet = f32[3,24,128]{2,1,0:T(8,128)S(1)} collective-permute-done((f32[3,24,128]{2,1,0:T(8,128)S(1)}, f32[3,24,128]{2,1,0:T(8,128)S(1)}, u32[]{:S(2)}, u32[]{:S(2)}) %collective-permute-start.6) | collective-permute-done | bytes 36896 | tf_op jit(solution)/shard_map/ppermute | solution.py:560
  34.9 0.8 %dots.1 = (f32[2,3,64,128]{3,2,1,0:T(8,128)S(1)}, f32[3,24,128]{2,1,0:T(8,128)S(1)}, f32[256,128]{1,0:T(8,128)}) custom-call(f32[8,128]{1,0:T(8,128)S(1)} %get-tuple-element.31.dots, f32[8,128]{1,0:T(8,128)S(1)} %get-tuple-element.33.product, f32[3,32,128]{2,1,0:T(8,128)S(1)} %get-tuple-element.34.fsent0, f32[3,32,128]{2,1,0:T(8,128)S(1)} %get-tuple-element.35.fsent1, ...), custom_call_target="tpu_custom_call" | custom-call | flops 100000000 | bytes 2097152 | tf_op jit(solution)/shard_map/dots/pallas_call | solution.py:452
  35.7 18.6 %all-to-all-start = ((f32[256,1,128]{2,1,0:T(1,128)}), f32[256,1,128]{2,1,0:T(1,128)S(1)}, u32[]{:S(2)}, u32[]{:S(2)}) async-start(f32[256,1,128]{2,1,0:T(1,128)} %bitcast.27), calls=%async_computation | async-start | bytes 262144 | tf_op jit(solution)/shard_map/all_to_all | solution.py:571
  54.3 8.2 %collective-permute-start.7 = (f32[3,24,128]{2,1,0:T(8,128)S(1)}, f32[3,24,128]{2,1,0:T(8,128)S(1)}, u32[]{:S(2)}, u32[]{:S(2)}) collective-permute-start(f32[3,24,128]{2,1,0:T(8,128)S(1)} %get-tuple-element.45.svalues), channel_id=1, source_target_pairs={{0,15},{1,14},{2,13},{3,12},{4,11},{5,10},{6,9},{7,8},{8,23},{9,22... | collective-permute-start | bytes 110600 | tf_op jit(solution)/shard_map/ppermute | solution.py:572
  62.5 2.1 %last.1.extra = f32[36,128]{1,0:T(8,128)S(1)} custom-call(f32[36,128]{1,0:T(8,128)S(1)} %get-tuple-element.41.extra, bf16[2,18,64,128]{3,2,1,0:T(8,128)(2,1)S(1)} %bitcast.37, bf16[2,6,64,128]{3,2,1,0:T(8,128)(2,1)S(1)} %bitcast.46, s32[2,2,32,128]{3,2,1,0:T(8,128)S(1)} %bitcast.53, bf16[2,18,48,128]{3,2,1,0:T(8,128)(2,1)S(1)} %bitcast.40, ...), custom_call_target="tpu_custom_call" | custom-call | flops 5000000000 | bytes 2097152 | tf_op jit(solution)/shard_map/last/pallas_call | solution.py:452
  64.6 0.6 guest.1.second
  65.3 2.1 %all-to-all-done = f32[256,1,128]{2,1,0:T(1,128)S(1)} async-done(((f32[256,1,128]{2,1,0:T(1,128)}), f32[256,1,128]{2,1,0:T(1,128)S(1)}, u32[]{:S(2)}, u32[]{:S(2)}) %all-to-all-start) | async-done | bytes 131104 | tf_op jit(solution)/shard_map/all_to_all | solution.py:571
  67.3 0.8 %close.1 = (f32[9,1,512]{2,1,0:T(1,128)}, f32[9,1,512]{2,1,0:T(1,128)}) custom-call(f32[256,128]{1,0:T(8,128)S(1)} %bitcast.32, f32[9,1,512]{2,1,0:T(1,128)S(1)} %copy-done, f32[36,128]{1,0:T(8,128)S(1)} %get-tuple-element.32.values.first, f32[36,128]{1,0:T(8,128)S(1)} %guest.1.second), custom_call_target="tpu_custom_call" | custom-call | flops 1000000 | bytes 2097152 | tf_op jit(solution)/shard_map/close/pallas_call | solution.py:452
  (34 shorter events, 0.1 us)
Async XLA Ops:
  0.6 15.8 %copy-start = (f32[9,1,512]{2,1,0:T(1,128)S(1)}, f32[9,1,512]{2,1,0:T(1,128)}, u32[]{:S(2)}) copy-start(f32[9,1,512]{2,1,0:T(1,128)} %lines.3) | copy-start | bytes 55300
  0.6 15.8 %copy-start.1 = (bf16[18,6,1,2048]{3,1,2,0:T(8,128)(2,1)S(1)}, bf16[18,6,1,2048]{3,1,2,0:T(8,128)(2,1)}, u32[]{:S(2)}) copy-start(bf16[18,6,1,2048]{3,1,2,0:T(8,128)(2,1)} %param.13) | copy-start | bytes 1327108
  0.7 15.8 %copy-start.4 = (bf16[6,6,1,2048]{3,1,2,0:T(8,128)(2,1)S(1)}, bf16[6,6,1,2048]{3,1,2,0:T(8,128)(2,1)}, u32[]{:S(2)}) copy-start(bf16[6,6,1,2048]{3,1,2,0:T(8,128)(2,1)} %param.14) | copy-start | bytes 442372
  0.7 15.8 %copy-start.12 = (s32[6,1,2048]{2,1,0:T(1,128)S(1)}, s32[6,1,2048]{2,1,0:T(1,128)}, u32[]{:S(2)}) copy-start(s32[6,1,2048]{2,1,0:T(1,128)} %param.15) | copy-start | bytes 147460
  4.9 14.3 %collective-permute-start.2 = (f32[9,24,128]{2,1,0:T(8,128)}, f32[9,24,128]{2,1,0:T(8,128)S(1)}, u32[]{:S(2)}, u32[]{:S(2)}) collective-permute-start(f32[9,24,128]{2,1,0:T(8,128)} %get-tuple-element.29.ssent0), channel_id=1, source_target_pairs={{0,15},{1,14},{2,13},{3,12},{4,11},{5,10},{6,9},{7,8},{8,7},{9,6},... | collective-permute-start | bytes 331784 | tf_op jit(solution)/shard_map/ppermute | solution.py:503
  10.2 10.3 %collective-permute-start.3 = (f32[9,24,128]{2,1,0:T(8,128)}, f32[9,24,128]{2,1,0:T(8,128)S(1)}, u32[]{:S(2)}, u32[]{:S(2)}) collective-permute-start(f32[9,24,128]{2,1,0:T(8,128)} %get-tuple-element.30.ssent1), channel_id=1, source_target_pairs={{8,23},{9,22},{10,21},{11,20},{12,19},{13,18},{14,17},{15,16},{16,... | collective-permute-start | bytes 331784 | tf_op jit(solution)/shard_map/ppermute | solution.py:503
  14.8 5.7 %collective-permute-start = (f32[9,32,128]{2,1,0:T(8,128)}, f32[9,32,128]{2,1,0:T(8,128)S(1)}, u32[]{:S(2)}, u32[]{:S(2)}) collective-permute-start(f32[9,32,128]{2,1,0:T(8,128)} %get-tuple-element.26.fsent0), channel_id=1, source_target_pairs={{0,1},{1,0},{2,3},{3,2},{4,5},{5,4},{6,7},{7,6},{8,9},{9,8},{10,11... | collective-permute-start | bytes 442376 | tf_op jit(solution)/shard_map/ppermute | solution.py:503
  15.1 5.4 %collective-permute-start.1 = (f32[9,32,128]{2,1,0:T(8,128)}, f32[9,32,128]{2,1,0:T(8,128)S(1)}, u32[]{:S(2)}, u32[]{:S(2)}) collective-permute-start(f32[9,32,128]{2,1,0:T(8,128)} %get-tuple-element.27.fsent1), channel_id=1, source_target_pairs={{1,2},{2,1},{3,4},{4,3},{5,6},{6,5},{9,10},{10,9},{11,12},{12,11},... | collective-permute-start | bytes 442376 | tf_op jit(solution)/shard_map/ppermute | solution.py:503
  16.4 4.0 %copy-start.2 = (bf16[2,18,2,1,4096]{4,2,3,1,0:T(2,128)(2,1)S(1)}, bf16[2,18,2,1,4096]{4,2,3,1,0:T(2,128)(2,1)}, u32[]{:S(2)}) copy-start(bf16[2,18,2,1,4096]{4,2,3,1,0:T(2,128)(2,1)} %param.16) | copy-start | bytes 1769476
  16.4 4.0 %copy-start.3 = (bf16[2,18,2,1,3072]{4,2,3,1,0:T(2,128)(2,1)S(1)}, bf16[2,18,2,1,3072]{4,2,3,1,0:T(2,128)(2,1)}, u32[]{:S(2)}) copy-start(bf16[2,18,2,1,3072]{4,2,3,1,0:T(2,128)(2,1)} %param.19) | copy-start | bytes 1327108
  16.4 4.0 %copy-start.5 = (bf16[2,6,2,1,4096]{4,2,3,1,0:T(2,128)(2,1)S(1)}, bf16[2,6,2,1,4096]{4,2,3,1,0:T(2,128)(2,1)}, u32[]{:S(2)}) copy-start(bf16[2,6,2,1,4096]{4,2,3,1,0:T(2,128)(2,1)} %param.17) | copy-start | bytes 589828
  16.5 4.0 %copy-start.6 = (bf16[2,6,2,1,3072]{4,2,3,1,0:T(2,128)(2,1)S(1)}, bf16[2,6,2,1,3072]{4,2,3,1,0:T(2,128)(2,1)}, u32[]{:S(2)}) copy-start(bf16[2,6,2,1,3072]{4,2,3,1,0:T(2,128)(2,1)} %param.20) | copy-start | bytes 442372
  16.5 4.0 %copy-start.7 = (f32[9,32,128]{2,1,0:T(8,128)S(1)}, f32[9,32,128]{2,1,0:T(8,128)}, u32[]{:S(2)}) copy-start(f32[9,32,128]{2,1,0:T(8,128)} %get-tuple-element.26.fsent0) | copy-start | bytes 442372
  16.5 4.0 %copy-start.8 = (f32[9,32,128]{2,1,0:T(8,128)S(1)}, f32[9,32,128]{2,1,0:T(8,128)}, u32[]{:S(2)}) copy-start(f32[9,32,128]{2,1,0:T(8,128)} %get-tuple-element.27.fsent1) | copy-start | bytes 442372
  16.5 4.0 %copy-start.9 = (f32[9,24,128]{2,1,0:T(8,128)S(1)}, f32[9,24,128]{2,1,0:T(8,128)}, u32[]{:S(2)}) copy-start(f32[9,24,128]{2,1,0:T(8,128)} %get-tuple-element.29.ssent0) | copy-start | bytes 331780
  16.5 4.0 %copy-start.10 = (f32[9,24,128]{2,1,0:T(8,128)S(1)}, f32[9,24,128]{2,1,0:T(8,128)}, u32[]{:S(2)}) copy-start(f32[9,24,128]{2,1,0:T(8,128)} %get-tuple-element.30.ssent1) | copy-start | bytes 331780
  16.5 4.0 %copy-start.11 = (s32[2,2,1,4096]{3,2,1,0:T(1,128)S(1)}, s32[2,2,1,4096]{3,2,1,0:T(1,128)}, u32[]{:S(2)}) copy-start(s32[2,2,1,4096]{3,2,1,0:T(1,128)} %param.18) | copy-start | bytes 196612
  16.5 4.0 %copy-start.13 = (s32[2,2,1,3072]{3,2,1,0:T(1,128)S(1)}, s32[2,2,1,3072]{3,2,1,0:T(1,128)}, u32[]{:S(2)}) copy-start(s32[2,2,1,3072]{3,2,1,0:T(1,128)} %param.21) | copy-start | bytes 147460
  16.5 4.0 %copy-start.14 = (f32[2,2,64,128]{3,2,1,0:T(8,128)S(1)}, f32[2,2,64,128]{3,2,1,0:T(8,128)}, u32[]{:S(2)}) copy-start(f32[2,2,64,128]{3,2,1,0:T(8,128)} %get-tuple-element.25.fseen) | copy-start | bytes 393220
  25.7 9.2 %collective-permute-start.6 = (f32[3,24,128]{2,1,0:T(8,128)S(1)}, f32[3,24,128]{2,1,0:T(8,128)S(1)}, u32[]{:S(2)}, u32[]{:S(2)}) collective-permute-start(f32[3,24,128]{2,1,0:T(8,128)S(1)} %get-tuple-element.38), channel_id=1, source_target_pairs={{8,7},{9,6},{10,5},{11,4},{12,3},{13,2},{14,1},{15,0},{16,15},{17,... | collective-permute-start | bytes 110600 | tf_op jit(solution)/shard_map/ppermute | solution.py:560
  27.7 7.3 %collective-permute-start.4 = (f32[3,32,128]{2,1,0:T(8,128)S(1)}, f32[3,32,128]{2,1,0:T(8,128)S(1)}, u32[]{:S(2)}, u32[]{:S(2)}) collective-permute-start(f32[3,32,128]{2,1,0:T(8,128)S(1)} %get-tuple-element.34.fsent0), channel_id=1, source_target_pairs={{0,1},{1,0},{2,3},{3,2},{4,5},{5,4},{6,7},{7,6},{8,9},{9,8},{10,11... | collective-permute-start | bytes 147464 | tf_op jit(solution)/shard_map/ppermute | solution.py:503
  31.5 3.4 %collective-permute-start.5 = (f32[3,32,128]{2,1,0:T(8,128)S(1)}, f32[3,32,128]{2,1,0:T(8,128)S(1)}, u32[]{:S(2)}, u32[]{:S(2)}) collective-permute-start(f32[3,32,128]{2,1,0:T(8,128)S(1)} %get-tuple-element.35.fsent1), channel_id=1, source_target_pairs={{1,2},{2,1},{3,4},{4,3},{5,6},{6,5},{9,10},{10,9},{11,12},{12,11},... | collective-permute-start | bytes 147464 | tf_op jit(solution)/shard_map/ppermute | solution.py:503
  35.7 31.6 %all-to-all-start = ((f32[256,1,128]{2,1,0:T(1,128)}), f32[256,1,128]{2,1,0:T(1,128)S(1)}, u32[]{:S(2)}, u32[]{:S(2)}) async-start(f32[256,1,128]{2,1,0:T(1,128)} %bitcast.27), calls=%async_computation | async-start | bytes 262144 | tf_op jit(solution)/shard_map/all_to_all | solution.py:571
  54.3 10.3 %collective-permute-start.7 = (f32[3,24,128]{2,1,0:T(8,128)S(1)}, f32[3,24,128]{2,1,0:T(8,128)S(1)}, u32[]{:S(2)}, u32[]{:S(2)}) collective-permute-start(f32[3,24,128]{2,1,0:T(8,128)S(1)} %get-tuple-element.45.svalues), channel_id=1, source_target_pairs={{0,15},{1,14},{2,13},{3,12},{4,11},{5,10},{6,9},{7,8},{8,23},{9,22... | collective-permute-start | bytes 110600 | tf_op jit(solution)/shard_map/ppermute | solution.py:572
  (1 other events, 4.0 us)

commit v7 on v6

--- a/solution.py
+++ b/solution.py
@@ -326,7 +326,7 @@
         seen = predict(across, fetch(table, index))
         summed = [jnp.sum(x, axis=0, keepdims=True) for x in project(along, seen) + normal(along)]
         z = solve(invert(summed[3:]), summed[:3])
-        share = (i < live[0]).astype(F32)
+        share = (i < live[0, 0]).astype(F32)
         left = [share * e for e in residue(along, seen, z)]
         terms = [across[j] * left[0] + across[JAC + j] * left[1] for j in range(JAC)]
         seen = jnp.sum(seen[0] * left[0] + seen[1] * left[1], axis=0, keepdims=True)
@@ -341,7 +341,7 @@
         add_in([parts for _, parts in done], total)
         return carry
 
-    lax.fori_loop(0, (live[0] + LOCAL_GROUP - 1) // LOCAL_GROUP, body, 0)
+    lax.fori_loop(0, (live[0, 0] + LOCAL_GROUP - 1) // LOCAL_GROUP, body, 0)
     fold(total, out)
 
 
@@ -409,17 +409,17 @@
     result[...] += extra[...]
 
 
-def guest_kernel(extra, scam, spoint, scams, sseen, svalues, result, sindex, sz, stage, total):
+def close_kernel(
+    extra, scam, spoint, scams, sseen, svalues, sums, lines, first,
+    step_out, residual_out, base, second, sindex, sz, stage, total,
+):
     _, (_, sheld) = place_of()
     weave(scams, sindex)
     total[...] = jnp.zeros_like(total)
     widened(svalues, sz, 1)
     pair_return(scam, spoint, sindex, sseen, sz, 0, sheld, stage, total, (1,))
-    fold(total, result)
-    result[...] += extra[...]
-
-
-def close_kernel(sums, lines, first, second, step_out, residual_out, base):
+    fold(total, second)
+    second[...] += extra[...]
     in_rows(lines, base)
     line = jnp.sum(sums[...], axis=0, keepdims=True)
     place = lax.broadcasted_iota(jnp.int32, line.shape, 1)
@@ -448,7 +448,7 @@
 
 def call(kernel, ins, outs, scratch, flops, name, place=VMEM, to=VMEM, room=12):
     outs = [jax.ShapeDtypeStruct(shape, F32) for shape in outs]
-    specs = [SMEM if i == 0 and x.ndim == 1 else place for i, x in enumerate(ins)]
+    specs = [SMEM if x.shape == (1, 1) else place for x in ins]
     return pl.pallas_call(
         kernel,
         out_shape=outs,
@@ -489,7 +489,6 @@
         pairs(lambda s, g: (s ^ 1, segs - 1 - g)),
         pairs(lambda s, g: ((s + 1 ^ 1) - 1, segs - 1 - g)),
     )
-    live = live_blocks.reshape(1)
     lcam, lpoint = loc_cam_jac[:, :, 0], loc_point_jac[:, :, 0]
     lcams = loc_cams.reshape(-1, LANES)
     fcam, fpoint = rows_of(fwd_cam_jac), rows_of(fwd_point_jac)
@@ -536,7 +535,7 @@
     def local(values):
         return call(
             local_kernel,
-            [live, values, lcam, lpoint, lcams],
+            [live_blocks, values, lcam, lpoint, lcams],
             [(ROWS, LANES), (8, LANES)],
             scatter_scratch(watched * LOCAL_GROUP) + table,
             5 * 10**9,
@@ -578,16 +577,13 @@
         5 * 10**9,
         "last",
     )
-    (t,) = call(
-        guest_kernel,
-        [t, scam, spoint, scams, sseen, ssent],
-        [(ROWS, LANES)],
-        index_scratch[1:] + z_scratch[1:] + total_scratch,
+    step, residual = call(
+        close_kernel,
+        [t, scam, spoint, scams, sseen, ssent, line, gradient, p],
+        [gradient.shape] * 2,
+        table * 2 + index_scratch[1:] + z_scratch[1:] + total_scratch,
         2 * 10**9,
-        "guest",
-    )
-    step, residual = call(
-        close_kernel, [line, gradient, p, t], [gradient.shape] * 2, table, 10**6, "close"
+        "close",
     )
     return step, residual
 

time: 68.4 us -> 68.8 us (level)
    pallas_call x8 -> x7, Pallas kernels: 18.2 us -> 18 us  [call(): pl.pallas_call(kernel, out_shape=outs, in_specs=specs, out_specs=[to] * l...]
  transfers between devices with their start and end apart: 9 -> 9, of which waited for: 3 -> 3; matrix products, arithmetic and copies ran while one was open for 0% -> 0% of each run, Pallas kernels for 11% -> 10%
where the time goes in v7:
time: 68.8 us; the launch traced here: 68.5 us
  starting transfers between devices  44 us (64%)
  Pallas kernels  18 us (26%)
  waiting for transfers between devices  4.85 us (7%)
  between operations  1.6 us (2%)
    all_to_all x1, starting transfers between devices, per_device(): line = lax.all_to_all(line, AXES, 0, 0, tiled=True)  18.6 us
    pallas_call x7, Pallas kernels, call(): pl.pallas_call(kernel, out_shape=outs, in_specs=specs, out_specs=[to] * l...  18 us
    ppermute x6, starting transfers between devices, meet(): lax.ppermute(send, AXES, pairs)  15.3 us
    ppermute x1, starting transfers between devices, per_device(): ssent = lax.ppermute(sz, AXES, side_up)  8.16 us
    all_to_all x1, waiting for transfers between devices, per_device(): line = lax.all_to_all(line, AXES, 0, 0, tiled=True)  2.72 us
    ppermute x1, starting transfers between devices, per_device(): smet = lax.ppermute(sguest, AXES, side_down)  1.92 us
  transfers between devices with their start and end apart: 9, of which 3 were waited for; matrix products, arithmetic and copies ran while one was open for 0% of the time, Pallas kernels for 10%

profile of v7, /device:TPU:1, one launch (start us, length us, event | category | flops | bytes accessed | tf_op | source)
XLA Modules:
  0.0 68.5 jit_solution(17627690492743984870)
XLA Ops:
  0.7 4.2 %look.1 = (f32[2,2,64,128]{3,2,1,0:T(8,128)}, f32[9,32,128]{2,1,0:T(8,128)}, f32[9,32,128]{2,1,0:T(8,128)}, f32[2,2,48,128]{3,2,1,0:T(8,128)}, f32[9,24,128]{2,1,0:T(8,128)}, /*index=5*/f32[9,24,128]{2,1,0:T(8,128)}) custom-call(f32[9,1,512]{2,1,0:T(1,128)} %lines.3, bf16[2,18,64,128]{3,2,1,0:T(8,128)(2,1)} %bitcast.32, bf16[2,6,64,128]{3,2,1,0:T(8,128)(2,1)} %bitcast.41, ...), custom_call_target="tpu_custom_call" | custom-call | flops 1000000000 | bytes 2097152 | tf_op jit(solution)/shard_map/look/pallas_call | solution.py:452
  4.9 5.3 %collective-permute-start.2 = (f32[9,24,128]{2,1,0:T(8,128)}, f32[9,24,128]{2,1,0:T(8,128)S(1)}, u32[]{:S(2)}, u32[]{:S(2)}) collective-permute-start(f32[9,24,128]{2,1,0:T(8,128)} %get-tuple-element.29.ssent0), channel_id=1, source_target_pairs={{0,15},{1,14},{2,13},{3,12},{4,11},{5,10},{6,9},{7,8},{8,7},{9,6},... | collective-permute-start | bytes 331784 | tf_op jit(solution)/shard_map/ppermute | solution.py:502
  10.2 4.6 %collective-permute-start.3 = (f32[9,24,128]{2,1,0:T(8,128)}, f32[9,24,128]{2,1,0:T(8,128)S(1)}, u32[]{:S(2)}, u32[]{:S(2)}) collective-permute-start(f32[9,24,128]{2,1,0:T(8,128)} %get-tuple-element.30.ssent1), channel_id=1, source_target_pairs={{8,23},{9,22},{10,21},{11,20},{12,19},{13,18},{14,17},{15,16},{16,... | collective-permute-start | bytes 331784 | tf_op jit(solution)/shard_map/ppermute | solution.py:502
  14.8 0.3 collective-permute-start
  15.1 0.7 collective-permute-start.1
  16.4 0.0 copy-start.1
  16.4 0.0 copy-start.2
  16.4 0.0 copy-start.4
  16.5 0.0 copy-start.5
  16.5 0.0 copy-start.10
  16.6 2.6 %local.2 = (f32[36,128]{1,0:T(8,128)S(1)}, f32[8,128]{1,0:T(8,128)}) custom-call(s32[1,1]{1,0:T(1,128)S(6)} %copy.22.live, f32[9,1,512]{2,1,0:T(1,128)S(1)} %copy-done.13, bf16[18,6,2048]{2,1,0:T(8,128)(2,1)S(1)} %bitcast.30, bf16[6,6,2048]{2,1,0:T(8,128)(2,1)S(1)} %bitcast.39, s32[96,128]{1,0:T(8,128)S(1)} %bitcast.51), custom_call_target="tpu_custom_call" | custom-call | flops 5000000000 | bytes 2097152 | tf_op jit(solution)/shard_map/local/pallas_call | solution.py:452
  19.1 1.3 %collective-permute-done.3.smet1 = f32[9,24,128]{2,1,0:T(8,128)S(1)} collective-permute-done((f32[9,24,128]{2,1,0:T(8,128)}, f32[9,24,128]{2,1,0:T(8,128)S(1)}, u32[]{:S(2)}, u32[]{:S(2)}) %collective-permute-start.3) | collective-permute-done | bytes 110624 | tf_op jit(solution)/shard_map/ppermute | solution.py:502
  20.6 5.1 %middle.1 = (f32[36,128]{1,0:T(8,128)S(1)}, f32[2,6,32,128]{3,2,1,0:T(8,128)S(1)}, f32[2,6,24,128]{3,2,1,0:T(8,128)S(1)}, f32[2,2,64,128]{3,2,1,0:T(8,128)S(1)},...) custom-call(f32[9,1,512]{2,1,0:T(1,128)S(1)} %copy-done.13, ...), custom_call_target="tpu_custom_call" | custom-call | flops 10000000000 | bytes 2097152 | tf_op jit(solution)/shard_map/middle/pallas_call | solution.py:452
  25.7 1.9 %collective-permute-start.6 = (f32[3,24,128]{2,1,0:T(8,128)S(1)}, f32[3,24,128]{2,1,0:T(8,128)S(1)}, u32[]{:S(2)}, u32[]{:S(2)}) collective-permute-start(f32[3,24,128]{2,1,0:T(8,128)S(1)} %get-tuple-element.40), channel_id=1, source_target_pairs={{8,7},{9,6},{10,5},{11,4},{12,3},{13,2},{14,1},{15,0},{16,15},{17,... | collective-permute-start | bytes 110600 | tf_op jit(solution)/shard_map/ppermute | solution.py:559
  27.6 3.8 %collective-permute-start.4 = (f32[3,32,128]{2,1,0:T(8,128)S(1)}, f32[3,32,128]{2,1,0:T(8,128)S(1)}, u32[]{:S(2)}, u32[]{:S(2)}) collective-permute-start(f32[3,32,128]{2,1,0:T(8,128)S(1)} %get-tuple-element.36.fsent0), channel_id=1, source_target_pairs={{0,1},{1,0},{2,3},{3,2},{4,5},{5,4},{6,7},{7,6},{8,9},{9,8},{10,11... | collective-permute-start | bytes 147464 | tf_op jit(solution)/shard_map/ppermute | solution.py:502
  31.4 0.7 collective-permute-start.5
  32.1 2.0 %local.3 = (f32[36,128]{1,0:T(8,128)S(1)}, f32[8,128]{1,0:T(8,128)S(1)}) custom-call(s32[1,1]{1,0:T(1,128)S(6)} %copy.22.live, f32[36,128]{1,0:T(8,128)S(1)} %get-tuple-element.31.values.first, bf16[18,6,2048]{2,1,0:T(8,128)(2,1)S(1)} %bitcast.31, bf16[6,6,2048]{2,1,0:T(8,128)(2,1)S(1)} %bitcast.40, s32[96,128]{1,0:T(8,128)S(1)} %bitcast.52), custom_call_target="tpu_custom_call" | custom-call | flops 5000000000 | bytes 2097152 | tf_op jit(solution)/shard_map/local/pallas_call | solution.py:452
  34.1 0.8 %collective-permute-done.6.smet = f32[3,24,128]{2,1,0:T(8,128)S(1)} collective-permute-done((f32[3,24,128]{2,1,0:T(8,128)S(1)}, f32[3,24,128]{2,1,0:T(8,128)S(1)}, u32[]{:S(2)}, u32[]{:S(2)}) %collective-permute-start.6) | collective-permute-done | bytes 36896 | tf_op jit(solution)/shard_map/ppermute | solution.py:559
  34.9 0.8 %dots.1 = (f32[2,3,64,128]{3,2,1,0:T(8,128)S(1)}, f32[3,24,128]{2,1,0:T(8,128)S(1)}, f32[256,128]{1,0:T(8,128)}) custom-call(f32[8,128]{1,0:T(8,128)S(1)} %get-tuple-element.34.dots, f32[8,128]{1,0:T(8,128)S(1)} %get-tuple-element.35.product, f32[3,32,128]{2,1,0:T(8,128)S(1)} %get-tuple-element.36.fsent0, f32[3,32,128]{2,1,0:T(8,128)S(1)} %get-tuple-element.37.fsent1, ...), custom_call_target="tpu_custom_call" | custom-call | flops 100000000 | bytes 2097152 | tf_op jit(solution)/shard_map/dots/pallas_call | solution.py:452
  35.7 18.6 %all-to-all-start = ((f32[256,1,128]{2,1,0:T(1,128)}), f32[256,1,128]{2,1,0:T(1,128)S(1)}, u32[]{:S(2)}, u32[]{:S(2)}) async-start(f32[256,1,128]{2,1,0:T(1,128)} %bitcast.26), calls=%async_computation | async-start | bytes 262144 | tf_op jit(solution)/shard_map/all_to_all | solution.py:570
  54.3 8.2 %collective-permute-start.7 = (f32[3,24,128]{2,1,0:T(8,128)S(1)}, f32[3,24,128]{2,1,0:T(8,128)S(1)}, u32[]{:S(2)}, u32[]{:S(2)}) collective-permute-start(f32[3,24,128]{2,1,0:T(8,128)S(1)} %get-tuple-element.44.svalues), channel_id=1, source_target_pairs={{0,15},{1,14},{2,13},{3,12},{4,11},{5,10},{6,9},{7,8},{8,23},{9,22... | collective-permute-start | bytes 110600 | tf_op jit(solution)/shard_map/ppermute | solution.py:571
  62.4 2.1 %last.1.extra = f32[36,128]{1,0:T(8,128)S(1)} custom-call(f32[36,128]{1,0:T(8,128)S(1)} %get-tuple-element.32.extra, bf16[2,18,64,128]{3,2,1,0:T(8,128)(2,1)S(1)} %bitcast.34, bf16[2,6,64,128]{3,2,1,0:T(8,128)(2,1)S(1)} %bitcast.43, s32[2,2,32,128]{3,2,1,0:T(8,128)S(1)} %bitcast.50, bf16[2,18,48,128]{3,2,1,0:T(8,128)(2,1)S(1)} %bitcast.37, ...), custom_call_target="tpu_custom_call" | custom-call | flops 5000000000 | bytes 2097152 | tf_op jit(solution)/shard_map/last/pallas_call | solution.py:452
  64.5 2.7 %all-to-all-done = f32[256,1,128]{2,1,0:T(1,128)S(1)} async-done(((f32[256,1,128]{2,1,0:T(1,128)}), f32[256,1,128]{2,1,0:T(1,128)S(1)}, u32[]{:S(2)}, u32[]{:S(2)}) %all-to-all-start) | async-done | bytes 131104 | tf_op jit(solution)/shard_map/all_to_all | solution.py:570
  67.2 1.3 %close.1 = (f32[9,1,512]{2,1,0:T(1,128)}, f32[9,1,512]{2,1,0:T(1,128)}) custom-call(f32[36,128]{1,0:T(8,128)S(1)} %last.1.extra, bf16[2,18,48,128]{3,2,1,0:T(8,128)(2,1)S(1)} %bitcast.38, bf16[2,6,48,128]{3,2,1,0:T(8,128)(2,1)S(1)} %bitcast.47, s32[2,2,24,128]{3,2,1,0:T(8,128)S(1)} %bitcast.56, f32[2,2,48,128]{3,2,1,0:T(8,128)S(1)} %get-tuple-element.43.sseen, ...), custom_call_target="tpu_custom_call" | custom-call | flops 2000000000 | bytes 2097152 | tf_op jit(solution)/shard_map/close/pallas_call | solution.py:452
  (33 shorter events, 0.1 us)
Async XLA Ops:
  0.6 15.8 %copy-start = (bf16[18,6,1,2048]{3,1,2,0:T(8,128)(2,1)S(1)}, bf16[18,6,1,2048]{3,1,2,0:T(8,128)(2,1)}, u32[]{:S(2)}) copy-start(bf16[18,6,1,2048]{3,1,2,0:T(8,128)(2,1)} %param.13) | copy-start | bytes 1327108
  0.6 15.8 %copy-start.3 = (bf16[6,6,1,2048]{3,1,2,0:T(8,128)(2,1)S(1)}, bf16[6,6,1,2048]{3,1,2,0:T(8,128)(2,1)}, u32[]{:S(2)}) copy-start(bf16[6,6,1,2048]{3,1,2,0:T(8,128)(2,1)} %param.14) | copy-start | bytes 442372
  0.7 15.8 %copy-start.11 = (s32[6,1,2048]{2,1,0:T(1,128)S(1)}, s32[6,1,2048]{2,1,0:T(1,128)}, u32[]{:S(2)}) copy-start(s32[6,1,2048]{2,1,0:T(1,128)} %param.15) | copy-start | bytes 147460
  0.7 15.8 %copy-start.13 = (f32[9,1,512]{2,1,0:T(1,128)S(1)}, f32[9,1,512]{2,1,0:T(1,128)}, u32[]{:S(2)}) copy-start(f32[9,1,512]{2,1,0:T(1,128)} %lines.3) | copy-start | bytes 55300
  4.9 14.3 %collective-permute-start.2 = (f32[9,24,128]{2,1,0:T(8,128)}, f32[9,24,128]{2,1,0:T(8,128)S(1)}, u32[]{:S(2)}, u32[]{:S(2)}) collective-permute-start(f32[9,24,128]{2,1,0:T(8,128)} %get-tuple-element.29.ssent0), channel_id=1, source_target_pairs={{0,15},{1,14},{2,13},{3,12},{4,11},{5,10},{6,9},{7,8},{8,7},{9,6},... | collective-permute-start | bytes 331784 | tf_op jit(solution)/shard_map/ppermute | solution.py:502
  10.2 10.3 %collective-permute-start.3 = (f32[9,24,128]{2,1,0:T(8,128)}, f32[9,24,128]{2,1,0:T(8,128)S(1)}, u32[]{:S(2)}, u32[]{:S(2)}) collective-permute-start(f32[9,24,128]{2,1,0:T(8,128)} %get-tuple-element.30.ssent1), channel_id=1, source_target_pairs={{8,23},{9,22},{10,21},{11,20},{12,19},{13,18},{14,17},{15,16},{16,... | collective-permute-start | bytes 331784 | tf_op jit(solution)/shard_map/ppermute | solution.py:502
  14.8 5.7 %collective-permute-start = (f32[9,32,128]{2,1,0:T(8,128)}, f32[9,32,128]{2,1,0:T(8,128)S(1)}, u32[]{:S(2)}, u32[]{:S(2)}) collective-permute-start(f32[9,32,128]{2,1,0:T(8,128)} %get-tuple-element.26.fsent0), channel_id=1, source_target_pairs={{0,1},{1,0},{2,3},{3,2},{4,5},{5,4},{6,7},{7,6},{8,9},{9,8},{10,11... | collective-permute-start | bytes 442376 | tf_op jit(solution)/shard_map/ppermute | solution.py:502
  15.1 5.4 %collective-permute-start.1 = (f32[9,32,128]{2,1,0:T(8,128)}, f32[9,32,128]{2,1,0:T(8,128)S(1)}, u32[]{:S(2)}, u32[]{:S(2)}) collective-permute-start(f32[9,32,128]{2,1,0:T(8,128)} %get-tuple-element.27.fsent1), channel_id=1, source_target_pairs={{1,2},{2,1},{3,4},{4,3},{5,6},{6,5},{9,10},{10,9},{11,12},{12,11},... | collective-permute-start | bytes 442376 | tf_op jit(solution)/shard_map/ppermute | solution.py:502
  16.4 4.0 %copy-start.1 = (bf16[2,18,2,1,4096]{4,2,3,1,0:T(2,128)(2,1)S(1)}, bf16[2,18,2,1,4096]{4,2,3,1,0:T(2,128)(2,1)}, u32[]{:S(2)}) copy-start(bf16[2,18,2,1,4096]{4,2,3,1,0:T(2,128)(2,1)} %param.16) | copy-start | bytes 1769476
  16.4 4.0 %copy-start.2 = (bf16[2,18,2,1,3072]{4,2,3,1,0:T(2,128)(2,1)S(1)}, bf16[2,18,2,1,3072]{4,2,3,1,0:T(2,128)(2,1)}, u32[]{:S(2)}) copy-start(bf16[2,18,2,1,3072]{4,2,3,1,0:T(2,128)(2,1)} %param.19) | copy-start | bytes 1327108
  16.4 4.0 %copy-start.4 = (bf16[2,6,2,1,4096]{4,2,3,1,0:T(2,128)(2,1)S(1)}, bf16[2,6,2,1,4096]{4,2,3,1,0:T(2,128)(2,1)}, u32[]{:S(2)}) copy-start(bf16[2,6,2,1,4096]{4,2,3,1,0:T(2,128)(2,1)} %param.17) | copy-start | bytes 589828
  16.5 4.0 %copy-start.5 = (bf16[2,6,2,1,3072]{4,2,3,1,0:T(2,128)(2,1)S(1)}, bf16[2,6,2,1,3072]{4,2,3,1,0:T(2,128)(2,1)}, u32[]{:S(2)}) copy-start(bf16[2,6,2,1,3072]{4,2,3,1,0:T(2,128)(2,1)} %param.20) | copy-start | bytes 442372
  16.5 4.0 %copy-start.6 = (f32[9,32,128]{2,1,0:T(8,128)S(1)}, f32[9,32,128]{2,1,0:T(8,128)}, u32[]{:S(2)}) copy-start(f32[9,32,128]{2,1,0:T(8,128)} %get-tuple-element.26.fsent0) | copy-start | bytes 442372
  16.5 4.0 %copy-start.7 = (f32[9,32,128]{2,1,0:T(8,128)S(1)}, f32[9,32,128]{2,1,0:T(8,128)}, u32[]{:S(2)}) copy-start(f32[9,32,128]{2,1,0:T(8,128)} %get-tuple-element.27.fsent1) | copy-start | bytes 442372
  16.5 4.0 %copy-start.8 = (f32[9,24,128]{2,1,0:T(8,128)S(1)}, f32[9,24,128]{2,1,0:T(8,128)}, u32[]{:S(2)}) copy-start(f32[9,24,128]{2,1,0:T(8,128)} %get-tuple-element.29.ssent0) | copy-start | bytes 331780
  16.5 4.0 %copy-start.9 = (f32[9,24,128]{2,1,0:T(8,128)S(1)}, f32[9,24,128]{2,1,0:T(8,128)}, u32[]{:S(2)}) copy-start(f32[9,24,128]{2,1,0:T(8,128)} %get-tuple-element.30.ssent1) | copy-start | bytes 331780
  16.5 4.0 %copy-start.10 = (s32[2,2,1,4096]{3,2,1,0:T(1,128)S(1)}, s32[2,2,1,4096]{3,2,1,0:T(1,128)}, u32[]{:S(2)}) copy-start(s32[2,2,1,4096]{3,2,1,0:T(1,128)} %param.18) | copy-start | bytes 196612
  16.5 4.0 %copy-start.12 = (s32[2,2,1,3072]{3,2,1,0:T(1,128)S(1)}, s32[2,2,1,3072]{3,2,1,0:T(1,128)}, u32[]{:S(2)}) copy-start(s32[2,2,1,3072]{3,2,1,0:T(1,128)} %param.21) | copy-start | bytes 147460
  16.5 4.0 %copy-start.14 = (f32[2,2,64,128]{3,2,1,0:T(8,128)S(1)}, f32[2,2,64,128]{3,2,1,0:T(8,128)}, u32[]{:S(2)}) copy-start(f32[2,2,64,128]{3,2,1,0:T(8,128)} %get-tuple-element.25.fseen) | copy-start | bytes 393220
  25.7 9.2 %collective-permute-start.6 = (f32[3,24,128]{2,1,0:T(8,128)S(1)}, f32[3,24,128]{2,1,0:T(8,128)S(1)}, u32[]{:S(2)}, u32[]{:S(2)}) collective-permute-start(f32[3,24,128]{2,1,0:T(8,128)S(1)} %get-tuple-element.40), channel_id=1, source_target_pairs={{8,7},{9,6},{10,5},{11,4},{12,3},{13,2},{14,1},{15,0},{16,15},{17,... | collective-permute-start | bytes 110600 | tf_op jit(solution)/shard_map/ppermute | solution.py:559
  27.6 7.3 %collective-permute-start.4 = (f32[3,32,128]{2,1,0:T(8,128)S(1)}, f32[3,32,128]{2,1,0:T(8,128)S(1)}, u32[]{:S(2)}, u32[]{:S(2)}) collective-permute-start(f32[3,32,128]{2,1,0:T(8,128)S(1)} %get-tuple-element.36.fsent0), channel_id=1, source_target_pairs={{0,1},{1,0},{2,3},{3,2},{4,5},{5,4},{6,7},{7,6},{8,9},{9,8},{10,11... | collective-permute-start | bytes 147464 | tf_op jit(solution)/shard_map/ppermute | solution.py:502
  31.4 3.4 %collective-permute-start.5 = (f32[3,32,128]{2,1,0:T(8,128)S(1)}, f32[3,32,128]{2,1,0:T(8,128)S(1)}, u32[]{:S(2)}, u32[]{:S(2)}) collective-permute-start(f32[3,32,128]{2,1,0:T(8,128)S(1)} %get-tuple-element.37.fsent1), channel_id=1, source_target_pairs={{1,2},{2,1},{3,4},{4,3},{5,6},{6,5},{9,10},{10,9},{11,12},{12,11},... | collective-permute-start | bytes 147464 | tf_op jit(solution)/shard_map/ppermute | solution.py:502
  35.7 31.6 %all-to-all-start = ((f32[256,1,128]{2,1,0:T(1,128)}), f32[256,1,128]{2,1,0:T(1,128)S(1)}, u32[]{:S(2)}, u32[]{:S(2)}) async-start(f32[256,1,128]{2,1,0:T(1,128)} %bitcast.26), calls=%async_computation | async-start | bytes 262144 | tf_op jit(solution)/shard_map/all_to_all | solution.py:570
  54.3 10.2 %collective-permute-start.7 = (f32[3,24,128]{2,1,0:T(8,128)S(1)}, f32[3,24,128]{2,1,0:T(8,128)S(1)}, u32[]{:S(2)}, u32[]{:S(2)}) collective-permute-start(f32[3,24,128]{2,1,0:T(8,128)S(1)} %get-tuple-element.44.svalues), channel_id=1, source_target_pairs={{0,15},{1,14},{2,13},{3,12},{4,11},{5,10},{6,9},{7,8},{8,23},{9,22... | collective-permute-start | bytes 110600 | tf_op jit(solution)/shard_map/ppermute | solution.py:571
  (1 other events, 4.0 us)

commit v8 on v7

--- a/solution.py
+++ b/solution.py
@@ -16,7 +16,6 @@
 SYM = ((0, 0), (0, 1), (0, 2), (1, 1), (1, 2), (2, 2))
 DAMP = 1.0
 VMEM = pl.BlockSpec(memory_space=pltpu.VMEM)
-SMEM = pl.BlockSpec(memory_space=pltpu.SMEM)
 FAR = pl.BlockSpec(memory_space=pltpu.HBM)
 F32 = jnp.float32
 
@@ -243,7 +242,7 @@
 
 def place_of():
     seg, strip = lax.axis_index("seg"), lax.axis_index("strip")
-    return (seg & 1, jnp.minimum(seg, 1)), (strip & 1, jnp.minimum(strip, 1))
+    return (1 - (seg & 1), jnp.minimum(seg, 1)), (1 - (strip & 1), jnp.minimum(strip, 1))
 
 
 def in_rows(lines, table):
@@ -316,7 +315,8 @@
         in_rows(values, table)
     else:
         table = values
-    watched = cams.shape[0] // 16
+    watched, blocks = cams.shape[0] // 16, cam.shape[2] // LANES
+    lives = jnp.broadcast_to(live[...], (1, LANES))
 
     def block(i, stage):
         at = pl.ds(pl.multiple_of(i * LANES, LANES), LANES)
@@ -326,7 +326,7 @@
         seen = predict(across, fetch(table, index))
         summed = [jnp.sum(x, axis=0, keepdims=True) for x in project(along, seen) + normal(along)]
         z = solve(invert(summed[3:]), summed[:3])
-        share = (i < live[0, 0]).astype(F32)
+        share = jnp.where(lives > i, 1.0, 0.0)
         left = [share * e for e in residue(along, seen, z)]
         terms = [across[j] * left[0] + across[JAC + j] * left[1] for j in range(JAC)]
         seen = jnp.sum(seen[0] * left[0] + seen[1] * left[1], axis=0, keepdims=True)
@@ -341,7 +341,7 @@
         add_in([parts for _, parts in done], total)
         return carry
 
-    lax.fori_loop(0, (live[0, 0] + LOCAL_GROUP - 1) // LOCAL_GROUP, body, 0)
+    lax.fori_loop(0, blocks // LOCAL_GROUP, body, 0)
     fold(total, out)
 
 
@@ -448,7 +448,7 @@
 
 def call(kernel, ins, outs, scratch, flops, name, place=VMEM, to=VMEM, room=12):
     outs = [jax.ShapeDtypeStruct(shape, F32) for shape in outs]
-    specs = [SMEM if x.shape == (1, 1) else place for x in ins]
+    specs = [place] * len(ins)
     return pl.pallas_call(
         kernel,
         out_shape=outs,
@@ -482,12 +482,12 @@
                 found.append((s * segs + g, t * segs + h))
         return found
 
-    fwd_rounds = pairs(lambda s, g: (s, g ^ 1)), pairs(lambda s, g: (s, (g + 1 ^ 1) - 1))
+    fwd_rounds = pairs(lambda s, g: (s, (g + 1 ^ 1) - 1)), pairs(lambda s, g: (s, g ^ 1))
     side_down = pairs(lambda s, g: (s - 1, segs - 1 - g))
     side_up = pairs(lambda s, g: (s + 1, segs - 1 - g))
     side_rounds = (
+        pairs(lambda s, g: ((s + 1 ^ 1) - 1, segs - 1 - g)),
         pairs(lambda s, g: (s ^ 1, segs - 1 - g)),
-        pairs(lambda s, g: ((s + 1 ^ 1) - 1, segs - 1 - g)),
     )
     lcam, lpoint = loc_cam_jac[:, :, 0], loc_point_jac[:, :, 0]
     lcams = loc_cams.reshape(-1, LANES)

time: 68.8 us -> 68.1 us (0.990)
  starting transfers between devices: 44 us -> 41 us
  waiting for transfers between devices: 4.85 us -> 7.22 us
    all_to_all x1, starting transfers between devices: 18.6 us -> 11.5 us  [per_device(): line = lax.all_to_all(line, AXES, 0, 0, tiled=True)]
    ppermute x1, starting transfers between devices: 1.92 us -> 5.17 us  [per_device(): smet = lax.ppermute(sguest, AXES, side_down)]
    ppermute x6, waiting for transfers between devices: 1.33 us -> 4.5 us  [meet(): lax.ppermute(send, AXES, pairs)]
    ppermute x6, starting transfers between devices: 15.3 us -> 16.2 us  [meet(): lax.ppermute(send, AXES, pairs)]
    ppermute x1, waiting for transfers between devices: 0.79 us -> 0.01 us  [per_device(): smet = lax.ppermute(sguest, AXES, side_down)]
where the time goes in v8:
time: 68.1 us; the launch traced here: 67.8 us
  starting transfers between devices  41 us (60%)
  Pallas kernels  17.8 us (26%)
  waiting for transfers between devices  7.22 us (11%)
  between operations  1.63 us (2%)
    pallas_call x7, Pallas kernels, call(): pl.pallas_call(kernel, out_shape=outs, in_specs=specs, out_specs=[to] * l...  17.8 us
    ppermute x6, starting transfers between devices, meet(): lax.ppermute(send, AXES, pairs)  16.2 us
    all_to_all x1, starting transfers between devices, per_device(): line = lax.all_to_all(line, AXES, 0, 0, tiled=True)  11.5 us
    ppermute x1, starting transfers between devices, per_device(): ssent = lax.ppermute(sz, AXES, side_up)  8.16 us
    ppermute x1, starting transfers between devices, per_device(): smet = lax.ppermute(sguest, AXES, side_down)  5.17 us
    ppermute x6, waiting for transfers between devices, meet(): lax.ppermute(send, AXES, pairs)  4.5 us
    all_to_all x1, waiting for transfers between devices, per_device(): line = lax.all_to_all(line, AXES, 0, 0, tiled=True)  2.72 us
  transfers between devices with their start and end apart: 9, of which 3 were waited for; matrix products, arithmetic and copies ran while one was open for 0% of the time, Pallas kernels for 10%

profile of v8, /device:TPU:1, one launch (start us, length us, event | category | flops | bytes accessed | tf_op | source)
XLA Modules:
  0.0 67.8 jit_solution(8695756286730872195)
XLA Ops:
  0.7 4.2 %look.1 = (f32[2,2,64,128]{3,2,1,0:T(8,128)}, f32[9,32,128]{2,1,0:T(8,128)}, f32[9,32,128]{2,1,0:T(8,128)}, f32[2,2,48,128]{3,2,1,0:T(8,128)}, f32[9,24,128]{2,1,0:T(8,128)}, /*index=5*/f32[9,24,128]{2,1,0:T(8,128)}) custom-call(f32[9,1,512]{2,1,0:T(1,128)} %lines.3, bf16[2,18,64,128]{3,2,1,0:T(8,128)(2,1)} %bitcast.32, bf16[2,6,64,128]{3,2,1,0:T(8,128)(2,1)} %bitcast.41, ...), custom_call_target="tpu_custom_call" | custom-call | flops 1000000000 | bytes 2097152 | tf_op jit(solution)/shard_map/look/pallas_call | solution.py:452
  4.9 9.8 %collective-permute-start.2 = (f32[9,24,128]{2,1,0:T(8,128)}, f32[9,24,128]{2,1,0:T(8,128)S(1)}, u32[]{:S(2)}, u32[]{:S(2)}) collective-permute-start(f32[9,24,128]{2,1,0:T(8,128)} %get-tuple-element.29.ssent0), channel_id=1, source_target_pairs={{8,23},{9,22},{10,21},{11,20},{12,19},{13,18},{14,17},{15,16},{16,... | collective-permute-start | bytes 331784 | tf_op jit(solution)/shard_map/ppermute | solution.py:502
  14.7 0.1 collective-permute-start.3
  14.8 0.7 collective-permute-start
  15.5 2.5 %collective-permute-start.1 = (f32[9,32,128]{2,1,0:T(8,128)}, f32[9,32,128]{2,1,0:T(8,128)S(1)}, u32[]{:S(2)}, u32[]{:S(2)}) collective-permute-start(f32[9,32,128]{2,1,0:T(8,128)} %get-tuple-element.27.fsent1), channel_id=1, source_target_pairs={{0,1},{1,0},{2,3},{3,2},{4,5},{5,4},{6,7},{7,6},{8,9},{9,8},{10,11... | collective-permute-start | bytes 442376 | tf_op jit(solution)/shard_map/ppermute | solution.py:502
  18.6 0.0 copy-start.1
  18.6 0.0 copy-start.2
  18.7 0.0 copy-start.4
  18.7 0.0 copy-start.5
  18.7 0.0 copy-start.10
  18.8 2.4 %local.2 = (f32[36,128]{1,0:T(8,128)S(1)}, f32[8,128]{1,0:T(8,128)}) custom-call(s32[1,1]{1,0:T(1,128)S(6)} %copy.22.live, f32[9,1,512]{2,1,0:T(1,128)S(1)} %copy-done.13, bf16[18,6,2048]{2,1,0:T(8,128)(2,1)S(1)} %bitcast.30, bf16[6,6,2048]{2,1,0:T(8,128)(2,1)S(1)} %bitcast.39, s32[96,128]{1,0:T(8,128)S(1)} %bitcast.51), custom_call_target="tpu_custom_call" | custom-call | flops 5000000000 | bytes 2097152 | tf_op jit(solution)/shard_map/local/pallas_call | solution.py:452
  21.1 1.0 %collective-permute-done.3.smet1 = f32[9,24,128]{2,1,0:T(8,128)S(1)} collective-permute-done((f32[9,24,128]{2,1,0:T(8,128)}, f32[9,24,128]{2,1,0:T(8,128)S(1)}, u32[]{:S(2)}, u32[]{:S(2)}) %collective-permute-start.3) | collective-permute-done | bytes 110624 | tf_op jit(solution)/shard_map/ppermute | solution.py:502
  22.1 3.5 %collective-permute-done.1.fmet1 = f32[9,32,128]{2,1,0:T(8,128)S(1)} collective-permute-done((f32[9,32,128]{2,1,0:T(8,128)}, f32[9,32,128]{2,1,0:T(8,128)S(1)}, u32[]{:S(2)}, u32[]{:S(2)}) %collective-permute-start.1) | collective-permute-done | bytes 147488 | tf_op jit(solution)/shard_map/ppermute | solution.py:502
  25.7 5.1 %middle.1 = (f32[36,128]{1,0:T(8,128)S(1)}, f32[2,6,32,128]{3,2,1,0:T(8,128)S(1)}, f32[2,6,24,128]{3,2,1,0:T(8,128)S(1)}, f32[2,2,64,128]{3,2,1,0:T(8,128)S(1)},...) custom-call(f32[9,1,512]{2,1,0:T(1,128)S(1)} %copy-done.13, ...), custom_call_target="tpu_custom_call" | custom-call | flops 10000000000 | bytes 2097152 | tf_op jit(solution)/shard_map/middle/pallas_call | solution.py:452
  30.9 5.2 %collective-permute-start.6 = (f32[3,24,128]{2,1,0:T(8,128)S(1)}, f32[3,24,128]{2,1,0:T(8,128)S(1)}, u32[]{:S(2)}, u32[]{:S(2)}) collective-permute-start(f32[3,24,128]{2,1,0:T(8,128)S(1)} %get-tuple-element.40), channel_id=1, source_target_pairs={{8,7},{9,6},{10,5},{11,4},{12,3},{13,2},{14,1},{15,0},{16,15},{17,... | collective-permute-start | bytes 110600 | tf_op jit(solution)/shard_map/ppermute | solution.py:559
  36.0 0.7 collective-permute-start.4
  36.7 2.5 %collective-permute-start.5 = (f32[3,32,128]{2,1,0:T(8,128)S(1)}, f32[3,32,128]{2,1,0:T(8,128)S(1)}, u32[]{:S(2)}, u32[]{:S(2)}) collective-permute-start(f32[3,32,128]{2,1,0:T(8,128)S(1)} %get-tuple-element.37.fsent1), channel_id=1, source_target_pairs={{0,1},{1,0},{2,3},{3,2},{4,5},{5,4},{6,7},{7,6},{8,9},{9,8},{10,11... | collective-permute-start | bytes 147464 | tf_op jit(solution)/shard_map/ppermute | solution.py:502
  39.2 2.0 %local.3 = (f32[36,128]{1,0:T(8,128)S(1)}, f32[8,128]{1,0:T(8,128)S(1)}) custom-call(s32[1,1]{1,0:T(1,128)S(6)} %copy.22.live, f32[36,128]{1,0:T(8,128)S(1)} %get-tuple-element.31.values.first, bf16[18,6,2048]{2,1,0:T(8,128)(2,1)S(1)} %bitcast.31, bf16[6,6,2048]{2,1,0:T(8,128)(2,1)S(1)} %bitcast.40, s32[96,128]{1,0:T(8,128)S(1)} %bitcast.52), custom_call_target="tpu_custom_call" | custom-call | flops 5000000000 | bytes 2097152 | tf_op jit(solution)/shard_map/local/pallas_call | solution.py:452
  41.3 0.8 %dots.1 = (f32[2,3,64,128]{3,2,1,0:T(8,128)S(1)}, f32[3,24,128]{2,1,0:T(8,128)S(1)}, f32[256,128]{1,0:T(8,128)}) custom-call(f32[8,128]{1,0:T(8,128)S(1)} %get-tuple-element.34.dots, f32[8,128]{1,0:T(8,128)S(1)} %get-tuple-element.35.product, f32[3,32,128]{2,1,0:T(8,128)S(1)} %get-tuple-element.36.fsent0, f32[3,32,128]{2,1,0:T(8,128)S(1)} %get-tuple-element.37.fsent1, ...), custom_call_target="tpu_custom_call" | custom-call | flops 100000000 | bytes 2097152 | tf_op jit(solution)/shard_map/dots/pallas_call | solution.py:452
  42.1 11.5 %all-to-all-start = ((f32[256,1,128]{2,1,0:T(1,128)}), f32[256,1,128]{2,1,0:T(1,128)S(1)}, u32[]{:S(2)}, u32[]{:S(2)}) async-start(f32[256,1,128]{2,1,0:T(1,128)} %bitcast.26), calls=%async_computation | async-start | bytes 262144 | tf_op jit(solution)/shard_map/all_to_all | solution.py:570
  53.6 8.2 %collective-permute-start.7 = (f32[3,24,128]{2,1,0:T(8,128)S(1)}, f32[3,24,128]{2,1,0:T(8,128)S(1)}, u32[]{:S(2)}, u32[]{:S(2)}) collective-permute-start(f32[3,24,128]{2,1,0:T(8,128)S(1)} %get-tuple-element.44.svalues), channel_id=1, source_target_pairs={{0,15},{1,14},{2,13},{3,12},{4,11},{5,10},{6,9},{7,8},{8,23},{9,22... | collective-permute-start | bytes 110600 | tf_op jit(solution)/shard_map/ppermute | solution.py:571
  61.7 2.1 %last.1.extra = f32[36,128]{1,0:T(8,128)S(1)} custom-call(f32[36,128]{1,0:T(8,128)S(1)} %get-tuple-element.32.extra, bf16[2,18,64,128]{3,2,1,0:T(8,128)(2,1)S(1)} %bitcast.34, bf16[2,6,64,128]{3,2,1,0:T(8,128)(2,1)S(1)} %bitcast.43, s32[2,2,32,128]{3,2,1,0:T(8,128)S(1)} %bitcast.50, bf16[2,18,48,128]{3,2,1,0:T(8,128)(2,1)S(1)} %bitcast.37, ...), custom_call_target="tpu_custom_call" | custom-call | flops 5000000000 | bytes 2097152 | tf_op jit(solution)/shard_map/last/pallas_call | solution.py:452
  63.8 2.7 %all-to-all-done = f32[256,1,128]{2,1,0:T(1,128)S(1)} async-done(((f32[256,1,128]{2,1,0:T(1,128)}), f32[256,1,128]{2,1,0:T(1,128)S(1)}, u32[]{:S(2)}, u32[]{:S(2)}) %all-to-all-start) | async-done | bytes 131104 | tf_op jit(solution)/shard_map/all_to_all | solution.py:570
  66.6 1.3 %close.1 = (f32[9,1,512]{2,1,0:T(1,128)}, f32[9,1,512]{2,1,0:T(1,128)}) custom-call(f32[36,128]{1,0:T(8,128)S(1)} %last.1.extra, bf16[2,18,48,128]{3,2,1,0:T(8,128)(2,1)S(1)} %bitcast.38, bf16[2,6,48,128]{3,2,1,0:T(8,128)(2,1)S(1)} %bitcast.47, s32[2,2,24,128]{3,2,1,0:T(8,128)S(1)} %bitcast.56, f32[2,2,48,128]{3,2,1,0:T(8,128)S(1)} %get-tuple-element.43.sseen, ...), custom_call_target="tpu_custom_call" | custom-call | flops 2000000000 | bytes 2097152 | tf_op jit(solution)/shard_map/close/pallas_call | solution.py:452
  (33 shorter events, 0.1 us)
Async XLA Ops:
  0.6 18.0 %copy-start = (bf16[18,6,1,2048]{3,1,2,0:T(8,128)(2,1)S(1)}, bf16[18,6,1,2048]{3,1,2,0:T(8,128)(2,1)}, u32[]{:S(2)}) copy-start(bf16[18,6,1,2048]{3,1,2,0:T(8,128)(2,1)} %param.13) | copy-start | bytes 1327108
  0.6 18.0 %copy-start.3 = (bf16[6,6,1,2048]{3,1,2,0:T(8,128)(2,1)S(1)}, bf16[6,6,1,2048]{3,1,2,0:T(8,128)(2,1)}, u32[]{:S(2)}) copy-start(bf16[6,6,1,2048]{3,1,2,0:T(8,128)(2,1)} %param.14) | copy-start | bytes 442372
  0.7 18.0 %copy-start.11 = (s32[6,1,2048]{2,1,0:T(1,128)S(1)}, s32[6,1,2048]{2,1,0:T(1,128)}, u32[]{:S(2)}) copy-start(s32[6,1,2048]{2,1,0:T(1,128)} %param.15) | copy-start | bytes 147460
  0.7 18.0 %copy-start.13 = (f32[9,1,512]{2,1,0:T(1,128)S(1)}, f32[9,1,512]{2,1,0:T(1,128)}, u32[]{:S(2)}) copy-start(f32[9,1,512]{2,1,0:T(1,128)} %lines.3) | copy-start | bytes 55300
  4.9 16.3 %collective-permute-start.2 = (f32[9,24,128]{2,1,0:T(8,128)}, f32[9,24,128]{2,1,0:T(8,128)S(1)}, u32[]{:S(2)}, u32[]{:S(2)}) collective-permute-start(f32[9,24,128]{2,1,0:T(8,128)} %get-tuple-element.29.ssent0), channel_id=1, source_target_pairs={{8,23},{9,22},{10,21},{11,20},{12,19},{13,18},{14,17},{15,16},{16,... | collective-permute-start | bytes 331784 | tf_op jit(solution)/shard_map/ppermute | solution.py:502
  14.7 7.4 %collective-permute-start.3 = (f32[9,24,128]{2,1,0:T(8,128)}, f32[9,24,128]{2,1,0:T(8,128)S(1)}, u32[]{:S(2)}, u32[]{:S(2)}) collective-permute-start(f32[9,24,128]{2,1,0:T(8,128)} %get-tuple-element.30.ssent1), channel_id=1, source_target_pairs={{0,15},{1,14},{2,13},{3,12},{4,11},{5,10},{6,9},{7,8},{8,7},{9,6},... | collective-permute-start | bytes 331784 | tf_op jit(solution)/shard_map/ppermute | solution.py:502
  14.8 7.3 %collective-permute-start = (f32[9,32,128]{2,1,0:T(8,128)}, f32[9,32,128]{2,1,0:T(8,128)S(1)}, u32[]{:S(2)}, u32[]{:S(2)}) collective-permute-start(f32[9,32,128]{2,1,0:T(8,128)} %get-tuple-element.26.fsent0), channel_id=1, source_target_pairs={{1,2},{2,1},{3,4},{4,3},{5,6},{6,5},{9,10},{10,9},{11,12},{12,11},... | collective-permute-start | bytes 442376 | tf_op jit(solution)/shard_map/ppermute | solution.py:502
  15.5 10.1 %collective-permute-start.1 = (f32[9,32,128]{2,1,0:T(8,128)}, f32[9,32,128]{2,1,0:T(8,128)S(1)}, u32[]{:S(2)}, u32[]{:S(2)}) collective-permute-start(f32[9,32,128]{2,1,0:T(8,128)} %get-tuple-element.27.fsent1), channel_id=1, source_target_pairs={{0,1},{1,0},{2,3},{3,2},{4,5},{5,4},{6,7},{7,6},{8,9},{9,8},{10,11... | collective-permute-start | bytes 442376 | tf_op jit(solution)/shard_map/ppermute | solution.py:502
  18.6 7.0 %copy-start.1 = (bf16[2,18,2,1,4096]{4,2,3,1,0:T(2,128)(2,1)S(1)}, bf16[2,18,2,1,4096]{4,2,3,1,0:T(2,128)(2,1)}, u32[]{:S(2)}) copy-start(bf16[2,18,2,1,4096]{4,2,3,1,0:T(2,128)(2,1)} %param.16) | copy-start | bytes 1769476
  18.6 7.0 %copy-start.2 = (bf16[2,18,2,1,3072]{4,2,3,1,0:T(2,128)(2,1)S(1)}, bf16[2,18,2,1,3072]{4,2,3,1,0:T(2,128)(2,1)}, u32[]{:S(2)}) copy-start(bf16[2,18,2,1,3072]{4,2,3,1,0:T(2,128)(2,1)} %param.19) | copy-start | bytes 1327108
  18.7 7.0 %copy-start.4 = (bf16[2,6,2,1,4096]{4,2,3,1,0:T(2,128)(2,1)S(1)}, bf16[2,6,2,1,4096]{4,2,3,1,0:T(2,128)(2,1)}, u32[]{:S(2)}) copy-start(bf16[2,6,2,1,4096]{4,2,3,1,0:T(2,128)(2,1)} %param.17) | copy-start | bytes 589828
  18.7 7.0 %copy-start.5 = (bf16[2,6,2,1,3072]{4,2,3,1,0:T(2,128)(2,1)S(1)}, bf16[2,6,2,1,3072]{4,2,3,1,0:T(2,128)(2,1)}, u32[]{:S(2)}) copy-start(bf16[2,6,2,1,3072]{4,2,3,1,0:T(2,128)(2,1)} %param.20) | copy-start | bytes 442372
  18.7 7.0 %copy-start.6 = (f32[9,32,128]{2,1,0:T(8,128)S(1)}, f32[9,32,128]{2,1,0:T(8,128)}, u32[]{:S(2)}) copy-start(f32[9,32,128]{2,1,0:T(8,128)} %get-tuple-element.26.fsent0) | copy-start | bytes 442372
  18.7 7.0 %copy-start.7 = (f32[9,32,128]{2,1,0:T(8,128)S(1)}, f32[9,32,128]{2,1,0:T(8,128)}, u32[]{:S(2)}) copy-start(f32[9,32,128]{2,1,0:T(8,128)} %get-tuple-element.27.fsent1) | copy-start | bytes 442372
  18.7 7.0 %copy-start.8 = (f32[9,24,128]{2,1,0:T(8,128)S(1)}, f32[9,24,128]{2,1,0:T(8,128)}, u32[]{:S(2)}) copy-start(f32[9,24,128]{2,1,0:T(8,128)} %get-tuple-element.29.ssent0) | copy-start | bytes 331780
  18.7 7.0 %copy-start.9 = (f32[9,24,128]{2,1,0:T(8,128)S(1)}, f32[9,24,128]{2,1,0:T(8,128)}, u32[]{:S(2)}) copy-start(f32[9,24,128]{2,1,0:T(8,128)} %get-tuple-element.30.ssent1) | copy-start | bytes 331780
  18.7 7.0 %copy-start.10 = (s32[2,2,1,4096]{3,2,1,0:T(1,128)S(1)}, s32[2,2,1,4096]{3,2,1,0:T(1,128)}, u32[]{:S(2)}) copy-start(s32[2,2,1,4096]{3,2,1,0:T(1,128)} %param.18) | copy-start | bytes 196612
  18.7 7.0 %copy-start.12 = (s32[2,2,1,3072]{3,2,1,0:T(1,128)S(1)}, s32[2,2,1,3072]{3,2,1,0:T(1,128)}, u32[]{:S(2)}) copy-start(s32[2,2,1,3072]{3,2,1,0:T(1,128)} %param.21) | copy-start | bytes 147460
  18.7 7.0 %copy-start.14 = (f32[2,2,64,128]{3,2,1,0:T(8,128)S(1)}, f32[2,2,64,128]{3,2,1,0:T(8,128)}, u32[]{:S(2)}) copy-start(f32[2,2,64,128]{3,2,1,0:T(8,128)} %get-tuple-element.25.fseen) | copy-start | bytes 393220
  30.9 10.4 %collective-permute-start.6 = (f32[3,24,128]{2,1,0:T(8,128)S(1)}, f32[3,24,128]{2,1,0:T(8,128)S(1)}, u32[]{:S(2)}, u32[]{:S(2)}) collective-permute-start(f32[3,24,128]{2,1,0:T(8,128)S(1)} %get-tuple-element.40), channel_id=1, source_target_pairs={{8,7},{9,6},{10,5},{11,4},{12,3},{13,2},{14,1},{15,0},{16,15},{17,... | collective-permute-start | bytes 110600 | tf_op jit(solution)/shard_map/ppermute | solution.py:559
  36.0 5.2 %collective-permute-start.4 = (f32[3,32,128]{2,1,0:T(8,128)S(1)}, f32[3,32,128]{2,1,0:T(8,128)S(1)}, u32[]{:S(2)}, u32[]{:S(2)}) collective-permute-start(f32[3,32,128]{2,1,0:T(8,128)S(1)} %get-tuple-element.36.fsent0), channel_id=1, source_target_pairs={{1,2},{2,1},{3,4},{4,3},{5,6},{6,5},{9,10},{10,9},{11,12},{12,11},... | collective-permute-start | bytes 147464 | tf_op jit(solution)/shard_map/ppermute | solution.py:502
  36.7 4.6 %collective-permute-start.5 = (f32[3,32,128]{2,1,0:T(8,128)S(1)}, f32[3,32,128]{2,1,0:T(8,128)S(1)}, u32[]{:S(2)}, u32[]{:S(2)}) collective-permute-start(f32[3,32,128]{2,1,0:T(8,128)S(1)} %get-tuple-element.37.fsent1), channel_id=1, source_target_pairs={{0,1},{1,0},{2,3},{3,2},{4,5},{5,4},{6,7},{7,6},{8,9},{9,8},{10,11... | collective-permute-start | bytes 147464 | tf_op jit(solution)/shard_map/ppermute | solution.py:502
  42.1 24.5 %all-to-all-start = ((f32[256,1,128]{2,1,0:T(1,128)}), f32[256,1,128]{2,1,0:T(1,128)S(1)}, u32[]{:S(2)}, u32[]{:S(2)}) async-start(f32[256,1,128]{2,1,0:T(1,128)} %bitcast.26), calls=%async_computation | async-start | bytes 262144 | tf_op jit(solution)/shard_map/all_to_all | solution.py:570
  53.6 10.3 %collective-permute-start.7 = (f32[3,24,128]{2,1,0:T(8,128)S(1)}, f32[3,24,128]{2,1,0:T(8,128)S(1)}, u32[]{:S(2)}, u32[]{:S(2)}) collective-permute-start(f32[3,24,128]{2,1,0:T(8,128)S(1)} %get-tuple-element.44.svalues), channel_id=1, source_target_pairs={{0,15},{1,14},{2,13},{3,12},{4,11},{5,10},{6,9},{7,8},{8,23},{9,22... | collective-permute-start | bytes 110600 | tf_op jit(solution)/shard_map/ppermute | solution.py:571
  (1 other events, 7.0 us)

commit v9 on v8

--- a/solution.py
+++ b/solution.py
@@ -73,8 +73,23 @@
     return [seen[r] - sum(along[3 * r + k] * z[k] for k in range(3)) for r in range(2)]
 
 
-def spread(terms, index, stage, total):
-    add_in([stacked(terms, index, stage)], total)
+def mark(row):
+    wide = jnp.broadcast_to((row & (LANES - 1)).astype(F32), (16, LANES)).astype(jnp.bfloat16)
+    wide = jnp.concatenate([wide] * (LANES // 16), axis=0)
+    place = lax.broadcasted_iota(jnp.int32, (LANES, LANES), 0).astype(F32).astype(jnp.bfloat16)
+    return jnp.where(wide == place, jnp.ones((), jnp.bfloat16), jnp.zeros((), jnp.bfloat16))
+
+
+def marks_kernel(fcams, scams, fmarks, smarks):
+    for cams, marks in ((fcams, fmarks), (scams, smarks)):
+        for s in range(2):
+            for o in range(2):
+
+                def body(r, carry, cams=cams, marks=marks, s=s, o=o):
+                    marks[s, 2 * r + o] = mark(cams[s, o, pl.ds(r, 1), :])
+                    return carry
+
+                lax.fori_loop(0, cams.shape[2], body, 0, unroll=8)
 
 
 def add_in(parts, total):
@@ -86,7 +101,7 @@
     )
 
 
-def stacked(terms, index, stage):
+def stacked(terms, index, stage, marked=None):
     count = index.shape[0]
     page = index >> 7
     coarse = terms[JAC - 1].astype(jnp.bfloat16).astype(F32)
@@ -97,9 +112,7 @@
         stage[pl.ds(8 + h, count, stride=16), :] = jnp.where(page == h, coarse, 0.0)
         stage[pl.ds(12 + h, count, stride=16), :] = jnp.where(page == h, fine, 0.0)
     page = page.astype(F32)
-    lane = (index & (LANES - 1)).astype(F32)
-    place = lax.broadcasted_iota(jnp.int32, (LANES, LANES), 0).astype(F32).astype(jnp.bfloat16)
-    one, none = jnp.ones((), jnp.bfloat16), jnp.zeros((), jnp.bfloat16)
+    none = jnp.zeros((), jnp.bfloat16)
     left, right = [], []
     for row in range(count):
         raw = stage[pl.ds(16 * row, 8), :]
@@ -110,9 +123,7 @@
         tiles = [jnp.where(wide == h, both, none) for h in range(PAGES)]
         tiles.append(jnp.concatenate([rest, jnp.zeros_like(rest)], axis=0).astype(jnp.bfloat16))
         left.append(jnp.concatenate(tiles, axis=0))
-        wide = jnp.broadcast_to(lane[row : row + 1], (16, LANES)).astype(jnp.bfloat16)
-        wide = jnp.concatenate([wide] * (LANES // 16), axis=0)
-        right.append(jnp.where(wide == place, one, none))
+        right.append(mark(index[row : row + 1]) if marked is None else marked(row))
     return left, right
 
 
@@ -173,7 +184,9 @@
     return jnp.where(side == 0, 1, held).astype(F32)
 
 
-def pair_return(cam, point, index, seen_in, z, odd, held, stage, total, turns=(0, 1)):
+def pair_return(
+    cam, point, index, marks, seen_in, z, odd, held, stage, total, turns=(0, 1)
+):
     rows = cam.shape[2]
     for turn in turns:
         s = turn ^ odd
@@ -190,7 +203,11 @@
             )
             left = [share * e for e in left]
             terms = [across[j] * left[0] + across[JAC + j] * left[1] for j in range(JAC)]
-            spread(terms, index[s, at, :], stage, total)
+
+            def marked(row):
+                return marks[s, i * STEP + row]
+
+            add_in([stacked(terms, index[s, at, :], stage, marked)], total)
             return carry
 
         lax.fori_loop(0, rows // STEP, body, 0, unroll=True)
@@ -346,7 +363,7 @@
 
 
 def middle_kernel(
-    lines, extra, fcam, fpoint, fcams, scam, spoint, scams,
+    lines, extra, fcam, fpoint, fcams, scam, spoint, scams, fmarks, smarks,
     fseen, fsent0, fsent1, fmet0, fmet1, sseen, ssent0, ssent1, smet0, smet1,
     result, finverse, sinverse, fseen2, fsend0, fsend1, sseen2, sown, sguest, dots,
     table, findex, sindex, floose, sloose, fz, sz, stage, total, squares,
@@ -357,9 +374,9 @@
     weave(scams, sindex)
     total[...] = jnp.zeros_like(total)
     pair_solve((fsent0, fsent1), (fmet0, fmet1), finverse, fz)
-    pair_return(fcam, fpoint, findex, fseen, fz, fodd, fheld, stage, total)
+    pair_return(fcam, fpoint, findex, fmarks, fseen, fz, fodd, fheld, stage, total)
     pair_solve((ssent0, ssent1), (smet0, smet1), sinverse, sz)
-    pair_return(scam, spoint, sindex, sseen, sz, sodd, sheld, stage, total)
+    pair_return(scam, spoint, sindex, smarks, sseen, sz, sodd, sheld, stage, total)
     fold(total, result)
     step = result[...] + extra[...]
     result[...] = step
@@ -395,29 +412,29 @@
 
 
 def last_kernel(
-    extra, fcam, fpoint, fcams, scam, spoint, scams, fseen, fz, sseen, svalues,
+    extra, fcam, fpoint, fcams, scam, spoint, scams, fmarks, smarks, fseen, fz, sseen, svalues,
     result, findex, sindex, sz, stage, total,
 ):
     (fodd, fheld), (_, sheld) = place_of()
     weave(fcams, findex)
     weave(scams, sindex)
     total[...] = jnp.zeros_like(total)
-    pair_return(fcam, fpoint, findex, fseen, fz, fodd, fheld, stage, total)
+    pair_return(fcam, fpoint, findex, fmarks, fseen, fz, fodd, fheld, stage, total)
     widened(svalues, sz, 0)
-    pair_return(scam, spoint, sindex, sseen, sz, 0, sheld, stage, total, (0,))
+    pair_return(scam, spoint, sindex, smarks, sseen, sz, 0, sheld, stage, total, (0,))
     fold(total, result)
     result[...] += extra[...]
 
 
 def close_kernel(
-    extra, scam, spoint, scams, sseen, svalues, sums, lines, first,
+    extra, scam, spoint, scams, smarks, sseen, svalues, sums, lines, first,
     step_out, residual_out, base, second, sindex, sz, stage, total,
 ):
     _, (_, sheld) = place_of()
     weave(scams, sindex)
     total[...] = jnp.zeros_like(total)
     widened(svalues, sz, 1)
-    pair_return(scam, spoint, sindex, sseen, sz, 0, sheld, stage, total, (1,))
+    pair_return(scam, spoint, sindex, smarks, sseen, sz, 0, sheld, stage, total, (1,))
     fold(total, second)
     second[...] += extra[...]
     in_rows(lines, base)
@@ -446,8 +463,8 @@
             residual_out[j, :, pl.ds(LANES * k, LANES)] = residual[row : row + 1, :]
 
 
-def call(kernel, ins, outs, scratch, flops, name, place=VMEM, to=VMEM, room=12):
-    outs = [jax.ShapeDtypeStruct(shape, F32) for shape in outs]
+def call(kernel, ins, outs, scratch, flops, name, place=VMEM, to=VMEM, room=12, kind=F32):
+    outs = [jax.ShapeDtypeStruct(shape, kind) for shape in outs]
     specs = [place] * len(ins)
     return pl.pallas_call(
         kernel,
@@ -543,10 +560,19 @@
         )
 
     extra, _ = local(gradient)
+    fmarks, smarks = call(
+        marks_kernel,
+        [fcams, scams],
+        [(2, fr, LANES, LANES), (2, sr, LANES, LANES)],
+        [],
+        10**9,
+        "marks",
+        kind=jnp.bfloat16,
+    )
     fshapes, sshapes = sends_of(3)
     p, finverse, sinverse, fseen, fsend0, fsend1, sseen, sown, sguest, dots = call(
         middle_kernel,
-        [gradient, extra, fcam, fpoint, fcams, scam, spoint, scams,
+        [gradient, extra, fcam, fpoint, fcams, scam, spoint, scams, fmarks, smarks,
          fseen, *fsent, *fmet, sseen, *ssent, *smet],
         [(ROWS, LANES), (2, 6, fr // 2, LANES), (2, 6, sr // 2, LANES), (2, 2, fr, LANES)]
         + fshapes + [(2, 2, sr, LANES)] + sshapes + [(8, LANES)],
@@ -571,7 +597,7 @@
     ssent = lax.ppermute(sz, AXES, side_up)
     (t,) = call(
         last_kernel,
-        [extra, fcam, fpoint, fcams, scam, spoint, scams, fseen, fz, sseen, sz],
+        [extra, fcam, fpoint, fcams, scam, spoint, scams, fmarks, smarks, fseen, fz, sseen, sz],
         [(ROWS, LANES)],
         index_scratch + z_scratch[1:] + total_scratch,
         5 * 10**9,
@@ -579,7 +605,7 @@
     )
     step, residual = call(
         close_kernel,
-        [t, scam, spoint, scams, sseen, ssent, line, gradient, p],
+        [t, scam, spoint, scams, smarks, sseen, ssent, line, gradient, p],
         [gradient.shape] * 2,
         table * 2 + index_scratch[1:] + z_scratch[1:] + total_scratch,
         2 * 10**9,

time: 68.1 us -> 74.3 us (1.091)
  local copies, waits for them, and re-layouts: 0.08 us -> 9.54 us
  waiting for transfers between devices: 7.22 us -> 0.02 us
  starting transfers between devices: 41 us -> 42.9 us
  Pallas kernels: 17.8 us -> 19.6 us
    unnamed x32 -> x50, local copies, waits for them, and re-layouts: 0.08 us -> 9.54 us
    ppermute x6, waiting for transfers between devices: 4.5 us -> 0.02 us  [meet(): lax.ppermute(send, AXES, pairs)]
    all_to_all x1, waiting for transfers between devices: 2.72 us -> 0.01 us  [per_device(): line = lax.all_to_all(line, AXES, 0, 0, tiled=True)]
    pallas_call x7 -> x8, Pallas kernels: 17.8 us -> 19.6 us  [call(): pl.pallas_call(kernel, out_shape=outs, in_specs=specs, out_specs=[to] * l...]
    all_to_all x1, starting transfers between devices: 11.5 us -> 13.2 us  [per_device(): line = lax.all_to_all(line, AXES, 0, 0, tiled=True)]
  transfers between devices with their start and end apart: 9 -> 9, of which waited for: 3 -> 0; matrix products, arithmetic and copies ran while one was open for 0% -> 0% of each run, Pallas kernels for 10% -> 11%
where the time goes in v9:
time: 74.3 us; the launch traced here: 73.8 us
  starting transfers between devices  42.9 us (58%)
  Pallas kernels  19.6 us (26%)
  local copies, waits for them, and re-layouts  9.54 us (13%)
  between operations  1.68 us (2%)
    pallas_call x8, Pallas kernels, call(): pl.pallas_call(kernel, out_shape=outs, in_specs=specs, out_specs=[to] * l...  19.6 us
    ppermute x6, starting transfers between devices, meet(): lax.ppermute(send, AXES, pairs)  15.9 us
    all_to_all x1, starting transfers between devices, per_device(): line = lax.all_to_all(line, AXES, 0, 0, tiled=True)  13.2 us
    unnamed x50, local copies, waits for them, and re-layouts  9.54 us
    ppermute x1, starting transfers between devices, per_device(): ssent = lax.ppermute(sz, AXES, side_up)  8.16 us
    ppermute x1, starting transfers between devices, per_device(): smet = lax.ppermute(sguest, AXES, side_down)  5.71 us
  transfers between devices with their start and end apart: 9, of which 0 were waited for; matrix products, arithmetic and copies ran while one was open for 0% of the time, Pallas kernels for 11%

profile of v9, /device:TPU:1, one launch (start us, length us, event | category | flops | bytes accessed | tf_op | source)
XLA Modules:
  0.0 73.8 jit_solution(7173175375575367403)
XLA Ops:
  0.6 4.1 %look.1 = (f32[2,2,64,128]{3,2,1,0:T(8,128)}, f32[9,32,128]{2,1,0:T(8,128)}, f32[9,32,128]{2,1,0:T(8,128)}, f32[2,2,48,128]{3,2,1,0:T(8,128)}, f32[9,24,128]{2,1,0:T(8,128)}, /*index=5*/f32[9,24,128]{2,1,0:T(8,128)}) custom-call(f32[9,1,512]{2,1,0:T(1,128)} %lines.3, bf16[2,18,64,128]{3,2,1,0:T(8,128)(2,1)} %bitcast.32, bf16[2,6,64,128]{3,2,1,0:T(8,128)(2,1)} %bitcast.41, ...), custom_call_target="tpu_custom_call" | custom-call | flops 1000000000 | bytes 2097152 | tf_op jit(solution)/shard_map/look/pallas_call | solution.py:469
  4.8 9.8 %collective-permute-start.2 = (f32[9,24,128]{2,1,0:T(8,128)}, f32[9,24,128]{2,1,0:T(8,128)S(1)}, u32[]{:S(2)}, u32[]{:S(2)}) collective-permute-start(f32[9,24,128]{2,1,0:T(8,128)} %get-tuple-element.33.ssent0), channel_id=1, source_target_pairs={{8,23},{9,22},{10,21},{11,20},{12,19},{13,18},{14,17},{15,16},{16,... | collective-permute-start | bytes 331784 | tf_op jit(solution)/shard_map/ppermute | solution.py:519
  14.6 0.1 collective-permute-start.3
  14.7 0.7 collective-permute-start
  15.4 2.5 %collective-permute-start.1 = (f32[9,32,128]{2,1,0:T(8,128)}, f32[9,32,128]{2,1,0:T(8,128)S(1)}, u32[]{:S(2)}, u32[]{:S(2)}) collective-permute-start(f32[9,32,128]{2,1,0:T(8,128)} %get-tuple-element.31.fsent1), channel_id=1, source_target_pairs={{0,1},{1,0},{2,3},{3,2},{4,5},{5,4},{6,7},{7,6},{8,9},{9,8},{10,11... | collective-permute-start | bytes 442376 | tf_op jit(solution)/shard_map/ppermute | solution.py:519
  18.5 1.1 %copy-done = bf16[18,6,1,2048]{3,1,2,0:T(8,128)(2,1)S(1)} copy-done((bf16[18,6,1,2048]{3,1,2,0:T(8,128)(2,1)S(1)}, bf16[18,6,1,2048]{3,1,2,0:T(8,128)(2,1)}, u32[]{:S(2)}) %copy-start) | copy-done | bytes 442392
  19.6 0.9 %copy-done.4 = bf16[6,6,1,2048]{3,1,2,0:T(8,128)(2,1)S(1)} copy-done((bf16[6,6,1,2048]{3,1,2,0:T(8,128)(2,1)S(1)}, bf16[6,6,1,2048]{3,1,2,0:T(8,128)(2,1)}, u32[]{:S(2)}) %copy-start.4) | copy-done | bytes 147480
  20.5 0.8 %copy-done.13 = s32[6,1,2048]{2,1,0:T(1,128)S(1)} copy-done((s32[6,1,2048]{2,1,0:T(1,128)S(1)}, s32[6,1,2048]{2,1,0:T(1,128)}, u32[]{:S(2)}) %copy-start.13) | copy-done | bytes 49176
  21.3 0.7 copy-done.16
  22.1 2.4 %local.2 = (f32[36,128]{1,0:T(8,128)S(1)}, f32[8,128]{1,0:T(8,128)}) custom-call(s32[1,1]{1,0:T(1,128)S(6)} %copy.22.live, f32[9,1,512]{2,1,0:T(1,128)S(1)} %copy-done.16, bf16[18,6,2048]{2,1,0:T(8,128)(2,1)S(1)} %bitcast.30, bf16[6,6,2048]{2,1,0:T(8,128)(2,1)S(1)} %bitcast.39, s32[96,128]{1,0:T(8,128)S(1)} %bitcast.52), custom_call_target="tpu_custom_call" | custom-call | flops 5000000000 | bytes 2097152 | tf_op jit(solution)/shard_map/local/pallas_call | solution.py:469
  24.5 1.3 %marks.1 = (bf16[2,64,128,128]{3,2,1,0:T(8,128)(2,1)S(1)}, bf16[2,48,128,128]{3,2,1,0:T(8,128)(2,1)S(1)}) custom-call(s32[2,2,32,128]{3,2,1,0:T(8,128)S(1)} %bitcast.49, s32[2,2,24,128]{3,2,1,0:T(8,128)S(1)} %bitcast.55), custom_call_target="tpu_custom_call" | custom-call | flops 1000000000 | bytes 2097152 | tf_op jit(solution)/shard_map/marks/pallas_call | solution.py:469
  26.0 5.3 %middle.1 = (f32[36,128]{1,0:T(8,128)S(1)}, f32[2,6,32,128]{3,2,1,0:T(8,128)S(1)}, f32[2,6,24,128]{3,2,1,0:T(8,128)S(1)}, f32[2,2,64,128]{3,2,1,0:T(8,128)S(1)},...) custom-call(f32[9,1,512]{2,1,0:T(1,128)S(1)} %copy-done.16, ...), custom_call_target="tpu_custom_call" | custom-call | flops 10000000000 | bytes 2097152 | tf_op jit(solution)/shard_map/middle/pallas_call | solution.py:469
  31.3 5.7 %collective-permute-start.6 = (f32[3,24,128]{2,1,0:T(8,128)S(1)}, f32[3,24,128]{2,1,0:T(8,128)S(1)}, u32[]{:S(2)}, u32[]{:S(2)}) collective-permute-start(f32[3,24,128]{2,1,0:T(8,128)S(1)} %get-tuple-element.44), channel_id=1, source_target_pairs={{8,7},{9,6},{10,5},{11,4},{12,3},{13,2},{14,1},{15,0},{16,15},{17,... | collective-permute-start | bytes 110600 | tf_op jit(solution)/shard_map/ppermute | solution.py:585
  37.0 0.7 collective-permute-start.4
  37.7 2.2 %collective-permute-start.5 = (f32[3,32,128]{2,1,0:T(8,128)S(1)}, f32[3,32,128]{2,1,0:T(8,128)S(1)}, u32[]{:S(2)}, u32[]{:S(2)}) collective-permute-start(f32[3,32,128]{2,1,0:T(8,128)S(1)} %get-tuple-element.41.fsent1), channel_id=1, source_target_pairs={{0,1},{1,0},{2,3},{3,2},{4,5},{5,4},{6,7},{7,6},{8,9},{9,8},{10,11... | collective-permute-start | bytes 147464 | tf_op jit(solution)/shard_map/ppermute | solution.py:519
  39.9 2.0 %local.3 = (f32[36,128]{1,0:T(8,128)S(1)}, f32[8,128]{1,0:T(8,128)S(1)}) custom-call(s32[1,1]{1,0:T(1,128)S(6)} %copy.22.live, f32[36,128]{1,0:T(8,128)S(1)} %get-tuple-element.35.values.first, bf16[18,6,2048]{2,1,0:T(8,128)(2,1)S(1)} %bitcast.31, bf16[6,6,2048]{2,1,0:T(8,128)(2,1)S(1)} %bitcast.40, s32[96,128]{1,0:T(8,128)S(1)} %bitcast.53), custom_call_target="tpu_custom_call" | custom-call | flops 5000000000 | bytes 2097152 | tf_op jit(solution)/shard_map/local/pallas_call | solution.py:469
  42.0 0.8 %dots.1 = (f32[2,3,64,128]{3,2,1,0:T(8,128)S(1)}, f32[3,24,128]{2,1,0:T(8,128)S(1)}, f32[256,128]{1,0:T(8,128)}) custom-call(f32[8,128]{1,0:T(8,128)S(1)} %get-tuple-element.38.dots, f32[8,128]{1,0:T(8,128)S(1)} %get-tuple-element.39.product, f32[3,32,128]{2,1,0:T(8,128)S(1)} %get-tuple-element.40.fsent0, f32[3,32,128]{2,1,0:T(8,128)S(1)} %get-tuple-element.41.fsent1, ...), custom_call_target="tpu_custom_call" | custom-call | flops 100000000 | bytes 2097152 | tf_op jit(solution)/shard_map/dots/pallas_call | solution.py:469
  42.8 13.2 %all-to-all-start = ((f32[256,1,128]{2,1,0:T(1,128)}), f32[256,1,128]{2,1,0:T(1,128)S(1)}, u32[]{:S(2)}, u32[]{:S(2)}) async-start(f32[256,1,128]{2,1,0:T(1,128)} %bitcast.26), calls=%async_computation | async-start | bytes 262144 | tf_op jit(solution)/shard_map/all_to_all | solution.py:596
  56.0 8.2 %collective-permute-start.7 = (f32[3,24,128]{2,1,0:T(8,128)S(1)}, f32[3,24,128]{2,1,0:T(8,128)S(1)}, u32[]{:S(2)}, u32[]{:S(2)}) collective-permute-start(f32[3,24,128]{2,1,0:T(8,128)S(1)} %get-tuple-element.48.svalues), channel_id=1, source_target_pairs={{0,15},{1,14},{2,13},{3,12},{4,11},{5,10},{6,9},{7,8},{8,23},{9,22... | collective-permute-start | bytes 110600 | tf_op jit(solution)/shard_map/ppermute | solution.py:597
  64.1 2.2 %copy-done.19 = bf16[2,64,128,128]{3,2,1,0:T(8,128)(2,1)S(1)} copy-done((bf16[2,64,128,128]{3,2,1,0:T(8,128)(2,1)S(1)}, bf16[2,64,128,128]{3,2,1,0:T(8,128)(2,1)}, u32[]{:S(2)}) %copy-start.19) | copy-done | bytes 4194328
  66.3 1.9 %copy-done.21 = bf16[2,48,128,128]{3,2,1,0:T(8,128)(2,1)S(1)} copy-done((bf16[2,48,128,128]{3,2,1,0:T(8,128)(2,1)S(1)}, bf16[2,48,128,128]{3,2,1,0:T(8,128)(2,1)}, u32[]{:S(2)}) %copy-start.21) | copy-done | bytes 3145752
  68.2 2.4 %last.1.extra = f32[36,128]{1,0:T(8,128)S(1)} custom-call(f32[36,128]{1,0:T(8,128)S(1)} %get-tuple-element.36.extra, bf16[2,18,64,128]{3,2,1,0:T(8,128)(2,1)S(1)} %bitcast.34, bf16[2,6,64,128]{3,2,1,0:T(8,128)(2,1)S(1)} %bitcast.43, s32[2,2,32,128]{3,2,1,0:T(8,128)S(1)} %bitcast.51, bf16[2,18,48,128]{3,2,1,0:T(8,128)(2,1)S(1)} %bitcast.37, ...), custom_call_target="tpu_custom_call" | custom-call | flops 5000000000 | bytes 2097152 | tf_op jit(solution)/shard_map/last/pallas_call | solution.py:469
  70.6 1.9 %copy-done.22 = bf16[2,48,128,128]{3,2,1,0:T(8,128)(2,1)S(1)} copy-done((bf16[2,48,128,128]{3,2,1,0:T(8,128)(2,1)S(1)}, bf16[2,48,128,128]{3,2,1,0:T(8,128)(2,1)}, u32[]{:S(2)}) %copy-start.22) | copy-done | bytes 3145752
  72.5 1.2 %close.1 = (f32[9,1,512]{2,1,0:T(1,128)}, f32[9,1,512]{2,1,0:T(1,128)}) custom-call(f32[36,128]{1,0:T(8,128)S(1)} %last.1.extra, bf16[2,18,48,128]{3,2,1,0:T(8,128)(2,1)S(1)} %bitcast.38, bf16[2,6,48,128]{3,2,1,0:T(8,128)(2,1)S(1)} %bitcast.47, s32[2,2,24,128]{3,2,1,0:T(8,128)S(1)} %bitcast.58, bf16[2,48,128,128]{3,2,1,0:T(8,128)(2,1)S(1)} %copy-done.22, ...), custom_call_target="tpu_custom_call" | custom-call | flops 2000000000 | bytes 2097152 | tf_op jit(solution)/shard_map/close/pallas_call | solution.py:469
  (52 shorter events, 0.1 us)
Async XLA Ops:
  4.8 21.0 %collective-permute-start.2 = (f32[9,24,128]{2,1,0:T(8,128)}, f32[9,24,128]{2,1,0:T(8,128)S(1)}, u32[]{:S(2)}, u32[]{:S(2)}) collective-permute-start(f32[9,24,128]{2,1,0:T(8,128)} %get-tuple-element.33.ssent0), channel_id=1, source_target_pairs={{8,23},{9,22},{10,21},{11,20},{12,19},{13,18},{14,17},{15,16},{16,... | collective-permute-start | bytes 331784 | tf_op jit(solution)/shard_map/ppermute | solution.py:519
  14.6 11.2 %collective-permute-start.3 = (f32[9,24,128]{2,1,0:T(8,128)}, f32[9,24,128]{2,1,0:T(8,128)S(1)}, u32[]{:S(2)}, u32[]{:S(2)}) collective-permute-start(f32[9,24,128]{2,1,0:T(8,128)} %get-tuple-element.34.ssent1), channel_id=1, source_target_pairs={{0,15},{1,14},{2,13},{3,12},{4,11},{5,10},{6,9},{7,8},{8,7},{9,6},... | collective-permute-start | bytes 331784 | tf_op jit(solution)/shard_map/ppermute | solution.py:519
  14.7 11.1 %collective-permute-start = (f32[9,32,128]{2,1,0:T(8,128)}, f32[9,32,128]{2,1,0:T(8,128)S(1)}, u32[]{:S(2)}, u32[]{:S(2)}) collective-permute-start(f32[9,32,128]{2,1,0:T(8,128)} %get-tuple-element.30.fsent0), channel_id=1, source_target_pairs={{1,2},{2,1},{3,4},{4,3},{5,6},{6,5},{9,10},{10,9},{11,12},{12,11},... | collective-permute-start | bytes 442376 | tf_op jit(solution)/shard_map/ppermute | solution.py:519
  15.4 10.4 %collective-permute-start.1 = (f32[9,32,128]{2,1,0:T(8,128)}, f32[9,32,128]{2,1,0:T(8,128)S(1)}, u32[]{:S(2)}, u32[]{:S(2)}) collective-permute-start(f32[9,32,128]{2,1,0:T(8,128)} %get-tuple-element.31.fsent1), channel_id=1, source_target_pairs={{0,1},{1,0},{2,3},{3,2},{4,5},{5,4},{6,7},{7,6},{8,9},{9,8},{10,11... | collective-permute-start | bytes 442376 | tf_op jit(solution)/shard_map/ppermute | solution.py:519
  22.0 3.8 %copy-start.2 = (bf16[2,18,2,1,4096]{4,2,3,1,0:T(2,128)(2,1)S(1)}, bf16[2,18,2,1,4096]{4,2,3,1,0:T(2,128)(2,1)}, u32[]{:S(2)}) copy-start(bf16[2,18,2,1,4096]{4,2,3,1,0:T(2,128)(2,1)} %param.16) | copy-start | bytes 1769476
  22.0 3.8 %copy-start.3 = (bf16[2,18,2,1,3072]{4,2,3,1,0:T(2,128)(2,1)S(1)}, bf16[2,18,2,1,3072]{4,2,3,1,0:T(2,128)(2,1)}, u32[]{:S(2)}) copy-start(bf16[2,18,2,1,3072]{4,2,3,1,0:T(2,128)(2,1)} %param.19) | copy-start | bytes 1327108
  22.0 3.8 %copy-start.6 = (bf16[2,6,2,1,4096]{4,2,3,1,0:T(2,128)(2,1)S(1)}, bf16[2,6,2,1,4096]{4,2,3,1,0:T(2,128)(2,1)}, u32[]{:S(2)}) copy-start(bf16[2,6,2,1,4096]{4,2,3,1,0:T(2,128)(2,1)} %param.17) | copy-start | bytes 589828
  22.1 3.8 %copy-start.7 = (bf16[2,6,2,1,3072]{4,2,3,1,0:T(2,128)(2,1)S(1)}, bf16[2,6,2,1,3072]{4,2,3,1,0:T(2,128)(2,1)}, u32[]{:S(2)}) copy-start(bf16[2,6,2,1,3072]{4,2,3,1,0:T(2,128)(2,1)} %param.20) | copy-start | bytes 442372
  22.1 3.8 %copy-start.8 = (f32[9,32,128]{2,1,0:T(8,128)S(1)}, f32[9,32,128]{2,1,0:T(8,128)}, u32[]{:S(2)}) copy-start(f32[9,32,128]{2,1,0:T(8,128)} %get-tuple-element.30.fsent0) | copy-start | bytes 442372
  22.1 3.8 %copy-start.9 = (f32[9,32,128]{2,1,0:T(8,128)S(1)}, f32[9,32,128]{2,1,0:T(8,128)}, u32[]{:S(2)}) copy-start(f32[9,32,128]{2,1,0:T(8,128)} %get-tuple-element.31.fsent1) | copy-start | bytes 442372
  22.1 3.8 %copy-start.10 = (f32[9,24,128]{2,1,0:T(8,128)S(1)}, f32[9,24,128]{2,1,0:T(8,128)}, u32[]{:S(2)}) copy-start(f32[9,24,128]{2,1,0:T(8,128)} %get-tuple-element.33.ssent0) | copy-start | bytes 331780
  22.1 3.8 %copy-start.11 = (f32[9,24,128]{2,1,0:T(8,128)S(1)}, f32[9,24,128]{2,1,0:T(8,128)}, u32[]{:S(2)}) copy-start(f32[9,24,128]{2,1,0:T(8,128)} %get-tuple-element.34.ssent1) | copy-start | bytes 331780
  22.1 3.8 %copy-start.23 = (f32[2,2,64,128]{3,2,1,0:T(8,128)S(1)}, f32[2,2,64,128]{3,2,1,0:T(8,128)}, u32[]{:S(2)}) copy-start(f32[2,2,64,128]{3,2,1,0:T(8,128)} %get-tuple-element.29.fseen) | copy-start | bytes 393220
  22.1 3.8 %copy-start.24 = (f32[2,2,48,128]{3,2,1,0:T(8,128)S(1)}, f32[2,2,48,128]{3,2,1,0:T(8,128)}, u32[]{:S(2)}) copy-start(f32[2,2,48,128]{3,2,1,0:T(8,128)} %get-tuple-element.32.sseen) | copy-start | bytes 294916
  25.8 5.6 %copy-start.18 = (bf16[2,64,128,128]{3,2,1,0:T(8,128)(2,1)}, bf16[2,64,128,128]{3,2,1,0:T(8,128)(2,1)S(1)}, u32[]{:S(2)}) copy-start(bf16[2,64,128,128]{3,2,1,0:T(8,128)(2,1)S(1)} %get-tuple-element.27.fmarks) | copy-start | bytes 12582916
  25.8 5.6 %copy-start.20 = (bf16[2,48,128,128]{3,2,1,0:T(8,128)(2,1)}, bf16[2,48,128,128]{3,2,1,0:T(8,128)(2,1)S(1)}, u32[]{:S(2)}) copy-start(bf16[2,48,128,128]{3,2,1,0:T(8,128)(2,1)S(1)} %get-tuple-element.28.smarks) | copy-start | bytes 9437188
  25.9 14.0 %copy-start.1 = (bf16[18,6,1,2048]{3,1,2,0:T(8,128)(2,1)S(1)}, bf16[18,6,1,2048]{3,1,2,0:T(8,128)(2,1)}, u32[]{:S(2)}) copy-start(bf16[18,6,1,2048]{3,1,2,0:T(8,128)(2,1)} %param.13) | copy-start | bytes 1327108
  25.9 14.0 %copy-start.5 = (bf16[6,6,1,2048]{3,1,2,0:T(8,128)(2,1)S(1)}, bf16[6,6,1,2048]{3,1,2,0:T(8,128)(2,1)}, u32[]{:S(2)}) copy-start(bf16[6,6,1,2048]{3,1,2,0:T(8,128)(2,1)} %param.14) | copy-start | bytes 442372
  25.9 13.9 %copy-start.14 = (s32[6,1,2048]{2,1,0:T(1,128)S(1)}, s32[6,1,2048]{2,1,0:T(1,128)}, u32[]{:S(2)}) copy-start(s32[6,1,2048]{2,1,0:T(1,128)} %param.15) | copy-start | bytes 147460
  31.3 10.6 %collective-permute-start.6 = (f32[3,24,128]{2,1,0:T(8,128)S(1)}, f32[3,24,128]{2,1,0:T(8,128)S(1)}, u32[]{:S(2)}, u32[]{:S(2)}) collective-permute-start(f32[3,24,128]{2,1,0:T(8,128)S(1)} %get-tuple-element.44), channel_id=1, source_target_pairs={{8,7},{9,6},{10,5},{11,4},{12,3},{13,2},{14,1},{15,0},{16,15},{17,... | collective-permute-start | bytes 110600 | tf_op jit(solution)/shard_map/ppermute | solution.py:585
  37.0 4.9 %collective-permute-start.4 = (f32[3,32,128]{2,1,0:T(8,128)S(1)}, f32[3,32,128]{2,1,0:T(8,128)S(1)}, u32[]{:S(2)}, u32[]{:S(2)}) collective-permute-start(f32[3,32,128]{2,1,0:T(8,128)S(1)} %get-tuple-element.40.fsent0), channel_id=1, source_target_pairs={{1,2},{2,1},{3,4},{4,3},{5,6},{6,5},{9,10},{10,9},{11,12},{12,11},... | collective-permute-start | bytes 147464 | tf_op jit(solution)/shard_map/ppermute | solution.py:519
  37.7 4.2 %collective-permute-start.5 = (f32[3,32,128]{2,1,0:T(8,128)S(1)}, f32[3,32,128]{2,1,0:T(8,128)S(1)}, u32[]{:S(2)}, u32[]{:S(2)}) collective-permute-start(f32[3,32,128]{2,1,0:T(8,128)S(1)} %get-tuple-element.41.fsent1), channel_id=1, source_target_pairs={{0,1},{1,0},{2,3},{3,2},{4,5},{5,4},{6,7},{7,6},{8,9},{9,8},{10,11... | collective-permute-start | bytes 147464 | tf_op jit(solution)/shard_map/ppermute | solution.py:519
  42.8 27.8 %all-to-all-start = ((f32[256,1,128]{2,1,0:T(1,128)}), f32[256,1,128]{2,1,0:T(1,128)S(1)}, u32[]{:S(2)}, u32[]{:S(2)}) async-start(f32[256,1,128]{2,1,0:T(1,128)} %bitcast.26), calls=%async_computation | async-start | bytes 262144 | tf_op jit(solution)/shard_map/all_to_all | solution.py:596
  56.0 14.6 %collective-permute-start.7 = (f32[3,24,128]{2,1,0:T(8,128)S(1)}, f32[3,24,128]{2,1,0:T(8,128)S(1)}, u32[]{:S(2)}, u32[]{:S(2)}) collective-permute-start(f32[3,24,128]{2,1,0:T(8,128)S(1)} %get-tuple-element.48.svalues), channel_id=1, source_target_pairs={{0,15},{1,14},{2,13},{3,12},{4,11},{5,10},{6,9},{7,8},{8,23},{9,22... | collective-permute-start | bytes 110600 | tf_op jit(solution)/shard_map/ppermute | solution.py:597
  (10 other events, 16.8 us)

commit v10 on v8

--- a/solution.py
+++ b/solution.py
@@ -251,30 +251,21 @@
             table[pl.ds(PAGES * j + k, 1), :] = lines[j, :, pl.ds(LANES * k, LANES)]
 
 
-def look_kernel(
-    gradient, fcam_at, fpoint_at, fcams_at, scam_at, spoint_at, scams_at,
-    fseen_at, fsend0_at, fsend1_at, sseen_at, ssend0_at, ssend1_at,
-    lines, fcam, fpoint, fcams, scam, spoint, scams,
-    fseen, fsend0, fsend1, sseen, ssend0, ssend1,
-    table, findex, sindex, floose, sloose, arrived, left,
+def side_look_kernel(
+    gradient, scam_at, spoint_at, scams_at, sseen_at, ssend0_at, ssend1_at,
+    lines, scam, spoint, scams, sseen, ssend0, ssend1, table, sindex, sloose, arrived, left,
 ):
-    (fodd, _), (sodd, _) = place_of()
+    _, (sodd, _) = place_of()
     moves = [
         pltpu.make_async_copy(source, target, arrived.at[n])
         for n, (source, target) in enumerate(
-            (
-                (gradient, lines), (scams_at, scams), (scam_at, scam), (spoint_at, spoint),
-                (fcams_at, fcams), (fcam_at, fcam), (fpoint_at, fpoint),
-            )
+            ((gradient, lines), (scams_at, scams), (scam_at, scam), (spoint_at, spoint))
         )
     ]
     back = [
         pltpu.make_async_copy(source, target, left.at[n])
         for n, (source, target) in enumerate(
-            (
-                (ssend0, ssend0_at), (ssend1, ssend1_at), (sseen, sseen_at),
-                (fsend0, fsend0_at), (fsend1, fsend1_at), (fseen, fseen_at),
-            )
+            ((ssend0, ssend0_at), (ssend1, ssend1_at), (sseen, sseen_at))
         )
     ]
     for move in moves:
@@ -283,29 +274,30 @@
         move.wait()
     in_rows(lines, table)
     weave(scams, sindex)
-    for move in moves[2:4]:
+    for move in moves[2:]:
         move.wait()
 
-    def sent(first):
-        def done(turn):
-            back[first + turn].start()
-            if turn == 1:
-                back[first + 2].start()
-
-        return done
+    def done(turn):
+        back[turn].start()
+        if turn == 1:
+            back[2].start()
 
     pair_look(
-        scam, spoint, sindex, table, sseen, sloose, (ssend0, ssend1), sodd, True, None, 0, sent(0)
-    )
-    moves[4].wait()
-    weave(fcams, findex)
-    for move in moves[5:]:
-        move.wait()
-    pair_look(
-        fcam, fpoint, findex, table, fseen, floose, (fsend0, fsend1), fodd, True, None, 0, sent(3)
+        scam, spoint, sindex, table, sseen, sloose, (ssend0, ssend1), sodd, True, None, 0, done
     )
     for move in back:
         move.wait()
+
+
+def forward_look_kernel(
+    lines, fcam, fpoint, fcams, fseen, fsend0, fsend1, table, findex, floose
+):
+    (fodd, _), _ = place_of()
+    in_rows(lines, table)
+    weave(fcams, findex)
+    pair_look(
+        fcam, fpoint, findex, table, fseen, floose, (fsend0, fsend1), fodd, True, None, 0, None
+    )
 
 
 def local_kernel(live, values, cam, point, cams, out, product, stage, total, table):
@@ -508,19 +500,19 @@
     def sends_of(parts):
         return [(parts, fr // 2, LANES)] * 2, [(parts, sr // 2, LANES)] * 2
 
-    far = [gradient, fcam, fpoint, fcams, scam, spoint, scams]
+    far = [gradient, scam, spoint, scams]
     table = [pltpu.VMEM((ROWS, LANES), F32)]
     fshapes, sshapes = sends_of(9)
-    shapes = [(2, 2, fr, LANES)] + fshapes + [(2, 2, sr, LANES)] + sshapes
-    fseen, *fsent, sseen, ssent0, ssent1 = call(
-        look_kernel,
+    shapes = [(2, 2, sr, LANES)] + sshapes
+    sseen, *ssent = call(
+        side_look_kernel,
         far,
         shapes,
         [pltpu.VMEM(x.shape, x.dtype) for x in far]
         + [pltpu.VMEM(shape, F32) for shape in shapes]
         + table
-        + index_scratch
-        + [pltpu.VMEM((9, fr, LANES), F32), pltpu.VMEM((9, sr, LANES), F32)]
+        + index_scratch[1:]
+        + [pltpu.VMEM((9, sr, LANES), F32)]
         + [pltpu.SemaphoreType.DMA((len(far),)), pltpu.SemaphoreType.DMA((len(shapes),))],
         10**9,
         "look",
@@ -528,7 +520,14 @@
         FAR,
         63,
     )
-    ssent = [ssent0, ssent1]
+    fseen, *fsent = call(
+        forward_look_kernel,
+        [gradient, fcam, fpoint, fcams],
+        [(2, 2, fr, LANES)] + fshapes,
+        table + index_scratch[:1] + [pltpu.VMEM((9, fr, LANES), F32)],
+        10**9,
+        "forward_look",
+    )
     smet = meet(ssent, side_rounds)
     fmet = meet(fsent, fwd_rounds)
 

time: 68.1 us -> 67 us (0.984)
  waiting for transfers between devices: 7.22 us -> 6.32 us
    ppermute x6, waiting for transfers between devices: 4.5 us -> 3.58 us  [meet(): lax.ppermute(send, AXES, pairs)]
    pallas_call x7 -> x8, Pallas kernels: 17.8 us -> 17.8 us  [call(): pl.pallas_call(kernel, out_shape=outs, in_specs=specs, out_specs=[to] * l...]
  transfers between devices with their start and end apart: 9 -> 9, of which waited for: 3 -> 2; matrix products, arithmetic and copies ran while one was open for 0% -> 0% of each run, Pallas kernels for 10% -> 12%
where the time goes in v10:
time: 67 us; the launch traced here: 66.7 us
  starting transfers between devices  41 us (61%)
  Pallas kernels  17.8 us (27%)
  waiting for transfers between devices  6.32 us (9%)
  between operations  1.59 us (2%)
    pallas_call x8, Pallas kernels, call(): pl.pallas_call(kernel, out_shape=outs, in_specs=specs, out_specs=[to] * l...  17.8 us
    ppermute x6, starting transfers between devices, meet(): lax.ppermute(send, AXES, pairs)  16.2 us
    all_to_all x1, starting transfers between devices, per_device(): line = lax.all_to_all(line, AXES, 0, 0, tiled=True)  11.8 us
    ppermute x1, starting transfers between devices, per_device(): ssent = lax.ppermute(sz, AXES, side_up)  8.16 us
    ppermute x1, starting transfers between devices, per_device(): smet = lax.ppermute(sguest, AXES, side_down)  4.81 us
    ppermute x6, waiting for transfers between devices, meet(): lax.ppermute(send, AXES, pairs)  3.58 us
    all_to_all x1, waiting for transfers between devices, per_device(): line = lax.all_to_all(line, AXES, 0, 0, tiled=True)  2.74 us
  transfers between devices with their start and end apart: 9, of which 2 were waited for; matrix products, arithmetic and copies ran while one was open for 0% of the time, Pallas kernels for 12%

profile of v10, /device:TPU:1, one launch (start us, length us, event | category | flops | bytes accessed | tf_op | source)
XLA Modules:
  0.0 66.7 jit_solution(17728256010876706611)
XLA Ops:
  0.7 2.8 %look.1 = (f32[2,2,48,128]{3,2,1,0:T(8,128)}, f32[9,24,128]{2,1,0:T(8,128)}, f32[9,24,128]{2,1,0:T(8,128)}) custom-call(f32[9,1,512]{2,1,0:T(1,128)} %lines.5, bf16[2,18,48,128]{3,2,1,0:T(8,128)(2,1)} %bitcast.35, bf16[2,6,48,128]{3,2,1,0:T(8,128)(2,1)} %bitcast.44, s32[2,2,24,128]{3,2,1,0:T(8,128)} %bitcast.53), custom_call_target="tpu_custom_call" | custom-call | flops 1000000000 | bytes 2097152 | tf_op jit(solution)/shard_map/look/pallas_call | solution.py:444
  3.5 9.8 %collective-permute-start.2 = (f32[9,24,128]{2,1,0:T(8,128)}, f32[9,24,128]{2,1,0:T(8,128)S(1)}, u32[]{:S(2)}, u32[]{:S(2)}) collective-permute-start(f32[9,24,128]{2,1,0:T(8,128)} %get-tuple-element.29.ssent0), channel_id=1, source_target_pairs={{8,23},{9,22},{10,21},{11,20},{12,19},{13,18},{14,17},{15,16},{16,... | collective-permute-start | bytes 331784 | tf_op jit(solution)/shard_map/ppermute | solution.py:494
  13.4 0.1 collective-permute-start.3
  13.5 0.0 copy-start
  13.5 0.0 copy-start.3
  13.5 0.0 copy-start.9
  13.5 1.3 %forward_look.1 = (f32[2,2,64,128]{3,2,1,0:T(8,128)S(1)}, f32[9,32,128]{2,1,0:T(8,128)S(1)}, f32[9,32,128]{2,1,0:T(8,128)S(1)}) custom-call(f32[9,1,512]{2,1,0:T(1,128)S(1)} %copy-done.11, bf16[2,18,64,128]{3,2,1,0:T(8,128)(2,1)S(1)} %bitcast.32, bf16[2,6,64,128]{3,2,1,0:T(8,128)(2,1)S(1)} %bitcast.41, s32[2,2,32,128]{3,2,1,0:T(8,128)S(1)} %bitcast.48), custom_call_target="tpu_custom_call" | custom-call | flops 1000000000 | bytes 2097152 | tf_op jit(solution)/shard_map/forward_look/pallas_call | solution.py:444
  14.8 0.7 %collective-permute-start = (f32[9,32,128]{2,1,0:T(8,128)S(1)}, f32[9,32,128]{2,1,0:T(8,128)S(1)}, u32[]{:S(2)}, u32[]{:S(2)}) collective-permute-start(f32[9,32,128]{2,1,0:T(8,128)S(1)} %get-tuple-element.26.fsent0), channel_id=1, source_target_pairs={{1,2},{2,1},{3,4},{4,3},{5,6},{6,5},{9,10},{10,9},{11,12},{12,11},... | collective-permute-start | bytes 442376 | tf_op jit(solution)/shard_map/ppermute | solution.py:494
  15.5 2.5 %collective-permute-start.1 = (f32[9,32,128]{2,1,0:T(8,128)S(1)}, f32[9,32,128]{2,1,0:T(8,128)S(1)}, u32[]{:S(2)}, u32[]{:S(2)}) collective-permute-start(f32[9,32,128]{2,1,0:T(8,128)S(1)} %get-tuple-element.27.fsent1), channel_id=1, source_target_pairs={{0,1},{1,0},{2,3},{3,2},{4,5},{5,4},{6,7},{7,6},{8,9},{9,8},{10,11... | collective-permute-start | bytes 442376 | tf_op jit(solution)/shard_map/ppermute | solution.py:494
  18.6 0.0 copy-start.2
  18.6 0.0 copy-start.5
  18.7 2.4 %local.2 = (f32[36,128]{1,0:T(8,128)S(1)}, f32[8,128]{1,0:T(8,128)}) custom-call(s32[1,1]{1,0:T(1,128)S(6)} %copy.22.live, f32[9,1,512]{2,1,0:T(1,128)S(1)} %copy-done.11, bf16[18,6,2048]{2,1,0:T(8,128)(2,1)S(1)} %bitcast.30, bf16[6,6,2048]{2,1,0:T(8,128)(2,1)S(1)} %bitcast.39, s32[96,128]{1,0:T(8,128)S(1)} %bitcast.51), custom_call_target="tpu_custom_call" | custom-call | flops 5000000000 | bytes 2097152 | tf_op jit(solution)/shard_map/local/pallas_call | solution.py:444
  21.0 3.6 %collective-permute-done.1.fmet1 = f32[9,32,128]{2,1,0:T(8,128)S(1)} collective-permute-done((f32[9,32,128]{2,1,0:T(8,128)S(1)}, f32[9,32,128]{2,1,0:T(8,128)S(1)}, u32[]{:S(2)}, u32[]{:S(2)}) %collective-permute-start.1) | collective-permute-done | bytes 147488 | tf_op jit(solution)/shard_map/ppermute | solution.py:494
  24.6 5.2 %middle.1 = (f32[36,128]{1,0:T(8,128)S(1)}, f32[2,6,32,128]{3,2,1,0:T(8,128)S(1)}, f32[2,6,24,128]{3,2,1,0:T(8,128)S(1)}, f32[2,2,64,128]{3,2,1,0:T(8,128)S(1)},...) custom-call(f32[9,1,512]{2,1,0:T(1,128)S(1)} %copy-done.11, ...), custom_call_target="tpu_custom_call" | custom-call | flops 10000000000 | bytes 2097152 | tf_op jit(solution)/shard_map/middle/pallas_call | solution.py:444
  29.8 4.8 %collective-permute-start.6 = (f32[3,24,128]{2,1,0:T(8,128)S(1)}, f32[3,24,128]{2,1,0:T(8,128)S(1)}, u32[]{:S(2)}, u32[]{:S(2)}) collective-permute-start(f32[3,24,128]{2,1,0:T(8,128)S(1)} %get-tuple-element.40), channel_id=1, source_target_pairs={{8,7},{9,6},{10,5},{11,4},{12,3},{13,2},{14,1},{15,0},{16,15},{17,... | collective-permute-start | bytes 110600 | tf_op jit(solution)/shard_map/ppermute | solution.py:558
  34.6 0.7 collective-permute-start.4
  35.3 2.5 %collective-permute-start.5 = (f32[3,32,128]{2,1,0:T(8,128)S(1)}, f32[3,32,128]{2,1,0:T(8,128)S(1)}, u32[]{:S(2)}, u32[]{:S(2)}) collective-permute-start(f32[3,32,128]{2,1,0:T(8,128)S(1)} %get-tuple-element.37.fsent1), channel_id=1, source_target_pairs={{0,1},{1,0},{2,3},{3,2},{4,5},{5,4},{6,7},{7,6},{8,9},{9,8},{10,11... | collective-permute-start | bytes 147464 | tf_op jit(solution)/shard_map/ppermute | solution.py:494
  37.8 2.0 %local.3 = (f32[36,128]{1,0:T(8,128)S(1)}, f32[8,128]{1,0:T(8,128)S(1)}) custom-call(s32[1,1]{1,0:T(1,128)S(6)} %copy.22.live, f32[36,128]{1,0:T(8,128)S(1)} %get-tuple-element.31.values.first, bf16[18,6,2048]{2,1,0:T(8,128)(2,1)S(1)} %bitcast.31, bf16[6,6,2048]{2,1,0:T(8,128)(2,1)S(1)} %bitcast.40, s32[96,128]{1,0:T(8,128)S(1)} %bitcast.52), custom_call_target="tpu_custom_call" | custom-call | flops 5000000000 | bytes 2097152 | tf_op jit(solution)/shard_map/local/pallas_call | solution.py:444
  39.9 0.8 %dots.1 = (f32[2,3,64,128]{3,2,1,0:T(8,128)S(1)}, f32[3,24,128]{2,1,0:T(8,128)S(1)}, f32[256,128]{1,0:T(8,128)}) custom-call(f32[8,128]{1,0:T(8,128)S(1)} %get-tuple-element.34.dots, f32[8,128]{1,0:T(8,128)S(1)} %get-tuple-element.35.product, f32[3,32,128]{2,1,0:T(8,128)S(1)} %get-tuple-element.36.fsent0, f32[3,32,128]{2,1,0:T(8,128)S(1)} %get-tuple-element.37.fsent1, ...), custom_call_target="tpu_custom_call" | custom-call | flops 100000000 | bytes 2097152 | tf_op jit(solution)/shard_map/dots/pallas_call | solution.py:444
  40.7 11.8 %all-to-all-start = ((f32[256,1,128]{2,1,0:T(1,128)}), f32[256,1,128]{2,1,0:T(1,128)S(1)}, u32[]{:S(2)}, u32[]{:S(2)}) async-start(f32[256,1,128]{2,1,0:T(1,128)} %bitcast.26), calls=%async_computation | async-start | bytes 262144 | tf_op jit(solution)/shard_map/all_to_all | solution.py:569
  52.5 8.2 %collective-permute-start.7 = (f32[3,24,128]{2,1,0:T(8,128)S(1)}, f32[3,24,128]{2,1,0:T(8,128)S(1)}, u32[]{:S(2)}, u32[]{:S(2)}) collective-permute-start(f32[3,24,128]{2,1,0:T(8,128)S(1)} %get-tuple-element.44.svalues), channel_id=1, source_target_pairs={{0,15},{1,14},{2,13},{3,12},{4,11},{5,10},{6,9},{7,8},{8,23},{9,22... | collective-permute-start | bytes 110600 | tf_op jit(solution)/shard_map/ppermute | solution.py:570
  60.6 2.1 %last.1.extra = f32[36,128]{1,0:T(8,128)S(1)} custom-call(f32[36,128]{1,0:T(8,128)S(1)} %get-tuple-element.32.extra, bf16[2,18,64,128]{3,2,1,0:T(8,128)(2,1)S(1)} %bitcast.34, bf16[2,6,64,128]{3,2,1,0:T(8,128)(2,1)S(1)} %bitcast.43, s32[2,2,32,128]{3,2,1,0:T(8,128)S(1)} %bitcast.50, bf16[2,18,48,128]{3,2,1,0:T(8,128)(2,1)S(1)} %bitcast.37, ...), custom_call_target="tpu_custom_call" | custom-call | flops 5000000000 | bytes 2097152 | tf_op jit(solution)/shard_map/last/pallas_call | solution.py:444
  62.7 2.7 %all-to-all-done = f32[256,1,128]{2,1,0:T(1,128)S(1)} async-done(((f32[256,1,128]{2,1,0:T(1,128)}), f32[256,1,128]{2,1,0:T(1,128)S(1)}, u32[]{:S(2)}, u32[]{:S(2)}) %all-to-all-start) | async-done | bytes 131104 | tf_op jit(solution)/shard_map/all_to_all | solution.py:569
  65.5 1.3 %close.1 = (f32[9,1,512]{2,1,0:T(1,128)}, f32[9,1,512]{2,1,0:T(1,128)}) custom-call(f32[36,128]{1,0:T(8,128)S(1)} %last.1.extra, bf16[2,18,48,128]{3,2,1,0:T(8,128)(2,1)S(1)} %bitcast.38, bf16[2,6,48,128]{3,2,1,0:T(8,128)(2,1)S(1)} %bitcast.47, s32[2,2,24,128]{3,2,1,0:T(8,128)S(1)} %bitcast.56, f32[2,2,48,128]{3,2,1,0:T(8,128)S(1)} %get-tuple-element.43.sseen, ...), custom_call_target="tpu_custom_call" | custom-call | flops 2000000000 | bytes 2097152 | tf_op jit(solution)/shard_map/close/pallas_call | solution.py:444
  (28 shorter events, 0.1 us)
Async XLA Ops:
  0.6 12.8 %copy-start.1 = (bf16[2,18,2,1,4096]{4,2,3,1,0:T(2,128)(2,1)S(1)}, bf16[2,18,2,1,4096]{4,2,3,1,0:T(2,128)(2,1)}, u32[]{:S(2)}) copy-start(bf16[2,18,2,1,4096]{4,2,3,1,0:T(2,128)(2,1)} %param.16) | copy-start | bytes 1769476
  0.6 12.8 %copy-start.4 = (bf16[2,6,2,1,4096]{4,2,3,1,0:T(2,128)(2,1)S(1)}, bf16[2,6,2,1,4096]{4,2,3,1,0:T(2,128)(2,1)}, u32[]{:S(2)}) copy-start(bf16[2,6,2,1,4096]{4,2,3,1,0:T(2,128)(2,1)} %param.17) | copy-start | bytes 589828
  0.7 12.8 %copy-start.8 = (s32[2,2,1,4096]{3,2,1,0:T(1,128)S(1)}, s32[2,2,1,4096]{3,2,1,0:T(1,128)}, u32[]{:S(2)}) copy-start(s32[2,2,1,4096]{3,2,1,0:T(1,128)} %param.18) | copy-start | bytes 196612
  0.7 12.8 %copy-start.11 = (f32[9,1,512]{2,1,0:T(1,128)S(1)}, f32[9,1,512]{2,1,0:T(1,128)}, u32[]{:S(2)}) copy-start(f32[9,1,512]{2,1,0:T(1,128)} %lines.5) | copy-start | bytes 55300
  3.5 17.5 %collective-permute-start.2 = (f32[9,24,128]{2,1,0:T(8,128)}, f32[9,24,128]{2,1,0:T(8,128)S(1)}, u32[]{:S(2)}, u32[]{:S(2)}) collective-permute-start(f32[9,24,128]{2,1,0:T(8,128)} %get-tuple-element.29.ssent0), channel_id=1, source_target_pairs={{8,23},{9,22},{10,21},{11,20},{12,19},{13,18},{14,17},{15,16},{16,... | collective-permute-start | bytes 331784 | tf_op jit(solution)/shard_map/ppermute | solution.py:494
  13.4 7.7 %collective-permute-start.3 = (f32[9,24,128]{2,1,0:T(8,128)}, f32[9,24,128]{2,1,0:T(8,128)S(1)}, u32[]{:S(2)}, u32[]{:S(2)}) collective-permute-start(f32[9,24,128]{2,1,0:T(8,128)} %get-tuple-element.30.ssent1), channel_id=1, source_target_pairs={{0,15},{1,14},{2,13},{3,12},{4,11},{5,10},{6,9},{7,8},{8,7},{9,6},... | collective-permute-start | bytes 331784 | tf_op jit(solution)/shard_map/ppermute | solution.py:494
  13.5 5.1 %copy-start = (bf16[18,6,1,2048]{3,1,2,0:T(8,128)(2,1)S(1)}, bf16[18,6,1,2048]{3,1,2,0:T(8,128)(2,1)}, u32[]{:S(2)}) copy-start(bf16[18,6,1,2048]{3,1,2,0:T(8,128)(2,1)} %param.13) | copy-start | bytes 1327108
  13.5 5.1 %copy-start.3 = (bf16[6,6,1,2048]{3,1,2,0:T(8,128)(2,1)S(1)}, bf16[6,6,1,2048]{3,1,2,0:T(8,128)(2,1)}, u32[]{:S(2)}) copy-start(bf16[6,6,1,2048]{3,1,2,0:T(8,128)(2,1)} %param.14) | copy-start | bytes 442372
  13.5 5.1 %copy-start.9 = (s32[6,1,2048]{2,1,0:T(1,128)S(1)}, s32[6,1,2048]{2,1,0:T(1,128)}, u32[]{:S(2)}) copy-start(s32[6,1,2048]{2,1,0:T(1,128)} %param.15) | copy-start | bytes 147460
  14.8 6.2 %collective-permute-start = (f32[9,32,128]{2,1,0:T(8,128)S(1)}, f32[9,32,128]{2,1,0:T(8,128)S(1)}, u32[]{:S(2)}, u32[]{:S(2)}) collective-permute-start(f32[9,32,128]{2,1,0:T(8,128)S(1)} %get-tuple-element.26.fsent0), channel_id=1, source_target_pairs={{1,2},{2,1},{3,4},{4,3},{5,6},{6,5},{9,10},{10,9},{11,12},{12,11},... | collective-permute-start | bytes 442376 | tf_op jit(solution)/shard_map/ppermute | solution.py:494
  15.5 9.1 %collective-permute-start.1 = (f32[9,32,128]{2,1,0:T(8,128)S(1)}, f32[9,32,128]{2,1,0:T(8,128)S(1)}, u32[]{:S(2)}, u32[]{:S(2)}) collective-permute-start(f32[9,32,128]{2,1,0:T(8,128)S(1)} %get-tuple-element.27.fsent1), channel_id=1, source_target_pairs={{0,1},{1,0},{2,3},{3,2},{4,5},{5,4},{6,7},{7,6},{8,9},{9,8},{10,11... | collective-permute-start | bytes 442376 | tf_op jit(solution)/shard_map/ppermute | solution.py:494
  18.6 6.0 %copy-start.2 = (bf16[2,18,2,1,3072]{4,2,3,1,0:T(2,128)(2,1)S(1)}, bf16[2,18,2,1,3072]{4,2,3,1,0:T(2,128)(2,1)}, u32[]{:S(2)}) copy-start(bf16[2,18,2,1,3072]{4,2,3,1,0:T(2,128)(2,1)} %param.19) | copy-start | bytes 1327108
  18.6 6.0 %copy-start.5 = (bf16[2,6,2,1,3072]{4,2,3,1,0:T(2,128)(2,1)S(1)}, bf16[2,6,2,1,3072]{4,2,3,1,0:T(2,128)(2,1)}, u32[]{:S(2)}) copy-start(bf16[2,6,2,1,3072]{4,2,3,1,0:T(2,128)(2,1)} %param.20) | copy-start | bytes 442372
  18.6 6.0 %copy-start.6 = (f32[9,24,128]{2,1,0:T(8,128)S(1)}, f32[9,24,128]{2,1,0:T(8,128)}, u32[]{:S(2)}) copy-start(f32[9,24,128]{2,1,0:T(8,128)} %get-tuple-element.29.ssent0) | copy-start | bytes 331780
  18.6 6.0 %copy-start.7 = (f32[9,24,128]{2,1,0:T(8,128)S(1)}, f32[9,24,128]{2,1,0:T(8,128)}, u32[]{:S(2)}) copy-start(f32[9,24,128]{2,1,0:T(8,128)} %get-tuple-element.30.ssent1) | copy-start | bytes 331780
  18.7 6.0 %copy-start.10 = (s32[2,2,1,3072]{3,2,1,0:T(1,128)S(1)}, s32[2,2,1,3072]{3,2,1,0:T(1,128)}, u32[]{:S(2)}) copy-start(s32[2,2,1,3072]{3,2,1,0:T(1,128)} %param.21) | copy-start | bytes 147460
  18.7 6.0 %copy-start.12 = (f32[2,2,48,128]{3,2,1,0:T(8,128)S(1)}, f32[2,2,48,128]{3,2,1,0:T(8,128)}, u32[]{:S(2)}) copy-start(f32[2,2,48,128]{3,2,1,0:T(8,128)} %get-tuple-element.28.sseen) | copy-start | bytes 294916
  29.8 10.0 %collective-permute-start.6 = (f32[3,24,128]{2,1,0:T(8,128)S(1)}, f32[3,24,128]{2,1,0:T(8,128)S(1)}, u32[]{:S(2)}, u32[]{:S(2)}) collective-permute-start(f32[3,24,128]{2,1,0:T(8,128)S(1)} %get-tuple-element.40), channel_id=1, source_target_pairs={{8,7},{9,6},{10,5},{11,4},{12,3},{13,2},{14,1},{15,0},{16,15},{17,... | collective-permute-start | bytes 110600 | tf_op jit(solution)/shard_map/ppermute | solution.py:558
  34.6 5.2 %collective-permute-start.4 = (f32[3,32,128]{2,1,0:T(8,128)S(1)}, f32[3,32,128]{2,1,0:T(8,128)S(1)}, u32[]{:S(2)}, u32[]{:S(2)}) collective-permute-start(f32[3,32,128]{2,1,0:T(8,128)S(1)} %get-tuple-element.36.fsent0), channel_id=1, source_target_pairs={{1,2},{2,1},{3,4},{4,3},{5,6},{6,5},{9,10},{10,9},{11,12},{12,11},... | collective-permute-start | bytes 147464 | tf_op jit(solution)/shard_map/ppermute | solution.py:494
  35.3 4.6 %collective-permute-start.5 = (f32[3,32,128]{2,1,0:T(8,128)S(1)}, f32[3,32,128]{2,1,0:T(8,128)S(1)}, u32[]{:S(2)}, u32[]{:S(2)}) collective-permute-start(f32[3,32,128]{2,1,0:T(8,128)S(1)} %get-tuple-element.37.fsent1), channel_id=1, source_target_pairs={{0,1},{1,0},{2,3},{3,2},{4,5},{5,4},{6,7},{7,6},{8,9},{9,8},{10,11... | collective-permute-start | bytes 147464 | tf_op jit(solution)/shard_map/ppermute | solution.py:494
  40.7 24.8 %all-to-all-start = ((f32[256,1,128]{2,1,0:T(1,128)}), f32[256,1,128]{2,1,0:T(1,128)S(1)}, u32[]{:S(2)}, u32[]{:S(2)}) async-start(f32[256,1,128]{2,1,0:T(1,128)} %bitcast.26), calls=%async_computation | async-start | bytes 262144 | tf_op jit(solution)/shard_map/all_to_all | solution.py:569
  52.5 10.2 %collective-permute-start.7 = (f32[3,24,128]{2,1,0:T(8,128)S(1)}, f32[3,24,128]{2,1,0:T(8,128)S(1)}, u32[]{:S(2)}, u32[]{:S(2)}) collective-permute-start(f32[3,24,128]{2,1,0:T(8,128)S(1)} %get-tuple-element.44.svalues), channel_id=1, source_target_pairs={{0,15},{1,14},{2,13},{3,12},{4,11},{5,10},{6,9},{7,8},{8,23},{9,22... | collective-permute-start | bytes 110600 | tf_op jit(solution)/shard_map/ppermute | solution.py:570

commit v11 on v10

--- a/solution.py
+++ b/solution.py
@@ -135,9 +135,19 @@
             index[s, pl.ds(o, half, stride=2), :] = cams[s, o]
 
 
-def pair_look(cam, point, index, table, seen_out, loose, sends, odd, with_h, squares, held, done):
+def pair_look(
+    cam, point, index, table, seen_out, loose, sends, odd, with_h, squares, held, done,
+    kept=None, ready=None,
+):
     rows = cam.shape[2]
     half = rows // 2
+    if kept is not None:
+        for s in range(2):
+            for i in range(rows // STEP):
+                at = pl.ds(i * STEP, STEP)
+                for j, found in enumerate(fetch(table, index[s, at, :])):
+                    kept[s, j, at, :] = found
+        ready()
     for turn in range(2):
         s = turn ^ odd
         share = part_of(s, held)
@@ -146,7 +156,11 @@
             at = pl.ds(pl.multiple_of(i * STEP, STEP), STEP)
             across = [cam[s, j, at, :].astype(F32) for j in range(2 * JAC)]
             along = [point[s, j, at, :].astype(F32) for j in range(6)]
-            seen = predict(across, fetch(table, index[s, at, :]))
+            if kept is None:
+                values = fetch(table, index[s, at, :])
+            else:
+                values = [kept[s, j, at, :] for j in range(JAC)]
+            seen = predict(across, values)
             for r in range(2):
                 seen_out[turn, r, at, :] = seen[r]
             parts = project(along, seen)
@@ -253,7 +267,8 @@
 
 def side_look_kernel(
     gradient, scam_at, spoint_at, scams_at, sseen_at, ssend0_at, ssend1_at,
-    lines, scam, spoint, scams, sseen, ssend0, ssend1, table, sindex, sloose, arrived, left,
+    lines, scam, spoint, scams, sseen, ssend0, ssend1, table, sindex, sloose, kept,
+    arrived, left,
 ):
     _, (sodd, _) = place_of()
     moves = [
@@ -274,8 +289,10 @@
         move.wait()
     in_rows(lines, table)
     weave(scams, sindex)
-    for move in moves[2:]:
-        move.wait()
+
+    def ready():
+        for move in moves[2:]:
+            move.wait()
 
     def done(turn):
         back[turn].start()
@@ -283,7 +300,8 @@
             back[2].start()
 
     pair_look(
-        scam, spoint, sindex, table, sseen, sloose, (ssend0, ssend1), sodd, True, None, 0, done
+        scam, spoint, sindex, table, sseen, sloose, (ssend0, ssend1), sodd, True, None, 0, done,
+        kept, ready,
     )
     for move in back:
         move.wait()
@@ -401,17 +419,17 @@
     result[...] += extra[...]
 
 
-def close_kernel(
-    extra, scam, spoint, scams, sseen, svalues, sums, lines, first,
-    step_out, residual_out, base, second, sindex, sz, stage, total,
-):
+def guest_kernel(extra, scam, spoint, scams, sseen, svalues, result, sindex, sz, stage, total):
     _, (_, sheld) = place_of()
     weave(scams, sindex)
     total[...] = jnp.zeros_like(total)
     widened(svalues, sz, 1)
     pair_return(scam, spoint, sindex, sseen, sz, 0, sheld, stage, total, (1,))
-    fold(total, second)
-    second[...] += extra[...]
+    fold(total, result)
+    result[...] += extra[...]
+
+
+def close_kernel(sums, lines, first, second, step_out, residual_out, base):
     in_rows(lines, base)
     line = jnp.sum(sums[...], axis=0, keepdims=True)
     place = lax.broadcasted_iota(jnp.int32, line.shape, 1)
@@ -512,7 +530,7 @@
         + [pltpu.VMEM(shape, F32) for shape in shapes]
         + table
         + index_scratch[1:]
-        + [pltpu.VMEM((9, sr, LANES), F32)]
+        + [pltpu.VMEM((9, sr, LANES), F32), pltpu.VMEM((2, JAC, sr, LANES), F32)]
         + [pltpu.SemaphoreType.DMA((len(far),)), pltpu.SemaphoreType.DMA((len(shapes),))],
         10**9,
         "look",
@@ -576,13 +594,16 @@
         5 * 10**9,
         "last",
     )
+    (t,) = call(
+        guest_kernel,
+        [t, scam, spoint, scams, sseen, ssent],
+        [(ROWS, LANES)],
+        index_scratch[1:] + z_scratch[1:] + total_scratch,
+        2 * 10**9,
+        "guest",
+    )
     step, residual = call(
-        close_kernel,
-        [t, scam, spoint, scams, sseen, ssent, line, gradient, p],
-        [gradient.shape] * 2,
-        table * 2 + index_scratch[1:] + z_scratch[1:] + total_scratch,
-        2 * 10**9,
-        "close",
+        close_kernel, [line, gradient, p, t], [gradient.shape] * 2, table, 10**6, "close"
     )
     return step, residual
 

time: 67 us -> 66.5 us (level)
    pallas_call x8 -> x9, Pallas kernels: 17.8 us -> 17.9 us  [call(): pl.pallas_call(kernel, out_shape=outs, in_specs=specs, out_specs=[to] * l...]
  transfers between devices with their start and end apart: 9 -> 9, of which waited for: 2 -> 2; matrix products, arithmetic and copies ran while one was open for 0% -> 0% of each run, Pallas kernels for 12% -> 13%
where the time goes in v11:
time: 66.5 us; the launch traced here: 66.2 us
  starting transfers between devices  41 us (62%)
  Pallas kernels  17.9 us (27%)
  waiting for transfers between devices  5.65 us (8%)
  between operations  1.59 us (2%)
    pallas_call x9, Pallas kernels, call(): pl.pallas_call(kernel, out_shape=outs, in_specs=specs, out_specs=[to] * l...  17.9 us
    ppermute x6, starting transfers between devices, meet(): lax.ppermute(send, AXES, pairs)  16.2 us
    all_to_all x1, starting transfers between devices, per_device(): line = lax.all_to_all(line, AXES, 0, 0, tiled=True)  11.8 us
    ppermute x1, starting transfers between devices, per_device(): ssent = lax.ppermute(sz, AXES, side_up)  8.16 us
    ppermute x1, starting transfers between devices, per_device(): smet = lax.ppermute(sguest, AXES, side_down)  4.81 us
    ppermute x6, waiting for transfers between devices, meet(): lax.ppermute(send, AXES, pairs)  3.57 us
    all_to_all x1, waiting for transfers between devices, per_device(): line = lax.all_to_all(line, AXES, 0, 0, tiled=True)  2.07 us
  transfers between devices with their start and end apart: 9, of which 2 were waited for; matrix products, arithmetic and copies ran while one was open for 0% of the time, Pallas kernels for 13%

profile of v11, /device:TPU:1, one launch (start us, length us, event | category | flops | bytes accessed | tf_op | source)
XLA Modules:
  0.0 66.2 jit_solution(16594810321251904595)
XLA Ops:
  0.7 2.7 %look.1 = (f32[2,2,48,128]{3,2,1,0:T(8,128)}, f32[9,24,128]{2,1,0:T(8,128)}, f32[9,24,128]{2,1,0:T(8,128)}) custom-call(f32[9,1,512]{2,1,0:T(1,128)} %lines.5, bf16[2,18,48,128]{3,2,1,0:T(8,128)(2,1)} %bitcast.35, bf16[2,6,48,128]{3,2,1,0:T(8,128)(2,1)} %bitcast.44, s32[2,2,24,128]{3,2,1,0:T(8,128)} %bitcast.53), custom_call_target="tpu_custom_call" | custom-call | flops 1000000000 | bytes 2097152 | tf_op jit(solution)/shard_map/look/pallas_call | solution.py:462
  3.4 9.8 %collective-permute-start.2 = (f32[9,24,128]{2,1,0:T(8,128)}, f32[9,24,128]{2,1,0:T(8,128)S(1)}, u32[]{:S(2)}, u32[]{:S(2)}) collective-permute-start(f32[9,24,128]{2,1,0:T(8,128)} %get-tuple-element.29.ssent0), channel_id=1, source_target_pairs={{8,23},{9,22},{10,21},{11,20},{12,19},{13,18},{14,17},{15,16},{16,... | collective-permute-start | bytes 331784 | tf_op jit(solution)/shard_map/ppermute | solution.py:512
  13.2 0.1 collective-permute-start.3
  13.4 0.0 copy-start.4
  13.4 0.0 copy-start.10
  13.4 1.3 %forward_look.1 = (f32[2,2,64,128]{3,2,1,0:T(8,128)S(1)}, f32[9,32,128]{2,1,0:T(8,128)S(1)}, f32[9,32,128]{2,1,0:T(8,128)S(1)}) custom-call(f32[9,1,512]{2,1,0:T(1,128)S(1)} %copy-done, bf16[2,18,64,128]{3,2,1,0:T(8,128)(2,1)S(1)} %bitcast.32, bf16[2,6,64,128]{3,2,1,0:T(8,128)(2,1)S(1)} %bitcast.41, s32[2,2,32,128]{3,2,1,0:T(8,128)S(1)} %bitcast.48), custom_call_target="tpu_custom_call" | custom-call | flops 1000000000 | bytes 2097152 | tf_op jit(solution)/shard_map/forward_look/pallas_call | solution.py:462
  14.7 0.7 %collective-permute-start = (f32[9,32,128]{2,1,0:T(8,128)S(1)}, f32[9,32,128]{2,1,0:T(8,128)S(1)}, u32[]{:S(2)}, u32[]{:S(2)}) collective-permute-start(f32[9,32,128]{2,1,0:T(8,128)S(1)} %get-tuple-element.26.fsent0), channel_id=1, source_target_pairs={{1,2},{2,1},{3,4},{4,3},{5,6},{6,5},{9,10},{10,9},{11,12},{12,11},... | collective-permute-start | bytes 442376 | tf_op jit(solution)/shard_map/ppermute | solution.py:512
  15.4 2.5 %collective-permute-start.1 = (f32[9,32,128]{2,1,0:T(8,128)S(1)}, f32[9,32,128]{2,1,0:T(8,128)S(1)}, u32[]{:S(2)}, u32[]{:S(2)}) collective-permute-start(f32[9,32,128]{2,1,0:T(8,128)S(1)} %get-tuple-element.27.fsent1), channel_id=1, source_target_pairs={{0,1},{1,0},{2,3},{3,2},{4,5},{5,4},{6,7},{7,6},{8,9},{9,8},{10,11... | collective-permute-start | bytes 442376 | tf_op jit(solution)/shard_map/ppermute | solution.py:512
  18.5 0.0 copy-start.6
  18.5 0.0 copy-start.11
  18.6 2.4 %local.2 = (f32[36,128]{1,0:T(8,128)S(1)}, f32[8,128]{1,0:T(8,128)}) custom-call(s32[1,1]{1,0:T(1,128)S(6)} %copy.22.live, f32[9,1,512]{2,1,0:T(1,128)S(1)} %copy-done, bf16[18,6,2048]{2,1,0:T(8,128)(2,1)S(1)} %bitcast.30, bf16[6,6,2048]{2,1,0:T(8,128)(2,1)S(1)} %bitcast.39, s32[96,128]{1,0:T(8,128)S(1)} %bitcast.51), custom_call_target="tpu_custom_call" | custom-call | flops 5000000000 | bytes 2097152 | tf_op jit(solution)/shard_map/local/pallas_call | solution.py:462
  20.9 3.6 %collective-permute-done.1.fmet1 = f32[9,32,128]{2,1,0:T(8,128)S(1)} collective-permute-done((f32[9,32,128]{2,1,0:T(8,128)S(1)}, f32[9,32,128]{2,1,0:T(8,128)S(1)}, u32[]{:S(2)}, u32[]{:S(2)}) %collective-permute-start.1) | collective-permute-done | bytes 147488 | tf_op jit(solution)/shard_map/ppermute | solution.py:512
  24.5 5.2 %middle.1 = (f32[36,128]{1,0:T(8,128)S(1)}, f32[2,6,32,128]{3,2,1,0:T(8,128)S(1)}, f32[2,6,24,128]{3,2,1,0:T(8,128)S(1)}, f32[2,2,64,128]{3,2,1,0:T(8,128)S(1)},...) custom-call(f32[9,1,512]{2,1,0:T(1,128)S(1)} %copy-done, ...), custom_call_target="tpu_custom_call" | custom-call | flops 10000000000 | bytes 2097152 | tf_op jit(solution)/shard_map/middle/pallas_call | solution.py:462
  29.7 4.8 %collective-permute-start.6 = (f32[3,24,128]{2,1,0:T(8,128)S(1)}, f32[3,24,128]{2,1,0:T(8,128)S(1)}, u32[]{:S(2)}, u32[]{:S(2)}) collective-permute-start(f32[3,24,128]{2,1,0:T(8,128)S(1)} %get-tuple-element.38), channel_id=1, source_target_pairs={{8,7},{9,6},{10,5},{11,4},{12,3},{13,2},{14,1},{15,0},{16,15},{17,... | collective-permute-start | bytes 110600 | tf_op jit(solution)/shard_map/ppermute | solution.py:576
  34.5 0.7 %collective-permute-start.4 = (f32[3,32,128]{2,1,0:T(8,128)S(1)}, f32[3,32,128]{2,1,0:T(8,128)S(1)}, u32[]{:S(2)}, u32[]{:S(2)}) collective-permute-start(f32[3,32,128]{2,1,0:T(8,128)S(1)} %get-tuple-element.34.fsent0), channel_id=1, source_target_pairs={{1,2},{2,1},{3,4},{4,3},{5,6},{6,5},{9,10},{10,9},{11,12},{12,11},... | collective-permute-start | bytes 147464 | tf_op jit(solution)/shard_map/ppermute | solution.py:512
  35.2 2.5 %collective-permute-start.5 = (f32[3,32,128]{2,1,0:T(8,128)S(1)}, f32[3,32,128]{2,1,0:T(8,128)S(1)}, u32[]{:S(2)}, u32[]{:S(2)}) collective-permute-start(f32[3,32,128]{2,1,0:T(8,128)S(1)} %get-tuple-element.35.fsent1), channel_id=1, source_target_pairs={{0,1},{1,0},{2,3},{3,2},{4,5},{5,4},{6,7},{7,6},{8,9},{9,8},{10,11... | collective-permute-start | bytes 147464 | tf_op jit(solution)/shard_map/ppermute | solution.py:512
  37.7 2.0 %local.3 = (f32[36,128]{1,0:T(8,128)S(1)}, f32[8,128]{1,0:T(8,128)S(1)}) custom-call(s32[1,1]{1,0:T(1,128)S(6)} %copy.22.live, f32[36,128]{1,0:T(8,128)S(1)} %get-tuple-element.32.values.first, bf16[18,6,2048]{2,1,0:T(8,128)(2,1)S(1)} %bitcast.31, bf16[6,6,2048]{2,1,0:T(8,128)(2,1)S(1)} %bitcast.40, s32[96,128]{1,0:T(8,128)S(1)} %bitcast.52), custom_call_target="tpu_custom_call" | custom-call | flops 5000000000 | bytes 2097152 | tf_op jit(solution)/shard_map/local/pallas_call | solution.py:462
  39.8 0.8 %dots.1 = (f32[2,3,64,128]{3,2,1,0:T(8,128)S(1)}, f32[3,24,128]{2,1,0:T(8,128)S(1)}, f32[256,128]{1,0:T(8,128)}) custom-call(f32[8,128]{1,0:T(8,128)S(1)} %get-tuple-element.31.dots, f32[8,128]{1,0:T(8,128)S(1)} %get-tuple-element.33.product, f32[3,32,128]{2,1,0:T(8,128)S(1)} %get-tuple-element.34.fsent0, f32[3,32,128]{2,1,0:T(8,128)S(1)} %get-tuple-element.35.fsent1, ...), custom_call_target="tpu_custom_call" | custom-call | flops 100000000 | bytes 2097152 | tf_op jit(solution)/shard_map/dots/pallas_call | solution.py:462
  40.6 11.8 %all-to-all-start = ((f32[256,1,128]{2,1,0:T(1,128)}), f32[256,1,128]{2,1,0:T(1,128)S(1)}, u32[]{:S(2)}, u32[]{:S(2)}) async-start(f32[256,1,128]{2,1,0:T(1,128)} %bitcast.26), calls=%async_computation | async-start | bytes 262144 | tf_op jit(solution)/shard_map/all_to_all | solution.py:587
  52.4 8.2 %collective-permute-start.7 = (f32[3,24,128]{2,1,0:T(8,128)S(1)}, f32[3,24,128]{2,1,0:T(8,128)S(1)}, u32[]{:S(2)}, u32[]{:S(2)}) collective-permute-start(f32[3,24,128]{2,1,0:T(8,128)S(1)} %get-tuple-element.45.svalues), channel_id=1, source_target_pairs={{0,15},{1,14},{2,13},{3,12},{4,11},{5,10},{6,9},{7,8},{8,23},{9,22... | collective-permute-start | bytes 110600 | tf_op jit(solution)/shard_map/ppermute | solution.py:588
  60.6 2.1 %last.1.extra = f32[36,128]{1,0:T(8,128)S(1)} custom-call(f32[36,128]{1,0:T(8,128)S(1)} %get-tuple-element.41.extra, bf16[2,18,64,128]{3,2,1,0:T(8,128)(2,1)S(1)} %bitcast.34, bf16[2,6,64,128]{3,2,1,0:T(8,128)(2,1)S(1)} %bitcast.43, s32[2,2,32,128]{3,2,1,0:T(8,128)S(1)} %bitcast.50, bf16[2,18,48,128]{3,2,1,0:T(8,128)(2,1)S(1)} %bitcast.37, ...), custom_call_target="tpu_custom_call" | custom-call | flops 5000000000 | bytes 2097152 | tf_op jit(solution)/shard_map/last/pallas_call | solution.py:462
  62.7 0.6 guest.1.second
  63.3 2.1 %all-to-all-done = f32[256,1,128]{2,1,0:T(1,128)S(1)} async-done(((f32[256,1,128]{2,1,0:T(1,128)}), f32[256,1,128]{2,1,0:T(1,128)S(1)}, u32[]{:S(2)}, u32[]{:S(2)}) %all-to-all-start) | async-done | bytes 131104 | tf_op jit(solution)/shard_map/all_to_all | solution.py:587
  65.4 0.8 %close.1 = (f32[9,1,512]{2,1,0:T(1,128)}, f32[9,1,512]{2,1,0:T(1,128)}) custom-call(f32[256,128]{1,0:T(8,128)S(1)} %bitcast.29, f32[9,1,512]{2,1,0:T(1,128)S(1)} %copy-done, f32[36,128]{1,0:T(8,128)S(1)} %get-tuple-element.32.values.first, f32[36,128]{1,0:T(8,128)S(1)} %guest.1.second), custom_call_target="tpu_custom_call" | custom-call | flops 1000000 | bytes 2097152 | tf_op jit(solution)/shard_map/close/pallas_call | solution.py:462
  (29 shorter events, 0.1 us)
Async XLA Ops:
  0.6 12.7 %copy-start = (f32[9,1,512]{2,1,0:T(1,128)S(1)}, f32[9,1,512]{2,1,0:T(1,128)}, u32[]{:S(2)}) copy-start(f32[9,1,512]{2,1,0:T(1,128)} %lines.5) | copy-start | bytes 55300
  0.6 12.7 %copy-start.2 = (bf16[2,18,2,1,4096]{4,2,3,1,0:T(2,128)(2,1)S(1)}, bf16[2,18,2,1,4096]{4,2,3,1,0:T(2,128)(2,1)}, u32[]{:S(2)}) copy-start(bf16[2,18,2,1,4096]{4,2,3,1,0:T(2,128)(2,1)} %param.16) | copy-start | bytes 1769476
  0.7 12.7 %copy-start.5 = (bf16[2,6,2,1,4096]{4,2,3,1,0:T(2,128)(2,1)S(1)}, bf16[2,6,2,1,4096]{4,2,3,1,0:T(2,128)(2,1)}, u32[]{:S(2)}) copy-start(bf16[2,6,2,1,4096]{4,2,3,1,0:T(2,128)(2,1)} %param.17) | copy-start | bytes 589828
  0.7 12.7 %copy-start.9 = (s32[2,2,1,4096]{3,2,1,0:T(1,128)S(1)}, s32[2,2,1,4096]{3,2,1,0:T(1,128)}, u32[]{:S(2)}) copy-start(s32[2,2,1,4096]{3,2,1,0:T(1,128)} %param.18) | copy-start | bytes 196612
  3.4 17.5 %collective-permute-start.2 = (f32[9,24,128]{2,1,0:T(8,128)}, f32[9,24,128]{2,1,0:T(8,128)S(1)}, u32[]{:S(2)}, u32[]{:S(2)}) collective-permute-start(f32[9,24,128]{2,1,0:T(8,128)} %get-tuple-element.29.ssent0), channel_id=1, source_target_pairs={{8,23},{9,22},{10,21},{11,20},{12,19},{13,18},{14,17},{15,16},{16,... | collective-permute-start | bytes 331784 | tf_op jit(solution)/shard_map/ppermute | solution.py:512
  13.2 7.7 %collective-permute-start.3 = (f32[9,24,128]{2,1,0:T(8,128)}, f32[9,24,128]{2,1,0:T(8,128)S(1)}, u32[]{:S(2)}, u32[]{:S(2)}) collective-permute-start(f32[9,24,128]{2,1,0:T(8,128)} %get-tuple-element.30.ssent1), channel_id=1, source_target_pairs={{0,15},{1,14},{2,13},{3,12},{4,11},{5,10},{6,9},{7,8},{8,7},{9,6},... | collective-permute-start | bytes 331784 | tf_op jit(solution)/shard_map/ppermute | solution.py:512
  13.4 5.1 %copy-start.1 = (bf16[18,6,1,2048]{3,1,2,0:T(8,128)(2,1)S(1)}, bf16[18,6,1,2048]{3,1,2,0:T(8,128)(2,1)}, u32[]{:S(2)}) copy-start(bf16[18,6,1,2048]{3,1,2,0:T(8,128)(2,1)} %param.13) | copy-start | bytes 1327108
  13.4 5.1 %copy-start.4 = (bf16[6,6,1,2048]{3,1,2,0:T(8,128)(2,1)S(1)}, bf16[6,6,1,2048]{3,1,2,0:T(8,128)(2,1)}, u32[]{:S(2)}) copy-start(bf16[6,6,1,2048]{3,1,2,0:T(8,128)(2,1)} %param.14) | copy-start | bytes 442372
  13.4 5.1 %copy-start.10 = (s32[6,1,2048]{2,1,0:T(1,128)S(1)}, s32[6,1,2048]{2,1,0:T(1,128)}, u32[]{:S(2)}) copy-start(s32[6,1,2048]{2,1,0:T(1,128)} %param.15) | copy-start | bytes 147460
  14.7 6.2 %collective-permute-start = (f32[9,32,128]{2,1,0:T(8,128)S(1)}, f32[9,32,128]{2,1,0:T(8,128)S(1)}, u32[]{:S(2)}, u32[]{:S(2)}) collective-permute-start(f32[9,32,128]{2,1,0:T(8,128)S(1)} %get-tuple-element.26.fsent0), channel_id=1, source_target_pairs={{1,2},{2,1},{3,4},{4,3},{5,6},{6,5},{9,10},{10,9},{11,12},{12,11},... | collective-permute-start | bytes 442376 | tf_op jit(solution)/shard_map/ppermute | solution.py:512
  15.4 9.1 %collective-permute-start.1 = (f32[9,32,128]{2,1,0:T(8,128)S(1)}, f32[9,32,128]{2,1,0:T(8,128)S(1)}, u32[]{:S(2)}, u32[]{:S(2)}) collective-permute-start(f32[9,32,128]{2,1,0:T(8,128)S(1)} %get-tuple-element.27.fsent1), channel_id=1, source_target_pairs={{0,1},{1,0},{2,3},{3,2},{4,5},{5,4},{6,7},{7,6},{8,9},{9,8},{10,11... | collective-permute-start | bytes 442376 | tf_op jit(solution)/shard_map/ppermute | solution.py:512
  18.5 6.0 %copy-start.3 = (bf16[2,18,2,1,3072]{4,2,3,1,0:T(2,128)(2,1)S(1)}, bf16[2,18,2,1,3072]{4,2,3,1,0:T(2,128)(2,1)}, u32[]{:S(2)}) copy-start(bf16[2,18,2,1,3072]{4,2,3,1,0:T(2,128)(2,1)} %param.19) | copy-start | bytes 1327108
  18.5 6.0 %copy-start.6 = (bf16[2,6,2,1,3072]{4,2,3,1,0:T(2,128)(2,1)S(1)}, bf16[2,6,2,1,3072]{4,2,3,1,0:T(2,128)(2,1)}, u32[]{:S(2)}) copy-start(bf16[2,6,2,1,3072]{4,2,3,1,0:T(2,128)(2,1)} %param.20) | copy-start | bytes 442372
  18.5 6.0 %copy-start.7 = (f32[9,24,128]{2,1,0:T(8,128)S(1)}, f32[9,24,128]{2,1,0:T(8,128)}, u32[]{:S(2)}) copy-start(f32[9,24,128]{2,1,0:T(8,128)} %get-tuple-element.29.ssent0) | copy-start | bytes 331780
  18.5 6.0 %copy-start.8 = (f32[9,24,128]{2,1,0:T(8,128)S(1)}, f32[9,24,128]{2,1,0:T(8,128)}, u32[]{:S(2)}) copy-start(f32[9,24,128]{2,1,0:T(8,128)} %get-tuple-element.30.ssent1) | copy-start | bytes 331780
  18.5 6.0 %copy-start.11 = (s32[2,2,1,3072]{3,2,1,0:T(1,128)S(1)}, s32[2,2,1,3072]{3,2,1,0:T(1,128)}, u32[]{:S(2)}) copy-start(s32[2,2,1,3072]{3,2,1,0:T(1,128)} %param.21) | copy-start | bytes 147460
  18.6 6.0 %copy-start.12 = (f32[2,2,48,128]{3,2,1,0:T(8,128)S(1)}, f32[2,2,48,128]{3,2,1,0:T(8,128)}, u32[]{:S(2)}) copy-start(f32[2,2,48,128]{3,2,1,0:T(8,128)} %get-tuple-element.28.sseen) | copy-start | bytes 294916
  29.7 10.0 %collective-permute-start.6 = (f32[3,24,128]{2,1,0:T(8,128)S(1)}, f32[3,24,128]{2,1,0:T(8,128)S(1)}, u32[]{:S(2)}, u32[]{:S(2)}) collective-permute-start(f32[3,24,128]{2,1,0:T(8,128)S(1)} %get-tuple-element.38), channel_id=1, source_target_pairs={{8,7},{9,6},{10,5},{11,4},{12,3},{13,2},{14,1},{15,0},{16,15},{17,... | collective-permute-start | bytes 110600 | tf_op jit(solution)/shard_map/ppermute | solution.py:576
  34.5 5.2 %collective-permute-start.4 = (f32[3,32,128]{2,1,0:T(8,128)S(1)}, f32[3,32,128]{2,1,0:T(8,128)S(1)}, u32[]{:S(2)}, u32[]{:S(2)}) collective-permute-start(f32[3,32,128]{2,1,0:T(8,128)S(1)} %get-tuple-element.34.fsent0), channel_id=1, source_target_pairs={{1,2},{2,1},{3,4},{4,3},{5,6},{6,5},{9,10},{10,9},{11,12},{12,11},... | collective-permute-start | bytes 147464 | tf_op jit(solution)/shard_map/ppermute | solution.py:512
  35.2 4.6 %collective-permute-start.5 = (f32[3,32,128]{2,1,0:T(8,128)S(1)}, f32[3,32,128]{2,1,0:T(8,128)S(1)}, u32[]{:S(2)}, u32[]{:S(2)}) collective-permute-start(f32[3,32,128]{2,1,0:T(8,128)S(1)} %get-tuple-element.35.fsent1), channel_id=1, source_target_pairs={{0,1},{1,0},{2,3},{3,2},{4,5},{5,4},{6,7},{7,6},{8,9},{9,8},{10,11... | collective-permute-start | bytes 147464 | tf_op jit(solution)/shard_map/ppermute | solution.py:512
  40.6 24.8 %all-to-all-start = ((f32[256,1,128]{2,1,0:T(1,128)}), f32[256,1,128]{2,1,0:T(1,128)S(1)}, u32[]{:S(2)}, u32[]{:S(2)}) async-start(f32[256,1,128]{2,1,0:T(1,128)} %bitcast.26), calls=%async_computation | async-start | bytes 262144 | tf_op jit(solution)/shard_map/all_to_all | solution.py:587
  52.4 10.3 %collective-permute-start.7 = (f32[3,24,128]{2,1,0:T(8,128)S(1)}, f32[3,24,128]{2,1,0:T(8,128)S(1)}, u32[]{:S(2)}, u32[]{:S(2)}) collective-permute-start(f32[3,24,128]{2,1,0:T(8,128)S(1)} %get-tuple-element.45.svalues), channel_id=1, source_target_pairs={{0,15},{1,14},{2,13},{3,12},{4,11},{5,10},{6,9},{7,8},{8,23},{9,22... | collective-permute-start | bytes 110600 | tf_op jit(solution)/shard_map/ppermute | solution.py:588

commit v12 on v11

--- a/solution.py
+++ b/solution.py
@@ -12,7 +12,7 @@
 ROWS = JAC * PAGES
 STACK = 80
 STEP = 16
-LOCAL_GROUP = 8
+LOCAL_GROUP = 16
 SYM = ((0, 0), (0, 1), (0, 2), (1, 1), (1, 2), (2, 2))
 DAMP = 1.0
 VMEM = pl.BlockSpec(memory_space=pltpu.VMEM)

time: 66.5 us -> 66.5 us (level)
  transfers between devices with their start and end apart: 9 -> 9, of which waited for: 2 -> 3; matrix products, arithmetic and copies ran while one was open for 0% -> 0% of each run, Pallas kernels for 13% -> 12%
where the time goes in v12:
time: 66.5 us; the launch traced here: 66.2 us
  starting transfers between devices  41.2 us (62%)
  Pallas kernels  17.6 us (26%)
  waiting for transfers between devices  5.84 us (9%)
  between operations  1.57 us (2%)
    pallas_call x9, Pallas kernels, call(): pl.pallas_call(kernel, out_shape=outs, in_specs=specs, out_specs=[to] * l...  17.6 us
    ppermute x6, starting transfers between devices, meet(): lax.ppermute(send, AXES, pairs)  16.2 us
    all_to_all x1, starting transfers between devices, per_device(): line = lax.all_to_all(line, AXES, 0, 0, tiled=True)  12 us
    ppermute x1, starting transfers between devices, per_device(): ssent = lax.ppermute(sz, AXES, side_up)  8.16 us
    ppermute x1, starting transfers between devices, per_device(): smet = lax.ppermute(sguest, AXES, side_down)  4.81 us
    ppermute x6, waiting for transfers between devices, meet(): lax.ppermute(send, AXES, pairs)  3.76 us
    all_to_all x1, waiting for transfers between devices, per_device(): line = lax.all_to_all(line, AXES, 0, 0, tiled=True)  2.07 us
  transfers between devices with their start and end apart: 9, of which 3 were waited for; matrix products, arithmetic and copies ran while one was open for 0% of the time, Pallas kernels for 12%

profile of v12, /device:TPU:1, one launch (start us, length us, event | category | flops | bytes accessed | tf_op | source)
XLA Modules:
  0.0 66.2 jit_solution(6303994595055381234)
XLA Ops:
  0.7 2.7 %look.1 = (f32[2,2,48,128]{3,2,1,0:T(8,128)}, f32[9,24,128]{2,1,0:T(8,128)}, f32[9,24,128]{2,1,0:T(8,128)}) custom-call(f32[9,1,512]{2,1,0:T(1,128)} %lines.5, bf16[2,18,48,128]{3,2,1,0:T(8,128)(2,1)} %bitcast.35, bf16[2,6,48,128]{3,2,1,0:T(8,128)(2,1)} %bitcast.44, s32[2,2,24,128]{3,2,1,0:T(8,128)} %bitcast.53), custom_call_target="tpu_custom_call" | custom-call | flops 1000000000 | bytes 2097152 | tf_op jit(solution)/shard_map/look/pallas_call | solution.py:462
  3.4 9.8 %collective-permute-start.2 = (f32[9,24,128]{2,1,0:T(8,128)}, f32[9,24,128]{2,1,0:T(8,128)S(1)}, u32[]{:S(2)}, u32[]{:S(2)}) collective-permute-start(f32[9,24,128]{2,1,0:T(8,128)} %get-tuple-element.29.ssent0), channel_id=1, source_target_pairs={{8,23},{9,22},{10,21},{11,20},{12,19},{13,18},{14,17},{15,16},{16,... | collective-permute-start | bytes 331784 | tf_op jit(solution)/shard_map/ppermute | solution.py:512
  13.2 0.1 collective-permute-start.3
  13.4 0.0 copy-start.1
  13.4 0.0 copy-start.4
  13.4 1.3 %forward_look.1 = (f32[2,2,64,128]{3,2,1,0:T(8,128)S(1)}, f32[9,32,128]{2,1,0:T(8,128)S(1)}, f32[9,32,128]{2,1,0:T(8,128)S(1)}) custom-call(f32[9,1,512]{2,1,0:T(1,128)S(1)} %copy-done, bf16[2,18,64,128]{3,2,1,0:T(8,128)(2,1)S(1)} %bitcast.32, bf16[2,6,64,128]{3,2,1,0:T(8,128)(2,1)S(1)} %bitcast.41, s32[2,2,32,128]{3,2,1,0:T(8,128)S(1)} %bitcast.48), custom_call_target="tpu_custom_call" | custom-call | flops 1000000000 | bytes 2097152 | tf_op jit(solution)/shard_map/forward_look/pallas_call | solution.py:462
  14.7 0.7 %collective-permute-start = (f32[9,32,128]{2,1,0:T(8,128)S(1)}, f32[9,32,128]{2,1,0:T(8,128)S(1)}, u32[]{:S(2)}, u32[]{:S(2)}) collective-permute-start(f32[9,32,128]{2,1,0:T(8,128)S(1)} %get-tuple-element.26.fsent0), channel_id=1, source_target_pairs={{1,2},{2,1},{3,4},{4,3},{5,6},{6,5},{9,10},{10,9},{11,12},{12,11},... | collective-permute-start | bytes 442376 | tf_op jit(solution)/shard_map/ppermute | solution.py:512
  15.4 2.5 %collective-permute-start.1 = (f32[9,32,128]{2,1,0:T(8,128)S(1)}, f32[9,32,128]{2,1,0:T(8,128)S(1)}, u32[]{:S(2)}, u32[]{:S(2)}) collective-permute-start(f32[9,32,128]{2,1,0:T(8,128)S(1)} %get-tuple-element.27.fsent1), channel_id=1, source_target_pairs={{0,1},{1,0},{2,3},{3,2},{4,5},{5,4},{6,7},{7,6},{8,9},{9,8},{10,11... | collective-permute-start | bytes 442376 | tf_op jit(solution)/shard_map/ppermute | solution.py:512
  18.5 0.0 copy-start.3
  18.6 2.3 %local.2 = (f32[36,128]{1,0:T(8,128)S(1)}, f32[8,128]{1,0:T(8,128)}) custom-call(s32[1,1]{1,0:T(1,128)S(6)} %copy.22.live, f32[9,1,512]{2,1,0:T(1,128)S(1)} %copy-done, bf16[18,6,2048]{2,1,0:T(8,128)(2,1)S(1)} %bitcast.30, bf16[6,6,2048]{2,1,0:T(8,128)(2,1)S(1)} %bitcast.39, s32[96,128]{1,0:T(8,128)S(1)} %bitcast.51), custom_call_target="tpu_custom_call" | custom-call | flops 5000000000 | bytes 2097152 | tf_op jit(solution)/shard_map/local/pallas_call | solution.py:462
  20.9 3.6 %collective-permute-done.1.fmet1 = f32[9,32,128]{2,1,0:T(8,128)S(1)} collective-permute-done((f32[9,32,128]{2,1,0:T(8,128)S(1)}, f32[9,32,128]{2,1,0:T(8,128)S(1)}, u32[]{:S(2)}, u32[]{:S(2)}) %collective-permute-start.1) | collective-permute-done | bytes 147488 | tf_op jit(solution)/shard_map/ppermute | solution.py:512
  24.5 5.2 %middle.1 = (f32[36,128]{1,0:T(8,128)S(1)}, f32[2,6,32,128]{3,2,1,0:T(8,128)S(1)}, f32[2,6,24,128]{3,2,1,0:T(8,128)S(1)}, f32[2,2,64,128]{3,2,1,0:T(8,128)S(1)},...) custom-call(f32[9,1,512]{2,1,0:T(1,128)S(1)} %copy-done, ...), custom_call_target="tpu_custom_call" | custom-call | flops 10000000000 | bytes 2097152 | tf_op jit(solution)/shard_map/middle/pallas_call | solution.py:462
  29.7 4.8 %collective-permute-start.6 = (f32[3,24,128]{2,1,0:T(8,128)S(1)}, f32[3,24,128]{2,1,0:T(8,128)S(1)}, u32[]{:S(2)}, u32[]{:S(2)}) collective-permute-start(f32[3,24,128]{2,1,0:T(8,128)S(1)} %get-tuple-element.38), channel_id=1, source_target_pairs={{8,7},{9,6},{10,5},{11,4},{12,3},{13,2},{14,1},{15,0},{16,15},{17,... | collective-permute-start | bytes 110600 | tf_op jit(solution)/shard_map/ppermute | solution.py:576
  34.5 0.7 %collective-permute-start.4 = (f32[3,32,128]{2,1,0:T(8,128)S(1)}, f32[3,32,128]{2,1,0:T(8,128)S(1)}, u32[]{:S(2)}, u32[]{:S(2)}) collective-permute-start(f32[3,32,128]{2,1,0:T(8,128)S(1)} %get-tuple-element.34.fsent0), channel_id=1, source_target_pairs={{1,2},{2,1},{3,4},{4,3},{5,6},{6,5},{9,10},{10,9},{11,12},{12,11},... | collective-permute-start | bytes 147464 | tf_op jit(solution)/shard_map/ppermute | solution.py:512
  35.2 2.5 %collective-permute-start.5 = (f32[3,32,128]{2,1,0:T(8,128)S(1)}, f32[3,32,128]{2,1,0:T(8,128)S(1)}, u32[]{:S(2)}, u32[]{:S(2)}) collective-permute-start(f32[3,32,128]{2,1,0:T(8,128)S(1)} %get-tuple-element.35.fsent1), channel_id=1, source_target_pairs={{0,1},{1,0},{2,3},{3,2},{4,5},{5,4},{6,7},{7,6},{8,9},{9,8},{10,11... | collective-permute-start | bytes 147464 | tf_op jit(solution)/shard_map/ppermute | solution.py:512
  37.7 1.8 %local.3 = (f32[36,128]{1,0:T(8,128)S(1)}, f32[8,128]{1,0:T(8,128)S(1)}) custom-call(s32[1,1]{1,0:T(1,128)S(6)} %copy.22.live, f32[36,128]{1,0:T(8,128)S(1)} %get-tuple-element.32.values.first, bf16[18,6,2048]{2,1,0:T(8,128)(2,1)S(1)} %bitcast.31, bf16[6,6,2048]{2,1,0:T(8,128)(2,1)S(1)} %bitcast.40, s32[96,128]{1,0:T(8,128)S(1)} %bitcast.52), custom_call_target="tpu_custom_call" | custom-call | flops 5000000000 | bytes 2097152 | tf_op jit(solution)/shard_map/local/pallas_call | solution.py:462
  39.5 0.1 collective-permute-done.5.fmet1
  39.6 0.8 %dots.1 = (f32[2,3,64,128]{3,2,1,0:T(8,128)S(1)}, f32[3,24,128]{2,1,0:T(8,128)S(1)}, f32[256,128]{1,0:T(8,128)}) custom-call(f32[8,128]{1,0:T(8,128)S(1)} %get-tuple-element.31.dots, f32[8,128]{1,0:T(8,128)S(1)} %get-tuple-element.33.product, f32[3,32,128]{2,1,0:T(8,128)S(1)} %get-tuple-element.34.fsent0, f32[3,32,128]{2,1,0:T(8,128)S(1)} %get-tuple-element.35.fsent1, ...), custom_call_target="tpu_custom_call" | custom-call | flops 100000000 | bytes 2097152 | tf_op jit(solution)/shard_map/dots/pallas_call | solution.py:462
  40.4 12.0 %all-to-all-start = ((f32[256,1,128]{2,1,0:T(1,128)}), f32[256,1,128]{2,1,0:T(1,128)S(1)}, u32[]{:S(2)}, u32[]{:S(2)}) async-start(f32[256,1,128]{2,1,0:T(1,128)} %bitcast.26), calls=%async_computation | async-start | bytes 262144 | tf_op jit(solution)/shard_map/all_to_all | solution.py:587
  52.4 8.2 %collective-permute-start.7 = (f32[3,24,128]{2,1,0:T(8,128)S(1)}, f32[3,24,128]{2,1,0:T(8,128)S(1)}, u32[]{:S(2)}, u32[]{:S(2)}) collective-permute-start(f32[3,24,128]{2,1,0:T(8,128)S(1)} %get-tuple-element.45.svalues), channel_id=1, source_target_pairs={{0,15},{1,14},{2,13},{3,12},{4,11},{5,10},{6,9},{7,8},{8,23},{9,22... | collective-permute-start | bytes 110600 | tf_op jit(solution)/shard_map/ppermute | solution.py:588
  60.6 2.1 %last.1.extra = f32[36,128]{1,0:T(8,128)S(1)} custom-call(f32[36,128]{1,0:T(8,128)S(1)} %get-tuple-element.41.extra, bf16[2,18,64,128]{3,2,1,0:T(8,128)(2,1)S(1)} %bitcast.34, bf16[2,6,64,128]{3,2,1,0:T(8,128)(2,1)S(1)} %bitcast.43, s32[2,2,32,128]{3,2,1,0:T(8,128)S(1)} %bitcast.50, bf16[2,18,48,128]{3,2,1,0:T(8,128)(2,1)S(1)} %bitcast.37, ...), custom_call_target="tpu_custom_call" | custom-call | flops 5000000000 | bytes 2097152 | tf_op jit(solution)/shard_map/last/pallas_call | solution.py:462
  62.7 0.6 guest.1.second
  63.3 2.1 %all-to-all-done = f32[256,1,128]{2,1,0:T(1,128)S(1)} async-done(((f32[256,1,128]{2,1,0:T(1,128)}), f32[256,1,128]{2,1,0:T(1,128)S(1)}, u32[]{:S(2)}, u32[]{:S(2)}) %all-to-all-start) | async-done | bytes 131104 | tf_op jit(solution)/shard_map/all_to_all | solution.py:587
  65.4 0.8 %close.1 = (f32[9,1,512]{2,1,0:T(1,128)}, f32[9,1,512]{2,1,0:T(1,128)}) custom-call(f32[256,128]{1,0:T(8,128)S(1)} %bitcast.29, f32[9,1,512]{2,1,0:T(1,128)S(1)} %copy-done, f32[36,128]{1,0:T(8,128)S(1)} %get-tuple-element.32.values.first, f32[36,128]{1,0:T(8,128)S(1)} %guest.1.second), custom_call_target="tpu_custom_call" | custom-call | flops 1000000 | bytes 2097152 | tf_op jit(solution)/shard_map/close/pallas_call | solution.py:462
  (29 shorter events, 0.1 us)
Async XLA Ops:
  0.6 12.7 %copy-start = (f32[9,1,512]{2,1,0:T(1,128)S(1)}, f32[9,1,512]{2,1,0:T(1,128)}, u32[]{:S(2)}) copy-start(f32[9,1,512]{2,1,0:T(1,128)} %lines.5) | copy-start | bytes 55300
  0.6 12.7 %copy-start.2 = (bf16[2,18,2,1,4096]{4,2,3,1,0:T(2,128)(2,1)S(1)}, bf16[2,18,2,1,4096]{4,2,3,1,0:T(2,128)(2,1)}, u32[]{:S(2)}) copy-start(bf16[2,18,2,1,4096]{4,2,3,1,0:T(2,128)(2,1)} %param.16) | copy-start | bytes 1769476
  0.7 12.7 %copy-start.5 = (bf16[2,6,2,1,4096]{4,2,3,1,0:T(2,128)(2,1)S(1)}, bf16[2,6,2,1,4096]{4,2,3,1,0:T(2,128)(2,1)}, u32[]{:S(2)}) copy-start(bf16[2,6,2,1,4096]{4,2,3,1,0:T(2,128)(2,1)} %param.17) | copy-start | bytes 589828
  0.7 12.7 %copy-start.9 = (s32[2,2,1,4096]{3,2,1,0:T(1,128)S(1)}, s32[2,2,1,4096]{3,2,1,0:T(1,128)}, u32[]{:S(2)}) copy-start(s32[2,2,1,4096]{3,2,1,0:T(1,128)} %param.18) | copy-start | bytes 196612
  3.4 17.5 %collective-permute-start.2 = (f32[9,24,128]{2,1,0:T(8,128)}, f32[9,24,128]{2,1,0:T(8,128)S(1)}, u32[]{:S(2)}, u32[]{:S(2)}) collective-permute-start(f32[9,24,128]{2,1,0:T(8,128)} %get-tuple-element.29.ssent0), channel_id=1, source_target_pairs={{8,23},{9,22},{10,21},{11,20},{12,19},{13,18},{14,17},{15,16},{16,... | collective-permute-start | bytes 331784 | tf_op jit(solution)/shard_map/ppermute | solution.py:512
  13.2 7.6 %collective-permute-start.3 = (f32[9,24,128]{2,1,0:T(8,128)}, f32[9,24,128]{2,1,0:T(8,128)S(1)}, u32[]{:S(2)}, u32[]{:S(2)}) collective-permute-start(f32[9,24,128]{2,1,0:T(8,128)} %get-tuple-element.30.ssent1), channel_id=1, source_target_pairs={{0,15},{1,14},{2,13},{3,12},{4,11},{5,10},{6,9},{7,8},{8,7},{9,6},... | collective-permute-start | bytes 331784 | tf_op jit(solution)/shard_map/ppermute | solution.py:512
  13.4 5.1 %copy-start.1 = (bf16[18,6,1,2048]{3,1,2,0:T(8,128)(2,1)S(1)}, bf16[18,6,1,2048]{3,1,2,0:T(8,128)(2,1)}, u32[]{:S(2)}) copy-start(bf16[18,6,1,2048]{3,1,2,0:T(8,128)(2,1)} %param.13) | copy-start | bytes 1327108
  13.4 5.1 %copy-start.4 = (bf16[6,6,1,2048]{3,1,2,0:T(8,128)(2,1)S(1)}, bf16[6,6,1,2048]{3,1,2,0:T(8,128)(2,1)}, u32[]{:S(2)}) copy-start(bf16[6,6,1,2048]{3,1,2,0:T(8,128)(2,1)} %param.14) | copy-start | bytes 442372
  13.4 5.1 %copy-start.10 = (s32[6,1,2048]{2,1,0:T(1,128)S(1)}, s32[6,1,2048]{2,1,0:T(1,128)}, u32[]{:S(2)}) copy-start(s32[6,1,2048]{2,1,0:T(1,128)} %param.15) | copy-start | bytes 147460
  14.7 6.2 %collective-permute-start = (f32[9,32,128]{2,1,0:T(8,128)S(1)}, f32[9,32,128]{2,1,0:T(8,128)S(1)}, u32[]{:S(2)}, u32[]{:S(2)}) collective-permute-start(f32[9,32,128]{2,1,0:T(8,128)S(1)} %get-tuple-element.26.fsent0), channel_id=1, source_target_pairs={{1,2},{2,1},{3,4},{4,3},{5,6},{6,5},{9,10},{10,9},{11,12},{12,11},... | collective-permute-start | bytes 442376 | tf_op jit(solution)/shard_map/ppermute | solution.py:512
  15.4 9.1 %collective-permute-start.1 = (f32[9,32,128]{2,1,0:T(8,128)S(1)}, f32[9,32,128]{2,1,0:T(8,128)S(1)}, u32[]{:S(2)}, u32[]{:S(2)}) collective-permute-start(f32[9,32,128]{2,1,0:T(8,128)S(1)} %get-tuple-element.27.fsent1), channel_id=1, source_target_pairs={{0,1},{1,0},{2,3},{3,2},{4,5},{5,4},{6,7},{7,6},{8,9},{9,8},{10,11... | collective-permute-start | bytes 442376 | tf_op jit(solution)/shard_map/ppermute | solution.py:512
  18.5 6.0 %copy-start.3 = (bf16[2,18,2,1,3072]{4,2,3,1,0:T(2,128)(2,1)S(1)}, bf16[2,18,2,1,3072]{4,2,3,1,0:T(2,128)(2,1)}, u32[]{:S(2)}) copy-start(bf16[2,18,2,1,3072]{4,2,3,1,0:T(2,128)(2,1)} %param.19) | copy-start | bytes 1327108
  18.5 6.0 %copy-start.6 = (bf16[2,6,2,1,3072]{4,2,3,1,0:T(2,128)(2,1)S(1)}, bf16[2,6,2,1,3072]{4,2,3,1,0:T(2,128)(2,1)}, u32[]{:S(2)}) copy-start(bf16[2,6,2,1,3072]{4,2,3,1,0:T(2,128)(2,1)} %param.20) | copy-start | bytes 442372
  18.5 6.0 %copy-start.7 = (f32[9,24,128]{2,1,0:T(8,128)S(1)}, f32[9,24,128]{2,1,0:T(8,128)}, u32[]{:S(2)}) copy-start(f32[9,24,128]{2,1,0:T(8,128)} %get-tuple-element.29.ssent0) | copy-start | bytes 331780
  18.5 6.0 %copy-start.8 = (f32[9,24,128]{2,1,0:T(8,128)S(1)}, f32[9,24,128]{2,1,0:T(8,128)}, u32[]{:S(2)}) copy-start(f32[9,24,128]{2,1,0:T(8,128)} %get-tuple-element.30.ssent1) | copy-start | bytes 331780
  18.5 6.0 %copy-start.11 = (s32[2,2,1,3072]{3,2,1,0:T(1,128)S(1)}, s32[2,2,1,3072]{3,2,1,0:T(1,128)}, u32[]{:S(2)}) copy-start(s32[2,2,1,3072]{3,2,1,0:T(1,128)} %param.21) | copy-start | bytes 147460
  18.6 6.0 %copy-start.12 = (f32[2,2,48,128]{3,2,1,0:T(8,128)S(1)}, f32[2,2,48,128]{3,2,1,0:T(8,128)}, u32[]{:S(2)}) copy-start(f32[2,2,48,128]{3,2,1,0:T(8,128)} %get-tuple-element.28.sseen) | copy-start | bytes 294916
  29.7 9.8 %collective-permute-start.6 = (f32[3,24,128]{2,1,0:T(8,128)S(1)}, f32[3,24,128]{2,1,0:T(8,128)S(1)}, u32[]{:S(2)}, u32[]{:S(2)}) collective-permute-start(f32[3,24,128]{2,1,0:T(8,128)S(1)} %get-tuple-element.38), channel_id=1, source_target_pairs={{8,7},{9,6},{10,5},{11,4},{12,3},{13,2},{14,1},{15,0},{16,15},{17,... | collective-permute-start | bytes 110600 | tf_op jit(solution)/shard_map/ppermute | solution.py:576
  34.5 5.0 %collective-permute-start.4 = (f32[3,32,128]{2,1,0:T(8,128)S(1)}, f32[3,32,128]{2,1,0:T(8,128)S(1)}, u32[]{:S(2)}, u32[]{:S(2)}) collective-permute-start(f32[3,32,128]{2,1,0:T(8,128)S(1)} %get-tuple-element.34.fsent0), channel_id=1, source_target_pairs={{1,2},{2,1},{3,4},{4,3},{5,6},{6,5},{9,10},{10,9},{11,12},{12,11},... | collective-permute-start | bytes 147464 | tf_op jit(solution)/shard_map/ppermute | solution.py:512
  35.2 4.4 %collective-permute-start.5 = (f32[3,32,128]{2,1,0:T(8,128)S(1)}, f32[3,32,128]{2,1,0:T(8,128)S(1)}, u32[]{:S(2)}, u32[]{:S(2)}) collective-permute-start(f32[3,32,128]{2,1,0:T(8,128)S(1)} %get-tuple-element.35.fsent1), channel_id=1, source_target_pairs={{0,1},{1,0},{2,3},{3,2},{4,5},{5,4},{6,7},{7,6},{8,9},{9,8},{10,11... | collective-permute-start | bytes 147464 | tf_op jit(solution)/shard_map/ppermute | solution.py:512
  40.4 25.0 %all-to-all-start = ((f32[256,1,128]{2,1,0:T(1,128)}), f32[256,1,128]{2,1,0:T(1,128)S(1)}, u32[]{:S(2)}, u32[]{:S(2)}) async-start(f32[256,1,128]{2,1,0:T(1,128)} %bitcast.26), calls=%async_computation | async-start | bytes 262144 | tf_op jit(solution)/shard_map/all_to_all | solution.py:587
  52.4 10.3 %collective-permute-start.7 = (f32[3,24,128]{2,1,0:T(8,128)S(1)}, f32[3,24,128]{2,1,0:T(8,128)S(1)}, u32[]{:S(2)}, u32[]{:S(2)}) collective-permute-start(f32[3,24,128]{2,1,0:T(8,128)S(1)} %get-tuple-element.45.svalues), channel_id=1, source_target_pairs={{0,15},{1,14},{2,13},{3,12},{4,11},{5,10},{6,9},{7,8},{8,23},{9,22... | collective-permute-start | bytes 110600 | tf_op jit(solution)/shard_map/ppermute | solution.py:588
